TPU v7x, 256 devices: a whole 4x4x8 slice. The times are simulated.
256 devices in a mesh: dp: 16 (over z, x_lo), seq: 16 (over y, x_hi, core).
Axes of the slice: x: 4 (x_hi: 2, x_lo: 2; x = x_hi * 2 + x_lo), y: 4, z: 8, core: 2. Of those that a mesh axis runs over, the one named last changes fastest.
Arguments:
- states: bfloat16 [16, 1024, 4096], P('dp', 'seq'), may hold values from -6 to 6
- kv_weight: bfloat16 [4096, 1536], P('seq'), may hold values from -0.09375 to 0.09375
- queries: bfloat16 [16, 4096, 768], P('dp', 'seq'), may hold values from -150 to 150
- hidden: bfloat16 [16, 4096, 1536], P('dp', 'seq'), may hold values from -3 to 3
- out_proj: bfloat16 [768, 1536], P('seq'), may hold values from -0.21875 to 0.21875
- disc_in: bfloat16 [1536, 1024], replicated, may hold values from -0.15625 to 0.15625
- conv_weight: bfloat16 [41, 64, 1024], replicated, may hold values from -0.125 to 0.125
- score_weight: float32 [1024], replicated, may hold values from -0.1875 to 0.1875
- frame_len: int32 [16], replicated, may hold values from 1024 to 4096, as said below
- state_len: int32 [16], replicated, may hold values from 256 to 1024, as said below
Outputs:
- grad_out_proj: float32 [768, 1536], P('seq')
- loss_mean: float32 [], replicated
Inputs may be any that keep to these rules, and one draw needn't show every extreme that they name: `frame_len`: one clip has all 4096 frames live in every draw. `state_len`: one clip has all 1024 backbone frames live in every draw.
All inputs are finite; a program needn't handle non-finite values.
Results may differ from a plain program's by a relative error of at most 0.005.
Values may be sent and summed in bfloat16 or wider, within the bound.
No kernel may reach another device: no remote copies, remote signals or barrier semaphores. Data moves between devices by JAX's collectives and lax.ppermute only.
A program may use at most 128 MiB of HBM per device.

v0:
```python
import math

import jax
import jax.numpy as jnp
from jax import lax
from jax.sharding import PartitionSpec as P

HEAD_DIM = 128
GROUPS = 16
STRIDE = 4


def with_halo(array, sides, width):
    for axis, dim in sides:
        size, length = (lax.axis_size(axis), array.shape[dim])
        up = [(i, (i + 1) % size) for i in range(size - 1)]
        down = [(j, i) for i, j in up]
        last = lax.slice_in_dim(array, length - width, length, axis=dim)
        initial = lax.slice_in_dim(array, 0, width, axis=dim)
        before = lax.ppermute(last, axis, up)
        after = lax.ppermute(initial, axis, down)
        array = jnp.concatenate([before, array, after], axis=dim)
    return array


def regroup(weight_taps, group_count):
    kernel, group_in, channels = weight_taps.shape
    blocks = weight_taps.reshape(kernel, group_in, group_count, channels // group_count)
    turned = jnp.transpose(blocks, (0, 3, 2, 1)).reshape(kernel, channels // group_count, channels)
    return jnp.flip(turned, 0)


def disc_conv(padded, weight_taps, group_count, stride):
    return lax.conv_general_dilated(
        padded[None],
        weight_taps,
        (stride,),
        "VALID",
        dimension_numbers=("NWC", "WIO", "NWC"),
        feature_group_count=group_count,
        preferred_element_type=jnp.float32,
    )[0]


def disc_back(grad_wide, flipped, group_count, stride, high_pad):
    return lax.conv_general_dilated(
        grad_wide[None],
        flipped,
        (1,),
        [(0, high_pad)],
        lhs_dilation=(stride,),
        dimension_numbers=("NWC", "WIO", "NWC"),
        feature_group_count=group_count,
        preferred_element_type=jnp.float32,
    )[0]


def attend(query, keys_values, live_keys):
    row_count, att_width = query.shape
    head_count = att_width // HEAD_DIM
    query_heads = query.astype(jnp.float32).reshape(row_count, head_count, HEAD_DIM)
    key_heads = keys_values[:, :att_width].reshape(-1, head_count, HEAD_DIM)
    value_heads = keys_values[:, att_width:].reshape(-1, head_count, HEAD_DIM)
    scores = jnp.einsum(
        "qhd,khd->hqk", query_heads, key_heads, precision=lax.Precision.HIGHEST
    ) / math.sqrt(HEAD_DIM)
    scores = jnp.where(live_keys[None, None, :], scores, -1e30)
    row_max = jnp.max(scores, axis=2, keepdims=True)
    expo_scores = jnp.where(live_keys[None, None, :], jnp.exp(scores - row_max), 0.0)
    denom = jnp.sum(expo_scores, axis=2)
    weights = expo_scores.astype(jnp.bfloat16)
    mixed_heads = jnp.einsum(
        "hqk,khd->qhd", weights.astype(jnp.float32), value_heads, precision=lax.Precision.HIGHEST
    )
    mixed_heads = mixed_heads / jnp.transpose(denom)[:, :, None]
    return mixed_heads.reshape(row_count, att_width).astype(jnp.bfloat16)


def shards(
    states,
    kv_weight,
    queries,
    hidden,
    out_proj,
    disc_in,
    conv_weight,
    score_weight,
    frame_len,
    state_len,
):
    states_local = states[0]
    frame_count = hidden.shape[1]
    clip_index = lax.axis_index("dp")
    seq_index = lax.axis_index("seq")
    clip_pick = jnp.arange(frame_len.shape[0]) == clip_index
    clip_frames = jnp.sum(jnp.where(clip_pick, frame_len, 0))
    clip_states = jnp.sum(jnp.where(clip_pick, state_len, 0))
    sliced = states_local
    projected = jnp.dot(
        sliced,
        lax.all_gather(kv_weight, "seq", axis=0, tiled=True),
        preferred_element_type=jnp.float32,
    )
    keys_values = lax.all_gather(projected, "seq", axis=0, tiled=True)
    live_keys = jnp.arange(keys_values.shape[0]) < clip_states
    attended = attend(queries[0], keys_values, live_keys)
    sliced = attended
    lifted = hidden[0].astype(jnp.float32) + jnp.dot(
        sliced,
        lax.all_gather(out_proj, "seq", axis=0, tiled=True),
        preferred_element_type=jnp.float32,
    )
    mixed_rows = lifted.astype(jnp.bfloat16)
    frame_ids = seq_index * frame_count + jnp.arange(frame_count)
    inside = (frame_ids < clip_frames)[:, None]
    disc_feed = jnp.where(
        inside, jnp.dot(mixed_rows, disc_in, preferred_element_type=jnp.float32), 0.0
    ).astype(jnp.bfloat16)
    margin_rows = (conv_weight.shape[0] - 1) // 2
    padded = with_halo(disc_feed, (("seq", 0),), margin_rows)
    pre = disc_conv(padded, conv_weight, GROUPS, STRIDE)
    sigmoid_pre = jax.nn.sigmoid(pre)
    critic = jnp.dot(pre * sigmoid_pre, score_weight, precision=lax.Precision.HIGHEST)
    out_count = pre.shape[0]
    valid_out = STRIDE * (seq_index * out_count + jnp.arange(out_count)) < clip_frames
    shortfall = 1.0 - critic
    local_loss = jnp.sum(jnp.where(valid_out, shortfall * shortfall, 0.0))
    push_score = jnp.where(valid_out, -2.0 * shortfall, 0.0)
    slope_pre = sigmoid_pre * (1.0 + pre * (1.0 - sigmoid_pre))
    grad_pre = (push_score[:, None] * score_weight[None, :] * slope_pre).astype(jnp.bfloat16)
    reach_out = margin_rows // STRIDE
    grad_wide = with_halo(grad_pre, (("seq", 0),), reach_out)
    grad_feed = disc_back(grad_wide, regroup(conv_weight, GROUPS), GROUPS, STRIDE, STRIDE - 1)
    grad_feed = jnp.where(inside, grad_feed, 0.0).astype(jnp.bfloat16)
    grad_mixed = lax.dot_general(
        grad_feed, disc_in, (((1,), (1,)), ((), ())), preferred_element_type=jnp.float32
    ).astype(jnp.bfloat16)
    full_term = lax.dot_general(
        attended, grad_mixed, (((0,), (0,)), ((), ())), preferred_element_type=jnp.float32
    )
    summed_clips = lax.psum(full_term, "dp")
    grad_proj = lax.psum_scatter(summed_clips, "seq", scatter_dimension=0, tiled=True)
    total_loss = lax.psum(local_loss, ("dp", "seq"))
    counted = jnp.sum((frame_len + STRIDE - 1) // STRIDE).astype(jnp.float32)
    return (grad_proj, total_loss / counted)


def solution(mesh):
    return jax.shard_map(
        shards,
        mesh=mesh,
        in_specs=(
            P("dp", "seq", None),
            P("seq", None),
            P("dp", "seq", None),
            P("dp", "seq", None),
            P("seq", None),
            P(),
            P(),
            P(),
            P(),
            P(),
        ),
        out_specs=(P("seq", None), P()),
        check_vma=False,
    )
```

profile of v0, /device:TPU:32, one launch (start us, length us, event | category | flops | bytes accessed | tf_op | source)
XLA Modules:
  0.0 665.6 jit_solution(14477105413284666974)
XLA Ops:
  7.2 0.0 all-gather.4.cloned.1.call-start
  7.2 0.7 all-gather.4.cloned.1.call-update
  7.9 0.0 all-gather.6.cloned.1.call-start
  8.0 101.2 %all-gather.4.cloned.1.call-done = bf16[4096,1536]{1,0:T(8,128)(2,1)} async-done(((bf16[256,1536]{1,0:T(8,128)(2,1)}), bf16[4096,1536]{1,0:T(8,128)(2,1)}) %all-gather.4.cloned.1.call-update) | async-done | bytes 12582928 | tf_op jit(solution)/shard_map/all_gather | solution.py:101
  109.2 7.8 %fusion.31 = f32[64,1536]{1,0:T(8,128)} fusion(bf16[4096,1536]{1,0:T(8,128)(2,1)} %all-gather.4.cloned.1.call-done, bf16[1,64,4096]{2,1,0:T(8,128)(2,1)} %param.10), kind=kOutput, calls=%fused_computation.30 | convolution fusion | flops 805306368 | bytes 13500416 | tf_op jit(solution)/shard_map/dot_general | solution.py:99
  117.0 0.0 all-gather.8.cloned.1.call-start
  117.0 0.7 all-gather.8.cloned.1.call-update
  117.7 0.0 reduce-scatter.2.cloned.1.call-start
  117.7 1.2 copy.20
  118.9 0.7 fusion.42
  119.6 0.7 add_compare_fusion
  120.3 0.7 iota_compare_fusion
  121.0 63.0 %all-gather.6.cloned.1.call-done = f32[1024,1536]{1,0:T(8,128)} async-done(((f32[64,1536]{1,0:T(8,128)}), f32[1024,1536]{1,0:T(8,128)}) %all-gather.6.cloned.1.call-update) | async-done | bytes 6291472 | tf_op jit(solution)/shard_map/all_gather | solution.py:104
  184.0 5.9 fusion.48
  190.0 3.5 copy.19
  193.5 3.6 copy.18
  197.1 4.6 fusion.52
  201.7 2.4 fusion.51
  204.1 1.7 fusion.24
  205.8 32.3 %all-gather.8.cloned.1.call-done = bf16[768,1536]{1,0:T(8,128)(2,1)} async-done(((bf16[48,1536]{1,0:T(8,128)(2,1)}), bf16[768,1536]{1,0:T(8,128)(2,1)}) %all-gather.8.cloned.1.call-update) | async-done | bytes 2359312 | tf_op jit(solution)/shard_map/all_gather | solution.py:110
  238.1 4.3 fusion.23
  242.4 1.5 fusion.49
  243.9 2.1 collective-permute-start
  246.0 1.3 collective-permute-start.1
  247.3 14.8 %shard_map.115 = bf16[41,64,16,64]{3,2,1,0:T(8,128)(2,1)} reshape(bf16[41,64,1024]{2,1,0:T(8,128)(2,1)} %param.16) | data formatting | bytes 10747904 | tf_op jit(solution)/shard_map/shard_map
  262.1 2.0 pad_maximum_fusion
  264.1 2.3 copy.24
  266.4 6.3 copy.25
  272.7 18.9 %fusion.27 = f32[64,16,64]{2,1,0:T(8,128)} fusion(bf16[1,296,16,64]{3,0,2,1:T(2,128)(2,1)} %copy.25, bf16[41,64,16,64]{3,2,1,0:T(8,128)(2,1)} %shard_map.115), kind=kOutput, calls=%fused_computation.25 | convolution fusion | flops 343932928 | bytes 6242304 | tf_op jit(solution)/shard_map/conv_general_dilated | solution.py:34
  291.6 1.2 squeeze.12
  292.8 1.6 fusion.41
  294.4 0.1 multiply_convert_fusion
  294.6 3.0 collective-permute-start.2
  297.6 1.3 collective-permute-start.3
  298.9 19.1 %copy.27 = bf16[41,64,16,64]{1,2,3,0:T(8,128)(2,1)} copy(bf16[41,64,16,64]{3,2,1,0:T(8,128)(2,1)} %shard_map.115) | data formatting | bytes 10747904 | tf_op jit(solution)/shard_map/shard_map
  318.1 15.0 %reshape.48 = bf16[41,64,1024]{2,1,0:T(8,128)(2,1)} reshape(bf16[41,64,16,64]{3,2,1,0:T(8,128)(2,1)} %bitcast.55) | data formatting | bytes 10747904 | tf_op jit(solution)/shard_map/reshape | solution.py:29
  333.1 5.9 rev.6
  339.0 14.8 %rev.7 = bf16[41,64,16,64]{3,2,1,0:T(8,128)(2,1)} reshape(bf16[41,64,1024]{2,1,0:T(8,128)(2,1)} %rev.6) | data formatting | bytes 10747904 | tf_op jit(solution)/shard_map/jit(_flip)/rev | solution.py:30
  353.8 1.2 broadcast_in_dim.69
  355.0 54.6 %fusion.1 = bf16[1,256,16,64]{3,0,2,1:T(2,128)(2,1)} fusion(bf16[1,74,16,64]{3,0,2,1:T(2,128)(2,1)} %broadcast_in_dim.69, bf16[41,64,16,64]{3,2,1,0:T(8,128)(2,1)} %rev.7), kind=kOutput, calls=%fused_computation.1 | convolution fusion | flops 343932928 | bytes 6049792 | tf_op jit(solution)/shard_map/conv_general_dilated | solution.py:46
  409.7 5.7 copy.30
  415.3 2.1 copy.31
  417.4 4.8 fusion.16
  422.2 0.0 all-reduce.2.cloned.1.call-start
  422.3 97.0 %reduce-scatter.2.cloned.1.call-done = f32[48,1536]{1,0:T(8,128)} async-done(((f32[768,1536]{1,0:T(8,128)}), f32[48,1536]{1,0:T(8,128)}) %reduce-scatter.2.cloned.1.call-update) | async-done | bytes 294928 | tf_op jit(solution)/shard_map/reduce_scatter | solution.py:142
  520.0 76.1 %psum.15 = f32[]{:T(128)} all-reduce(f32[]{:T(128)} %get-tuple-element.10), channel_id=1, replica_groups=mesh['dp'=16,'seq'=16] {'dp','seq'}, use_global_device_ids=true, to_apply=%region_7.8 | all-reduce | flops 1 | bytes 8 | tf_op jit(solution)/shard_map/psum | solution.py:143
  596.8 59.0 %all-reduce.2.cloned.1.call-done = f32[48,1536]{1,0:T(8,128)} async-done(((f32[48,1536]{1,0:T(8,128)}), f32[48,1536]{1,0:T(8,128)}) %all-reduce.2.cloned.1.call-update) | async-done | bytes 294928 | tf_op jit(solution)/shard_map/psum | solution.py:141
  655.8 1.7 copy.42
  (27 shorter events, 0.2 us)
Async XLA Ops:
  7.2 231.0 %copy-start = (bf16[1536,1024]{1,0:T(8,128)(2,1)S(1)}, bf16[1536,1024]{1,0:T(8,128)(2,1)}, u32[]{:S(2)}) copy-start(bf16[1536,1024]{1,0:T(8,128)(2,1)} %param.15) | copy-start | bytes 9437188
  7.2 102.0 %all-gather.4.cloned.1.call-start = ((), (), s32[]{:S(2)}) async-start(), calls=%async_computation.1 | async-start | bytes 13369344 | tf_op jit(solution)/shard_map/all_gather | solution.py:101
  7.9 111.0 %copy-start.7 = (s32[16]{0:T(128)S(1)}, s32[16]{0:T(128)}, u32[]{:S(2)}) copy-start(s32[16]{0:T(128)} %param.18) | copy-start | bytes 196
  7.9 111.0 %copy-start.8 = (s32[16]{0:T(128)S(1)}, s32[16]{0:T(128)}, u32[]{:S(2)}) copy-start(s32[16]{0:T(128)} %param.19) | copy-start | bytes 196
  7.9 176.1 %all-gather.6.cloned.1.call-start = ((), (), s32[]{:S(2)}) async-start(), calls=%async_computation.2 | async-start | bytes 6684672 | tf_op jit(solution)/shard_map/all_gather | solution.py:104
  117.0 121.2 %all-gather.8.cloned.1.call-start = ((), (), s32[]{:S(2)}) async-start(), calls=%async_computation.3 | async-start | bytes 2506752 | tf_op jit(solution)/shard_map/all_gather | solution.py:110
  117.7 401.6 %reduce-scatter.2.cloned.1.call-start = ((), (), s32[]{:S(2)}) async-start(), calls=%async_computation.4 | async-start | bytes 5013504 | tf_op jit(solution)/shard_map/reduce_scatter | solution.py:142
  120.3 117.8 %copy-start.5 = (pred[256]{0:T(512)(128)(4,1)}, pred[256]{0:T(512)(128)(4,1)S(1)}, u32[]{:S(2)}) copy-start(pred[256]{0:T(512)(128)(4,1)S(1)} %add_compare_fusion) | copy-start | bytes 772
  201.7 2.4 copy-start.1
  205.8 36.6 %copy-start.2 = (bf16[256,6,128]{0,2,1:T(8,128)(2,1)}, bf16[256,6,128]{0,2,1:T(8,128)(2,1)S(1)}, u32[]{:S(2)}) copy-start(bf16[256,6,128]{0,2,1:T(8,128)(2,1)S(1)} %fusion.24) | copy-start | bytes 1179652
  243.9 18.2 %collective-permute-start = (bf16[20,1024]{1,0:T(8,128)(2,1)}, bf16[20,1024]{1,0:T(8,128)(2,1)S(1)}, u32[]{:S(2)}, u32[]{:S(2)}) collective-permute-start(bf16[20,1024]{1,0:T(8,128)(2,1)} %get-tuple-element.6), channel_id=1, source_target_pairs={{0,1},{1,2},{2,3},{3,4},{4,5},{5,6},{6,7},{7,8},{8,9},{9,10},{10,1... | collective-permute-start | bytes 122888 | tf_op jit(solution)/shard_map/ppermute | solution.py:20
  246.0 16.1 %collective-permute-start.1 = (bf16[20,1024]{1,0:T(8,128)(2,1)}, bf16[20,1024]{1,0:T(8,128)(2,1)S(1)}, u32[]{:S(2)}, u32[]{:S(2)}) collective-permute-start(bf16[20,1024]{1,0:T(8,128)(2,1)} %get-tuple-element.7), channel_id=1, source_target_pairs={{1,0},{2,1},{3,2},{4,3},{5,4},{6,5},{7,6},{8,7},{9,8},{10,9},{11,1... | collective-permute-start | bytes 122888 | tf_op jit(solution)/shard_map/ppermute | solution.py:21
  272.7 20.1 %copy-start.4 = (f32[1024]{0:T(1024)S(1)}, f32[1024]{0:T(1024)}, u32[]{:S(2)}) copy-start(f32[1024]{0:T(1024)} %param.17) | copy-start | bytes 12292
  294.6 59.2 %collective-permute-start.2 = (bf16[5,1024]{1,0:T(8,128)(2,1)S(1)}, bf16[5,1024]{1,0:T(8,128)(2,1)S(1)}, u32[]{:S(2)}, u32[]{:S(2)}) collective-permute-start(bf16[5,1024]{1,0:T(8,128)(2,1)S(1)} %get-tuple-element.8), channel_id=1, source_target_pairs={{0,1},{1,2},{2,3},{3,4},{4,5},{5,6},{6,7},{7,8},{8,9},{9,10},{10,1... | collective-permute-start | bytes 30728 | tf_op jit(solution)/shard_map/ppermute | solution.py:20
  297.6 56.2 %collective-permute-start.3 = (bf16[5,1024]{1,0:T(8,128)(2,1)S(1)}, bf16[5,1024]{1,0:T(8,128)(2,1)S(1)}, u32[]{:S(2)}, u32[]{:S(2)}) collective-permute-start(bf16[5,1024]{1,0:T(8,128)(2,1)S(1)} %get-tuple-element.9), channel_id=1, source_target_pairs={{1,0},{2,1},{3,2},{4,3},{5,4},{6,5},{7,6},{8,7},{9,8},{10,9},{11,1... | collective-permute-start | bytes 30728 | tf_op jit(solution)/shard_map/ppermute | solution.py:21
  409.7 7.7 %copy-start.3 = (bf16[256,6,128]{0,2,1:T(8,128)(2,1)S(1)}, bf16[256,6,128]{0,2,1:T(8,128)(2,1)}, u32[]{:S(2)}) copy-start(bf16[256,6,128]{0,2,1:T(8,128)(2,1)} %copy-done.2) | copy-start | bytes 1179652
  409.7 7.7 %copy-start.6 = (pred[256]{0:T(512)(128)(4,1)S(1)}, pred[256]{0:T(512)(128)(4,1)}, u32[]{:S(2)}) copy-start(pred[256]{0:T(512)(128)(4,1)} %copy-done.5) | copy-start | bytes 772
  422.2 233.6 %all-reduce.2.cloned.1.call-start = ((), (), s32[]{:S(2)}) async-start(), calls=%async_computation.5 | async-start | bytes 589824 | tf_op jit(solution)/shard_map/psum | solution.py:141
Sparse Core Ops, SparseCore 0:
  10.8 98.3 all-gather.3
  117.1 66.9 all-gather.5
  186.8 51.2 all-gather.7
  422.4 96.9 reduce-scatter.1
  522.0 133.8 all-reduce.1
where the time goes:
time: 678 us; the launch traced here: 666 us
  waiting for transfers between devices  354 us (52%)
  local copies, waits for them, and re-layouts  106 us (16%)
  matrix products  98.3 us (14%)
  blocking collectives  76.1 us (11%)
  between operations  16.8 us (2%)
  starting transfers between devices  7.96 us (1%)
    all_gather x1, waiting for transfers between devices, shards(): lax.all_gather(kv_weight, 'seq', axis=0, tiled=True)  101 us
    reduce_scatter x1, waiting for transfers between devices, shards(): lax.psum_scatter(summed_clips, 'seq', scatter_dimension=0, tiled=True)  97 us
    psum x1, blocking collectives, shards(): total_loss = lax.psum(local_loss, ('dp', 'seq'))  76.1 us
    all_gather x1, waiting for transfers between devices, shards(): keys_values = lax.all_gather(projected, 'seq', axis=0, tiled=True)  63 us
    psum x1, waiting for transfers between devices, shards(): summed_clips = lax.psum(full_term, 'dp')  59 us
    conv_general_dilated x1, matrix products, disc_back(): lax.conv_general_dilated(grad_wide[None], flipped, (1,), [(0, high_pad)],...  54.6 us
    another operation x2, local copies, waits for them, and re-layouts  33.9 us
    all_gather x1, waiting for transfers between devices, shards(): lax.all_gather(out_proj, 'seq', axis=0, tiled=True)  32.3 us
  transfers between devices with their start and end apart: 9, of which 5 were waited for; matrix products, arithmetic and copies ran while one was open for 14% of the time, Pallas kernels for 0%

commit v1 on v0

v1 whole, which is shorter than its diff:
```python
import functools
import math

import jax
import jax.numpy as jnp
from jax import lax
from jax.experimental import pallas as pl
from jax.experimental.pallas import tpu as pltpu
from jax.sharding import PartitionSpec as P

HEAD_DIM = 128
HALF_HEADS = 3
HALF_ATT = HEAD_DIM * HALF_HEADS
GROUP_CH = 64
STRIDE = 4
TAPS = 41
TAP_SETS = 12
MARGIN = 20
HALO = 40
REACH = 5
F32 = jnp.float32
BF16 = jnp.bfloat16
VMEM_LIMIT = 50 * 1024 * 1024


def params():
    return pltpu.CompilerParams(vmem_limit_bytes=VMEM_LIMIT)


def smem():
    return pl.BlockSpec(memory_space=pltpu.SMEM)


def vmem():
    return pl.BlockSpec(memory_space=pltpu.VMEM)


def low_lanes(shape):
    return lax.broadcasted_iota(jnp.int32, shape, 1) % 128 < 64


def roll_half(x):
    return pltpu.roll(x, 64, 1)


def arrange_kernel(w_ref, o_ref):
    low = low_lanes((GROUP_CH, 128))
    zero = jnp.zeros((GROUP_CH, 128), F32)

    def tap(k):
        return w_ref[k].astype(F32) if k < TAPS else zero

    for b in range(STRIDE):
        for pair in range(TAP_SETS // 2):
            first = tap(8 * pair + b)
            second = tap(8 * pair + 4 + b)
            rows, lanes = (slice(b * 64, b * 64 + 64), slice(pair * 128, pair * 128 + 128))
            o_ref[0, rows, lanes] = jnp.where(low, first, roll_half(second)).astype(BF16)
            o_ref[1, rows, lanes] = jnp.where(low, roll_half(first), second).astype(BF16)


def arrange(conv_weight):
    taps, group_in, channels = conv_weight.shape
    groups = channels // GROUP_CH
    return pl.pallas_call(
        arrange_kernel,
        grid=(channels // 128,),
        in_specs=[pl.BlockSpec((taps, group_in, 128), lambda l: (0, 0, l))],
        out_specs=pl.BlockSpec((2, STRIDE * 64, TAP_SETS * 64), lambda l: (l, 0, 0)),
        out_shape=jax.ShapeDtypeStruct((groups, STRIDE * 64, TAP_SETS * 64), BF16),
        compiler_params=params(),
        cost_estimate=pl.CostEstimate(flops=20_000_000, bytes_accessed=20_000_000, transcendentals=0),
    )(conv_weight)


def project_kernel(cols_ref, *refs):
    states, weights, o_ref = (refs[:4], refs[4:12], refs[12])
    total = None
    for i, weight in enumerate(weights):
        for half in range(2):
            start = pl.multiple_of(cols_ref[2 * i + half], 256)
            left = jnp.concatenate([s[:, pl.ds(start, 256)] for s in states], axis=0)
            part = jnp.dot(left, weight[256 * half : 256 * half + 256, :], preferred_element_type=F32)
            total = part if total is None else total + part
    o_ref[...] = total


def project(cols, states, weights):
    return pl.pallas_call(
        project_kernel,
        in_specs=[smem()] + [vmem()] * 12,
        out_specs=vmem(),
        out_shape=jax.ShapeDtypeStruct((256, HALF_ATT), F32),
        compiler_params=params(),
        cost_estimate=pl.CostEstimate(flops=800_000_000, bytes_accessed=6_000_000, transcendentals=0),
    )(cols, *states, *weights)


def split(x):
    high = x.astype(BF16)
    return high, (x - high.astype(F32)).astype(BF16)


def attend_kernel(meta_ref, q_ref, *refs):
    mine, other, o_ref = (refs[:4], refs[4:8], refs[8])
    live, core, half, row = (meta_ref[0], meta_ref[1], meta_ref[2], meta_ref[3])
    first = core == 0
    keys, values = ([], [])
    for m, o in zip(mine, other):
        keys.append(jnp.where(first, m[...], o[...]))
        turned = []
        for j in range(4):
            k = slice(64 * (j ^ 1), 64 * (j ^ 1) + 64)
            turned.append(jnp.where(first, o[k, :], m[k, :]))
        values.extend(turned)
    key_high, key_low = split(jnp.concatenate(keys, axis=0))
    value_high, value_low = split(jnp.concatenate(values, axis=0))
    spot = lax.broadcasted_iota(jnp.int32, (1, 1024), 1)
    hop, block, rest = (spot // 256, (spot // 64) % 4, spot % 64)
    where_y = (row - hop + 4) % 4
    where_h = (half + block // 2) % 2
    position = ((where_y * 2 + where_h) * 2 + block % 2) * 64 + rest
    alive = position < live
    contract = (((1,), (1,)), ((), ()))
    rows = 112
    for start in range(0, q_ref.shape[0], rows):
        q = q_ref[start : start + rows, :]
        scores = lax.dot_general(q, key_high, contract, preferred_element_type=F32)
        scores = scores + lax.dot_general(q, key_low, contract, preferred_element_type=F32)
        scores = jnp.where(alive, scores * (1.0 / math.sqrt(HEAD_DIM)), -1e30)
        top = jnp.max(scores, axis=1, keepdims=True)
        expo = jnp.where(alive, jnp.exp(scores - top), 0.0)
        denom = jnp.sum(expo, axis=1, keepdims=True)
        weights = expo.astype(BF16)
        mixed = jnp.dot(weights, value_high, preferred_element_type=F32)
        mixed = mixed + jnp.dot(weights, value_low, preferred_element_type=F32)
        o_ref[start : start + rows, :] = (mixed / denom).astype(BF16)


def attend(meta, query, mine, other):
    rows, width = query.shape
    block = lambda n: pl.BlockSpec((n, HEAD_DIM), lambda h: (0, h))
    return pl.pallas_call(
        attend_kernel,
        grid=(width // HEAD_DIM,),
        in_specs=[smem(), block(rows)] + [block(256)] * 8,
        out_specs=block(rows),
        out_shape=jax.ShapeDtypeStruct((rows, width), BF16),
        compiler_params=params(),
        cost_estimate=pl.CostEstimate(
            flops=8 * rows * 1024 * width, bytes_accessed=4_000_000, transcendentals=rows * 3072
        ),
    )(meta, query, *mine, *other)


def critic_kernel(
    meta_ref, lifted_ref, mine_ref, other_ref, proj_ref, conv_ref, score_ref,
    out_ref, loss_ref,
    feed_s, y_s, pre_s, grad_s, turned_s, back_s, att_s,
):
    live, first_frame, half = (meta_ref[0], meta_ref[1], meta_ref[2])
    total_frames = meta_ref[3]
    ext = lifted_ref.shape[0]
    own_out = (ext - 2 * HALO) // STRIDE
    tiles = lifted_ref.shape[1] // 128
    feed = lifted_ref[...]
    feed = feed + jnp.dot(mine_ref[...], proj_ref[half], preferred_element_type=F32)
    feed = feed + jnp.dot(other_ref[...], proj_ref[1 - half], preferred_element_type=F32)
    frame = first_frame - HALO + lax.broadcasted_iota(jnp.int32, (ext, 1), 0)
    inside = (frame >= 0) & (frame < live)
    feed = jnp.where(inside, feed, 0.0).astype(BF16).astype(F32)
    for i in range(tiles):
        feed_s[i, :ext, :] = feed[:, 128 * i : 128 * i + 128]
        feed_s[i, ext:, :] = jnp.zeros((feed_s.shape[1] - ext, 128), F32)
    rows = y_s.shape[0]
    low = low_lanes((rows, 128))
    low_out = low_lanes((80, 128))

    @pl.loop(0, tiles)
    def _(tile):
        lanes = pl.ds(pl.multiple_of(tile * 128, 128), 128)
        phase = [feed_s[tile, pl.ds(b, rows, stride=STRIDE), :] for b in range(STRIDE)]
        turned = [roll_half(p) for p in phase]
        even = [jnp.where(low, phase[b], turned[b + 1]) for b in (0, 2)]
        odd = [jnp.where(low, turned[b], phase[b + 1]) for b in (0, 2)]
        sums = []
        for g, pieces in enumerate((even, odd)):
            left = jnp.concatenate(pieces, axis=1).astype(BF16)
            y_s[...] = jnp.dot(left, conv_ref[2 * tile + g], preferred_element_type=F32)
            at, after = (None, None)
            for pair in range(TAP_SETS // 2):
                cols = slice(128 * pair, 128 * pair + 128)
                a = y_s[2 * pair : 2 * pair + 80, cols]
                b = y_s[2 * pair + 1 : 2 * pair + 81, cols]
                at = a if at is None else at + a
                after = b if after is None else after + b
            sums.append((at, after))
        pre_even = sums[0][0] + roll_half(sums[0][1])
        pre_odd = roll_half(sums[1][0]) + sums[1][1]
        pre_s[:, lanes] = jnp.where(low_out, pre_even, pre_odd)

    pre = pre_s[...]
    sig = 1.0 / (1.0 + jnp.exp(-pre))
    score = score_ref[...]
    critic = jnp.sum(pre * sig * score, axis=1, keepdims=True)
    slot = lax.broadcasted_iota(jnp.int32, (80, 1), 0)
    frame_out = first_frame - STRIDE * REACH + STRIDE * slot
    valid = (frame_out >= 0) & (frame_out < total_frames) & (frame_out < live) & (slot < own_out + 2 * REACH)
    shortfall = 1.0 - critic
    own = valid & (slot >= REACH) & (slot < REACH + own_out)
    loss = jnp.sum(jnp.where(own, shortfall * shortfall, 0.0), axis=0, keepdims=True)
    loss_ref[...] = jnp.broadcast_to(loss, loss_ref.shape)
    push = jnp.where(valid, -2.0 * shortfall, 0.0)
    grad = push * score * (sig * (1.0 + pre * (1.0 - sig)))
    grad = jnp.where(valid, grad, 0.0).astype(BF16).astype(F32)
    grad_s[:8, :] = jnp.zeros((8, grad_s.shape[1]), F32)
    grad_s[8:, :] = grad

    contract = (((1,), (1,)), ((), ()))
    low_back = low_lanes((own_out, 128))

    @pl.loop(0, tiles)
    def _(tile):
        lanes = pl.ds(pl.multiple_of(tile * 128, 128), 128)
        turned_s[...] = roll_half(grad_s[:, lanes])
        even, odd = ([], [])
        for pair in range(TAP_SETS // 2):
            up, down = (18 - 2 * pair, 17 - 2 * pair)
            even.append(
                jnp.where(low_back, grad_s[up : up + own_out, lanes], turned_s[down : down + own_out, :])
            )
            odd.append(
                jnp.where(low_back, turned_s[up : up + own_out, :], grad_s[down : down + own_out, lanes])
            )
        back = []
        for g, pieces in enumerate((even, odd)):
            left = jnp.concatenate(pieces, axis=1).astype(BF16)
            back.append(
                lax.dot_general(left, conv_ref[2 * tile + g], contract, preferred_element_type=F32)
            )
        step = lax.broadcasted_iota(jnp.int32, (own_out, 1), 0)
        for b in range(STRIDE):
            cols = slice(128 * (b // 2), 128 * (b // 2) + 128)
            e, o = (back[0][:, cols], back[1][:, cols])
            both = jnp.where(low_back, e, roll_half(o)) if b % 2 == 0 else jnp.where(low_back, roll_half(e), o)
            both = jnp.where(first_frame + STRIDE * step + b < live, both, 0.0)
            back_s[b * own_out : (b + 1) * own_out, lanes] = both.astype(BF16)

    for part, ref in enumerate((mine_ref, other_ref)):
        own_rows = ref[...].astype(F32)[HALO : ext - HALO, :]
        for c in range(HALF_HEADS):
            cols = slice(c * 128, c * 128 + 128)
            att_s[...] = own_rows[:, cols]
            left = jnp.concatenate(
                [att_s[pl.ds(b, own_out, stride=STRIDE), :] for b in range(STRIDE)], axis=0
            )
            left = jnp.transpose(left).astype(BF16)
            which = half if part == 0 else 1 - half
            out_ref[which, cols, :] = jnp.dot(left, back_s[...], preferred_element_type=F32)


def critic(meta, lifted, mine, other, proj, conv, score):
    ext, channels = lifted.shape
    own = ext - 2 * HALO
    return pl.pallas_call(
        critic_kernel,
        in_specs=[smem()] + [vmem()] * 6,
        out_specs=[vmem(), vmem()],
        out_shape=[
            jax.ShapeDtypeStruct((2, HALF_ATT, channels), F32),
            jax.ShapeDtypeStruct((8, 128), F32),
        ],
        scratch_shapes=[
            pltpu.VMEM((channels // 128, 384, 128), F32),
            pltpu.VMEM((96, TAP_SETS * 64), F32),
            pltpu.VMEM((80, channels), F32),
            pltpu.VMEM((88, channels), F32),
            pltpu.VMEM((88, 128), F32),
            pltpu.VMEM((own, channels), BF16),
            pltpu.VMEM((own, 128), F32),
        ],
        compiler_params=params(),
        cost_estimate=pl.CostEstimate(
            flops=3_000_000_000, bytes_accessed=14_000_000, transcendentals=100_000
        ),
    )(meta, lifted, mine, other, proj, conv, score)


def shards(
    states, kv_weight, queries, hidden, out_proj, disc_in, conv_weight, score_weight, frame_len, state_len
):
    frames = hidden.shape[1]
    dp_size, seq_size = (lax.axis_size("dp"), lax.axis_size("seq"))
    clip, seq = (lax.axis_index("dp"), lax.axis_index("seq"))
    core, half, row = (seq % 2, (seq // 2) % 2, seq // 4)
    pick = jnp.arange(frame_len.shape[0]) == clip
    clip_frames = jnp.sum(jnp.where(pick, frame_len, 0))
    clip_states = jnp.sum(jnp.where(pick, state_len, 0))

    def flip(x, bit):
        return lax.ppermute(x, "seq", [(i, i ^ bit) for i in range(seq_size)])

    def turn(x, hops):
        return lax.ppermute(x, "seq", [(i, (i + 4 * hops) % seq_size) for i in range(seq_size)])

    def across(x):
        pairs = []
        for i in range(dp_size * seq_size):
            d, s = divmod(i, seq_size)
            pairs.append((i, (d ^ 1) * seq_size + (s ^ 2)))
        return lax.ppermute(x, ("dp", "seq"), pairs)

    att = 2 * HALF_ATT
    own_cols = lax.dynamic_slice_in_dim(kv_weight, core * att, att, axis=1)
    partner_cols = lax.dynamic_slice_in_dim(kv_weight, (1 - core) * att, att, axis=1)
    pair_rows = jnp.concatenate([own_cols, flip(partner_cols, 1)], axis=0)
    near = lax.dynamic_slice_in_dim(pair_rows, half * HALF_ATT, HALF_ATT, axis=1)
    far = across(lax.dynamic_slice_in_dim(pair_rows, (1 - half) * HALF_ATT, HALF_ATT, axis=1))
    hops = (1, 3, 2)
    near_blocks = [near] + [turn(near, j) for j in hops]
    far_blocks = [far] + [turn(far, j) for j in hops]

    rows_in = jnp.concatenate([queries[0], hidden[0]], axis=1)
    up = [(i, i + 1) for i in range(seq_size - 1)]
    down = [(i + 1, i) for i in range(seq_size - 1)]
    before = lax.ppermute(rows_in[frames - HALO :], "seq", up)
    after = lax.ppermute(rows_in[:HALO], "seq", down)
    rows_ext = jnp.concatenate([before, rows_in, after], axis=0)
    query_ext, hidden_ext = (rows_ext[:, :att], rows_ext[:, att:])
    query_mine = lax.dynamic_slice_in_dim(query_ext, half * HALF_ATT, HALF_ATT, axis=1)
    query_far = flip(lax.dynamic_slice_in_dim(query_ext, (1 - half) * HALF_ATT, HALF_ATT, axis=1), 2)

    state_far = flip(states[0], 2)
    state_parts = [states[0], flip(states[0], 1), state_far, flip(state_far, 1)]

    proj_own = jnp.dot(out_proj, disc_in, preferred_element_type=F32).astype(BF16)
    proj = lax.all_gather(proj_own, "seq", axis=0, tiled=True).reshape(2, HALF_ATT, disc_in.shape[1])
    lifted = jnp.dot(hidden_ext, disc_in, preferred_element_type=F32)
    conv = arrange(conv_weight)

    cols = []
    for hop in (0,) + hops:
        for flip_half in (0, 1):
            for flip_core in (0, 1):
                where = (((row - hop) % 4) * 2 + (half ^ flip_half)) * 2 + (core ^ flip_core)
                cols.append(where * kv_weight.shape[0])
    blocks = [b for pair in zip(near_blocks, far_blocks) for b in pair]
    mine_kv = project(jnp.stack(cols).astype(jnp.int32), state_parts, blocks)
    got = [mine_kv] + [turn(mine_kv, j) for j in (1, 2, 3)]
    other = [flip(g, 1) for g in got]

    meta = jnp.stack([clip_states, core, half, row]).astype(jnp.int32)
    attended_far = flip(attend(meta, query_far, got, other), 2)
    attended_mine = attend(meta, query_mine, got, other)

    total_frames = frames * seq_size
    meta2 = jnp.stack([clip_frames, seq * frames, half, jnp.int32(total_frames)]).astype(jnp.int32)
    grown, loss = critic(
        meta2, lifted, attended_mine, attended_far, proj, conv, score_weight.reshape(1, -1)
    )

    own_rows = att // seq_size
    channels = disc_in.shape[1]

    def at(x, i):
        return lax.dynamic_index_in_dim(x, i, axis=0, keepdims=False)

    by_core = grown.reshape(seq_size // 2, 2, own_rows, channels)
    pick_core = lambda c: lax.dynamic_index_in_dim(by_core, c, axis=1, keepdims=False)
    total = pick_core(core) + flip(pick_core(1 - core), 1)
    loss = loss + flip(loss, 1)
    by_row = total.reshape(4, 2, own_rows, channels)
    sent = [turn(at(by_row, (row + j) % 4).astype(BF16), j) for j in (1, 2, 3)]
    sent_loss = [turn(loss, j) for j in (1, 2, 3)]
    total = at(by_row, row)
    for s, l in zip(sent, sent_loss):
        total, loss = (total + s.astype(F32), loss + l)
    total = at(total, half) + flip(at(total, 1 - half), 2)
    loss = loss + flip(loss, 2)
    share = own_rows // dp_size
    pieces = total.reshape(dp_size, share, channels)
    loss_row = jnp.broadcast_to(loss[:1, :1], (dp_size, 1, channels))
    pieces = lax.all_to_all(jnp.concatenate([pieces, loss_row], axis=1), "dp", 0, 0, tiled=True)
    pieces = jnp.sum(pieces, axis=0)
    total_loss = pieces[share, 0]
    spread = jnp.broadcast_to(pieces[None, :share], (dp_size, share, channels))
    full = lax.all_to_all(spread, "dp", 0, 0, tiled=True).reshape(own_rows, channels)
    high = lax.reduce_precision(full, 8, 7)
    high, low = (high.astype(BF16), (full - high).astype(BF16))
    contract = (((1,), (1,)), ((), ()))
    grad_proj = lax.dot_general(high, disc_in, contract, preferred_element_type=F32)
    grad_proj = grad_proj + lax.dot_general(low, disc_in, contract, preferred_element_type=F32)
    counted = jnp.sum((frame_len + STRIDE - 1) // STRIDE).astype(F32)
    return (grad_proj, total_loss / counted)


def solution(mesh):
    return jax.shard_map(
        shards,
        mesh=mesh,
        in_specs=(
            P("dp", "seq", None),
            P("seq", None),
            P("dp", "seq", None),
            P("dp", "seq", None),
            P("seq", None),
            P(),
            P(),
            P(),
            P(),
            P(),
        ),
        out_specs=(P("seq", None), P()),
        check_vma=False,
    )
```

time: 678 us -> 227 us (0.33); the launches traced: 666 us -> 223 us
  waiting for transfers between devices: 354 us -> 57.8 us
  matrix products: 98.3 us -> 7.45 us
  local copies, waits for them, and re-layouts: 106 us -> 22.7 us
  blocking collectives: 76.1 us -> 17.8 us
  starting transfers between devices: 7.96 us -> 50.8 us
  Pallas kernels: 0 us -> 37.9 us
    all_gather x3 -> x1, waiting for transfers between devices: 197 us -> 0.01 us  [shards(): lax.all_gather(proj_own, 'seq', axis=0, tiled=True)]
    reduce_scatter x1 -> x0, waiting for transfers between devices: 97 us -> none  [shards(): lax.psum_scatter(summed_clips, 'seq', scatter_dimension=0, tiled=True)]
    psum x1 -> x0, blocking collectives: 76.1 us -> none  [shards(): total_loss = lax.psum(local_loss, ('dp', 'seq'))]
    conv_general_dilated x2 -> x0, matrix products: 73.5 us -> none  [the longest x1 54.6 us: disc_back(): lax.conv_general_dilated(grad_wide[None], flipped, (1,), [(0, high_pad)],...]
    psum x1 -> x0, waiting for transfers between devices: 59 us -> none  [shards(): summed_clips = lax.psum(full_term, 'dp')]
    ppermute x4 -> x32, waiting for transfers between devices: 0.01 us -> 50.1 us  [the longest x15 23 us: turn(): lax.ppermute(x, 'seq', [(i, (i + 4 * hops) % seq_size) for i in range(seq...]
    pallas_call x0 -> x5, Pallas kernels: none -> 37.9 us  [the longest x1 13.1 us: critic(): pl.pallas_call(critic_kernel, in_specs=[smem()] + [vmem()] * 6, out_specs...]
    ppermute x4 -> x32, starting transfers between devices: 7.76 us -> 45.4 us  [the longest x15 25.5 us: turn(): lax.ppermute(x, 'seq', [(i, (i + 4 * hops) % seq_size) for i in range(seq...]
  transfers between devices with their start and end apart: 9 -> 34, of which waited for: 5 -> 13; matrix products, arithmetic and copies ran while one was open for 14% -> 7% of each run, Pallas kernels for 0% -> 11%
where the time goes in v1:
time: 227 us; the launch traced here: 223 us
  waiting for transfers between devices  57.8 us (25%)
  starting transfers between devices  50.8 us (22%)
  Pallas kernels  37.9 us (17%)
  local copies, waits for them, and re-layouts  22.7 us (10%)
  blocking collectives  17.8 us (8%)
  between operations  16.8 us (7%)
  other arithmetic  12.3 us (5%)
  matrix products  7.45 us (3%)
    ppermute x15, starting transfers between devices, turn(): lax.ppermute(x, 'seq', [(i, (i + 4 * hops) % seq_size) for i in range(seq...  25.5 us
    ppermute x15, waiting for transfers between devices, turn(): lax.ppermute(x, 'seq', [(i, (i + 4 * hops) % seq_size) for i in range(seq...  23 us
    ppermute x14, waiting for transfers between devices, flip(): return lax.ppermute(x, 'seq', [(i, i ^ bit) for i in range(seq_size)])  20.7 us
    all_to_all x1, blocking collectives, shards(): lax.all_to_all(jnp.concatenate([pieces, loss_row], axis=1), 'dp', 0, 0, t...  17.8 us
    ppermute x14, starting transfers between devices, flip(): return lax.ppermute(x, 'seq', [(i, i ^ bit) for i in range(seq_size)])  15.2 us
    pallas_call x1, Pallas kernels, critic(): pl.pallas_call(critic_kernel, in_specs=[smem()] + [vmem()] * 6, out_specs...  13.1 us
    pallas_call x2, Pallas kernels, attend(): pl.pallas_call(attend_kernel, grid=(width // HEAD_DIM,), in_specs=[smem()...  12.3 us
    unnamed x40, local copies, waits for them, and re-layouts  11.4 us
  transfers between devices with their start and end apart: 34, of which 13 were waited for; matrix products, arithmetic and copies ran while one was open for 7% of the time, Pallas kernels for 11%

profile of v1, /device:TPU:32, one launch (start us, length us, event | category | flops | bytes accessed | tf_op | source)
XLA Modules:
  0.0 223.5 jit_solution(5770461639125740039)
XLA Ops:
  7.3 2.2 constant_dynamic-slice_fusion.1
  9.5 2.2 convolution_convert_fusion
  11.7 3.1 %collective-permute-start.3 = (bf16[64,4096]{1,0:T(8,128)(2,1)}, bf16[64,4096]{1,0:T(8,128)(2,1)}, u32[]{:S(2)}, u32[]{:S(2)}) collective-permute-start(bf16[64,4096]{1,0:T(8,128)(2,1)} %bitcast.57), channel_id=1, source_target_pairs={{0,2},{1,3},{2,0},{3,1},{4,6},{5,7},{6,4},{7,5},{8,10},{9,11},{10,... | collective-permute-start | bytes 1572872 | tf_op jit(solution)/shard_map/ppermute | solution.py:301
  15.8 1.3 fusion.2
  17.1 1.2 collective-permute-start.6
  18.3 3.2 %collective-permute-start.11 = (bf16[512,384]{1,0:T(8,128)(2,1)S(1)}, bf16[512,384]{1,0:T(8,128)(2,1)S(1)}, u32[]{:S(2)}, u32[]{:S(2)}) collective-permute-start(bf16[512,384]{1,0:T(8,128)(2,1)S(1)} %get-tuple-element.14.refs_4_), channel_id=1, source_target_pairs={{0,8},{1,9},{2,10},{3,11},{4,12},{5,13},{6,14},{7,15},{8,0},{9,1},... | collective-permute-start | bytes 1179656 | tf_op jit(solution)/shard_map/ppermute | solution.py:304
  22.2 5.9 %collective-permute-done.3.refs_2_ = bf16[64,4096]{1,0:T(8,128)(2,1)} collective-permute-done((bf16[64,4096]{1,0:T(8,128)(2,1)}, bf16[64,4096]{1,0:T(8,128)(2,1)}, u32[]{:S(2)}, u32[]{:S(2)}) %collective-permute-start.3) | collective-permute-done | bytes 524320 | tf_op jit(solution)/shard_map/ppermute | solution.py:301
  28.0 3.0 %collective-permute-start.9 = (bf16[512,384]{1,0:T(8,128)(2,1)S(1)}, bf16[512,384]{1,0:T(8,128)(2,1)}, u32[]{:S(2)}, u32[]{:S(2)}) collective-permute-start(bf16[512,384]{1,0:T(8,128)(2,1)S(1)} %get-tuple-element.14.refs_4_), channel_id=1, source_target_pairs={{0,12},{1,13},{2,14},{3,15},{4,0},{5,1},{6,2},{7,3},{8,4},{9,5},{1... | collective-permute-start | bytes 1179656 | tf_op jit(solution)/shard_map/ppermute | solution.py:304
  31.1 6.4 %collective-permute-done.6.refs_5_ = bf16[512,384]{1,0:T(8,128)(2,1)} collective-permute-done((bf16[512,384]{1,0:T(8,128)(2,1)S(1)}, bf16[512,384]{1,0:T(8,128)(2,1)}, u32[]{:S(2)}, u32[]{:S(2)}) %collective-permute-start.6) | collective-permute-done | bytes 393248 | tf_op jit(solution)/shard_map/ppermute | solution.py:311
  37.4 3.0 %collective-permute-start.10 = (bf16[512,384]{1,0:T(8,128)(2,1)}, bf16[512,384]{1,0:T(8,128)(2,1)}, u32[]{:S(2)}, u32[]{:S(2)}) collective-permute-start(bf16[512,384]{1,0:T(8,128)(2,1)} %collective-permute-done.6.refs_5_), channel_id=1, source_target_pairs={{0,12},{1,13},{2,14},{3,15},{4,0},{5,1},{6,2},{7,3},{8,4},{9,5},{1... | collective-permute-start | bytes 1179656 | tf_op jit(solution)/shard_map/ppermute | solution.py:304
  43.7 1.7 pad_maximum_fusion.3
  45.4 2.1 collective-permute-start
  47.5 1.3 collective-permute-start.1
  48.8 10.1 %collective-permute-done.10.refs_9_ = bf16[512,384]{1,0:T(8,128)(2,1)} collective-permute-done((bf16[512,384]{1,0:T(8,128)(2,1)}, bf16[512,384]{1,0:T(8,128)(2,1)}, u32[]{:S(2)}, u32[]{:S(2)}) %collective-permute-start.10) | collective-permute-done | bytes 393248 | tf_op jit(solution)/shard_map/ppermute | solution.py:304
  58.9 5.5 %collective-permute-done.8.refs_7_ = bf16[512,384]{1,0:T(8,128)(2,1)} collective-permute-done((bf16[512,384]{1,0:T(8,128)(2,1)}, bf16[512,384]{1,0:T(8,128)(2,1)}, u32[]{:S(2)}, u32[]{:S(2)}) %collective-permute-start.8) | collective-permute-done | bytes 393248 | tf_op jit(solution)/shard_map/ppermute | solution.py:304
  67.5 4.0 %shard_map.113.refs_0_ = f32[256,384]{1,0:T(8,128)} custom-call(s32[16]{0:T(128)S(1)} %stack.100.cols_ref, bf16[64,4096]{1,0:T(8,128)(2,1)S(1)} %bitcast.59, bf16[64,4096]{1,0:T(8,128)(2,1)} %collective-permute-done.2.refs_1_, bf16[64,4096]{1,0:T(8,128)(2,1)} %collective-permute-done.3.refs_2_, bf16[64,4096]{1,0:T(8,128)(2,1)} %collective-permute-done.4.refs_3_, ...), custom_call_target="tpu_custom_call" | custom-call | flops 800000000 | bytes 6000000 | tf_op jit(solution)/shard_map/pallas_call | solution.py:89
  71.5 1.8 collective-permute-start.13
  73.3 3.2 %collective-permute-start.14 = (f32[256,384]{1,0:T(8,128)}, f32[256,384]{1,0:T(8,128)}, u32[]{:S(2)}, u32[]{:S(2)}) collective-permute-start(f32[256,384]{1,0:T(8,128)} %shard_map.113.refs_0_), channel_id=1, source_target_pairs={{0,8},{1,9},{2,10},{3,11},{4,12},{5,13},{6,14},{7,15},{8,0},{9,1},... | collective-permute-start | bytes 1179656 | tf_op jit(solution)/shard_map/ppermute | solution.py:304
  76.5 1.2 collective-permute-start.15
  78.3 8.5 %shard_map.116.conv_ref = bf16[16,256,768]{2,1,0:T(8,128)(2,1)} custom-call(bf16[41,64,1024]{2,1,0:T(8,128)(2,1)} %w_ref.1), custom_call_target="tpu_custom_call" | custom-call | flops 20000000 | bytes 20000000 | tf_op jit(solution)/shard_map/pallas_call | solution.py:65
  89.9 3.0 %collective-permute-done.14.refs_2_ = f32[256,384]{1,0:T(8,128)} collective-permute-done((f32[256,384]{1,0:T(8,128)}, f32[256,384]{1,0:T(8,128)}, u32[]{:S(2)}, u32[]{:S(2)}) %collective-permute-start.14) | collective-permute-done | bytes 393248 | tf_op jit(solution)/shard_map/ppermute | solution.py:304
  93.5 3.7 %collective-permute-start.20 = (bf16[336,384]{1,0:T(8,128)(2,1)S(1)}, bf16[336,384]{1,0:T(8,128)(2,1)S(1)}, u32[]{:S(2)}, u32[]{:S(2)}) collective-permute-start(bf16[336,384]{1,0:T(8,128)(2,1)S(1)} %get-tuple-element.17), channel_id=1, source_target_pairs={{0,2},{1,3},{2,0},{3,1},{4,6},{5,7},{6,4},{7,5},{8,10},{9,11},{10,... | collective-permute-start | bytes 774152 | tf_op jit(solution)/shard_map/ppermute | solution.py:301
  97.2 1.1 pad_maximum_fusion
  98.4 5.8 %collective-permute-done.20.q_ref = bf16[336,384]{1,0:T(8,128)(2,1)S(1)} collective-permute-done((bf16[336,384]{1,0:T(8,128)(2,1)S(1)}, bf16[336,384]{1,0:T(8,128)(2,1)S(1)}, u32[]{:S(2)}, u32[]{:S(2)}) %collective-permute-start.20) | collective-permute-done | bytes 258080 | tf_op jit(solution)/shard_map/ppermute | solution.py:301
  104.2 6.1 %shard_map.115 = bf16[336,384]{1,0:T(8,128)(2,1)S(1)} custom-call(s32[4]{0:T(128)S(1)} %pad_add_fusion.1.meta_ref, bf16[336,384]{1,0:T(8,128)(2,1)S(1)} %collective-permute-done.20.q_ref, f32[256,384]{1,0:T(8,128)} %shard_map.113.refs_0_, f32[256,384]{1,0:T(8,128)S(1)} %collective-permute-done.13.refs_1_, f32[256,384]{1,0:T(8,128)} %collective-permute-done.14.refs_2_, ...), custom_call_target="tpu_custom_call" | custom-call | flops 1056964608 | bytes 4000000 | tf_op jit(solution)/shard_map/pallas_call | solution.py:143
  110.3 3.3 %collective-permute-start.21 = (bf16[336,384]{1,0:T(8,128)(2,1)S(1)}, bf16[336,384]{1,0:T(8,128)(2,1)S(1)}, u32[]{:S(2)}, u32[]{:S(2)}) collective-permute-start(bf16[336,384]{1,0:T(8,128)(2,1)S(1)} %shard_map.115), channel_id=1, source_target_pairs={{0,2},{1,3},{2,0},{3,1},{4,6},{5,7},{6,4},{7,5},{8,10},{9,11},{10,... | collective-permute-start | bytes 774152 | tf_op jit(solution)/shard_map/ppermute | solution.py:301
  113.6 2.4 %fusion.lifted_ref = f32[336,1024]{1,0:T(8,128)} fusion(bf16[1536,1024]{1,0:T(8,128)(2,1)S(1)} %copy-done, bf16[336,2304]{1,0:T(8,128)(2,1)S(1)} %pad_maximum_fusion), kind=kOutput, calls=%fused_computation.5 | convolution fusion | flops 1056964608 | bytes 5554176 | tf_op jit(solution)/shard_map/dot_general | solution.py:338
  116.0 6.1 %shard_map.114.mine_ref = bf16[336,384]{1,0:T(8,128)(2,1)S(1)} custom-call(s32[4]{0:T(128)S(1)} %pad_add_fusion.1.meta_ref, bf16[336,384]{1,0:T(8,128)(2,1)S(1)} %get-tuple-element.18.q_ref, f32[256,384]{1,0:T(8,128)} %shard_map.113.refs_0_, f32[256,384]{1,0:T(8,128)S(1)} %collective-permute-done.13.refs_1_, f32[256,384]{1,0:T(8,128)} %collective-permute-done.14.refs_2_, ...), custom_call_target="tpu_custom_call" | custom-call | flops 1056964608 | bytes 4000000 | tf_op jit(solution)/shard_map/pallas_call | solution.py:143
  123.6 1.4 copy-done.6
  126.9 1.3 copy-done.12
  128.2 13.1 %shard_map.117 = (f32[2,384,1024]{2,1,0:T(8,128)}, f32[8,128]{1,0:T(8,128)S(1)}) custom-call(s32[4]{0:T(128)S(1)} %pad_add_fusion.meta_ref, f32[336,1024]{1,0:T(8,128)S(1)} %copy-done.12, bf16[336,384]{1,0:T(8,128)(2,1)S(1)} %copy-done.11, bf16[336,384]{1,0:T(8,128)(2,1)S(1)} %copy-done.8, bf16[2,384,1024]{2,1,0:T(8,128)(2,1)S(1)} %bitcast.60, ...), custom_call_target="tpu_custom_call" | custom-call | flops 3000000000 | bytes 14000000 | tf_op jit(solution)/shard_map/pallas_call | solution.py:265
  141.4 2.7 %dynamic-slice_bitcast_fusion = f32[8,48,1024]{2,1,0:T(8,128)} fusion(f32[8,2,48,1024]{3,2,1,0:T(8,128)} %bitcast.70, s32[]{:T(128)S(6)} %select_n.138), kind=kLoop, calls=%fused_computation.2 | loop fusion | bytes 3145732 | tf_op jit(solution)/shard_map/jit(dynamic_index_in_dim)/squeeze | solution.py:369
  144.1 3.7 %collective-permute-done.22 = f32[8,48,1024]{2,1,0:T(8,128)} collective-permute-done((f32[8,48,1024]{2,1,0:T(8,128)}, f32[8,48,1024]{2,1,0:T(8,128)}, u32[]{:S(2)}, u32[]{:S(2)}) %collective-permute-start.22) | collective-permute-done | bytes 1572896 | tf_op jit(solution)/shard_map/ppermute | solution.py:301
  147.8 2.1 bitcast_add_fusion
  151.2 3.5 %collective-permute-start.24 = (bf16[2,48,1024]{2,1,0:T(8,128)(2,1)}, bf16[2,48,1024]{2,1,0:T(8,128)(2,1)}, u32[]{:S(2)}, u32[]{:S(2)}) collective-permute-start(bf16[2,48,1024]{2,1,0:T(8,128)(2,1)} %get-tuple-element.10), channel_id=1, source_target_pairs={{0,8},{1,9},{2,10},{3,11},{4,12},{5,13},{6,14},{7,15},{8,0},{9,1},... | collective-permute-start | bytes 589832 | tf_op jit(solution)/shard_map/ppermute | solution.py:304
  154.8 1.1 collective-permute-done.27
  155.9 2.0 collective-permute-start.28
  158.3 1.3 collective-permute-done.23
  159.5 1.7 collective-permute-start.30
  161.2 3.0 %collective-permute-done.24 = bf16[2,48,1024]{2,1,0:T(8,128)(2,1)} collective-permute-done((bf16[2,48,1024]{2,1,0:T(8,128)(2,1)}, bf16[2,48,1024]{2,1,0:T(8,128)(2,1)}, u32[]{:S(2)}, u32[]{:S(2)}) %collective-permute-start.24) | collective-permute-done | bytes 196640 | tf_op jit(solution)/shard_map/ppermute | solution.py:304
  164.3 1.4 fusion.5
  166.7 3.3 %collective-permute-start.31 = (f32[8,128]{1,0:T(8,128)S(1)}, f32[8,128]{1,0:T(8,128)S(1)}, u32[]{:S(2)}, u32[]{:S(2)}) collective-permute-start(f32[8,128]{1,0:T(8,128)S(1)} %add_add_fusion), channel_id=1, source_target_pairs={{0,2},{1,3},{2,0},{3,1},{4,6},{5,7},{6,4},{7,5},{8,10},{9,11},{10,... | collective-permute-start | bytes 12296 | tf_op jit(solution)/shard_map/ppermute | solution.py:301
  170.0 4.2 %collective-permute-done.31 = f32[8,128]{1,0:T(8,128)S(1)} collective-permute-done((f32[8,128]{1,0:T(8,128)S(1)}, f32[8,128]{1,0:T(8,128)S(1)}, u32[]{:S(2)}, u32[]{:S(2)}) %collective-permute-start.31) | collective-permute-done | bytes 4128 | tf_op jit(solution)/shard_map/ppermute | solution.py:301
  174.8 1.6 bitcast_add_fusion.2
  178.1 17.8 %all_to_all.10 = f32[16,4,1024]{2,1,0:T(4,128)S(1)} all-to-all(f32[16,4,1024]{2,1,0:T(4,128)S(1)} %concatenate.15), channel_id=1, replica_groups=mesh['dp'=16,'seq'=16] {'dp'}, dimensions={0} | all-to-all | bytes 524288 | tf_op jit(solution)/shard_map/all_to_all | solution.py:383
  196.7 5.4 %all-to-all-start.1 = ((f32[16,3,1024]{2,1,0:T(4,128)}), f32[16,3,1024]{2,1,0:T(4,128)}, u32[]{:S(2)}, u32[]{:S(2)}) async-start(f32[16,3,1024]{2,1,0:T(4,128)} %broadcast_in_dim.8), calls=%async_computation.1 | async-start | bytes 524288 | tf_op jit(solution)/shard_map/all_to_all | solution.py:387
  204.0 7.6 %all-to-all-done.1 = f32[16,3,1024]{2,1,0:T(4,128)} async-done(((f32[16,3,1024]{2,1,0:T(4,128)}), f32[16,3,1024]{2,1,0:T(4,128)}, u32[]{:S(2)}, u32[]{:S(2)}) %all-to-all-start.1) | async-done | bytes 196640 | tf_op jit(solution)/shard_map/all_to_all | solution.py:387
  213.7 1.8 convolution_add_fusion
  (97 shorter events, 23.9 us)
Async XLA Ops:
  7.2 2.3 %copy-start = (bf16[1536,1024]{1,0:T(8,128)(2,1)S(1)}, bf16[1536,1024]{1,0:T(8,128)(2,1)}, u32[]{:S(2)}) copy-start(bf16[1536,1024]{1,0:T(8,128)(2,1)} %param.15) | copy-start | bytes 9437188
  7.2 116.4 %all-gather.2.cloned.1.call-start = ((), (), s32[]{:S(2)}) async-start(), calls=%async_computation.2 | async-start | bytes 1671168 | tf_op jit(solution)/shard_map/all_gather | solution.py:337
  9.5 5.6 %collective-permute-start.5 = (bf16[256,768]{1,0:T(8,128)(2,1)}, bf16[256,768]{1,0:T(8,128)(2,1)S(1)}, u32[]{:S(2)}, u32[]{:S(2)}) collective-permute-start(bf16[256,768]{1,0:T(8,128)(2,1)} %get-tuple-element.15), channel_id=1, source_target_pairs={{0,1},{1,0},{2,3},{3,2},{4,5},{5,4},{6,7},{7,6},{8,9},{9,8},{10,11... | collective-permute-start | bytes 1179656 | tf_op jit(solution)/shard_map/ppermute | solution.py:301
  11.7 16.3 %collective-permute-start.3 = (bf16[64,4096]{1,0:T(8,128)(2,1)}, bf16[64,4096]{1,0:T(8,128)(2,1)}, u32[]{:S(2)}, u32[]{:S(2)}) collective-permute-start(bf16[64,4096]{1,0:T(8,128)(2,1)} %bitcast.57), channel_id=1, source_target_pairs={{0,2},{1,3},{2,0},{3,1},{4,6},{5,7},{6,4},{7,5},{8,10},{9,11},{10,... | collective-permute-start | bytes 1572872 | tf_op jit(solution)/shard_map/ppermute | solution.py:301
  14.8 13.2 %collective-permute-start.2 = (bf16[64,4096]{1,0:T(8,128)(2,1)}, bf16[64,4096]{1,0:T(8,128)(2,1)}, u32[]{:S(2)}, u32[]{:S(2)}) collective-permute-start(bf16[64,4096]{1,0:T(8,128)(2,1)} %bitcast.58), channel_id=1, source_target_pairs={{0,1},{1,0},{2,3},{3,2},{4,5},{5,4},{6,7},{7,6},{8,9},{9,8},{10,11... | collective-permute-start | bytes 1572872 | tf_op jit(solution)/shard_map/ppermute | solution.py:301
  17.1 20.3 %collective-permute-start.6 = (bf16[512,384]{1,0:T(8,128)(2,1)S(1)}, bf16[512,384]{1,0:T(8,128)(2,1)}, u32[]{:S(2)}, u32[]{:S(2)}) collective-permute-start(bf16[512,384]{1,0:T(8,128)(2,1)S(1)} %get-tuple-element.13), channel_id=1, source_target_pairs={{0,18},{1,19},{2,16},{3,17},{4,22},{5,23},{6,20},{7,21},{8,26},{9,... | collective-permute-start | bytes 1179656 | tf_op jit(solution)/shard_map/ppermute | solution.py:311
  18.3 22.1 %collective-permute-start.11 = (bf16[512,384]{1,0:T(8,128)(2,1)S(1)}, bf16[512,384]{1,0:T(8,128)(2,1)S(1)}, u32[]{:S(2)}, u32[]{:S(2)}) collective-permute-start(bf16[512,384]{1,0:T(8,128)(2,1)S(1)} %get-tuple-element.14.refs_4_), channel_id=1, source_target_pairs={{0,8},{1,9},{2,10},{3,11},{4,12},{5,13},{6,14},{7,15},{8,0},{9,1},... | collective-permute-start | bytes 1179656 | tf_op jit(solution)/shard_map/ppermute | solution.py:304
  21.5 20.3 %collective-permute-start.7 = (bf16[512,384]{1,0:T(8,128)(2,1)S(1)}, bf16[512,384]{1,0:T(8,128)(2,1)S(1)}, u32[]{:S(2)}, u32[]{:S(2)}) collective-permute-start(bf16[512,384]{1,0:T(8,128)(2,1)S(1)} %get-tuple-element.14.refs_4_), channel_id=1, source_target_pairs={{0,4},{1,5},{2,6},{3,7},{4,8},{5,9},{6,10},{7,11},{8,12},{9,13},{1... | collective-permute-start | bytes 1179656 | tf_op jit(solution)/shard_map/ppermute | solution.py:304
  28.0 19.5 %collective-permute-start.4 = (bf16[64,4096]{1,0:T(8,128)(2,1)}, bf16[64,4096]{1,0:T(8,128)(2,1)}, u32[]{:S(2)}, u32[]{:S(2)}) collective-permute-start(bf16[64,4096]{1,0:T(8,128)(2,1)} %collective-permute-done.3.refs_2_), channel_id=1, source_target_pairs={{0,1},{1,0},{2,3},{3,2},{4,5},{5,4},{6,7},{7,6},{8,9},{9,8},{10,11... | collective-permute-start | bytes 1572872 | tf_op jit(solution)/shard_map/ppermute | solution.py:301
  28.0 17.4 %collective-permute-start.9 = (bf16[512,384]{1,0:T(8,128)(2,1)S(1)}, bf16[512,384]{1,0:T(8,128)(2,1)}, u32[]{:S(2)}, u32[]{:S(2)}) collective-permute-start(bf16[512,384]{1,0:T(8,128)(2,1)S(1)} %get-tuple-element.14.refs_4_), channel_id=1, source_target_pairs={{0,12},{1,13},{2,14},{3,15},{4,0},{5,1},{6,2},{7,3},{8,4},{9,5},{1... | collective-permute-start | bytes 1179656 | tf_op jit(solution)/shard_map/ppermute | solution.py:304
  37.4 21.5 %collective-permute-start.10 = (bf16[512,384]{1,0:T(8,128)(2,1)}, bf16[512,384]{1,0:T(8,128)(2,1)}, u32[]{:S(2)}, u32[]{:S(2)}) collective-permute-start(bf16[512,384]{1,0:T(8,128)(2,1)} %collective-permute-done.6.refs_5_), channel_id=1, source_target_pairs={{0,12},{1,13},{2,14},{3,15},{4,0},{5,1},{6,2},{7,3},{8,4},{9,5},{1... | collective-permute-start | bytes 1179656 | tf_op jit(solution)/shard_map/ppermute | solution.py:304
  41.2 17.7 %collective-permute-start.12 = (bf16[512,384]{1,0:T(8,128)(2,1)}, bf16[512,384]{1,0:T(8,128)(2,1)}, u32[]{:S(2)}, u32[]{:S(2)}) collective-permute-start(bf16[512,384]{1,0:T(8,128)(2,1)} %collective-permute-done.6.refs_5_), channel_id=1, source_target_pairs={{0,8},{1,9},{2,10},{3,11},{4,12},{5,13},{6,14},{7,15},{8,0},{9,1},... | collective-permute-start | bytes 1179656 | tf_op jit(solution)/shard_map/ppermute | solution.py:304
  42.6 21.8 %collective-permute-start.8 = (bf16[512,384]{1,0:T(8,128)(2,1)}, bf16[512,384]{1,0:T(8,128)(2,1)}, u32[]{:S(2)}, u32[]{:S(2)}) collective-permute-start(bf16[512,384]{1,0:T(8,128)(2,1)} %collective-permute-done.6.refs_5_), channel_id=1, source_target_pairs={{0,4},{1,5},{2,6},{3,7},{4,8},{5,9},{6,10},{7,11},{8,12},{9,13},{1... | collective-permute-start | bytes 1179656 | tf_op jit(solution)/shard_map/ppermute | solution.py:304
  45.4 32.2 %copy-start.18 = (s32[16]{0:T(128)S(1)}, s32[16]{0:T(128)}, u32[]{:S(2)}) copy-start(s32[16]{0:T(128)} %param.18) | copy-start | bytes 196
  45.4 32.2 %copy-start.19 = (s32[16]{0:T(128)S(1)}, s32[16]{0:T(128)}, u32[]{:S(2)}) copy-start(s32[16]{0:T(128)} %param.19) | copy-start | bytes 196
  45.4 42.8 %collective-permute-start = (bf16[40,2304]{1,0:T(8,128)(2,1)}, bf16[40,2304]{1,0:T(8,128)(2,1)}, u32[]{:S(2)}, u32[]{:S(2)}) collective-permute-start(bf16[40,2304]{1,0:T(8,128)(2,1)} %get-tuple-element.11), channel_id=1, source_target_pairs={{0,1},{1,2},{2,3},{3,4},{4,5},{5,6},{6,7},{7,8},{8,9},{9,10},{10,1... | collective-permute-start | bytes 552968 | tf_op jit(solution)/shard_map/ppermute | solution.py:326
  47.5 40.7 %collective-permute-start.1 = (bf16[40,2304]{1,0:T(8,128)(2,1)}, bf16[40,2304]{1,0:T(8,128)(2,1)}, u32[]{:S(2)}, u32[]{:S(2)}) collective-permute-start(bf16[40,2304]{1,0:T(8,128)(2,1)} %get-tuple-element.12), channel_id=1, source_target_pairs={{1,0},{2,1},{3,2},{4,3},{5,4},{6,5},{7,6},{8,7},{9,8},{10,9},{11,1... | collective-permute-start | bytes 552968 | tf_op jit(solution)/shard_map/ppermute | solution.py:327
  64.4 1.0 copy-start.1
  65.5 1.0 copy-start.3
  66.5 1.0 copy-start.5
  71.5 18.0 %collective-permute-start.13 = (f32[256,384]{1,0:T(8,128)}, f32[256,384]{1,0:T(8,128)S(1)}, u32[]{:S(2)}, u32[]{:S(2)}) collective-permute-start(f32[256,384]{1,0:T(8,128)} %shard_map.113.refs_0_), channel_id=1, source_target_pairs={{0,4},{1,5},{2,6},{3,7},{4,8},{5,9},{6,10},{7,11},{8,12},{9,13},{1... | collective-permute-start | bytes 1179656 | tf_op jit(solution)/shard_map/ppermute | solution.py:304
  73.3 19.7 %collective-permute-start.14 = (f32[256,384]{1,0:T(8,128)}, f32[256,384]{1,0:T(8,128)}, u32[]{:S(2)}, u32[]{:S(2)}) collective-permute-start(f32[256,384]{1,0:T(8,128)} %shard_map.113.refs_0_), channel_id=1, source_target_pairs={{0,8},{1,9},{2,10},{3,11},{4,12},{5,13},{6,14},{7,15},{8,0},{9,1},... | collective-permute-start | bytes 1179656 | tf_op jit(solution)/shard_map/ppermute | solution.py:304
  76.5 16.5 %collective-permute-start.15 = (f32[256,384]{1,0:T(8,128)}, f32[256,384]{1,0:T(8,128)}, u32[]{:S(2)}, u32[]{:S(2)}) collective-permute-start(f32[256,384]{1,0:T(8,128)} %shard_map.113.refs_0_), channel_id=1, source_target_pairs={{0,12},{1,13},{2,14},{3,15},{4,0},{5,1},{6,2},{7,3},{8,4},{9,5},{1... | collective-permute-start | bytes 1179656 | tf_op jit(solution)/shard_map/ppermute | solution.py:304
  78.3 9.9 %copy-start.13 = (bf16[1,256,1536]{2,1,0:T(8,128)(2,1)S(1)}, bf16[1,256,1536]{2,1,0:T(8,128)(2,1)}, u32[]{:S(2)}) copy-start(bf16[1,256,1536]{2,1,0:T(8,128)(2,1)} %param.13) | copy-start | bytes 2359300
  78.3 9.9 %copy-start.15 = (bf16[1,256,768]{2,1,0:T(8,128)(2,1)S(1)}, bf16[1,256,768]{2,1,0:T(8,128)(2,1)}, u32[]{:S(2)}) copy-start(bf16[1,256,768]{2,1,0:T(8,128)(2,1)} %param.12) | copy-start | bytes 1179652
  89.1 15.0 %collective-permute-start.16 = (f32[256,384]{1,0:T(8,128)}, f32[256,384]{1,0:T(8,128)S(1)}, u32[]{:S(2)}, u32[]{:S(2)}) collective-permute-start(f32[256,384]{1,0:T(8,128)} %shard_map.113.refs_0_), channel_id=1, source_target_pairs={{0,1},{1,0},{2,3},{3,2},{4,5},{5,4},{6,7},{7,6},{8,9},{9,8},{10,11... | collective-permute-start | bytes 1179656 | tf_op jit(solution)/shard_map/ppermute | solution.py:301
  89.4 14.7 %collective-permute-start.17 = (f32[256,384]{1,0:T(8,128)S(1)}, f32[256,384]{1,0:T(8,128)S(1)}, u32[]{:S(2)}, u32[]{:S(2)}) collective-permute-start(f32[256,384]{1,0:T(8,128)S(1)} %collective-permute-done.13.refs_1_), channel_id=1, source_target_pairs={{0,1},{1,0},{2,3},{3,2},{4,5},{5,4},{6,7},{7,6},{8,9},{9,8},{10,11... | collective-permute-start | bytes 1179656 | tf_op jit(solution)/shard_map/ppermute | solution.py:301
  92.9 11.2 %collective-permute-start.18 = (f32[256,384]{1,0:T(8,128)}, f32[256,384]{1,0:T(8,128)S(1)}, u32[]{:S(2)}, u32[]{:S(2)}) collective-permute-start(f32[256,384]{1,0:T(8,128)} %collective-permute-done.14.refs_2_), channel_id=1, source_target_pairs={{0,1},{1,0},{2,3},{3,2},{4,5},{5,4},{6,7},{7,6},{8,9},{9,8},{10,11... | collective-permute-start | bytes 1179656 | tf_op jit(solution)/shard_map/ppermute | solution.py:301
  93.0 11.2 %collective-permute-start.19 = (f32[256,384]{1,0:T(8,128)}, f32[256,384]{1,0:T(8,128)S(1)}, u32[]{:S(2)}, u32[]{:S(2)}) collective-permute-start(f32[256,384]{1,0:T(8,128)} %collective-permute-done.15.refs_3_), channel_id=1, source_target_pairs={{0,1},{1,0},{2,3},{3,2},{4,5},{5,4},{6,7},{7,6},{8,9},{9,8},{10,11... | collective-permute-start | bytes 1179656 | tf_op jit(solution)/shard_map/ppermute | solution.py:301
  93.5 10.6 %collective-permute-start.20 = (bf16[336,384]{1,0:T(8,128)(2,1)S(1)}, bf16[336,384]{1,0:T(8,128)(2,1)S(1)}, u32[]{:S(2)}, u32[]{:S(2)}) collective-permute-start(bf16[336,384]{1,0:T(8,128)(2,1)S(1)} %get-tuple-element.17), channel_id=1, source_target_pairs={{0,2},{1,3},{2,0},{3,1},{4,6},{5,7},{6,4},{7,5},{8,10},{9,11},{10,... | collective-permute-start | bytes 774152 | tf_op jit(solution)/shard_map/ppermute | solution.py:301
  110.3 12.6 %collective-permute-start.21 = (bf16[336,384]{1,0:T(8,128)(2,1)S(1)}, bf16[336,384]{1,0:T(8,128)(2,1)S(1)}, u32[]{:S(2)}, u32[]{:S(2)}) collective-permute-start(bf16[336,384]{1,0:T(8,128)(2,1)S(1)} %shard_map.115), channel_id=1, source_target_pairs={{0,2},{1,3},{2,0},{3,1},{4,6},{5,7},{6,4},{7,5},{8,10},{9,11},{10,... | collective-permute-start | bytes 774152 | tf_op jit(solution)/shard_map/ppermute | solution.py:301
  116.0 7.5 %copy-start.9 = (f32[1024]{0:T(1024)S(1)}, f32[1024]{0:T(1024)}, u32[]{:S(2)}) copy-start(f32[1024]{0:T(1024)} %param.17) | copy-start | bytes 12292
  123.6 1.4 copy-start.6
  125.0 0.9 copy-start.8
  126.9 1.3 copy-start.12
  144.1 3.8 %collective-permute-start.22 = (f32[8,48,1024]{2,1,0:T(8,128)}, f32[8,48,1024]{2,1,0:T(8,128)}, u32[]{:S(2)}, u32[]{:S(2)}) collective-permute-start(f32[8,48,1024]{2,1,0:T(8,128)} %dynamic-slice_bitcast_fusion), channel_id=1, source_target_pairs={{0,1},{1,0},{2,3},{3,2},{4,5},{5,4},{6,7},{7,6},{8,9},{9,8},{10,11... | collective-permute-start | bytes 4718600 | tf_op jit(solution)/shard_map/ppermute | solution.py:301
  150.0 4.7 %copy-start.14 = (f32[8,48,1024]{2,1,0:T(8,128)}, f32[8,48,1024]{2,1,0:T(8,128)S(1)}, u32[]{:S(2)}) copy-start(f32[8,48,1024]{2,1,0:T(8,128)S(1)} %bitcast_add_fusion) | copy-start | bytes 4718596
  150.9 8.6 %collective-permute-start.23 = (bf16[2,48,1024]{2,1,0:T(8,128)(2,1)}, bf16[2,48,1024]{2,1,0:T(8,128)(2,1)S(1)}, u32[]{:S(2)}, u32[]{:S(2)}) collective-permute-start(bf16[2,48,1024]{2,1,0:T(8,128)(2,1)} %get-tuple-element.8), channel_id=1, source_target_pairs={{0,4},{1,5},{2,6},{3,7},{4,8},{5,9},{6,10},{7,11},{8,12},{9,13},{1... | collective-permute-start | bytes 589832 | tf_op jit(solution)/shard_map/ppermute | solution.py:304
  151.2 13.1 %collective-permute-start.24 = (bf16[2,48,1024]{2,1,0:T(8,128)(2,1)}, bf16[2,48,1024]{2,1,0:T(8,128)(2,1)}, u32[]{:S(2)}, u32[]{:S(2)}) collective-permute-start(bf16[2,48,1024]{2,1,0:T(8,128)(2,1)} %get-tuple-element.10), channel_id=1, source_target_pairs={{0,8},{1,9},{2,10},{3,11},{4,12},{5,13},{6,14},{7,15},{8,0},{9,1},... | collective-permute-start | bytes 589832 | tf_op jit(solution)/shard_map/ppermute | solution.py:304
  154.7 9.6 %collective-permute-start.25 = (bf16[2,48,1024]{2,1,0:T(8,128)(2,1)S(1)}, bf16[2,48,1024]{2,1,0:T(8,128)(2,1)}, u32[]{:S(2)}, u32[]{:S(2)}) collective-permute-start(bf16[2,48,1024]{2,1,0:T(8,128)(2,1)S(1)} %get-tuple-element.9), channel_id=1, source_target_pairs={{0,12},{1,13},{2,14},{3,15},{4,0},{5,1},{6,2},{7,3},{8,4},{9,5},{1... | collective-permute-start | bytes 589832 | tf_op jit(solution)/shard_map/ppermute | solution.py:304
  154.7 1.2 collective-permute-start.27
  155.9 10.8 %collective-permute-start.28 = (f32[8,128]{1,0:T(8,128)S(1)}, f32[8,128]{1,0:T(8,128)S(1)}, u32[]{:S(2)}, u32[]{:S(2)}) collective-permute-start(f32[8,128]{1,0:T(8,128)S(1)} %add.270), channel_id=1, source_target_pairs={{0,4},{1,5},{2,6},{3,7},{4,8},{5,9},{6,10},{7,11},{8,12},{9,13},{1... | collective-permute-start | bytes 12296 | tf_op jit(solution)/shard_map/ppermute | solution.py:304
  157.9 8.8 %collective-permute-start.29 = (f32[8,128]{1,0:T(8,128)S(1)}, f32[8,128]{1,0:T(8,128)S(1)}, u32[]{:S(2)}, u32[]{:S(2)}) collective-permute-start(f32[8,128]{1,0:T(8,128)S(1)} %add.270), channel_id=1, source_target_pairs={{0,8},{1,9},{2,10},{3,11},{4,12},{5,13},{6,14},{7,15},{8,0},{9,1},... | collective-permute-start | bytes 12296 | tf_op jit(solution)/shard_map/ppermute | solution.py:304
  159.5 4.7 %copy-start.17 = (bf16[2,48,1024]{2,1,0:T(8,128)(2,1)}, bf16[2,48,1024]{2,1,0:T(8,128)(2,1)S(1)}, u32[]{:S(2)}) copy-start(bf16[2,48,1024]{2,1,0:T(8,128)(2,1)S(1)} %collective-permute-done.23) | copy-start | bytes 589828
  159.5 7.2 %collective-permute-start.30 = (f32[8,128]{1,0:T(8,128)S(1)}, f32[8,128]{1,0:T(8,128)S(1)}, u32[]{:S(2)}, u32[]{:S(2)}) collective-permute-start(f32[8,128]{1,0:T(8,128)S(1)} %add.270), channel_id=1, source_target_pairs={{0,12},{1,13},{2,14},{3,15},{4,0},{5,1},{6,2},{7,3},{8,4},{9,5},{1... | collective-permute-start | bytes 12296 | tf_op jit(solution)/shard_map/ppermute | solution.py:304
  166.4 8.4 %collective-permute-start.26 = (f32[48,1024]{1,0:T(8,128)}, f32[48,1024]{1,0:T(8,128)}, u32[]{:S(2)}, u32[]{:S(2)}) collective-permute-start(f32[48,1024]{1,0:T(8,128)} %dynamic-slice_bitcast_fusion.1), channel_id=1, source_target_pairs={{0,2},{1,3},{2,0},{3,1},{4,6},{5,7},{6,4},{7,5},{8,10},{9,11},{10,... | collective-permute-start | bytes 589832 | tf_op jit(solution)/shard_map/ppermute | solution.py:301
  166.7 7.5 %collective-permute-start.31 = (f32[8,128]{1,0:T(8,128)S(1)}, f32[8,128]{1,0:T(8,128)S(1)}, u32[]{:S(2)}, u32[]{:S(2)}) collective-permute-start(f32[8,128]{1,0:T(8,128)S(1)} %add_add_fusion), channel_id=1, source_target_pairs={{0,2},{1,3},{2,0},{3,1},{4,6},{5,7},{6,4},{7,5},{8,10},{9,11},{10,... | collective-permute-start | bytes 12296 | tf_op jit(solution)/shard_map/ppermute | solution.py:301
  196.7 14.9 %all-to-all-start.1 = ((f32[16,3,1024]{2,1,0:T(4,128)}), f32[16,3,1024]{2,1,0:T(4,128)}, u32[]{:S(2)}, u32[]{:S(2)}) async-start(f32[16,3,1024]{2,1,0:T(4,128)} %broadcast_in_dim.8), calls=%async_computation.1 | async-start | bytes 524288 | tf_op jit(solution)/shard_map/all_to_all | solution.py:387
  (6 other events, 4.6 us)
Sparse Core Ops, SparseCore 0:
  11.8 55.8 all-gather.1

commit v2 on v1

--- a/solution.py
+++ b/solution.py
@@ -20,11 +20,11 @@
 REACH = 5
 F32 = jnp.float32
 BF16 = jnp.bfloat16
-VMEM_LIMIT = 50 * 1024 * 1024
-
-
-def params():
-    return pltpu.CompilerParams(vmem_limit_bytes=VMEM_LIMIT)
+MIB = 1024 * 1024
+
+
+def params(mib):
+    return pltpu.CompilerParams(vmem_limit_bytes=mib * MIB)
 
 
 def smem():
@@ -33,6 +33,10 @@
 
 def vmem():
     return pl.BlockSpec(memory_space=pltpu.VMEM)
+
+
+def anywhere():
+    return pl.BlockSpec(memory_space=pltpu.HBM)
 
 
 def low_lanes(shape):
@@ -68,30 +72,59 @@
         in_specs=[pl.BlockSpec((taps, group_in, 128), lambda l: (0, 0, l))],
         out_specs=pl.BlockSpec((2, STRIDE * 64, TAP_SETS * 64), lambda l: (l, 0, 0)),
         out_shape=jax.ShapeDtypeStruct((groups, STRIDE * 64, TAP_SETS * 64), BF16),
-        compiler_params=params(),
+        compiler_params=params(58),
         cost_estimate=pl.CostEstimate(flops=20_000_000, bytes_accessed=20_000_000, transcendentals=0),
     )(conv_weight)
 
 
 def project_kernel(cols_ref, *refs):
-    states, weights, o_ref = (refs[:4], refs[4:12], refs[12])
-    total = None
-    for i, weight in enumerate(weights):
-        for half in range(2):
-            start = pl.multiple_of(cols_ref[2 * i + half], 256)
-            left = jnp.concatenate([s[:, pl.ds(start, 256)] for s in states], axis=0)
-            part = jnp.dot(left, weight[256 * half : 256 * half + 256, :], preferred_element_type=F32)
-            total = part if total is None else total + part
-    o_ref[...] = total
+    states, weights, (keep_ref, send_ref) = (refs[:4], refs[4:12], refs[12:14])
+    state_s, weight_s, total_s, state_sem, weight_sem = refs[14:]
+    core = cols_ref[8]
+    state_copies = [
+        pltpu.make_async_copy(s, state_s.at[i], state_sem.at[i]) for i, s in enumerate(states)
+    ]
+    weight_copies = [
+        pltpu.make_async_copy(w, weight_s.at[i], weight_sem.at[i]) for i, w in enumerate(weights)
+    ]
+    for copy in state_copies + weight_copies:
+        copy.start()
+    for copy in state_copies:
+        copy.wait()
+    for i, copy in enumerate(weight_copies):
+        copy.wait()
+        start = pl.multiple_of(cols_ref[i], 256)
+        left = jnp.concatenate([state_s[j, :, pl.ds(start, 256)] for j in range(4)], axis=0)
+        part = jnp.dot(left, weight_s[i], preferred_element_type=F32)
+        if i == 0:
+            total_s[...] = part
+        else:
+            total_s[...] += part
+    kept = pl.ds(pl.multiple_of(core * HALF_ATT, 128), HALF_ATT)
+    sent = pl.ds(pl.multiple_of((1 - core) * HALF_ATT, 128), HALF_ATT)
+    for j in range(4):
+        rows = slice(64 * j, 64 * j + 64)
+        block = 2 * (j // 2) + (core + j) % 2
+        keep_ref[block] = total_s[rows, kept]
+        send_ref[block] = total_s[rows, sent]
 
 
 def project(cols, states, weights):
+    width = 2 * HALF_ATT
+    out = jax.ShapeDtypeStruct((4, 64, HALF_ATT), F32)
     return pl.pallas_call(
         project_kernel,
-        in_specs=[smem()] + [vmem()] * 12,
-        out_specs=vmem(),
-        out_shape=jax.ShapeDtypeStruct((256, HALF_ATT), F32),
-        compiler_params=params(),
+        in_specs=[smem()] + [anywhere()] * 12,
+        out_specs=[vmem(), vmem()],
+        out_shape=[out, out],
+        scratch_shapes=[
+            pltpu.VMEM((4,) + states[0].shape, BF16),
+            pltpu.VMEM((8,) + weights[0].shape, BF16),
+            pltpu.VMEM((256, width), F32),
+            pltpu.SemaphoreType.DMA((4,)),
+            pltpu.SemaphoreType.DMA((8,)),
+        ],
+        compiler_params=params(58),
         cost_estimate=pl.CostEstimate(flops=800_000_000, bytes_accessed=6_000_000, transcendentals=0),
     )(cols, *states, *weights)
 
@@ -108,11 +141,7 @@
     keys, values = ([], [])
     for m, o in zip(mine, other):
         keys.append(jnp.where(first, m[...], o[...]))
-        turned = []
-        for j in range(4):
-            k = slice(64 * (j ^ 1), 64 * (j ^ 1) + 64)
-            turned.append(jnp.where(first, o[k, :], m[k, :]))
-        values.extend(turned)
+        values.append(jnp.where(first, o[...], m[...]))
     key_high, key_low = split(jnp.concatenate(keys, axis=0))
     value_high, value_low = split(jnp.concatenate(values, axis=0))
     spot = lax.broadcasted_iota(jnp.int32, (1, 1024), 1)
@@ -146,26 +175,139 @@
         in_specs=[smem(), block(rows)] + [block(256)] * 8,
         out_specs=block(rows),
         out_shape=jax.ShapeDtypeStruct((rows, width), BF16),
-        compiler_params=params(),
+        compiler_params=params(12),
         cost_estimate=pl.CostEstimate(
             flops=8 * rows * 1024 * width, bytes_accessed=4_000_000, transcendentals=rows * 3072
         ),
     )(meta, query, *mine, *other)
 
 
+def coded_rows(value):
+    high = value.astype(BF16).astype(F32)
+    middle = (value - high).astype(BF16).astype(F32)
+    low = value - high - middle
+    line = lax.broadcasted_iota(jnp.int32, value.shape, 0)
+    return jnp.where(line == 0, high, jnp.where(line == 1, middle, low)).astype(BF16)
+
+
+def decoded_rows(rows):
+    rows = rows.astype(F32)
+    return (rows[0:1] + rows[1:2]) + rows[2:3]
+
+
+def core_sum_kernel(meta_ref, kept_ref, arrived_ref, loss_ref, own_ref, *piece_refs):
+    row = meta_ref[0]
+    loss = loss_ref[:1] + decoded_rows(arrived_ref[384:, :])
+    cells = coded_rows(jnp.broadcast_to(loss, (16, loss.shape[1])))
+    for j in range(4):
+        where = (row + j) % 4 if j == 0 else lax.bitwise_xor(row, j)
+        for q in range(2):
+            rows = pl.ds(pl.multiple_of(96 * where + 48 * q, 48), 48)
+            total = kept_ref[2 * where + q] + arrived_ref[rows, :].astype(F32)
+            if j == 0:
+                own_ref[48 * q : 48 * q + 48, :] = total
+            else:
+                piece_refs[j - 1][48 * q : 48 * q + 48, :] = total.astype(BF16)
+        if j == 0:
+            own_ref[96:, :] = jnp.broadcast_to(loss, (8, loss.shape[1]))
+        else:
+            piece_refs[j - 1][96:, :] = cells
+
+
+def core_sum(meta, kept, arrived, loss):
+    channels = kept.shape[2]
+    return pl.pallas_call(
+        core_sum_kernel,
+        in_specs=[smem()] + [vmem()] * 3,
+        out_specs=[vmem()] * 4,
+        out_shape=[jax.ShapeDtypeStruct((104, channels), F32)]
+        + [jax.ShapeDtypeStruct((112, channels), BF16)] * 3,
+        compiler_params=params(12),
+        cost_estimate=pl.CostEstimate(flops=1_000_000, bytes_accessed=4_000_000, transcendentals=0),
+    )(meta, kept, arrived, loss)
+
+
+def row_sum_kernel(meta_ref, own_ref, one_ref, two_ref, three_ref, *out_refs):
+    place = meta_ref[1]
+    refs = (one_ref, two_ref, three_ref)
+    first, second, third = [decoded_rows(r[96:, :]) for r in refs]
+    loss = (own_ref[96:97, :] + first) + (second + third)
+    for j in range(4):
+        start = pl.multiple_of(24 * lax.bitwise_xor(place, j), 8)
+        at = 48 * (lax.bitwise_xor(place, j) // 2)
+        total = own_ref[pl.ds(start, 24), :]
+        upper = lax.bitwise_xor(place, j) % 2 == 1
+        for r in refs:
+            rows = r[pl.ds(pl.multiple_of(at, 48), 48), :].astype(F32)
+            total = total + jnp.where(upper, rows[24:], rows[:24])
+        out_refs[j][:24, :] = total
+        out_refs[j][24:, :] = jnp.broadcast_to(loss, (8, loss.shape[1]))
+
+
+def row_sum(meta, own, arrived):
+    channels = own.shape[1]
+    return pl.pallas_call(
+        row_sum_kernel,
+        in_specs=[smem()] + [vmem()] * 4,
+        out_specs=[vmem()] * 4,
+        out_shape=[jax.ShapeDtypeStruct((32, channels), F32)] * 4,
+        compiler_params=params(8),
+        cost_estimate=pl.CostEstimate(flops=1_000_000, bytes_accessed=2_000_000, transcendentals=0),
+    )(meta, own, *arrived)
+
+
+def lift_kernel(full_ref, disc_ref, out_ref):
+    rows = full_ref.shape[0]
+    both = jnp.concatenate(split(full_ref[...]), axis=0)
+    wide = disc_ref.shape[0] // 3
+    for i in range(3):
+        cols = slice(wide * i, wide * i + wide)
+        product = lax.dot_general(
+            both, disc_ref[cols, :], (((1,), (1,)), ((), ())), preferred_element_type=F32
+        )
+        out_ref[:, cols] = product[:rows] + product[rows:]
+
+
+def lift(full, disc_in):
+    return pl.pallas_call(
+        lift_kernel,
+        in_specs=[vmem()] * 2,
+        out_specs=vmem(),
+        out_shape=jax.ShapeDtypeStruct((full.shape[0], disc_in.shape[0]), F32),
+        compiler_params=params(12),
+        cost_estimate=pl.CostEstimate(flops=300_000_000, bytes_accessed=3_500_000, transcendentals=0),
+    )(full, disc_in)
+
+
 def critic_kernel(
-    meta_ref, lifted_ref, mine_ref, other_ref, proj_ref, conv_ref, score_ref,
-    out_ref, loss_ref,
-    feed_s, y_s, pre_s, grad_s, turned_s, back_s, att_s,
+    meta_ref, lifted_hbm, mine_hbm, other_hbm, proj_0, proj_1, proj_2, proj_3, conv_hbm, score_ref,
+    keep_ref, send_ref, loss_ref,
+    feed_s, y_s, pre_s, grad_s, turned_s, back_s, att_s, proj_s, conv_ref, lifted_ref, mine_ref, other_ref, proj_sem, conv_sem,
 ):
     live, first_frame, half = (meta_ref[0], meta_ref[1], meta_ref[2])
-    total_frames = meta_ref[3]
+    total_frames, core = (meta_ref[3], meta_ref[4])
+    row = meta_ref[5]
+    pairs = [(lifted_hbm, lifted_ref), (mine_hbm, mine_ref), (other_hbm, other_ref)]
+    for hop, block in enumerate((proj_0, proj_1, proj_2, proj_3)):
+        for j in range(4):
+            where = ((row - hop + 4) % 4) * 4 + ((half + j) % 2) * 2 + (core + j // 2) % 2
+            pairs.append((block.at[j], proj_s.at[where]))
+    proj_copies = [pltpu.make_async_copy(a, b, proj_sem.at[i]) for i, (a, b) in enumerate(pairs)]
+    conv_copies = [
+        pltpu.make_async_copy(conv_hbm.at[g], conv_ref.at[g], conv_sem.at[g])
+        for g in range(conv_ref.shape[0])
+    ]
+    for copy in proj_copies + conv_copies:
+        copy.start()
     ext = lifted_ref.shape[0]
     own_out = (ext - 2 * HALO) // STRIDE
     tiles = lifted_ref.shape[1] // 128
+    for copy in proj_copies:
+        copy.wait()
     feed = lifted_ref[...]
-    feed = feed + jnp.dot(mine_ref[...], proj_ref[half], preferred_element_type=F32)
-    feed = feed + jnp.dot(other_ref[...], proj_ref[1 - half], preferred_element_type=F32)
+    for ref, which in ((mine_ref, half), (other_ref, 1 - half)):
+        proj = proj_s[pl.ds(8 * which, 8)].reshape(HALF_ATT, lifted_ref.shape[1])
+        feed = feed + jnp.dot(ref[...], proj, preferred_element_type=F32)
     frame = first_frame - HALO + lax.broadcasted_iota(jnp.int32, (ext, 1), 0)
     inside = (frame >= 0) & (frame < live)
     feed = jnp.where(inside, feed, 0.0).astype(BF16).astype(F32)
@@ -175,6 +317,8 @@
     rows = y_s.shape[0]
     low = low_lanes((rows, 128))
     low_out = low_lanes((80, 128))
+    for copy in conv_copies:
+        copy.wait()
 
     @pl.loop(0, tiles)
     def _(tile):
@@ -210,6 +354,7 @@
     own = valid & (slot >= REACH) & (slot < REACH + own_out)
     loss = jnp.sum(jnp.where(own, shortfall * shortfall, 0.0), axis=0, keepdims=True)
     loss_ref[...] = jnp.broadcast_to(loss, loss_ref.shape)
+    send_ref[384:, :] = coded_rows(jnp.broadcast_to(loss, (16, send_ref.shape[1])))
     push = jnp.where(valid, -2.0 * shortfall, 0.0)
     grad = push * score * (sig * (1.0 + pre * (1.0 - sig)))
     grad = jnp.where(valid, grad, 0.0).astype(BF16).astype(F32)
@@ -246,17 +391,24 @@
             both = jnp.where(first_frame + STRIDE * step + b < live, both, 0.0)
             back_s[b * own_out : (b + 1) * own_out, lanes] = both.astype(BF16)
 
+    first = core == 0
     for part, ref in enumerate((mine_ref, other_ref)):
         own_rows = ref[...].astype(F32)[HALO : ext - HALO, :]
+        lefts = []
         for c in range(HALF_HEADS):
-            cols = slice(c * 128, c * 128 + 128)
-            att_s[...] = own_rows[:, cols]
+            att_s[...] = own_rows[:, c * 128 : c * 128 + 128]
             left = jnp.concatenate(
                 [att_s[pl.ds(b, own_out, stride=STRIDE), :] for b in range(STRIDE)], axis=0
             )
-            left = jnp.transpose(left).astype(BF16)
-            which = half if part == 0 else 1 - half
-            out_ref[which, cols, :] = jnp.dot(left, back_s[...], preferred_element_type=F32)
+            lefts.append(jnp.transpose(left))
+        left = jnp.concatenate(lefts, axis=0).astype(BF16)
+        which = half if part == 0 else 1 - half
+        for q in range(4):
+            block = jnp.dot(left[96 * q : 96 * q + 96], back_s[...], preferred_element_type=F32)
+            one, two = (block[:48], block[48:])
+            keep_ref[4 * which + q] = jnp.where(first, one, two)
+            rows = pl.ds(pl.multiple_of(48 * (4 * which + q), 48), 48)
+            send_ref[rows, :] = jnp.where(first, two, one).astype(BF16)
 
 
 def critic(meta, lifted, mine, other, proj, conv, score):
@@ -264,11 +416,12 @@
     own = ext - 2 * HALO
     return pl.pallas_call(
         critic_kernel,
-        in_specs=[smem()] + [vmem()] * 6,
-        out_specs=[vmem(), vmem()],
+        in_specs=[smem()] + [anywhere()] * 8 + [vmem()],
+        out_specs=[vmem(), vmem(), vmem()],
         out_shape=[
-            jax.ShapeDtypeStruct((2, HALF_ATT, channels), F32),
-            jax.ShapeDtypeStruct((8, 128), F32),
+            jax.ShapeDtypeStruct((8, 48, channels), F32),
+            jax.ShapeDtypeStruct((400, channels), BF16),
+            jax.ShapeDtypeStruct((8, channels), F32),
         ],
         scratch_shapes=[
             pltpu.VMEM((channels // 128, 384, 128), F32),
@@ -278,12 +431,19 @@
             pltpu.VMEM((88, 128), F32),
             pltpu.VMEM((own, channels), BF16),
             pltpu.VMEM((own, 128), F32),
+            pltpu.VMEM((16, 48, channels), BF16),
+            pltpu.VMEM(conv.shape, BF16),
+            pltpu.VMEM(lifted.shape, F32),
+            pltpu.VMEM(mine.shape, BF16),
+            pltpu.VMEM(other.shape, BF16),
+            pltpu.SemaphoreType.DMA((19,)),
+            pltpu.SemaphoreType.DMA((conv.shape[0],)),
         ],
-        compiler_params=params(),
+        compiler_params=params(58),
         cost_estimate=pl.CostEstimate(
             flops=3_000_000_000, bytes_accessed=14_000_000, transcendentals=100_000
         ),
-    )(meta, lifted, mine, other, proj, conv, score)
+    )(meta, lifted, mine, other, *proj, conv, score)
 
 
 def shards(
@@ -303,93 +463,107 @@
     def turn(x, hops):
         return lax.ppermute(x, "seq", [(i, (i + 4 * hops) % seq_size) for i in range(seq_size)])
 
-    def across(x):
+    def swap(x, dp_bits, seq_bits):
         pairs = []
         for i in range(dp_size * seq_size):
-            d, s = divmod(i, seq_size)
-            pairs.append((i, (d ^ 1) * seq_size + (s ^ 2)))
+            d, q = divmod(i, seq_size)
+            pairs.append((i, (d ^ dp_bits) * seq_size + (q ^ seq_bits)))
         return lax.ppermute(x, ("dp", "seq"), pairs)
 
+    def at(x, i):
+        return lax.dynamic_index_in_dim(x, i, axis=0, keepdims=False)
+
     att = 2 * HALF_ATT
-    own_cols = lax.dynamic_slice_in_dim(kv_weight, core * att, att, axis=1)
-    partner_cols = lax.dynamic_slice_in_dim(kv_weight, (1 - core) * att, att, axis=1)
-    pair_rows = jnp.concatenate([own_cols, flip(partner_cols, 1)], axis=0)
-    near = lax.dynamic_slice_in_dim(pair_rows, half * HALF_ATT, HALF_ATT, axis=1)
-    far = across(lax.dynamic_slice_in_dim(pair_rows, (1 - half) * HALF_ATT, HALF_ATT, axis=1))
+
+    def head_cols(which):
+        parts = [
+            lax.dynamic_slice_in_dim(kv_weight, kind * att + which * HALF_ATT, HALF_ATT, axis=1)
+            for kind in (0, 1)
+        ]
+        return jnp.concatenate(parts, axis=1)
+
+    near = head_cols(half)
+    far = swap(head_cols(1 - half), 1, 2)
     hops = (1, 3, 2)
-    near_blocks = [near] + [turn(near, j) for j in hops]
+    near_turned = [turn(near, j) for j in hops]
+    near, near_turned, far, states_in, queries_in, hidden_in, proj_in = lax.optimization_barrier(
+        (near, near_turned, far, states[0], queries[0], hidden[0], out_proj)
+    )
+
+    lower = clip % 2
+    channels = disc_in.shape[1]
+    near_blocks = [near] + near_turned
     far_blocks = [far] + [turn(far, j) for j in hops]
-
-    rows_in = jnp.concatenate([queries[0], hidden[0]], axis=1)
+    state_far = flip(states_in, 2)
+    state_near = flip(states_in, 1)
+    proj_own = jnp.dot(proj_in, disc_in, preferred_element_type=F32).astype(BF16)
+    proj_far = swap(proj_own, 1, 2)
     up = [(i, i + 1) for i in range(seq_size - 1)]
     down = [(i + 1, i) for i in range(seq_size - 1)]
-    before = lax.ppermute(rows_in[frames - HALO :], "seq", up)
-    after = lax.ppermute(rows_in[:HALO], "seq", down)
-    rows_ext = jnp.concatenate([before, rows_in, after], axis=0)
-    query_ext, hidden_ext = (rows_ext[:, :att], rows_ext[:, att:])
+    before = jnp.concatenate([queries_in[frames - HALO :], hidden_in[frames - HALO :]], axis=1)
+    after = jnp.concatenate([queries_in[:HALO], hidden_in[:HALO]], axis=1)
+    before, after = (lax.ppermute(before, "seq", up), lax.ppermute(after, "seq", down))
+    query_ext = jnp.concatenate([before[:, :att], queries_in, after[:, :att]], axis=0)
+    hidden_ext = jnp.concatenate([before[:, att:], hidden_in, after[:, att:]], axis=0)
     query_mine = lax.dynamic_slice_in_dim(query_ext, half * HALF_ATT, HALF_ATT, axis=1)
-    query_far = flip(lax.dynamic_slice_in_dim(query_ext, (1 - half) * HALF_ATT, HALF_ATT, axis=1), 2)
-
-    state_far = flip(states[0], 2)
-    state_parts = [states[0], flip(states[0], 1), state_far, flip(state_far, 1)]
-
-    proj_own = jnp.dot(out_proj, disc_in, preferred_element_type=F32).astype(BF16)
-    proj = lax.all_gather(proj_own, "seq", axis=0, tiled=True).reshape(2, HALF_ATT, disc_in.shape[1])
+    query_sent = lax.dynamic_slice_in_dim(query_ext, (1 - half) * HALF_ATT, HALF_ATT, axis=1)
     lifted = jnp.dot(hidden_ext, disc_in, preferred_element_type=F32)
-    conv = arrange(conv_weight)
 
     cols = []
-    for hop in (0,) + hops:
+    for hop in (0, 1, 3, 2):
         for flip_half in (0, 1):
-            for flip_core in (0, 1):
-                where = (((row - hop) % 4) * 2 + (half ^ flip_half)) * 2 + (core ^ flip_core)
-                cols.append(where * kv_weight.shape[0])
+            where = (((row - hop) % 4) * 2 + (half ^ flip_half)) * 2 + core
+            cols.append(where * kv_weight.shape[0])
+    total_frames = frames * seq_size
+    cols = jnp.stack(cols + [core]).astype(jnp.int32)
+    meta = jnp.stack([clip_states, core, half, row]).astype(jnp.int32)
+    meta2 = jnp.stack([clip_frames, seq * frames, half, jnp.int32(total_frames), core, row])
+    meta3 = jnp.stack([row, 2 * half + lower, clip // 2]).astype(jnp.int32)
     blocks = [b for pair in zip(near_blocks, far_blocks) for b in pair]
-    mine_kv = project(jnp.stack(cols).astype(jnp.int32), state_parts, blocks)
+    tables = (cols, meta, meta2.astype(jnp.int32), meta3)
+    blocks, state_far, state_near, tables, proj_far, query_mine, query_sent, lifted = lax.optimization_barrier(
+        (blocks, state_far, state_near, tables, proj_far, query_mine, query_sent, lifted)
+    )
+    cols, meta, meta2, meta3 = tables
+    state_parts = [states_in, state_near, state_far, flip(state_far, 1)]
+    kept, sent = project(cols, state_parts, blocks)
+    mine_kv = (kept + flip(sent, 1)).reshape(256, HALF_ATT)
+
+    mine_kv, conv_in, query_sent, proj_own, proj_far = lax.optimization_barrier(
+        (mine_kv, conv_weight, query_sent, proj_own, proj_far)
+    )
     got = [mine_kv] + [turn(mine_kv, j) for j in (1, 2, 3)]
+    query_far = flip(query_sent, 2)
+    proj_pair = jnp.stack([proj_own, proj_far])
+    proj_quad = jnp.concatenate([proj_pair, flip(proj_pair, 1)], axis=0)
+    conv = arrange(conv_in)
+    got, conv, query_far, proj_quad = lax.optimization_barrier((got, conv, query_far, proj_quad))
     other = [flip(g, 1) for g in got]
-
-    meta = jnp.stack([clip_states, core, half, row]).astype(jnp.int32)
+    proj = [proj_quad] + [turn(proj_quad, j) for j in (1, 2, 3)]
+
     attended_far = flip(attend(meta, query_far, got, other), 2)
     attended_mine = attend(meta, query_mine, got, other)
 
-    total_frames = frames * seq_size
-    meta2 = jnp.stack([clip_frames, seq * frames, half, jnp.int32(total_frames)]).astype(jnp.int32)
-    grown, loss = critic(
+    kept, sent, loss = critic(
         meta2, lifted, attended_mine, attended_far, proj, conv, score_weight.reshape(1, -1)
     )
 
     own_rows = att // seq_size
-    channels = disc_in.shape[1]
-
-    def at(x, i):
-        return lax.dynamic_index_in_dim(x, i, axis=0, keepdims=False)
-
-    by_core = grown.reshape(seq_size // 2, 2, own_rows, channels)
-    pick_core = lambda c: lax.dynamic_index_in_dim(by_core, c, axis=1, keepdims=False)
-    total = pick_core(core) + flip(pick_core(1 - core), 1)
-    loss = loss + flip(loss, 1)
-    by_row = total.reshape(4, 2, own_rows, channels)
-    sent = [turn(at(by_row, (row + j) % 4).astype(BF16), j) for j in (1, 2, 3)]
-    sent_loss = [turn(loss, j) for j in (1, 2, 3)]
-    total = at(by_row, row)
-    for s, l in zip(sent, sent_loss):
-        total, loss = (total + s.astype(F32), loss + l)
-    total = at(total, half) + flip(at(total, 1 - half), 2)
-    loss = loss + flip(loss, 2)
-    share = own_rows // dp_size
-    pieces = total.reshape(dp_size, share, channels)
-    loss_row = jnp.broadcast_to(loss[:1, :1], (dp_size, 1, channels))
-    pieces = lax.all_to_all(jnp.concatenate([pieces, loss_row], axis=1), "dp", 0, 0, tiled=True)
-    pieces = jnp.sum(pieces, axis=0)
-    total_loss = pieces[share, 0]
-    spread = jnp.broadcast_to(pieces[None, :share], (dp_size, share, channels))
-    full = lax.all_to_all(spread, "dp", 0, 0, tiled=True).reshape(own_rows, channels)
-    high = lax.reduce_precision(full, 8, 7)
-    high, low = (high.astype(BF16), (full - high).astype(BF16))
-    contract = (((1,), (1,)), ((), ()))
-    grad_proj = lax.dot_general(high, disc_in, contract, preferred_element_type=F32)
-    grad_proj = grad_proj + lax.dot_general(low, disc_in, contract, preferred_element_type=F32)
+    share = own_rows // 2
+    own, *pieces = core_sum(meta3, kept, flip(sent, 1), loss)
+    arrived = [flip(p, 4 * (j + 1)) for j, p in enumerate(pieces)]
+    own, *pieces = row_sum(meta3, own, arrived)
+    a, b, c = [swap(p, j & 1, j & 2) for j, p in zip((1, 2, 3), pieces)]
+    total = (own + a) + (b + c)
+    a, b, c = [swap(total, d, 0) for d in (2, 4, 6)]
+    total = (total + a) + (b + c)
+    total = total + swap(total, 8, 0)
+    total_loss = total[share, 0]
+    total = total[:share]
+    beside = swap(total, 1, 0)
+    first = lower == 0
+    total = jnp.concatenate([jnp.where(first, total, beside), jnp.where(first, beside, total)], axis=0)
+    grad_proj = lift(total, disc_in)
     counted = jnp.sum((frame_len + STRIDE - 1) // STRIDE).astype(F32)
     return (grad_proj, total_loss / counted)
 

time: 227 us -> 208 us (0.916)
  waiting for transfers between devices: 57.8 us -> 80.7 us
  blocking collectives: 17.8 us -> 0 us
  between operations: 16.8 us -> 3.5 us
  local copies, waits for them, and re-layouts: 22.7 us -> 12.3 us
  other arithmetic: 12.3 us -> 5.35 us
  Pallas kernels: 37.9 us -> 43.8 us
  starting transfers between devices: 50.8 us -> 56.3 us
  matrix products: 7.45 us -> 3.09 us
    ppermute x3 -> x12, waiting for transfers between devices: 6.36 us -> 34.1 us  [the longest x10 34.1 us: swap(): return lax.ppermute(x, ('dp', 'seq'), pairs)]
    ppermute x3 -> x12, starting transfers between devices: 4.61 us -> 24.1 us  [the longest x10 19.7 us: swap(): return lax.ppermute(x, ('dp', 'seq'), pairs)]
    all_to_all x1 -> x0, blocking collectives: 17.8 us -> none  [shards(): lax.all_to_all(jnp.concatenate([pieces, loss_row], axis=1), 'dp', 0, 0, t...]
    ppermute x15 -> x12, starting transfers between devices: 25.5 us -> 15 us  [turn(): lax.ppermute(x, 'seq', [(i, (i + 4 * hops) % seq_size) for i in range(seq...]
    all_to_all x1 -> x0, waiting for transfers between devices: 7.62 us -> none  [shards(): lax.all_to_all(spread, 'dp', 0, 0, tiled=True).reshape(own_rows, channels)]
    ppermute x15 -> x12, waiting for transfers between devices: 23 us -> 30.4 us  [turn(): lax.ppermute(x, 'seq', [(i, (i + 4 * hops) % seq_size) for i in range(seq...]
    pallas_call x2 -> x5, Pallas kernels: 17.1 us -> 24.1 us  [the longest x1 15 us: critic(): pl.pallas_call(critic_kernel, in_specs=[smem()] + [anywhere()] * 8 + [vme...]
    unnamed x40 -> x42, local copies, waits for them, and re-layouts: 11.4 us -> 5.76 us
  transfers between devices with their start and end apart: 34 -> 39, of which waited for: 13 -> 21; matrix products, arithmetic and copies ran while one was open for 7% -> 5% of each run, Pallas kernels for 11% -> 10%
where the time goes in v2:
time: 208 us; the launch traced here: 205 us
  waiting for transfers between devices  80.7 us (39%)
  starting transfers between devices  56.3 us (27%)
  Pallas kernels  43.8 us (21%)
  local copies, waits for them, and re-layouts  12.3 us (6%)
  other arithmetic  5.35 us (3%)
  between operations  3.5 us (2%)
  matrix products  3.09 us (1%)
    ppermute x10, waiting for transfers between devices, swap(): return lax.ppermute(x, ('dp', 'seq'), pairs)  34.1 us
    ppermute x12, waiting for transfers between devices, turn(): lax.ppermute(x, 'seq', [(i, (i + 4 * hops) % seq_size) for i in range(seq...  30.4 us
    ppermute x10, starting transfers between devices, swap(): return lax.ppermute(x, ('dp', 'seq'), pairs)  19.7 us
    ppermute x15, starting transfers between devices, flip(): return lax.ppermute(x, 'seq', [(i, i ^ bit) for i in range(seq_size)])  17.2 us
    ppermute x15, waiting for transfers between devices, flip(): return lax.ppermute(x, 'seq', [(i, i ^ bit) for i in range(seq_size)])  16.2 us
    pallas_call x1, Pallas kernels, critic(): pl.pallas_call(critic_kernel, in_specs=[smem()] + [anywhere()] * 8 + [vme...  15 us
    ppermute x12, starting transfers between devices, turn(): lax.ppermute(x, 'seq', [(i, (i + 4 * hops) % seq_size) for i in range(seq...  15 us
    pallas_call x2, Pallas kernels, attend(): pl.pallas_call(attend_kernel, grid=(width // HEAD_DIM,), in_specs=[smem()...  11.4 us
  transfers between devices with their start and end apart: 39, of which 21 were waited for; matrix products, arithmetic and copies ran while one was open for 5% of the time, Pallas kernels for 10%

profile of v2, /device:TPU:32, one launch (start us, length us, event | category | flops | bytes accessed | tf_op | source)
XLA Modules:
  0.0 205.1 jit_solution(13837496555703192176)
XLA Ops:
  0.7 1.5 constant_dynamic-slice_fusion.3
  3.0 3.2 %collective-permute-start.2 = (bf16[256,768]{1,0:T(8,128)(2,1)}, bf16[256,768]{1,0:T(8,128)(2,1)}, u32[]{:S(2)}, u32[]{:S(2)}) collective-permute-start(bf16[256,768]{1,0:T(8,128)(2,1)} %pad_maximum_fusion.1.refs_4_), channel_id=1, source_target_pairs={{0,8},{1,9},{2,10},{3,11},{4,12},{5,13},{6,14},{7,15},{8,0},{9,1},... | collective-permute-start | bytes 1179656 | tf_op jit(solution)/shard_map/ppermute | solution.py:464
  6.2 1.1 collective-permute-start.1
  9.0 2.8 %collective-permute-start.3 = (bf16[256,768]{1,0:T(8,128)(2,1)}, bf16[256,768]{1,0:T(8,128)(2,1)}, u32[]{:S(2)}, u32[]{:S(2)}) collective-permute-start(bf16[256,768]{1,0:T(8,128)(2,1)} %pad_maximum_fusion.2), channel_id=1, source_target_pairs={{0,18},{1,19},{2,16},{3,17},{4,22},{5,23},{6,20},{7,21},{8,26},{9,... | collective-permute-start | bytes 1179656 | tf_op jit(solution)/shard_map/ppermute | solution.py:471
  12.5 1.3 stack.90.meta_ref
  15.3 1.5 collective-permute-done.2.refs_10_
  16.8 7.6 %collective-permute-done.1.refs_8_ = bf16[256,768]{1,0:T(8,128)(2,1)} collective-permute-done((bf16[256,768]{1,0:T(8,128)(2,1)}, bf16[256,768]{1,0:T(8,128)(2,1)}, u32[]{:S(2)}, u32[]{:S(2)}) %collective-permute-start.1) | collective-permute-done | bytes 393248 | tf_op jit(solution)/shard_map/ppermute | solution.py:464
  24.5 2.8 %collective-permute-start.6 = (bf16[256,768]{1,0:T(8,128)(2,1)}, bf16[256,768]{1,0:T(8,128)(2,1)S(1)}, u32[]{:S(2)}, u32[]{:S(2)}) collective-permute-start(bf16[256,768]{1,0:T(8,128)(2,1)} %collective-permute-done.3.refs_5_), channel_id=1, source_target_pairs={{0,8},{1,9},{2,10},{3,11},{4,12},{5,13},{6,14},{7,15},{8,0},{9,1},... | collective-permute-start | bytes 1179656 | tf_op jit(solution)/shard_map/ppermute | solution.py:464
  27.3 1.2 collective-permute-start.5
  30.4 1.3 collective-permute-start.11
  31.7 3.2 %collective-permute-start.10 = (bf16[40,2304]{1,0:T(8,128)(2,1)S(1)}, bf16[40,2304]{1,0:T(8,128)(2,1)S(1)}, u32[]{:S(2)}, u32[]{:S(2)}) collective-permute-start(bf16[40,2304]{1,0:T(8,128)(2,1)S(1)} %pad_maximum_fusion.6), channel_id=1, source_target_pairs={{0,1},{1,2},{2,3},{3,4},{4,5},{5,6},{6,7},{7,8},{8,9},{9,10},{10,1... | collective-permute-start | bytes 552968 | tf_op jit(solution)/shard_map/ppermute | solution.py:505
  34.9 2.7 %collective-permute-start.8 = (bf16[64,4096]{1,0:T(8,128)(2,1)}, bf16[64,4096]{1,0:T(8,128)(2,1)S(1)}, u32[]{:S(2)}, u32[]{:S(2)}) collective-permute-start(bf16[64,4096]{1,0:T(8,128)(2,1)} %bitcast.37), channel_id=1, source_target_pairs={{0,1},{1,0},{2,3},{3,2},{4,5},{5,4},{6,7},{7,6},{8,9},{9,8},{10,11... | collective-permute-start | bytes 1572872 | tf_op jit(solution)/shard_map/ppermute | solution.py:461
  38.3 3.4 %collective-permute-start.7 = (bf16[64,4096]{1,0:T(8,128)(2,1)S(1)}, bf16[64,4096]{1,0:T(8,128)(2,1)S(1)}, u32[]{:S(2)}, u32[]{:S(2)}) collective-permute-start(bf16[64,4096]{1,0:T(8,128)(2,1)S(1)} %bitcast.39), channel_id=1, source_target_pairs={{0,2},{1,3},{2,0},{3,1},{4,6},{5,7},{6,4},{7,5},{8,10},{9,11},{10,... | collective-permute-start | bytes 1572872 | tf_op jit(solution)/shard_map/ppermute | solution.py:461
  41.7 2.2 %collective-permute-start.9 = (bf16[48,1024]{1,0:T(8,128)(2,1)S(1)}, bf16[48,1024]{1,0:T(8,128)(2,1)S(1)}, u32[]{:S(2)}, u32[]{:S(2)}) collective-permute-start(bf16[48,1024]{1,0:T(8,128)(2,1)S(1)} %convolution_convert_fusion), channel_id=1, source_target_pairs={{0,18},{1,19},{2,16},{3,17},{4,22},{5,23},{6,20},{7,21},{8,26},{9,... | collective-permute-start | bytes 294920 | tf_op jit(solution)/shard_map/ppermute | solution.py:471
  43.9 13.0 %collective-permute-done.9 = bf16[48,1024]{1,0:T(8,128)(2,1)S(1)} collective-permute-done((bf16[48,1024]{1,0:T(8,128)(2,1)S(1)}, bf16[48,1024]{1,0:T(8,128)(2,1)S(1)}, u32[]{:S(2)}, u32[]{:S(2)}) %collective-permute-start.9) | collective-permute-done | bytes 98336 | tf_op jit(solution)/shard_map/ppermute | solution.py:471
  58.8 2.4 %fusion.lifted_hbm = f32[336,1024]{1,0:T(8,128)} fusion(bf16[1536,1024]{1,0:T(8,128)(2,1)S(1)} %copy-done.1, bf16[40,1536]{1,0:T(8,128)(2,1)S(1)} %slice.43, bf16[256,1536]{1,0:T(8,128)(2,1)S(1)} %bitcast.43, bf16[40,1536]{1,0:T(8,128)(2,1)S(1)} %slice.42), kind=kOutput, calls=%fused_computation.1 | convolution fusion | flops 1060061184 | bytes 5554176 | tf_op jit(solution)/shard_map/dot_general | solution.py:510
  61.2 8.2 %collective-permute-done.4.refs_7_ = bf16[256,768]{1,0:T(8,128)(2,1)S(1)} collective-permute-done((bf16[256,768]{1,0:T(8,128)(2,1)}, bf16[256,768]{1,0:T(8,128)(2,1)S(1)}, u32[]{:S(2)}, u32[]{:S(2)}) %collective-permute-start.4) | collective-permute-done | bytes 393248 | tf_op jit(solution)/shard_map/ppermute | solution.py:464
  70.2 1.3 collective-permute-done.12.refs_3_
  72.3 5.8 %shard_map.113 = (f32[4,64,384]{2,1,0:T(8,128)}, f32[4,64,384]{2,1,0:T(8,128)}) custom-call(s32[9]{0:T(128)} %stack.83.cols_ref, bf16[64,4096]{1,0:T(8,128)(2,1)} %bitcast.38, bf16[64,4096]{1,0:T(8,128)(2,1)} %copy-done.7, bf16[64,4096]{1,0:T(8,128)(2,1)} %copy-done.8, bf16[64,4096]{1,0:T(8,128)(2,1)} %copy-done.9, ...), custom_call_target="tpu_custom_call" | custom-call | flops 800000000 | bytes 6000000 | tf_op jit(solution)/shard_map/pallas_call | solution.py:115
  78.4 1.8 collective-permute-done.13
  81.3 1.8 collective-permute-start.15
  83.4 2.2 %collective-permute-start.17 = (bf16[336,384]{1,0:T(8,128)(2,1)}, bf16[336,384]{1,0:T(8,128)(2,1)S(1)}, u32[]{:S(2)}, u32[]{:S(2)}) collective-permute-start(bf16[336,384]{1,0:T(8,128)(2,1)} %get-tuple-element.85), channel_id=1, source_target_pairs={{0,2},{1,3},{2,0},{3,1},{4,6},{5,7},{6,4},{7,5},{8,10},{9,11},{10,... | collective-permute-start | bytes 774152 | tf_op jit(solution)/shard_map/ppermute | solution.py:461
  85.6 8.4 %shard_map.114.conv_hbm = bf16[16,256,768]{2,1,0:T(8,128)(2,1)} custom-call(bf16[41,64,1024]{2,1,0:T(8,128)(2,1)} %w_ref), custom_call_target="tpu_custom_call" | custom-call | flops 20000000 | bytes 20000000 | tf_op jit(solution)/shard_map/pallas_call | solution.py:69
  95.1 7.6 %collective-permute-done.14.refs_1_ = f32[256,384]{1,0:T(8,128)S(1)} collective-permute-done((f32[256,384]{1,0:T(8,128)S(1)}, f32[256,384]{1,0:T(8,128)S(1)}, u32[]{:S(2)}, u32[]{:S(2)}) %collective-permute-start.14) | collective-permute-done | bytes 393248 | tf_op jit(solution)/shard_map/ppermute | solution.py:464
  104.6 1.1 collective-permute-start.25
  106.4 5.7 %shard_map.116 = bf16[336,384]{1,0:T(8,128)(2,1)S(1)} custom-call(s32[4]{0:T(128)S(1)} %pad_add_fusion.meta_ref, bf16[336,384]{1,0:T(8,128)(2,1)S(1)} %collective-permute-done.17.q_ref, f32[256,384]{1,0:T(8,128)S(1)} %bitcast.31, f32[256,384]{1,0:T(8,128)S(1)} %collective-permute-done.14.refs_1_, f32[256,384]{1,0:T(8,128)S(1)} %collective-permute-done.15.refs_2_, ...), custom_call_target="tpu_custom_call" | custom-call | flops 1056964608 | bytes 4000000 | tf_op jit(solution)/shard_map/pallas_call | solution.py:172
  112.1 2.6 %collective-permute-start.23 = (bf16[336,384]{1,0:T(8,128)(2,1)S(1)}, bf16[336,384]{1,0:T(8,128)(2,1)S(1)}, u32[]{:S(2)}, u32[]{:S(2)}) collective-permute-start(bf16[336,384]{1,0:T(8,128)(2,1)S(1)} %shard_map.116), channel_id=1, source_target_pairs={{0,2},{1,3},{2,0},{3,1},{4,6},{5,7},{6,4},{7,5},{8,10},{9,11},{10,... | collective-permute-start | bytes 774152 | tf_op jit(solution)/shard_map/ppermute | solution.py:461
  114.7 5.7 %shard_map.115.mine_hbm = bf16[336,384]{1,0:T(8,128)(2,1)S(1)} custom-call(s32[4]{0:T(128)S(1)} %pad_add_fusion.meta_ref, bf16[336,384]{1,0:T(8,128)(2,1)S(1)} %get-tuple-element.67.q_ref, f32[256,384]{1,0:T(8,128)S(1)} %bitcast.32, f32[256,384]{1,0:T(8,128)S(1)} %collective-permute-done.14.refs_1_, f32[256,384]{1,0:T(8,128)S(1)} %collective-permute-done.15.refs_2_, ...), custom_call_target="tpu_custom_call" | custom-call | flops 1056964608 | bytes 4000000 | tf_op jit(solution)/shard_map/pallas_call | solution.py:172
  121.1 4.4 %collective-permute-done.24.proj_1 = bf16[4,48,1024]{2,1,0:T(8,128)(2,1)S(1)} collective-permute-done((bf16[4,48,1024]{2,1,0:T(8,128)(2,1)S(1)}, bf16[4,48,1024]{2,1,0:T(8,128)(2,1)S(1)}, u32[]{:S(2)}, u32[]{:S(2)}) %collective-permute-start.24) | collective-permute-done | bytes 393248 | tf_op jit(solution)/shard_map/ppermute | solution.py:464
  126.9 15.0 %shard_map.117 = (f32[8,48,1024]{2,1,0:T(8,128)}, bf16[400,1024]{1,0:T(8,128)(2,1)}, f32[8,1024]{1,0:T(8,128)}) custom-call(s32[6]{0:T(128)} %stack.90.meta_ref, f32[336,1024]{1,0:T(8,128)} %fusion.lifted_hbm, bf16[336,384]{1,0:T(8,128)(2,1)} %copy-done.4, bf16[336,384]{1,0:T(8,128)(2,1)} %copy-done.20, bf16[4,48,1024]{2,1,0:T(8,128)(2,1)} %copy-done.10, ...), custom_call_target="tpu_custom_call" | custom-call | flops 3000000000 | bytes 14000000 | tf_op jit(solution)/shard_map/pallas_call | solution.py:417
  142.0 2.5 %collective-permute-done.27.arrived_ref = bf16[400,1024]{1,0:T(8,128)(2,1)S(1)} collective-permute-done((bf16[400,1024]{1,0:T(8,128)(2,1)}, bf16[400,1024]{1,0:T(8,128)(2,1)S(1)}, u32[]{:S(2)}, u32[]{:S(2)}) %collective-permute-start.27) | collective-permute-done | bytes 819232 | tf_op jit(solution)/shard_map/ppermute | solution.py:461
  144.6 1.4 copy-done.2
  147.5 2.0 collective-permute-start.29
  149.6 2.6 %collective-permute-start.30 = (bf16[112,1024]{1,0:T(8,128)(2,1)S(1)}, bf16[112,1024]{1,0:T(8,128)(2,1)S(1)}, u32[]{:S(2)}, u32[]{:S(2)}) collective-permute-start(bf16[112,1024]{1,0:T(8,128)(2,1)S(1)} %get-tuple-element.101), channel_id=1, source_target_pairs={{0,12},{1,13},{2,14},{3,15},{4,8},{5,9},{6,10},{7,11},{8,4},{9,5},... | collective-permute-start | bytes 688136 | tf_op jit(solution)/shard_map/ppermute | solution.py:461
  152.2 3.7 %collective-permute-done.28.one_ref = bf16[112,1024]{1,0:T(8,128)(2,1)S(1)} collective-permute-done((bf16[112,1024]{1,0:T(8,128)(2,1)S(1)}, bf16[112,1024]{1,0:T(8,128)(2,1)S(1)}, u32[]{:S(2)}, u32[]{:S(2)}) %collective-permute-start.28) | collective-permute-done | bytes 229408 | tf_op jit(solution)/shard_map/ppermute | solution.py:461
  156.0 4.3 %collective-permute-done.29.two_ref = bf16[112,1024]{1,0:T(8,128)(2,1)S(1)} collective-permute-done((bf16[112,1024]{1,0:T(8,128)(2,1)S(1)}, bf16[112,1024]{1,0:T(8,128)(2,1)S(1)}, u32[]{:S(2)}, u32[]{:S(2)}) %collective-permute-start.29) | collective-permute-done | bytes 229408 | tf_op jit(solution)/shard_map/ppermute | solution.py:461
  160.2 2.6 %collective-permute-done.30.three_ref = bf16[112,1024]{1,0:T(8,128)(2,1)S(1)} collective-permute-done((bf16[112,1024]{1,0:T(8,128)(2,1)S(1)}, bf16[112,1024]{1,0:T(8,128)(2,1)S(1)}, u32[]{:S(2)}, u32[]{:S(2)}) %collective-permute-start.30) | collective-permute-done | bytes 229408 | tf_op jit(solution)/shard_map/ppermute | solution.py:461
  164.2 3.1 %collective-permute-start.32 = (f32[32,1024]{1,0:T(8,128)S(1)}, f32[32,1024]{1,0:T(8,128)S(1)}, u32[]{:S(2)}, u32[]{:S(2)}) collective-permute-start(f32[32,1024]{1,0:T(8,128)S(1)} %get-tuple-element.104), channel_id=1, source_target_pairs={{0,2},{1,3},{2,0},{3,1},{4,6},{5,7},{6,4},{7,5},{8,10},{9,11},{10,... | collective-permute-start | bytes 393224 | tf_op jit(solution)/shard_map/ppermute | solution.py:471
  169.1 3.2 %collective-permute-done.32 = f32[32,1024]{1,0:T(8,128)S(1)} collective-permute-done((f32[32,1024]{1,0:T(8,128)S(1)}, f32[32,1024]{1,0:T(8,128)S(1)}, u32[]{:S(2)}, u32[]{:S(2)}) %collective-permute-start.32) | collective-permute-done | bytes 131104 | tf_op jit(solution)/shard_map/ppermute | solution.py:471
  172.3 1.5 collective-permute-done.33
  173.8 2.0 collective-permute-start.36
  175.8 1.5 collective-permute-start.35
  177.2 1.4 collective-permute-start.34
  178.6 6.4 %collective-permute-done.36 = f32[32,1024]{1,0:T(8,128)S(1)} collective-permute-done((f32[32,1024]{1,0:T(8,128)S(1)}, f32[32,1024]{1,0:T(8,128)S(1)}, u32[]{:S(2)}, u32[]{:S(2)}) %collective-permute-start.36) | collective-permute-done | bytes 131104 | tf_op jit(solution)/shard_map/ppermute | solution.py:471
  186.2 5.0 %collective-permute-start.37 = (f32[32,1024]{1,0:T(8,128)S(1)}, f32[32,1024]{1,0:T(8,128)S(1)}, u32[]{:S(2)}, u32[]{:S(2)}) collective-permute-start(f32[32,1024]{1,0:T(8,128)S(1)} %add_add_fusion), channel_id=1, source_target_pairs={{0,128},{1,129},{2,130},{3,131},{4,132},{5,133},{6,134},{7,135},{8... | collective-permute-start | bytes 393224 | tf_op jit(solution)/shard_map/ppermute | solution.py:471
  191.3 5.1 %collective-permute-done.37 = f32[32,1024]{1,0:T(8,128)S(1)} collective-permute-done((f32[32,1024]{1,0:T(8,128)S(1)}, f32[32,1024]{1,0:T(8,128)S(1)}, u32[]{:S(2)}, u32[]{:S(2)}) %collective-permute-start.37) | collective-permute-done | bytes 131104 | tf_op jit(solution)/shard_map/ppermute | solution.py:471
  198.3 2.9 %collective-permute-done.38 = f32[24,1024]{1,0:T(8,128)} collective-permute-done((f32[24,1024]{1,0:T(8,128)S(1)}, f32[24,1024]{1,0:T(8,128)}, u32[]{:S(2)}, u32[]{:S(2)}) %collective-permute-start.38) | collective-permute-done | bytes 98336 | tf_op jit(solution)/shard_map/ppermute | solution.py:471
  202.1 1.8 shard_map.120
  (110 shorter events, 25.9 us)
Async XLA Ops:
  0.6 37.0 %copy-start = (bf16[48,1536]{1,0:T(8,128)(2,1)S(1)}, bf16[48,1536]{1,0:T(8,128)(2,1)}, u32[]{:S(2)}) copy-start(bf16[48,1536]{1,0:T(8,128)(2,1)} %param.14) | copy-start | bytes 442372
  0.6 11.1 %copy-start.16 = (s32[16]{0:T(128)S(1)}, s32[16]{0:T(128)}, u32[]{:S(2)}) copy-start(s32[16]{0:T(128)} %param.19) | copy-start | bytes 196
  0.7 11.1 %copy-start.15 = (s32[16]{0:T(128)S(1)}, s32[16]{0:T(128)}, u32[]{:S(2)}) copy-start(s32[16]{0:T(128)} %param.18) | copy-start | bytes 196
  0.7 36.9 %copy-start.1 = (bf16[1536,1024]{1,0:T(8,128)(2,1)S(1)}, bf16[1536,1024]{1,0:T(8,128)(2,1)}, u32[]{:S(2)}) copy-start(bf16[1536,1024]{1,0:T(8,128)(2,1)} %disc_ref.1) | copy-start | bytes 9437188
  3.0 13.9 %collective-permute-start.2 = (bf16[256,768]{1,0:T(8,128)(2,1)}, bf16[256,768]{1,0:T(8,128)(2,1)}, u32[]{:S(2)}, u32[]{:S(2)}) collective-permute-start(bf16[256,768]{1,0:T(8,128)(2,1)} %pad_maximum_fusion.1.refs_4_), channel_id=1, source_target_pairs={{0,8},{1,9},{2,10},{3,11},{4,12},{5,13},{6,14},{7,15},{8,0},{9,1},... | collective-permute-start | bytes 1179656 | tf_op jit(solution)/shard_map/ppermute | solution.py:464
  6.2 18.3 %collective-permute-start.1 = (bf16[256,768]{1,0:T(8,128)(2,1)}, bf16[256,768]{1,0:T(8,128)(2,1)}, u32[]{:S(2)}, u32[]{:S(2)}) collective-permute-start(bf16[256,768]{1,0:T(8,128)(2,1)} %pad_maximum_fusion.1.refs_4_), channel_id=1, source_target_pairs={{0,12},{1,13},{2,14},{3,15},{4,0},{5,1},{6,2},{7,3},{8,4},{9,5},{1... | collective-permute-start | bytes 1179656 | tf_op jit(solution)/shard_map/ppermute | solution.py:464
  7.2 17.2 %collective-permute-start = (bf16[256,768]{1,0:T(8,128)(2,1)}, bf16[256,768]{1,0:T(8,128)(2,1)}, u32[]{:S(2)}, u32[]{:S(2)}) collective-permute-start(bf16[256,768]{1,0:T(8,128)(2,1)} %pad_maximum_fusion.1.refs_4_), channel_id=1, source_target_pairs={{0,4},{1,5},{2,6},{3,7},{4,8},{5,9},{6,10},{7,11},{8,12},{9,13},{1... | collective-permute-start | bytes 1179656 | tf_op jit(solution)/shard_map/ppermute | solution.py:464
  9.0 15.5 %collective-permute-start.3 = (bf16[256,768]{1,0:T(8,128)(2,1)}, bf16[256,768]{1,0:T(8,128)(2,1)}, u32[]{:S(2)}, u32[]{:S(2)}) collective-permute-start(bf16[256,768]{1,0:T(8,128)(2,1)} %pad_maximum_fusion.2), channel_id=1, source_target_pairs={{0,18},{1,19},{2,16},{3,17},{4,22},{5,23},{6,20},{7,21},{8,26},{9,... | collective-permute-start | bytes 1179656 | tf_op jit(solution)/shard_map/ppermute | solution.py:471
  14.4 23.9 %copy-start.6 = (bf16[1,64,4096]{2,1,0:T(8,128)(2,1)S(1)}, bf16[1,64,4096]{2,1,0:T(8,128)(2,1)}, u32[]{:S(2)}) copy-start(bf16[1,64,4096]{2,1,0:T(8,128)(2,1)} %param.10) | copy-start | bytes 1572868
  14.4 29.5 %copy-start.5 = (bf16[1,256,768]{2,1,0:T(8,128)(2,1)S(1)}, bf16[1,256,768]{2,1,0:T(8,128)(2,1)}, u32[]{:S(2)}) copy-start(bf16[1,256,768]{2,1,0:T(8,128)(2,1)} %param.12) | copy-start | bytes 1179652
  24.5 36.7 %collective-permute-start.6 = (bf16[256,768]{1,0:T(8,128)(2,1)}, bf16[256,768]{1,0:T(8,128)(2,1)S(1)}, u32[]{:S(2)}, u32[]{:S(2)}) collective-permute-start(bf16[256,768]{1,0:T(8,128)(2,1)} %collective-permute-done.3.refs_5_), channel_id=1, source_target_pairs={{0,8},{1,9},{2,10},{3,11},{4,12},{5,13},{6,14},{7,15},{8,0},{9,1},... | collective-permute-start | bytes 1179656 | tf_op jit(solution)/shard_map/ppermute | solution.py:464
  27.3 33.9 %collective-permute-start.5 = (bf16[256,768]{1,0:T(8,128)(2,1)}, bf16[256,768]{1,0:T(8,128)(2,1)S(1)}, u32[]{:S(2)}, u32[]{:S(2)}) collective-permute-start(bf16[256,768]{1,0:T(8,128)(2,1)} %collective-permute-done.3.refs_5_), channel_id=1, source_target_pairs={{0,12},{1,13},{2,14},{3,15},{4,0},{5,1},{6,2},{7,3},{8,4},{9,5},{1... | collective-permute-start | bytes 1179656 | tf_op jit(solution)/shard_map/ppermute | solution.py:464
  30.4 7.9 %collective-permute-start.11 = (bf16[40,2304]{1,0:T(8,128)(2,1)S(1)}, bf16[40,2304]{1,0:T(8,128)(2,1)S(1)}, u32[]{:S(2)}, u32[]{:S(2)}) collective-permute-start(bf16[40,2304]{1,0:T(8,128)(2,1)S(1)} %pad_maximum_fusion.7), channel_id=1, source_target_pairs={{1,0},{2,1},{3,2},{4,3},{5,4},{6,5},{7,6},{8,7},{9,8},{10,9},{11,1... | collective-permute-start | bytes 552968 | tf_op jit(solution)/shard_map/ppermute | solution.py:505
  31.7 27.1 %copy-start.14 = (bf16[1,256,1536]{2,1,0:T(8,128)(2,1)S(1)}, bf16[1,256,1536]{2,1,0:T(8,128)(2,1)}, u32[]{:S(2)}) copy-start(bf16[1,256,1536]{2,1,0:T(8,128)(2,1)} %param.13) | copy-start | bytes 2359300
  31.7 10.0 %collective-permute-start.10 = (bf16[40,2304]{1,0:T(8,128)(2,1)S(1)}, bf16[40,2304]{1,0:T(8,128)(2,1)S(1)}, u32[]{:S(2)}, u32[]{:S(2)}) collective-permute-start(bf16[40,2304]{1,0:T(8,128)(2,1)S(1)} %pad_maximum_fusion.6), channel_id=1, source_target_pairs={{0,1},{1,2},{2,3},{3,4},{4,5},{5,6},{6,7},{7,8},{8,9},{9,10},{10,1... | collective-permute-start | bytes 552968 | tf_op jit(solution)/shard_map/ppermute | solution.py:505
  34.9 34.6 %collective-permute-start.8 = (bf16[64,4096]{1,0:T(8,128)(2,1)}, bf16[64,4096]{1,0:T(8,128)(2,1)S(1)}, u32[]{:S(2)}, u32[]{:S(2)}) collective-permute-start(bf16[64,4096]{1,0:T(8,128)(2,1)} %bitcast.37), channel_id=1, source_target_pairs={{0,1},{1,0},{2,3},{3,2},{4,5},{5,4},{6,7},{7,6},{8,9},{9,8},{10,11... | collective-permute-start | bytes 1572872 | tf_op jit(solution)/shard_map/ppermute | solution.py:461
  38.3 31.2 %collective-permute-start.7 = (bf16[64,4096]{1,0:T(8,128)(2,1)S(1)}, bf16[64,4096]{1,0:T(8,128)(2,1)S(1)}, u32[]{:S(2)}, u32[]{:S(2)}) collective-permute-start(bf16[64,4096]{1,0:T(8,128)(2,1)S(1)} %bitcast.39), channel_id=1, source_target_pairs={{0,2},{1,3},{2,0},{3,1},{4,6},{5,7},{6,4},{7,5},{8,10},{9,11},{10,... | collective-permute-start | bytes 1572872 | tf_op jit(solution)/shard_map/ppermute | solution.py:461
  41.7 15.3 %collective-permute-start.9 = (bf16[48,1024]{1,0:T(8,128)(2,1)S(1)}, bf16[48,1024]{1,0:T(8,128)(2,1)S(1)}, u32[]{:S(2)}, u32[]{:S(2)}) collective-permute-start(bf16[48,1024]{1,0:T(8,128)(2,1)S(1)} %convolution_convert_fusion), channel_id=1, source_target_pairs={{0,18},{1,19},{2,16},{3,17},{4,22},{5,23},{6,20},{7,21},{8,26},{9,... | collective-permute-start | bytes 294920 | tf_op jit(solution)/shard_map/ppermute | solution.py:471
  57.0 12.5 %collective-permute-start.4 = (bf16[256,768]{1,0:T(8,128)(2,1)}, bf16[256,768]{1,0:T(8,128)(2,1)S(1)}, u32[]{:S(2)}, u32[]{:S(2)}) collective-permute-start(bf16[256,768]{1,0:T(8,128)(2,1)} %collective-permute-done.3.refs_5_), channel_id=1, source_target_pairs={{0,4},{1,5},{2,6},{3,7},{4,8},{5,9},{6,10},{7,11},{8,12},{9,13},{1... | collective-permute-start | bytes 1179656 | tf_op jit(solution)/shard_map/ppermute | solution.py:464
  61.2 10.3 %copy-start.11 = (bf16[256,768]{1,0:T(8,128)(2,1)}, bf16[256,768]{1,0:T(8,128)(2,1)S(1)}, u32[]{:S(2)}) copy-start(bf16[256,768]{1,0:T(8,128)(2,1)S(1)} %collective-permute-done.6.refs_11_) | copy-start | bytes 1179652
  69.5 2.0 collective-permute-start.12
  78.1 2.0 collective-permute-start.13
  81.2 12.8 %collective-permute-start.16 = (f32[256,384]{1,0:T(8,128)S(1)}, f32[256,384]{1,0:T(8,128)S(1)}, u32[]{:S(2)}, u32[]{:S(2)}) collective-permute-start(f32[256,384]{1,0:T(8,128)S(1)} %bitcast.27), channel_id=1, source_target_pairs={{0,12},{1,13},{2,14},{3,15},{4,0},{5,1},{6,2},{7,3},{8,4},{9,5},{1... | collective-permute-start | bytes 1179656 | tf_op jit(solution)/shard_map/ppermute | solution.py:464
  81.3 13.8 %collective-permute-start.15 = (f32[256,384]{1,0:T(8,128)S(1)}, f32[256,384]{1,0:T(8,128)S(1)}, u32[]{:S(2)}, u32[]{:S(2)}) collective-permute-start(f32[256,384]{1,0:T(8,128)S(1)} %bitcast.28), channel_id=1, source_target_pairs={{0,8},{1,9},{2,10},{3,11},{4,12},{5,13},{6,14},{7,15},{8,0},{9,1},... | collective-permute-start | bytes 1179656 | tf_op jit(solution)/shard_map/ppermute | solution.py:464
  83.1 19.5 %collective-permute-start.14 = (f32[256,384]{1,0:T(8,128)S(1)}, f32[256,384]{1,0:T(8,128)S(1)}, u32[]{:S(2)}, u32[]{:S(2)}) collective-permute-start(f32[256,384]{1,0:T(8,128)S(1)} %bitcast.29), channel_id=1, source_target_pairs={{0,4},{1,5},{2,6},{3,7},{4,8},{5,9},{6,10},{7,11},{8,12},{9,13},{1... | collective-permute-start | bytes 1179656 | tf_op jit(solution)/shard_map/ppermute | solution.py:464
  83.3 10.6 %collective-permute-start.18 = (bf16[2,48,1024]{2,1,0:T(8,128)(2,1)S(1)}, bf16[2,48,1024]{2,1,0:T(8,128)(2,1)S(1)}, u32[]{:S(2)}, u32[]{:S(2)}) collective-permute-start(bf16[2,48,1024]{2,1,0:T(8,128)(2,1)S(1)} %pad_maximum_fusion.4), channel_id=1, source_target_pairs={{0,1},{1,0},{2,3},{3,2},{4,5},{5,4},{6,7},{7,6},{8,9},{9,8},{10,11... | collective-permute-start | bytes 589832 | tf_op jit(solution)/shard_map/ppermute | solution.py:461
  83.4 10.6 %collective-permute-start.17 = (bf16[336,384]{1,0:T(8,128)(2,1)}, bf16[336,384]{1,0:T(8,128)(2,1)S(1)}, u32[]{:S(2)}, u32[]{:S(2)}) collective-permute-start(bf16[336,384]{1,0:T(8,128)(2,1)} %get-tuple-element.85), channel_id=1, source_target_pairs={{0,2},{1,3},{2,0},{3,1},{4,6},{5,7},{6,4},{7,5},{8,10},{9,11},{10,... | collective-permute-start | bytes 774152 | tf_op jit(solution)/shard_map/ppermute | solution.py:461
  94.0 26.3 %copy-start.10 = (bf16[4,48,1024]{2,1,0:T(8,128)(2,1)}, bf16[4,48,1024]{2,1,0:T(8,128)(2,1)S(1)}, u32[]{:S(2)}) copy-start(bf16[4,48,1024]{2,1,0:T(8,128)(2,1)S(1)} %pad_maximum_fusion.3.proj_0) | copy-start | bytes 1179652
  102.6 1.9 collective-permute-start.19
  102.7 3.0 %collective-permute-start.20 = (f32[256,384]{1,0:T(8,128)S(1)}, f32[256,384]{1,0:T(8,128)S(1)}, u32[]{:S(2)}, u32[]{:S(2)}) collective-permute-start(f32[256,384]{1,0:T(8,128)S(1)} %collective-permute-done.14.refs_1_), channel_id=1, source_target_pairs={{0,1},{1,0},{2,3},{3,2},{4,5},{5,4},{6,7},{7,6},{8,9},{9,8},{10,11... | collective-permute-start | bytes 1179656 | tf_op jit(solution)/shard_map/ppermute | solution.py:461
  103.2 3.2 %collective-permute-start.21 = (f32[256,384]{1,0:T(8,128)S(1)}, f32[256,384]{1,0:T(8,128)S(1)}, u32[]{:S(2)}, u32[]{:S(2)}) collective-permute-start(f32[256,384]{1,0:T(8,128)S(1)} %collective-permute-done.15.refs_2_), channel_id=1, source_target_pairs={{0,1},{1,0},{2,3},{3,2},{4,5},{5,4},{6,7},{7,6},{8,9},{9,8},{10,11... | collective-permute-start | bytes 1179656 | tf_op jit(solution)/shard_map/ppermute | solution.py:461
  103.2 3.2 %collective-permute-start.22 = (f32[256,384]{1,0:T(8,128)S(1)}, f32[256,384]{1,0:T(8,128)S(1)}, u32[]{:S(2)}, u32[]{:S(2)}) collective-permute-start(f32[256,384]{1,0:T(8,128)S(1)} %collective-permute-done.16.refs_3_), channel_id=1, source_target_pairs={{0,1},{1,0},{2,3},{3,2},{4,5},{5,4},{6,7},{7,6},{8,9},{9,8},{10,11... | collective-permute-start | bytes 1179656 | tf_op jit(solution)/shard_map/ppermute | solution.py:461
  103.7 17.4 %collective-permute-start.26 = (bf16[4,48,1024]{2,1,0:T(8,128)(2,1)S(1)}, bf16[4,48,1024]{2,1,0:T(8,128)(2,1)S(1)}, u32[]{:S(2)}, u32[]{:S(2)}) collective-permute-start(bf16[4,48,1024]{2,1,0:T(8,128)(2,1)S(1)} %pad_maximum_fusion.3.proj_0), channel_id=1, source_target_pairs={{0,12},{1,13},{2,14},{3,15},{4,0},{5,1},{6,2},{7,3},{8,4},{9,5},{1... | collective-permute-start | bytes 1179656 | tf_op jit(solution)/shard_map/ppermute | solution.py:464
  104.6 16.5 %collective-permute-start.25 = (bf16[4,48,1024]{2,1,0:T(8,128)(2,1)S(1)}, bf16[4,48,1024]{2,1,0:T(8,128)(2,1)S(1)}, u32[]{:S(2)}, u32[]{:S(2)}) collective-permute-start(bf16[4,48,1024]{2,1,0:T(8,128)(2,1)S(1)} %pad_maximum_fusion.3.proj_0), channel_id=1, source_target_pairs={{0,8},{1,9},{2,10},{3,11},{4,12},{5,13},{6,14},{7,15},{8,0},{9,1},... | collective-permute-start | bytes 1179656 | tf_op jit(solution)/shard_map/ppermute | solution.py:464
  105.6 19.8 %collective-permute-start.24 = (bf16[4,48,1024]{2,1,0:T(8,128)(2,1)S(1)}, bf16[4,48,1024]{2,1,0:T(8,128)(2,1)S(1)}, u32[]{:S(2)}, u32[]{:S(2)}) collective-permute-start(bf16[4,48,1024]{2,1,0:T(8,128)(2,1)S(1)} %pad_maximum_fusion.3.proj_0), channel_id=1, source_target_pairs={{0,4},{1,5},{2,6},{3,7},{4,8},{5,9},{6,10},{7,11},{8,12},{9,13},{1... | collective-permute-start | bytes 1179656 | tf_op jit(solution)/shard_map/ppermute | solution.py:464
  112.1 13.4 %collective-permute-start.23 = (bf16[336,384]{1,0:T(8,128)(2,1)S(1)}, bf16[336,384]{1,0:T(8,128)(2,1)S(1)}, u32[]{:S(2)}, u32[]{:S(2)}) collective-permute-start(bf16[336,384]{1,0:T(8,128)(2,1)S(1)} %shard_map.116), channel_id=1, source_target_pairs={{0,2},{1,3},{2,0},{3,1},{4,6},{5,7},{6,4},{7,5},{8,10},{9,11},{10,... | collective-permute-start | bytes 774152 | tf_op jit(solution)/shard_map/ppermute | solution.py:461
  141.9 2.6 %collective-permute-start.27 = (bf16[400,1024]{1,0:T(8,128)(2,1)}, bf16[400,1024]{1,0:T(8,128)(2,1)S(1)}, u32[]{:S(2)}, u32[]{:S(2)}) collective-permute-start(bf16[400,1024]{1,0:T(8,128)(2,1)} %get-tuple-element.96), channel_id=1, source_target_pairs={{0,1},{1,0},{2,3},{3,2},{4,5},{5,4},{6,7},{7,6},{8,9},{9,8},{10,11... | collective-permute-start | bytes 2457608 | tf_op jit(solution)/shard_map/ppermute | solution.py:461
  147.4 8.5 %collective-permute-start.28 = (bf16[112,1024]{1,0:T(8,128)(2,1)S(1)}, bf16[112,1024]{1,0:T(8,128)(2,1)S(1)}, u32[]{:S(2)}, u32[]{:S(2)}) collective-permute-start(bf16[112,1024]{1,0:T(8,128)(2,1)S(1)} %get-tuple-element.99), channel_id=1, source_target_pairs={{0,4},{1,5},{2,6},{3,7},{4,0},{5,1},{6,2},{7,3},{8,12},{9,13},{10,... | collective-permute-start | bytes 688136 | tf_op jit(solution)/shard_map/ppermute | solution.py:461
  147.5 12.7 %collective-permute-start.29 = (bf16[112,1024]{1,0:T(8,128)(2,1)S(1)}, bf16[112,1024]{1,0:T(8,128)(2,1)S(1)}, u32[]{:S(2)}, u32[]{:S(2)}) collective-permute-start(bf16[112,1024]{1,0:T(8,128)(2,1)S(1)} %get-tuple-element.100), channel_id=1, source_target_pairs={{0,8},{1,9},{2,10},{3,11},{4,12},{5,13},{6,14},{7,15},{8,0},{9,1},... | collective-permute-start | bytes 688136 | tf_op jit(solution)/shard_map/ppermute | solution.py:461
  149.6 13.2 %collective-permute-start.30 = (bf16[112,1024]{1,0:T(8,128)(2,1)S(1)}, bf16[112,1024]{1,0:T(8,128)(2,1)S(1)}, u32[]{:S(2)}, u32[]{:S(2)}) collective-permute-start(bf16[112,1024]{1,0:T(8,128)(2,1)S(1)} %get-tuple-element.101), channel_id=1, source_target_pairs={{0,12},{1,13},{2,14},{3,15},{4,8},{5,9},{6,10},{7,11},{8,4},{9,5},... | collective-permute-start | bytes 688136 | tf_op jit(solution)/shard_map/ppermute | solution.py:461
  163.5 5.6 %collective-permute-start.31 = (f32[32,1024]{1,0:T(8,128)S(1)}, f32[32,1024]{1,0:T(8,128)S(1)}, u32[]{:S(2)}, u32[]{:S(2)}) collective-permute-start(f32[32,1024]{1,0:T(8,128)S(1)} %get-tuple-element.103), channel_id=1, source_target_pairs={{0,16},{1,17},{2,18},{3,19},{4,20},{5,21},{6,22},{7,23},{8,24},{9,... | collective-permute-start | bytes 393224 | tf_op jit(solution)/shard_map/ppermute | solution.py:471
  164.2 8.1 %collective-permute-start.32 = (f32[32,1024]{1,0:T(8,128)S(1)}, f32[32,1024]{1,0:T(8,128)S(1)}, u32[]{:S(2)}, u32[]{:S(2)}) collective-permute-start(f32[32,1024]{1,0:T(8,128)S(1)} %get-tuple-element.104), channel_id=1, source_target_pairs={{0,2},{1,3},{2,0},{3,1},{4,6},{5,7},{6,4},{7,5},{8,10},{9,11},{10,... | collective-permute-start | bytes 393224 | tf_op jit(solution)/shard_map/ppermute | solution.py:471
  167.3 6.4 %collective-permute-start.33 = (f32[32,1024]{1,0:T(8,128)S(1)}, f32[32,1024]{1,0:T(8,128)S(1)}, u32[]{:S(2)}, u32[]{:S(2)}) collective-permute-start(f32[32,1024]{1,0:T(8,128)S(1)} %get-tuple-element.105), channel_id=1, source_target_pairs={{0,18},{1,19},{2,16},{3,17},{4,22},{5,23},{6,20},{7,21},{8,26},{9,... | collective-permute-start | bytes 393224 | tf_op jit(solution)/shard_map/ppermute | solution.py:471
  173.8 11.2 %collective-permute-start.36 = (f32[32,1024]{1,0:T(8,128)S(1)}, f32[32,1024]{1,0:T(8,128)S(1)}, u32[]{:S(2)}, u32[]{:S(2)}) collective-permute-start(f32[32,1024]{1,0:T(8,128)S(1)} %add_add_fusion.1), channel_id=1, source_target_pairs={{0,96},{1,97},{2,98},{3,99},{4,100},{5,101},{6,102},{7,103},{8,104... | collective-permute-start | bytes 393224 | tf_op jit(solution)/shard_map/ppermute | solution.py:471
  175.8 10.0 %collective-permute-start.35 = (f32[32,1024]{1,0:T(8,128)S(1)}, f32[32,1024]{1,0:T(8,128)S(1)}, u32[]{:S(2)}, u32[]{:S(2)}) collective-permute-start(f32[32,1024]{1,0:T(8,128)S(1)} %add_add_fusion.1), channel_id=1, source_target_pairs={{0,64},{1,65},{2,66},{3,67},{4,68},{5,69},{6,70},{7,71},{8,72},{9,... | collective-permute-start | bytes 393224 | tf_op jit(solution)/shard_map/ppermute | solution.py:471
  177.2 9.0 %collective-permute-start.34 = (f32[32,1024]{1,0:T(8,128)S(1)}, f32[32,1024]{1,0:T(8,128)S(1)}, u32[]{:S(2)}, u32[]{:S(2)}) collective-permute-start(f32[32,1024]{1,0:T(8,128)S(1)} %add_add_fusion.1), channel_id=1, source_target_pairs={{0,32},{1,33},{2,34},{3,35},{4,36},{5,37},{6,38},{7,39},{8,40},{9,... | collective-permute-start | bytes 393224 | tf_op jit(solution)/shard_map/ppermute | solution.py:471
  186.2 10.1 %collective-permute-start.37 = (f32[32,1024]{1,0:T(8,128)S(1)}, f32[32,1024]{1,0:T(8,128)S(1)}, u32[]{:S(2)}, u32[]{:S(2)}) collective-permute-start(f32[32,1024]{1,0:T(8,128)S(1)} %add_add_fusion), channel_id=1, source_target_pairs={{0,128},{1,129},{2,130},{3,131},{4,132},{5,133},{6,134},{7,135},{8... | collective-permute-start | bytes 393224 | tf_op jit(solution)/shard_map/ppermute | solution.py:471
  196.4 4.8 %collective-permute-start.38 = (f32[24,1024]{1,0:T(8,128)S(1)}, f32[24,1024]{1,0:T(8,128)}, u32[]{:S(2)}, u32[]{:S(2)}) collective-permute-start(f32[24,1024]{1,0:T(8,128)S(1)} %slice.44), channel_id=1, source_target_pairs={{0,16},{1,17},{2,18},{3,19},{4,20},{5,21},{6,22},{7,23},{8,24},{9,... | collective-permute-start | bytes 294920 | tf_op jit(solution)/shard_map/ppermute | solution.py:471
  (12 other events, 27.7 us)

commit v3 on v2

--- a/solution.py
+++ b/solution.py
@@ -280,18 +280,13 @@
 
 
 def critic_kernel(
-    meta_ref, lifted_hbm, mine_hbm, other_hbm, proj_0, proj_1, proj_2, proj_3, conv_hbm, score_ref,
+    meta_ref, lifted_hbm, mine_hbm, other_hbm, proj_hbm, conv_hbm, score_ref,
     keep_ref, send_ref, loss_ref,
     feed_s, y_s, pre_s, grad_s, turned_s, back_s, att_s, proj_s, conv_ref, lifted_ref, mine_ref, other_ref, proj_sem, conv_sem,
 ):
     live, first_frame, half = (meta_ref[0], meta_ref[1], meta_ref[2])
     total_frames, core = (meta_ref[3], meta_ref[4])
-    row = meta_ref[5]
-    pairs = [(lifted_hbm, lifted_ref), (mine_hbm, mine_ref), (other_hbm, other_ref)]
-    for hop, block in enumerate((proj_0, proj_1, proj_2, proj_3)):
-        for j in range(4):
-            where = ((row - hop + 4) % 4) * 4 + ((half + j) % 2) * 2 + (core + j // 2) % 2
-            pairs.append((block.at[j], proj_s.at[where]))
+    pairs = [(lifted_hbm, lifted_ref), (mine_hbm, mine_ref), (other_hbm, other_ref), (proj_hbm, proj_s)]
     proj_copies = [pltpu.make_async_copy(a, b, proj_sem.at[i]) for i, (a, b) in enumerate(pairs)]
     conv_copies = [
         pltpu.make_async_copy(conv_hbm.at[g], conv_ref.at[g], conv_sem.at[g])
@@ -306,7 +301,7 @@
         copy.wait()
     feed = lifted_ref[...]
     for ref, which in ((mine_ref, half), (other_ref, 1 - half)):
-        proj = proj_s[pl.ds(8 * which, 8)].reshape(HALF_ATT, lifted_ref.shape[1])
+        proj = proj_s[pl.ds(pl.multiple_of(HALF_ATT * which, HALF_ATT), HALF_ATT), :]
         feed = feed + jnp.dot(ref[...], proj, preferred_element_type=F32)
     frame = first_frame - HALO + lax.broadcasted_iota(jnp.int32, (ext, 1), 0)
     inside = (frame >= 0) & (frame < live)
@@ -416,7 +411,7 @@
     own = ext - 2 * HALO
     return pl.pallas_call(
         critic_kernel,
-        in_specs=[smem()] + [anywhere()] * 8 + [vmem()],
+        in_specs=[smem()] + [anywhere()] * 5 + [vmem()],
         out_specs=[vmem(), vmem(), vmem()],
         out_shape=[
             jax.ShapeDtypeStruct((8, 48, channels), F32),
@@ -431,19 +426,19 @@
             pltpu.VMEM((88, 128), F32),
             pltpu.VMEM((own, channels), BF16),
             pltpu.VMEM((own, 128), F32),
-            pltpu.VMEM((16, 48, channels), BF16),
+            pltpu.VMEM(proj.shape, BF16),
             pltpu.VMEM(conv.shape, BF16),
             pltpu.VMEM(lifted.shape, F32),
             pltpu.VMEM(mine.shape, BF16),
             pltpu.VMEM(other.shape, BF16),
-            pltpu.SemaphoreType.DMA((19,)),
+            pltpu.SemaphoreType.DMA((4,)),
             pltpu.SemaphoreType.DMA((conv.shape[0],)),
         ],
         compiler_params=params(58),
         cost_estimate=pl.CostEstimate(
             flops=3_000_000_000, bytes_accessed=14_000_000, transcendentals=100_000
         ),
-    )(meta, lifted, mine, other, *proj, conv, score)
+    )(meta, lifted, mine, other, proj, conv, score)
 
 
 def shards(
@@ -475,6 +470,10 @@
 
     att = 2 * HALF_ATT
 
+    proj_own = jnp.dot(out_proj, disc_in, preferred_element_type=F32).astype(BF16)
+    kv_weight, proj_own = lax.optimization_barrier((kv_weight, proj_own))
+    proj = lax.all_gather(proj_own, "seq", axis=0, tiled=True)
+
     def head_cols(which):
         parts = [
             lax.dynamic_slice_in_dim(kv_weight, kind * att + which * HALF_ATT, HALF_ATT, axis=1)
@@ -486,28 +485,23 @@
     far = swap(head_cols(1 - half), 1, 2)
     hops = (1, 3, 2)
     near_turned = [turn(near, j) for j in hops]
-    near, near_turned, far, states_in, queries_in, hidden_in, proj_in = lax.optimization_barrier(
-        (near, near_turned, far, states[0], queries[0], hidden[0], out_proj)
+    states_in = states[0]
+    state_far, state_near = (flip(states_in, 2), flip(states_in, 1))
+    near, near_turned, far, state_far, state_near = lax.optimization_barrier(
+        (near, near_turned, far, state_far, state_near)
     )
 
     lower = clip % 2
     channels = disc_in.shape[1]
     near_blocks = [near] + near_turned
     far_blocks = [far] + [turn(far, j) for j in hops]
-    state_far = flip(states_in, 2)
-    state_near = flip(states_in, 1)
-    proj_own = jnp.dot(proj_in, disc_in, preferred_element_type=F32).astype(BF16)
-    proj_far = swap(proj_own, 1, 2)
+    far_blocks[1], queries_in, hidden_in = lax.optimization_barrier((far_blocks[1], queries[0], hidden[0]))
     up = [(i, i + 1) for i in range(seq_size - 1)]
     down = [(i + 1, i) for i in range(seq_size - 1)]
     before = jnp.concatenate([queries_in[frames - HALO :], hidden_in[frames - HALO :]], axis=1)
     after = jnp.concatenate([queries_in[:HALO], hidden_in[:HALO]], axis=1)
     before, after = (lax.ppermute(before, "seq", up), lax.ppermute(after, "seq", down))
-    query_ext = jnp.concatenate([before[:, :att], queries_in, after[:, :att]], axis=0)
-    hidden_ext = jnp.concatenate([before[:, att:], hidden_in, after[:, att:]], axis=0)
-    query_mine = lax.dynamic_slice_in_dim(query_ext, half * HALF_ATT, HALF_ATT, axis=1)
-    query_sent = lax.dynamic_slice_in_dim(query_ext, (1 - half) * HALF_ATT, HALF_ATT, axis=1)
-    lifted = jnp.dot(hidden_ext, disc_in, preferred_element_type=F32)
+    state_last = flip(state_far, 1)
 
     cols = []
     for hop in (0, 1, 3, 2):
@@ -517,29 +511,34 @@
     total_frames = frames * seq_size
     cols = jnp.stack(cols + [core]).astype(jnp.int32)
     meta = jnp.stack([clip_states, core, half, row]).astype(jnp.int32)
-    meta2 = jnp.stack([clip_frames, seq * frames, half, jnp.int32(total_frames), core, row])
+    meta2 = jnp.stack([clip_frames, seq * frames, half, jnp.int32(total_frames), core])
     meta3 = jnp.stack([row, 2 * half + lower, clip // 2]).astype(jnp.int32)
     blocks = [b for pair in zip(near_blocks, far_blocks) for b in pair]
     tables = (cols, meta, meta2.astype(jnp.int32), meta3)
-    blocks, state_far, state_near, tables, proj_far, query_mine, query_sent, lifted = lax.optimization_barrier(
-        (blocks, state_far, state_near, tables, proj_far, query_mine, query_sent, lifted)
+    blocks, state_last, tables, before, after = lax.optimization_barrier(
+        (blocks, state_last, tables, before, after)
     )
     cols, meta, meta2, meta3 = tables
-    state_parts = [states_in, state_near, state_far, flip(state_far, 1)]
+    state_parts = [states_in, state_near, state_far, state_last]
     kept, sent = project(cols, state_parts, blocks)
     mine_kv = (kept + flip(sent, 1)).reshape(256, HALF_ATT)
 
-    mine_kv, conv_in, query_sent, proj_own, proj_far = lax.optimization_barrier(
-        (mine_kv, conv_weight, query_sent, proj_own, proj_far)
+    mine_kv, conv_in, proj = lax.optimization_barrier((mine_kv, conv_weight, proj))
+    got = [mine_kv] + [turn(mine_kv, j) for j in (1, 2, 3)]
+    got[1], queries_in, hidden_in, before, after = lax.optimization_barrier(
+        (got[1], queries[0], hidden[0], before, after)
     )
-    got = [mine_kv] + [turn(mine_kv, j) for j in (1, 2, 3)]
-    query_far = flip(query_sent, 2)
-    proj_pair = jnp.stack([proj_own, proj_far])
-    proj_quad = jnp.concatenate([proj_pair, flip(proj_pair, 1)], axis=0)
+    rows_in = jnp.concatenate([queries_in, hidden_in], axis=1)
+    rows_ext = jnp.concatenate([before, rows_in, after], axis=0)
+    query_ext, hidden_ext = (rows_ext[:, :att], rows_ext[:, att:])
+    query_mine = lax.dynamic_slice_in_dim(query_ext, half * HALF_ATT, HALF_ATT, axis=1)
+    query_far = flip(lax.dynamic_slice_in_dim(query_ext, (1 - half) * HALF_ATT, HALF_ATT, axis=1), 2)
+    lifted = jnp.dot(hidden_ext, disc_in, preferred_element_type=F32)
     conv = arrange(conv_in)
-    got, conv, query_far, proj_quad = lax.optimization_barrier((got, conv, query_far, proj_quad))
+    got, conv, query_mine, query_far, lifted = lax.optimization_barrier(
+        (got, conv, query_mine, query_far, lifted)
+    )
     other = [flip(g, 1) for g in got]
-    proj = [proj_quad] + [turn(proj_quad, j) for j in (1, 2, 3)]
 
     attended_far = flip(attend(meta, query_far, got, other), 2)
     attended_mine = attend(meta, query_mine, got, other)

time: 208 us -> 225 us (1.082)
  waiting for transfers between devices: 80.7 us -> 94.9 us
  between operations: 3.5 us -> 16.8 us
  starting transfers between devices: 56.3 us -> 48.4 us
  local copies, waits for them, and re-layouts: 12.3 us -> 8.95 us
  matrix products: 3.09 us -> 5.58 us
    ppermute x15 -> x14, waiting for transfers between devices: 16.2 us -> 26.3 us  [flip(): return lax.ppermute(x, 'seq', [(i, i ^ bit) for i in range(seq_size)])]
    ppermute x12 -> x9, waiting for transfers between devices: 30.4 us -> 36 us  [turn(): lax.ppermute(x, 'seq', [(i, (i + 4 * hops) % seq_size) for i in range(seq...]
    ppermute x10 -> x9, waiting for transfers between devices: 34.1 us -> 28.7 us  [swap(): return lax.ppermute(x, ('dp', 'seq'), pairs)]
    ppermute x1, waiting for transfers between devices: 0.01 us -> 3.95 us  [shards(): lax.ppermute(after, 'seq', down)]
    ppermute x12 -> x9, starting transfers between devices: 15 us -> 12.1 us  [turn(): lax.ppermute(x, 'seq', [(i, (i + 4 * hops) % seq_size) for i in range(seq...]
    dot_general x1, matrix products: 0.66 us -> 3.25 us  [shards(): jnp.dot(out_proj, disc_in, preferred_element_type=F32).astype(BF16)]
    ppermute x15 -> x14, starting transfers between devices: 17.2 us -> 15 us  [flip(): return lax.ppermute(x, 'seq', [(i, i ^ bit) for i in range(seq_size)])]
    unnamed x42 -> x44, local copies, waits for them, and re-layouts: 5.76 us -> 4.44 us
  transfers between devices with their start and end apart: 39 -> 35, of which waited for: 21 -> 24; matrix products, arithmetic and copies ran while one was open for 5% -> 5% of each run, Pallas kernels for 10% -> 9%
where the time goes in v3:
time: 225 us; the launch traced here: 224 us
  waiting for transfers between devices  94.9 us (42%)
  starting transfers between devices  48.4 us (22%)
  Pallas kernels  44.6 us (20%)
  between operations  16.8 us (7%)
  local copies, waits for them, and re-layouts  8.95 us (4%)
  matrix products  5.58 us (2%)
  other arithmetic  4.44 us (2%)
    ppermute x9, waiting for transfers between devices, turn(): lax.ppermute(x, 'seq', [(i, (i + 4 * hops) % seq_size) for i in range(seq...  36 us
    ppermute x9, waiting for transfers between devices, swap(): return lax.ppermute(x, ('dp', 'seq'), pairs)  28.7 us
    ppermute x14, waiting for transfers between devices, flip(): return lax.ppermute(x, 'seq', [(i, i ^ bit) for i in range(seq_size)])  26.3 us
    ppermute x9, starting transfers between devices, swap(): return lax.ppermute(x, ('dp', 'seq'), pairs)  18.5 us
    ppermute x14, starting transfers between devices, flip(): return lax.ppermute(x, 'seq', [(i, i ^ bit) for i in range(seq_size)])  15 us
    pallas_call x1, Pallas kernels, critic(): pl.pallas_call(critic_kernel, in_specs=[smem()] + [anywhere()] * 5 + [vme...  14.9 us
    ppermute x9, starting transfers between devices, turn(): lax.ppermute(x, 'seq', [(i, (i + 4 * hops) % seq_size) for i in range(seq...  12.1 us
    pallas_call x2, Pallas kernels, attend(): pl.pallas_call(attend_kernel, grid=(width // HEAD_DIM,), in_specs=[smem()...  12.1 us
  transfers between devices with their start and end apart: 35, of which 24 were waited for; matrix products, arithmetic and copies ran while one was open for 5% of the time, Pallas kernels for 9%

profile of v3, /device:TPU:32, one launch (start us, length us, event | category | flops | bytes accessed | tf_op | source)
XLA Modules:
  0.0 223.8 jit_solution(2279949506570450846)
XLA Ops:
  8.1 3.2 %convolution_convert_fusion = bf16[48,1024]{1,0:T(8,128)(2,1)} fusion(bf16[48,1536]{1,0:T(8,128)(2,1)S(1)} %copy-done, bf16[1536,1024]{1,0:T(8,128)(2,1)} %disc_ref.1), kind=kOutput, calls=%fused_computation | convolution fusion | flops 151044096 | bytes 3391488 | tf_op jit(solution)/shard_map/dot_general | solution.py:473
  11.5 3.3 %collective-permute-start.2 = (bf16[256,768]{1,0:T(8,128)(2,1)S(1)}, bf16[256,768]{1,0:T(8,128)(2,1)S(1)}, u32[]{:S(2)}, u32[]{:S(2)}) collective-permute-start(bf16[256,768]{1,0:T(8,128)(2,1)S(1)} %pad_maximum_fusion.7.refs_4_), channel_id=1, source_target_pairs={{0,8},{1,9},{2,10},{3,11},{4,12},{5,13},{6,14},{7,15},{8,0},{9,1},... | collective-permute-start | bytes 1179656 | tf_op jit(solution)/shard_map/ppermute | solution.py:459
  14.8 3.0 %collective-permute-start.4 = (bf16[64,4096]{1,0:T(8,128)(2,1)S(1)}, bf16[64,4096]{1,0:T(8,128)(2,1)S(1)}, u32[]{:S(2)}, u32[]{:S(2)}) collective-permute-start(bf16[64,4096]{1,0:T(8,128)(2,1)S(1)} %bitcast.33), channel_id=1, source_target_pairs={{0,2},{1,3},{2,0},{3,1},{4,6},{5,7},{6,4},{7,5},{8,10},{9,11},{10,... | collective-permute-start | bytes 1572872 | tf_op jit(solution)/shard_map/ppermute | solution.py:456
  17.8 1.1 collective-permute-start.1
  19.9 5.2 %collective-permute-done.2.refs_10_ = bf16[256,768]{1,0:T(8,128)(2,1)S(1)} collective-permute-done((bf16[256,768]{1,0:T(8,128)(2,1)S(1)}, bf16[256,768]{1,0:T(8,128)(2,1)S(1)}, u32[]{:S(2)}, u32[]{:S(2)}) %collective-permute-start.2) | collective-permute-done | bytes 393248 | tf_op jit(solution)/shard_map/ppermute | solution.py:459
  25.1 2.8 %collective-permute-start.3 = (bf16[256,768]{1,0:T(8,128)(2,1)S(1)}, bf16[256,768]{1,0:T(8,128)(2,1)}, u32[]{:S(2)}, u32[]{:S(2)}) collective-permute-start(bf16[256,768]{1,0:T(8,128)(2,1)S(1)} %pad_maximum_fusion.8), channel_id=1, source_target_pairs={{0,18},{1,19},{2,16},{3,17},{4,22},{5,23},{6,20},{7,21},{8,26},{9,... | collective-permute-start | bytes 1179656 | tf_op jit(solution)/shard_map/ppermute | solution.py:466
  27.9 5.0 %collective-permute-done.1.refs_8_ = bf16[256,768]{1,0:T(8,128)(2,1)} collective-permute-done((bf16[256,768]{1,0:T(8,128)(2,1)S(1)}, bf16[256,768]{1,0:T(8,128)(2,1)}, u32[]{:S(2)}, u32[]{:S(2)}) %collective-permute-start.1) | collective-permute-done | bytes 393248 | tf_op jit(solution)/shard_map/ppermute | solution.py:459
  32.8 7.3 %collective-permute-done.3.refs_5_ = bf16[256,768]{1,0:T(8,128)(2,1)} collective-permute-done((bf16[256,768]{1,0:T(8,128)(2,1)S(1)}, bf16[256,768]{1,0:T(8,128)(2,1)}, u32[]{:S(2)}, u32[]{:S(2)}) %collective-permute-start.3) | collective-permute-done | bytes 393248 | tf_op jit(solution)/shard_map/ppermute | solution.py:466
  41.7 1.2 stack.80.meta_ref
  43.5 1.8 collective-permute-start.8
  46.4 16.3 %collective-permute-done.6.refs_7_ = bf16[256,768]{1,0:T(8,128)(2,1)S(1)} collective-permute-done((bf16[256,768]{1,0:T(8,128)(2,1)}, bf16[256,768]{1,0:T(8,128)(2,1)S(1)}, u32[]{:S(2)}, u32[]{:S(2)}) %collective-permute-start.6) | collective-permute-done | bytes 393248 | tf_op jit(solution)/shard_map/ppermute | solution.py:459
  64.7 1.4 collective-permute-start.10
  66.1 1.3 collective-permute-start.11
  68.2 4.0 %collective-permute-done.11 = bf16[40,2304]{1,0:T(8,128)(2,1)S(1)} collective-permute-done((bf16[40,2304]{1,0:T(8,128)(2,1)S(1)}, bf16[40,2304]{1,0:T(8,128)(2,1)S(1)}, u32[]{:S(2)}, u32[]{:S(2)}) %collective-permute-start.11) | collective-permute-done | bytes 184352 | tf_op jit(solution)/shard_map/ppermute | solution.py:503
  72.2 5.8 %shard_map.113 = (f32[4,64,384]{2,1,0:T(8,128)}, f32[4,64,384]{2,1,0:T(8,128)}) custom-call(s32[9]{0:T(128)} %stack.73.cols_ref, bf16[64,4096]{1,0:T(8,128)(2,1)} %bitcast.31, bf16[64,4096]{1,0:T(8,128)(2,1)} %copy-done.10, bf16[64,4096]{1,0:T(8,128)(2,1)} %copy-done.11, bf16[64,4096]{1,0:T(8,128)(2,1)} %copy-done.12, bf16[256,768]{1,0:T(8,128)(2,1)} %copy-done.5, ...), custom_call_target="tpu_custom_call" | custom-call | flops 800000000 | bytes 6000000 | tf_op jit(solution)/shard_map/pallas_call | solution.py:115
  78.1 5.6 %collective-permute-start.12 = (f32[4,64,384]{2,1,0:T(8,128)}, f32[4,64,384]{2,1,0:T(8,128)S(1)}, u32[]{:S(2)}, u32[]{:S(2)}) collective-permute-start(f32[4,64,384]{2,1,0:T(8,128)} %get-tuple-element.82), channel_id=1, source_target_pairs={{0,1},{1,0},{2,3},{3,2},{4,5},{5,4},{6,7},{7,6},{8,9},{9,8},{10,11... | collective-permute-start | bytes 1179656 | tf_op jit(solution)/shard_map/ppermute | solution.py:456
  83.7 1.6 collective-permute-done.12
  85.3 1.8 add.166
  87.2 3.2 %collective-permute-start.15 = (f32[256,384]{1,0:T(8,128)}, f32[256,384]{1,0:T(8,128)S(1)}, u32[]{:S(2)}, u32[]{:S(2)}) collective-permute-start(f32[256,384]{1,0:T(8,128)} %bitcast.19.refs_0_), channel_id=1, source_target_pairs={{0,12},{1,13},{2,14},{3,15},{4,0},{5,1},{6,2},{7,3},{8,4},{9,5},{1... | collective-permute-start | bytes 1179656 | tf_op jit(solution)/shard_map/ppermute | solution.py:459
  90.4 8.6 %shard_map.114.conv_hbm = bf16[16,256,768]{2,1,0:T(8,128)(2,1)} custom-call(bf16[41,64,1024]{2,1,0:T(8,128)(2,1)} %w_ref), custom_call_target="tpu_custom_call" | custom-call | flops 20000000 | bytes 20000000 | tf_op jit(solution)/shard_map/pallas_call | solution.py:69
  99.0 9.5 %collective-permute-done.13.refs_1_ = f32[256,384]{1,0:T(8,128)} collective-permute-done((f32[256,384]{1,0:T(8,128)}, f32[256,384]{1,0:T(8,128)}, u32[]{:S(2)}, u32[]{:S(2)}) %collective-permute-start.13) | collective-permute-done | bytes 393248 | tf_op jit(solution)/shard_map/ppermute | solution.py:459
  108.8 2.3 %fusion.lifted_hbm = f32[336,1024]{1,0:T(8,128)} fusion(bf16[1536,1024]{1,0:T(8,128)(2,1)S(1)} %copy-done.1, bf16[40,2304]{1,0:T(8,128)(2,1)S(1)} %copy-done.18, bf16[40,2304]{1,0:T(8,128)(2,1)S(1)} %collective-permute-done.10, bf16[256,1536]{1,0:T(8,128)(2,1)S(1)} %bitcast.27, bf16[256,768]{1,0:T(8,128)(2,1)S(1)} %bitcast.30), kind=kOutput, calls=%fused_computation.2 | convolution fusion | flops 1061093376 | bytes 6070272 | tf_op jit(solution)/shard_map/dot_general | solution.py:536
  111.1 6.8 %collective-permute-done.16.q_ref = bf16[336,384]{1,0:T(8,128)(2,1)S(1)} collective-permute-done((bf16[336,384]{1,0:T(8,128)(2,1)S(1)}, bf16[336,384]{1,0:T(8,128)(2,1)S(1)}, u32[]{:S(2)}, u32[]{:S(2)}) %collective-permute-start.16) | collective-permute-done | bytes 258080 | tf_op jit(solution)/shard_map/ppermute | solution.py:456
  119.9 1.1 collective-permute-done.18.refs_5_
  121.3 6.0 %shard_map.116 = bf16[336,384]{1,0:T(8,128)(2,1)S(1)} custom-call(s32[4]{0:T(128)S(1)} %pad_add_fusion.meta_ref, bf16[336,384]{1,0:T(8,128)(2,1)S(1)} %collective-permute-done.16.q_ref, f32[256,384]{1,0:T(8,128)} %bitcast.19.refs_0_, f32[256,384]{1,0:T(8,128)} %collective-permute-done.13.refs_1_, f32[256,384]{1,0:T(8,128)S(1)} %collective-permute-done.14.refs_2_, ...), custom_call_target="tpu_custom_call" | custom-call | flops 1056964608 | bytes 4000000 | tf_op jit(solution)/shard_map/pallas_call | solution.py:172
  127.8 6.0 %shard_map.115.mine_hbm = bf16[336,384]{1,0:T(8,128)(2,1)S(1)} custom-call(s32[4]{0:T(128)S(1)} %pad_add_fusion.meta_ref, bf16[336,384]{1,0:T(8,128)(2,1)S(1)} %get-tuple-element.95.q_ref, f32[256,384]{1,0:T(8,128)} %bitcast.19.refs_0_, f32[256,384]{1,0:T(8,128)} %collective-permute-done.13.refs_1_, f32[256,384]{1,0:T(8,128)S(1)} %collective-permute-done.14.refs_2_, ...), custom_call_target="tpu_custom_call" | custom-call | flops 1056964608 | bytes 4000000 | tf_op jit(solution)/shard_map/pallas_call | solution.py:172
  134.5 2.7 %collective-permute-done.21.other_hbm = bf16[336,384]{1,0:T(8,128)(2,1)S(1)} collective-permute-done((bf16[336,384]{1,0:T(8,128)(2,1)S(1)}, bf16[336,384]{1,0:T(8,128)(2,1)S(1)}, u32[]{:S(2)}, u32[]{:S(2)}) %collective-permute-start.21) | collective-permute-done | bytes 258080 | tf_op jit(solution)/shard_map/ppermute | solution.py:456
  137.9 14.9 %shard_map.117 = (f32[8,48,1024]{2,1,0:T(8,128)}, bf16[400,1024]{1,0:T(8,128)(2,1)}, f32[8,1024]{1,0:T(8,128)}) custom-call(s32[5]{0:T(128)} %stack.80.meta_ref, f32[336,1024]{1,0:T(8,128)} %fusion.lifted_hbm, bf16[336,384]{1,0:T(8,128)(2,1)} %copy-done.4, bf16[336,384]{1,0:T(8,128)(2,1)} %copy-done.21, ...), custom_call_target="tpu_custom_call" | custom-call | flops 3000000000 | bytes 14000000 | tf_op jit(solution)/shard_map/pallas_call | solution.py:412
  152.9 2.5 %collective-permute-done.22.arrived_ref = bf16[400,1024]{1,0:T(8,128)(2,1)S(1)} collective-permute-done((bf16[400,1024]{1,0:T(8,128)(2,1)}, bf16[400,1024]{1,0:T(8,128)(2,1)S(1)}, u32[]{:S(2)}, u32[]{:S(2)}) %collective-permute-start.22) | collective-permute-done | bytes 819232 | tf_op jit(solution)/shard_map/ppermute | solution.py:456
  155.5 1.4 copy-done.2
  159.4 3.7 %collective-permute-start.25 = (bf16[112,1024]{1,0:T(8,128)(2,1)S(1)}, bf16[112,1024]{1,0:T(8,128)(2,1)S(1)}, u32[]{:S(2)}, u32[]{:S(2)}) collective-permute-start(bf16[112,1024]{1,0:T(8,128)(2,1)S(1)} %get-tuple-element.109), channel_id=1, source_target_pairs={{0,12},{1,13},{2,14},{3,15},{4,8},{5,9},{6,10},{7,11},{8,4},{9,5},... | collective-permute-start | bytes 688136 | tf_op jit(solution)/shard_map/ppermute | solution.py:456
  163.1 3.7 %collective-permute-done.23.one_ref = bf16[112,1024]{1,0:T(8,128)(2,1)S(1)} collective-permute-done((bf16[112,1024]{1,0:T(8,128)(2,1)S(1)}, bf16[112,1024]{1,0:T(8,128)(2,1)S(1)}, u32[]{:S(2)}, u32[]{:S(2)}) %collective-permute-start.23) | collective-permute-done | bytes 229408 | tf_op jit(solution)/shard_map/ppermute | solution.py:456
  166.9 3.2 %collective-permute-done.24.two_ref = bf16[112,1024]{1,0:T(8,128)(2,1)S(1)} collective-permute-done((bf16[112,1024]{1,0:T(8,128)(2,1)S(1)}, bf16[112,1024]{1,0:T(8,128)(2,1)S(1)}, u32[]{:S(2)}, u32[]{:S(2)}) %collective-permute-start.24) | collective-permute-done | bytes 229408 | tf_op jit(solution)/shard_map/ppermute | solution.py:456
  170.1 3.3 %collective-permute-done.25.three_ref = bf16[112,1024]{1,0:T(8,128)(2,1)S(1)} collective-permute-done((bf16[112,1024]{1,0:T(8,128)(2,1)S(1)}, bf16[112,1024]{1,0:T(8,128)(2,1)S(1)}, u32[]{:S(2)}, u32[]{:S(2)}) %collective-permute-start.25) | collective-permute-done | bytes 229408 | tf_op jit(solution)/shard_map/ppermute | solution.py:456
  174.1 1.2 collective-permute-start.26
  175.4 1.1 collective-permute-start.27
  176.5 2.6 %collective-permute-start.28 = (f32[32,1024]{1,0:T(8,128)S(1)}, f32[32,1024]{1,0:T(8,128)S(1)}, u32[]{:S(2)}, u32[]{:S(2)}) collective-permute-start(f32[32,1024]{1,0:T(8,128)S(1)} %get-tuple-element.113), channel_id=1, source_target_pairs={{0,18},{1,19},{2,16},{3,17},{4,22},{5,23},{6,20},{7,21},{8,26},{9,... | collective-permute-start | bytes 393224 | tf_op jit(solution)/shard_map/ppermute | solution.py:466
  179.1 1.3 collective-permute-done.26
  180.4 1.9 collective-permute-done.27
  182.3 1.9 collective-permute-done.28
  184.3 2.3 %collective-permute-start.31 = (f32[32,1024]{1,0:T(8,128)S(1)}, f32[32,1024]{1,0:T(8,128)S(1)}, u32[]{:S(2)}, u32[]{:S(2)}) collective-permute-start(f32[32,1024]{1,0:T(8,128)S(1)} %add_add_fusion.1), channel_id=1, source_target_pairs={{0,96},{1,97},{2,98},{3,99},{4,100},{5,101},{6,102},{7,103},{8,104... | collective-permute-start | bytes 393224 | tf_op jit(solution)/shard_map/ppermute | solution.py:466
  186.5 1.5 collective-permute-start.30
  188.0 1.4 collective-permute-start.29
  189.3 6.9 %collective-permute-done.31 = f32[32,1024]{1,0:T(8,128)S(1)} collective-permute-done((f32[32,1024]{1,0:T(8,128)S(1)}, f32[32,1024]{1,0:T(8,128)S(1)}, u32[]{:S(2)}, u32[]{:S(2)}) %collective-permute-start.31) | collective-permute-done | bytes 131104 | tf_op jit(solution)/shard_map/ppermute | solution.py:466
  197.5 5.6 %collective-permute-start.32 = (f32[32,1024]{1,0:T(8,128)S(1)}, f32[32,1024]{1,0:T(8,128)S(1)}, u32[]{:S(2)}, u32[]{:S(2)}) collective-permute-start(f32[32,1024]{1,0:T(8,128)S(1)} %add_add_fusion), channel_id=1, source_target_pairs={{0,128},{1,129},{2,130},{3,131},{4,132},{5,133},{6,134},{7,135},{8... | collective-permute-start | bytes 393224 | tf_op jit(solution)/shard_map/ppermute | solution.py:466
  203.1 5.1 %collective-permute-done.32 = f32[32,1024]{1,0:T(8,128)S(1)} collective-permute-done((f32[32,1024]{1,0:T(8,128)S(1)}, f32[32,1024]{1,0:T(8,128)S(1)}, u32[]{:S(2)}, u32[]{:S(2)}) %collective-permute-start.32) | collective-permute-done | bytes 131104 | tf_op jit(solution)/shard_map/ppermute | solution.py:466
  210.1 3.0 %collective-permute-done.33 = f32[24,1024]{1,0:T(8,128)} collective-permute-done((f32[24,1024]{1,0:T(8,128)S(1)}, f32[24,1024]{1,0:T(8,128)}, u32[]{:S(2)}, u32[]{:S(2)}) %collective-permute-start.33) | collective-permute-done | bytes 98336 | tf_op jit(solution)/shard_map/ppermute | solution.py:466
  214.0 1.8 shard_map.120
  (99 shorter events, 18.4 us)
Async XLA Ops:
  7.2 80.0 %all-gather.2.cloned.1.call-start = ((), (), s32[]{:S(2)}) async-start(), calls=%async_computation | async-start | bytes 1671168 | tf_op jit(solution)/shard_map/all_gather | solution.py:475
  8.1 6.7 %copy-start.9 = (bf16[1,64,4096]{2,1,0:T(8,128)(2,1)S(1)}, bf16[1,64,4096]{2,1,0:T(8,128)(2,1)}, u32[]{:S(2)}) copy-start(bf16[1,64,4096]{2,1,0:T(8,128)(2,1)} %param.10) | copy-start | bytes 1572868
  11.3 29.6 %copy-start.19 = (s32[16]{0:T(128)S(1)}, s32[16]{0:T(128)}, u32[]{:S(2)}) copy-start(s32[16]{0:T(128)} %param.18) | copy-start | bytes 196
  11.3 29.6 %copy-start.20 = (s32[16]{0:T(128)S(1)}, s32[16]{0:T(128)}, u32[]{:S(2)}) copy-start(s32[16]{0:T(128)} %param.19) | copy-start | bytes 196
  11.5 60.7 %copy-start.5 = (bf16[256,768]{1,0:T(8,128)(2,1)}, bf16[256,768]{1,0:T(8,128)(2,1)S(1)}, u32[]{:S(2)}) copy-start(bf16[256,768]{1,0:T(8,128)(2,1)S(1)} %pad_maximum_fusion.7.refs_4_) | copy-start | bytes 1179652
  11.5 13.6 %collective-permute-start.2 = (bf16[256,768]{1,0:T(8,128)(2,1)S(1)}, bf16[256,768]{1,0:T(8,128)(2,1)S(1)}, u32[]{:S(2)}, u32[]{:S(2)}) collective-permute-start(bf16[256,768]{1,0:T(8,128)(2,1)S(1)} %pad_maximum_fusion.7.refs_4_), channel_id=1, source_target_pairs={{0,8},{1,9},{2,10},{3,11},{4,12},{5,13},{6,14},{7,15},{8,0},{9,1},... | collective-permute-start | bytes 1179656 | tf_op jit(solution)/shard_map/ppermute | solution.py:459
  14.8 25.4 %collective-permute-start.5 = (bf16[64,4096]{1,0:T(8,128)(2,1)S(1)}, bf16[64,4096]{1,0:T(8,128)(2,1)S(1)}, u32[]{:S(2)}, u32[]{:S(2)}) collective-permute-start(bf16[64,4096]{1,0:T(8,128)(2,1)S(1)} %bitcast.32), channel_id=1, source_target_pairs={{0,1},{1,0},{2,3},{3,2},{4,5},{5,4},{6,7},{7,6},{8,9},{9,8},{10,11... | collective-permute-start | bytes 1572872 | tf_op jit(solution)/shard_map/ppermute | solution.py:456
  14.8 25.4 %collective-permute-start.4 = (bf16[64,4096]{1,0:T(8,128)(2,1)S(1)}, bf16[64,4096]{1,0:T(8,128)(2,1)S(1)}, u32[]{:S(2)}, u32[]{:S(2)}) collective-permute-start(bf16[64,4096]{1,0:T(8,128)(2,1)S(1)} %bitcast.33), channel_id=1, source_target_pairs={{0,2},{1,3},{2,0},{3,1},{4,6},{5,7},{6,4},{7,5},{8,10},{9,11},{10,... | collective-permute-start | bytes 1572872 | tf_op jit(solution)/shard_map/ppermute | solution.py:456
  17.8 15.1 %collective-permute-start.1 = (bf16[256,768]{1,0:T(8,128)(2,1)S(1)}, bf16[256,768]{1,0:T(8,128)(2,1)}, u32[]{:S(2)}, u32[]{:S(2)}) collective-permute-start(bf16[256,768]{1,0:T(8,128)(2,1)S(1)} %pad_maximum_fusion.7.refs_4_), channel_id=1, source_target_pairs={{0,12},{1,13},{2,14},{3,15},{4,0},{5,1},{6,2},{7,3},{8,4},{9,5},{1... | collective-permute-start | bytes 1179656 | tf_op jit(solution)/shard_map/ppermute | solution.py:459
  18.8 14.0 %collective-permute-start = (bf16[256,768]{1,0:T(8,128)(2,1)S(1)}, bf16[256,768]{1,0:T(8,128)(2,1)}, u32[]{:S(2)}, u32[]{:S(2)}) collective-permute-start(bf16[256,768]{1,0:T(8,128)(2,1)S(1)} %pad_maximum_fusion.7.refs_4_), channel_id=1, source_target_pairs={{0,4},{1,5},{2,6},{3,7},{4,8},{5,9},{6,10},{7,11},{8,12},{9,13},{1... | collective-permute-start | bytes 1179656 | tf_op jit(solution)/shard_map/ppermute | solution.py:459
  25.1 47.1 %copy-start.13 = (bf16[256,768]{1,0:T(8,128)(2,1)}, bf16[256,768]{1,0:T(8,128)(2,1)S(1)}, u32[]{:S(2)}) copy-start(bf16[256,768]{1,0:T(8,128)(2,1)S(1)} %collective-permute-done.2.refs_10_) | copy-start | bytes 1179652
  25.1 15.1 %collective-permute-start.3 = (bf16[256,768]{1,0:T(8,128)(2,1)S(1)}, bf16[256,768]{1,0:T(8,128)(2,1)}, u32[]{:S(2)}, u32[]{:S(2)}) collective-permute-start(bf16[256,768]{1,0:T(8,128)(2,1)S(1)} %pad_maximum_fusion.8), channel_id=1, source_target_pairs={{0,18},{1,19},{2,16},{3,17},{4,22},{5,23},{6,20},{7,21},{8,26},{9,... | collective-permute-start | bytes 1179656 | tf_op jit(solution)/shard_map/ppermute | solution.py:466
  40.2 32.0 %copy-start.10 = (bf16[64,4096]{1,0:T(8,128)(2,1)}, bf16[64,4096]{1,0:T(8,128)(2,1)S(1)}, u32[]{:S(2)}) copy-start(bf16[64,4096]{1,0:T(8,128)(2,1)S(1)} %collective-permute-done.5.refs_1_) | copy-start | bytes 1572868
  40.2 32.0 %copy-start.11 = (bf16[64,4096]{1,0:T(8,128)(2,1)}, bf16[64,4096]{1,0:T(8,128)(2,1)S(1)}, u32[]{:S(2)}) copy-start(bf16[64,4096]{1,0:T(8,128)(2,1)S(1)} %collective-permute-done.4.refs_2_) | copy-start | bytes 1572868
  40.2 22.5 %collective-permute-start.6 = (bf16[256,768]{1,0:T(8,128)(2,1)}, bf16[256,768]{1,0:T(8,128)(2,1)S(1)}, u32[]{:S(2)}, u32[]{:S(2)}) collective-permute-start(bf16[256,768]{1,0:T(8,128)(2,1)} %collective-permute-done.3.refs_5_), channel_id=1, source_target_pairs={{0,4},{1,5},{2,6},{3,7},{4,8},{5,9},{6,10},{7,11},{8,12},{9,13},{1... | collective-permute-start | bytes 1179656 | tf_op jit(solution)/shard_map/ppermute | solution.py:459
  43.5 24.7 %collective-permute-start.8 = (bf16[256,768]{1,0:T(8,128)(2,1)}, bf16[256,768]{1,0:T(8,128)(2,1)S(1)}, u32[]{:S(2)}, u32[]{:S(2)}) collective-permute-start(bf16[256,768]{1,0:T(8,128)(2,1)} %collective-permute-done.3.refs_5_), channel_id=1, source_target_pairs={{0,8},{1,9},{2,10},{3,11},{4,12},{5,13},{6,14},{7,15},{8,0},{9,1},... | collective-permute-start | bytes 1179656 | tf_op jit(solution)/shard_map/ppermute | solution.py:459
  45.4 22.8 %collective-permute-start.7 = (bf16[256,768]{1,0:T(8,128)(2,1)}, bf16[256,768]{1,0:T(8,128)(2,1)S(1)}, u32[]{:S(2)}, u32[]{:S(2)}) collective-permute-start(bf16[256,768]{1,0:T(8,128)(2,1)} %collective-permute-done.3.refs_5_), channel_id=1, source_target_pairs={{0,12},{1,13},{2,14},{3,15},{4,0},{5,1},{6,2},{7,3},{8,4},{9,5},{1... | collective-permute-start | bytes 1179656 | tf_op jit(solution)/shard_map/ppermute | solution.py:459
  46.4 21.8 %collective-permute-start.9 = (bf16[64,4096]{1,0:T(8,128)(2,1)S(1)}, bf16[64,4096]{1,0:T(8,128)(2,1)S(1)}, u32[]{:S(2)}, u32[]{:S(2)}) collective-permute-start(bf16[64,4096]{1,0:T(8,128)(2,1)S(1)} %collective-permute-done.4.refs_2_), channel_id=1, source_target_pairs={{0,1},{1,0},{2,3},{3,2},{4,5},{5,4},{6,7},{7,6},{8,9},{9,8},{10,11... | collective-permute-start | bytes 1572872 | tf_op jit(solution)/shard_map/ppermute | solution.py:456
  62.7 9.5 %copy-start.14 = (bf16[256,768]{1,0:T(8,128)(2,1)}, bf16[256,768]{1,0:T(8,128)(2,1)S(1)}, u32[]{:S(2)}) copy-start(bf16[256,768]{1,0:T(8,128)(2,1)S(1)} %collective-permute-done.6.refs_7_) | copy-start | bytes 1179652
  64.7 3.5 %collective-permute-start.10 = (bf16[40,2304]{1,0:T(8,128)(2,1)S(1)}, bf16[40,2304]{1,0:T(8,128)(2,1)S(1)}, u32[]{:S(2)}, u32[]{:S(2)}) collective-permute-start(bf16[40,2304]{1,0:T(8,128)(2,1)S(1)} %pad_maximum_fusion.10), channel_id=1, source_target_pairs={{0,1},{1,2},{2,3},{3,4},{4,5},{5,6},{6,7},{7,8},{8,9},{9,10},{10,1... | collective-permute-start | bytes 552968 | tf_op jit(solution)/shard_map/ppermute | solution.py:503
  66.1 6.1 %collective-permute-start.11 = (bf16[40,2304]{1,0:T(8,128)(2,1)S(1)}, bf16[40,2304]{1,0:T(8,128)(2,1)S(1)}, u32[]{:S(2)}, u32[]{:S(2)}) collective-permute-start(bf16[40,2304]{1,0:T(8,128)(2,1)S(1)} %pad_maximum_fusion.11), channel_id=1, source_target_pairs={{1,0},{2,1},{3,2},{4,3},{5,4},{6,5},{7,6},{8,7},{9,8},{10,9},{11,1... | collective-permute-start | bytes 552968 | tf_op jit(solution)/shard_map/ppermute | solution.py:503
  72.2 5.9 %copy-start.17 = (bf16[40,2304]{1,0:T(8,128)(2,1)}, bf16[40,2304]{1,0:T(8,128)(2,1)S(1)}, u32[]{:S(2)}) copy-start(bf16[40,2304]{1,0:T(8,128)(2,1)S(1)} %collective-permute-done.11) | copy-start | bytes 552964
  78.1 7.2 %collective-permute-start.12 = (f32[4,64,384]{2,1,0:T(8,128)}, f32[4,64,384]{2,1,0:T(8,128)S(1)}, u32[]{:S(2)}, u32[]{:S(2)}) collective-permute-start(f32[4,64,384]{2,1,0:T(8,128)} %get-tuple-element.82), channel_id=1, source_target_pairs={{0,1},{1,0},{2,3},{3,2},{4,5},{5,4},{6,7},{7,6},{8,9},{9,8},{10,11... | collective-permute-start | bytes 1179656 | tf_op jit(solution)/shard_map/ppermute | solution.py:456
  87.2 21.3 %collective-permute-start.13 = (f32[256,384]{1,0:T(8,128)}, f32[256,384]{1,0:T(8,128)}, u32[]{:S(2)}, u32[]{:S(2)}) collective-permute-start(f32[256,384]{1,0:T(8,128)} %bitcast.19.refs_0_), channel_id=1, source_target_pairs={{0,4},{1,5},{2,6},{3,7},{4,8},{5,9},{6,10},{7,11},{8,12},{9,13},{1... | collective-permute-start | bytes 1179656 | tf_op jit(solution)/shard_map/ppermute | solution.py:459
  87.2 21.3 %copy-start.6 = (bf16[1,256,1536]{2,1,0:T(8,128)(2,1)S(1)}, bf16[1,256,1536]{2,1,0:T(8,128)(2,1)}, u32[]{:S(2)}) copy-start(bf16[1,256,1536]{2,1,0:T(8,128)(2,1)} %param.13) | copy-start | bytes 2359300
  87.2 21.3 %copy-start.8 = (bf16[1,256,768]{2,1,0:T(8,128)(2,1)S(1)}, bf16[1,256,768]{2,1,0:T(8,128)(2,1)}, u32[]{:S(2)}) copy-start(bf16[1,256,768]{2,1,0:T(8,128)(2,1)} %param.12) | copy-start | bytes 1179652
  87.2 21.3 %copy-start.18 = (bf16[40,2304]{1,0:T(8,128)(2,1)S(1)}, bf16[40,2304]{1,0:T(8,128)(2,1)}, u32[]{:S(2)}) copy-start(bf16[40,2304]{1,0:T(8,128)(2,1)} %copy-done.17) | copy-start | bytes 552964
  87.2 23.9 %collective-permute-start.15 = (f32[256,384]{1,0:T(8,128)}, f32[256,384]{1,0:T(8,128)S(1)}, u32[]{:S(2)}, u32[]{:S(2)}) collective-permute-start(f32[256,384]{1,0:T(8,128)} %bitcast.19.refs_0_), channel_id=1, source_target_pairs={{0,12},{1,13},{2,14},{3,15},{4,0},{5,1},{6,2},{7,3},{8,4},{9,5},{1... | collective-permute-start | bytes 1179656 | tf_op jit(solution)/shard_map/ppermute | solution.py:459
  90.4 20.7 %collective-permute-start.14 = (f32[256,384]{1,0:T(8,128)}, f32[256,384]{1,0:T(8,128)S(1)}, u32[]{:S(2)}, u32[]{:S(2)}) collective-permute-start(f32[256,384]{1,0:T(8,128)} %bitcast.19.refs_0_), channel_id=1, source_target_pairs={{0,8},{1,9},{2,10},{3,11},{4,12},{5,13},{6,14},{7,15},{8,0},{9,1},... | collective-permute-start | bytes 1179656 | tf_op jit(solution)/shard_map/ppermute | solution.py:459
  90.4 18.3 %copy-start.1 = (bf16[1536,1024]{1,0:T(8,128)(2,1)S(1)}, bf16[1536,1024]{1,0:T(8,128)(2,1)}, u32[]{:S(2)}) copy-start(bf16[1536,1024]{1,0:T(8,128)(2,1)} %disc_ref.1) | copy-start | bytes 9437188
  108.6 9.3 %collective-permute-start.16 = (bf16[336,384]{1,0:T(8,128)(2,1)S(1)}, bf16[336,384]{1,0:T(8,128)(2,1)S(1)}, u32[]{:S(2)}, u32[]{:S(2)}) collective-permute-start(bf16[336,384]{1,0:T(8,128)(2,1)S(1)} %get-tuple-element.122), channel_id=1, source_target_pairs={{0,2},{1,3},{2,0},{3,1},{4,6},{5,7},{6,4},{7,5},{8,10},{9,11},{10,... | collective-permute-start | bytes 774152 | tf_op jit(solution)/shard_map/ppermute | solution.py:456
  117.9 1.9 collective-permute-start.17
  117.9 3.1 %collective-permute-start.18 = (f32[256,384]{1,0:T(8,128)}, f32[256,384]{1,0:T(8,128)S(1)}, u32[]{:S(2)}, u32[]{:S(2)}) collective-permute-start(f32[256,384]{1,0:T(8,128)} %collective-permute-done.13.refs_1_), channel_id=1, source_target_pairs={{0,1},{1,0},{2,3},{3,2},{4,5},{5,4},{6,7},{7,6},{8,9},{9,8},{10,11... | collective-permute-start | bytes 1179656 | tf_op jit(solution)/shard_map/ppermute | solution.py:456
  118.4 2.6 %collective-permute-start.19 = (f32[256,384]{1,0:T(8,128)S(1)}, f32[256,384]{1,0:T(8,128)S(1)}, u32[]{:S(2)}, u32[]{:S(2)}) collective-permute-start(f32[256,384]{1,0:T(8,128)S(1)} %collective-permute-done.14.refs_2_), channel_id=1, source_target_pairs={{0,1},{1,0},{2,3},{3,2},{4,5},{5,4},{6,7},{7,6},{8,9},{9,8},{10,11... | collective-permute-start | bytes 1179656 | tf_op jit(solution)/shard_map/ppermute | solution.py:456
  118.4 2.9 %collective-permute-start.20 = (f32[256,384]{1,0:T(8,128)S(1)}, f32[256,384]{1,0:T(8,128)S(1)}, u32[]{:S(2)}, u32[]{:S(2)}) collective-permute-start(f32[256,384]{1,0:T(8,128)S(1)} %collective-permute-done.15.refs_3_), channel_id=1, source_target_pairs={{0,1},{1,0},{2,3},{3,2},{4,5},{5,4},{6,7},{7,6},{8,9},{9,8},{10,11... | collective-permute-start | bytes 1179656 | tf_op jit(solution)/shard_map/ppermute | solution.py:456
  127.4 9.8 %collective-permute-start.21 = (bf16[336,384]{1,0:T(8,128)(2,1)S(1)}, bf16[336,384]{1,0:T(8,128)(2,1)S(1)}, u32[]{:S(2)}, u32[]{:S(2)}) collective-permute-start(bf16[336,384]{1,0:T(8,128)(2,1)S(1)} %shard_map.116), channel_id=1, source_target_pairs={{0,2},{1,3},{2,0},{3,1},{4,6},{5,7},{6,4},{7,5},{8,10},{9,11},{10,... | collective-permute-start | bytes 774152 | tf_op jit(solution)/shard_map/ppermute | solution.py:456
  152.8 2.6 %collective-permute-start.22 = (bf16[400,1024]{1,0:T(8,128)(2,1)}, bf16[400,1024]{1,0:T(8,128)(2,1)S(1)}, u32[]{:S(2)}, u32[]{:S(2)}) collective-permute-start(bf16[400,1024]{1,0:T(8,128)(2,1)} %get-tuple-element.104), channel_id=1, source_target_pairs={{0,1},{1,0},{2,3},{3,2},{4,5},{5,4},{6,7},{7,6},{8,9},{9,8},{10,11... | collective-permute-start | bytes 2457608 | tf_op jit(solution)/shard_map/ppermute | solution.py:456
  158.3 8.5 %collective-permute-start.23 = (bf16[112,1024]{1,0:T(8,128)(2,1)S(1)}, bf16[112,1024]{1,0:T(8,128)(2,1)S(1)}, u32[]{:S(2)}, u32[]{:S(2)}) collective-permute-start(bf16[112,1024]{1,0:T(8,128)(2,1)S(1)} %get-tuple-element.107), channel_id=1, source_target_pairs={{0,4},{1,5},{2,6},{3,7},{4,0},{5,1},{6,2},{7,3},{8,12},{9,13},{10,... | collective-permute-start | bytes 688136 | tf_op jit(solution)/shard_map/ppermute | solution.py:456
  158.4 11.6 %collective-permute-start.24 = (bf16[112,1024]{1,0:T(8,128)(2,1)S(1)}, bf16[112,1024]{1,0:T(8,128)(2,1)S(1)}, u32[]{:S(2)}, u32[]{:S(2)}) collective-permute-start(bf16[112,1024]{1,0:T(8,128)(2,1)S(1)} %get-tuple-element.108), channel_id=1, source_target_pairs={{0,8},{1,9},{2,10},{3,11},{4,12},{5,13},{6,14},{7,15},{8,0},{9,1},... | collective-permute-start | bytes 688136 | tf_op jit(solution)/shard_map/ppermute | solution.py:456
  159.4 14.0 %collective-permute-start.25 = (bf16[112,1024]{1,0:T(8,128)(2,1)S(1)}, bf16[112,1024]{1,0:T(8,128)(2,1)S(1)}, u32[]{:S(2)}, u32[]{:S(2)}) collective-permute-start(bf16[112,1024]{1,0:T(8,128)(2,1)S(1)} %get-tuple-element.109), channel_id=1, source_target_pairs={{0,12},{1,13},{2,14},{3,15},{4,8},{5,9},{6,10},{7,11},{8,4},{9,5},... | collective-permute-start | bytes 688136 | tf_op jit(solution)/shard_map/ppermute | solution.py:456
  174.1 6.3 %collective-permute-start.26 = (f32[32,1024]{1,0:T(8,128)S(1)}, f32[32,1024]{1,0:T(8,128)S(1)}, u32[]{:S(2)}, u32[]{:S(2)}) collective-permute-start(f32[32,1024]{1,0:T(8,128)S(1)} %get-tuple-element.111), channel_id=1, source_target_pairs={{0,16},{1,17},{2,18},{3,19},{4,20},{5,21},{6,22},{7,23},{8,24},{9,... | collective-permute-start | bytes 393224 | tf_op jit(solution)/shard_map/ppermute | solution.py:466
  175.4 7.0 %collective-permute-start.27 = (f32[32,1024]{1,0:T(8,128)S(1)}, f32[32,1024]{1,0:T(8,128)S(1)}, u32[]{:S(2)}, u32[]{:S(2)}) collective-permute-start(f32[32,1024]{1,0:T(8,128)S(1)} %get-tuple-element.112), channel_id=1, source_target_pairs={{0,2},{1,3},{2,0},{3,1},{4,6},{5,7},{6,4},{7,5},{8,10},{9,11},{10,... | collective-permute-start | bytes 393224 | tf_op jit(solution)/shard_map/ppermute | solution.py:466
  176.5 7.7 %collective-permute-start.28 = (f32[32,1024]{1,0:T(8,128)S(1)}, f32[32,1024]{1,0:T(8,128)S(1)}, u32[]{:S(2)}, u32[]{:S(2)}) collective-permute-start(f32[32,1024]{1,0:T(8,128)S(1)} %get-tuple-element.113), channel_id=1, source_target_pairs={{0,18},{1,19},{2,16},{3,17},{4,22},{5,23},{6,20},{7,21},{8,26},{9,... | collective-permute-start | bytes 393224 | tf_op jit(solution)/shard_map/ppermute | solution.py:466
  184.3 12.0 %collective-permute-start.31 = (f32[32,1024]{1,0:T(8,128)S(1)}, f32[32,1024]{1,0:T(8,128)S(1)}, u32[]{:S(2)}, u32[]{:S(2)}) collective-permute-start(f32[32,1024]{1,0:T(8,128)S(1)} %add_add_fusion.1), channel_id=1, source_target_pairs={{0,96},{1,97},{2,98},{3,99},{4,100},{5,101},{6,102},{7,103},{8,104... | collective-permute-start | bytes 393224 | tf_op jit(solution)/shard_map/ppermute | solution.py:466
  186.5 10.5 %collective-permute-start.30 = (f32[32,1024]{1,0:T(8,128)S(1)}, f32[32,1024]{1,0:T(8,128)S(1)}, u32[]{:S(2)}, u32[]{:S(2)}) collective-permute-start(f32[32,1024]{1,0:T(8,128)S(1)} %add_add_fusion.1), channel_id=1, source_target_pairs={{0,64},{1,65},{2,66},{3,67},{4,68},{5,69},{6,70},{7,71},{8,72},{9,... | collective-permute-start | bytes 393224 | tf_op jit(solution)/shard_map/ppermute | solution.py:466
  188.0 9.5 %collective-permute-start.29 = (f32[32,1024]{1,0:T(8,128)S(1)}, f32[32,1024]{1,0:T(8,128)S(1)}, u32[]{:S(2)}, u32[]{:S(2)}) collective-permute-start(f32[32,1024]{1,0:T(8,128)S(1)} %add_add_fusion.1), channel_id=1, source_target_pairs={{0,32},{1,33},{2,34},{3,35},{4,36},{5,37},{6,38},{7,39},{8,40},{9,... | collective-permute-start | bytes 393224 | tf_op jit(solution)/shard_map/ppermute | solution.py:466
  197.5 10.7 %collective-permute-start.32 = (f32[32,1024]{1,0:T(8,128)S(1)}, f32[32,1024]{1,0:T(8,128)S(1)}, u32[]{:S(2)}, u32[]{:S(2)}) collective-permute-start(f32[32,1024]{1,0:T(8,128)S(1)} %add_add_fusion), channel_id=1, source_target_pairs={{0,128},{1,129},{2,130},{3,131},{4,132},{5,133},{6,134},{7,135},{8... | collective-permute-start | bytes 393224 | tf_op jit(solution)/shard_map/ppermute | solution.py:466
  208.2 4.8 %collective-permute-start.33 = (f32[24,1024]{1,0:T(8,128)S(1)}, f32[24,1024]{1,0:T(8,128)}, u32[]{:S(2)}, u32[]{:S(2)}) collective-permute-start(f32[24,1024]{1,0:T(8,128)S(1)} %slice.32), channel_id=1, source_target_pairs={{0,16},{1,17},{2,18},{3,19},{4,20},{5,21},{6,22},{7,23},{8,24},{9,... | collective-permute-start | bytes 294920 | tf_op jit(solution)/shard_map/ppermute | solution.py:466
  (9 other events, 20.7 us)
Sparse Core Ops, SparseCore 0:
  20.0 51.0 all-gather.1

commit v4 on v3

--- a/solution.py
+++ b/solution.py
@@ -78,11 +78,14 @@
 
 
 def project_kernel(cols_ref, *refs):
-    states, weights, (keep_ref, send_ref) = (refs[:4], refs[4:12], refs[12:14])
-    state_s, weight_s, total_s, state_sem, weight_sem = refs[14:]
+    states, weights, (keep_ref, send_ref) = (refs[:3], refs[3:11], refs[11:13])
+    state_s, weight_s, total_s, state_sem, weight_sem = refs[13:]
     core = cols_ref[8]
     state_copies = [
-        pltpu.make_async_copy(s, state_s.at[i], state_sem.at[i]) for i, s in enumerate(states)
+        pltpu.make_async_copy(s, state_s.at[place], state_sem.at[i])
+        for i, (s, place) in enumerate(
+            ((states[0], 0), (states[1], 2), (states[2].at[:64], 1), (states[2].at[64:], 3))
+        )
     ]
     weight_copies = [
         pltpu.make_async_copy(w, weight_s.at[i], weight_sem.at[i]) for i, w in enumerate(weights)
@@ -114,7 +117,7 @@
     out = jax.ShapeDtypeStruct((4, 64, HALF_ATT), F32)
     return pl.pallas_call(
         project_kernel,
-        in_specs=[smem()] + [anywhere()] * 12,
+        in_specs=[smem()] + [anywhere()] * 11,
         out_specs=[vmem(), vmem()],
         out_shape=[out, out],
         scratch_shapes=[
@@ -474,34 +477,34 @@
     kv_weight, proj_own = lax.optimization_barrier((kv_weight, proj_own))
     proj = lax.all_gather(proj_own, "seq", axis=0, tiled=True)
 
-    def head_cols(which):
+    def head_cols(which, kv_weight):
         parts = [
             lax.dynamic_slice_in_dim(kv_weight, kind * att + which * HALF_ATT, HALF_ATT, axis=1)
             for kind in (0, 1)
         ]
         return jnp.concatenate(parts, axis=1)
 
-    near = head_cols(half)
-    far = swap(head_cols(1 - half), 1, 2)
+    far = head_cols(1 - half, kv_weight)
+    far, kv_weight = lax.optimization_barrier((far, kv_weight))
+    near = head_cols(half, kv_weight)
+    far = swap(far, 1, 2)
     hops = (1, 3, 2)
     near_turned = [turn(near, j) for j in hops]
     states_in = states[0]
-    state_far, state_near = (flip(states_in, 2), flip(states_in, 1))
-    near, near_turned, far, state_far, state_near = lax.optimization_barrier(
-        (near, near_turned, far, state_far, state_near)
+    near, near_turned, far, state_far, queries_in, hidden_in = lax.optimization_barrier(
+        (near, near_turned, far, flip(states_in, 2), queries[0], hidden[0])
     )
 
     lower = clip % 2
     channels = disc_in.shape[1]
     near_blocks = [near] + near_turned
     far_blocks = [far] + [turn(far, j) for j in hops]
-    far_blocks[1], queries_in, hidden_in = lax.optimization_barrier((far_blocks[1], queries[0], hidden[0]))
+    state_pair = flip(jnp.concatenate([states_in, state_far], axis=0), 1)
     up = [(i, i + 1) for i in range(seq_size - 1)]
     down = [(i + 1, i) for i in range(seq_size - 1)]
     before = jnp.concatenate([queries_in[frames - HALO :], hidden_in[frames - HALO :]], axis=1)
+    before = lax.ppermute(before, "seq", up)
     after = jnp.concatenate([queries_in[:HALO], hidden_in[:HALO]], axis=1)
-    before, after = (lax.ppermute(before, "seq", up), lax.ppermute(after, "seq", down))
-    state_last = flip(state_far, 1)
 
     cols = []
     for hop in (0, 1, 3, 2):
@@ -515,21 +518,20 @@
     meta3 = jnp.stack([row, 2 * half + lower, clip // 2]).astype(jnp.int32)
     blocks = [b for pair in zip(near_blocks, far_blocks) for b in pair]
     tables = (cols, meta, meta2.astype(jnp.int32), meta3)
-    blocks, state_last, tables, before, after = lax.optimization_barrier(
-        (blocks, state_last, tables, before, after)
+    blocks, state_pair, tables, before, after = lax.optimization_barrier(
+        (blocks, state_pair, tables, before, after)
     )
     cols, meta, meta2, meta3 = tables
-    state_parts = [states_in, state_near, state_far, state_last]
+    state_parts = [states_in, state_far, state_pair]
     kept, sent = project(cols, state_parts, blocks)
     mine_kv = (kept + flip(sent, 1)).reshape(256, HALF_ATT)
 
-    mine_kv, conv_in, proj = lax.optimization_barrier((mine_kv, conv_weight, proj))
+    mine_kv, conv_in, proj, queries_in, hidden_in, before, after = lax.optimization_barrier(
+        (mine_kv, conv_weight, proj, queries[0], hidden[0], before, after)
+    )
     got = [mine_kv] + [turn(mine_kv, j) for j in (1, 2, 3)]
-    got[1], queries_in, hidden_in, before, after = lax.optimization_barrier(
-        (got[1], queries[0], hidden[0], before, after)
-    )
     rows_in = jnp.concatenate([queries_in, hidden_in], axis=1)
-    rows_ext = jnp.concatenate([before, rows_in, after], axis=0)
+    rows_ext = jnp.concatenate([before, rows_in, lax.ppermute(after, "seq", down)], axis=0)
     query_ext, hidden_ext = (rows_ext[:, :att], rows_ext[:, att:])
     query_mine = lax.dynamic_slice_in_dim(query_ext, half * HALF_ATT, HALF_ATT, axis=1)
     query_far = flip(lax.dynamic_slice_in_dim(query_ext, (1 - half) * HALF_ATT, HALF_ATT, axis=1), 2)

time: 225 us -> 209 us (0.929)
  waiting for transfers between devices: 94.9 us -> 71.8 us
  starting transfers between devices: 48.4 us -> 51 us
    ppermute x9, waiting for transfers between devices: 36 us -> 27.7 us  [turn(): lax.ppermute(x, 'seq', [(i, (i + 4 * hops) % seq_size) for i in range(seq...]
    ppermute x9, waiting for transfers between devices: 28.7 us -> 20.6 us  [swap(): return lax.ppermute(x, ('dp', 'seq'), pairs)]
    ppermute x9, starting transfers between devices: 12.1 us -> 16.7 us  [turn(): lax.ppermute(x, 'seq', [(i, (i + 4 * hops) % seq_size) for i in range(seq...]
    ppermute x1, waiting for transfers between devices: 3.95 us -> 0.01 us  [shards(): lax.ppermute(after, 'seq', down)]
    ppermute x14 -> x13, waiting for transfers between devices: 26.3 us -> 22.5 us  [flip(): return lax.ppermute(x, 'seq', [(i, i ^ bit) for i in range(seq_size)])]
    ppermute x9, starting transfers between devices: 18.5 us -> 16 us  [swap(): return lax.ppermute(x, ('dp', 'seq'), pairs)]
    ppermute x14 -> x13, starting transfers between devices: 15 us -> 14.6 us  [flip(): return lax.ppermute(x, 'seq', [(i, i ^ bit) for i in range(seq_size)])]
  transfers between devices with their start and end apart: 35 -> 34, of which waited for: 24 -> 25; matrix products, arithmetic and copies ran while one was open for 5% -> 6% of each run, Pallas kernels for 9% -> 10%
where the time goes in v4:
time: 209 us; the launch traced here: 207 us
  waiting for transfers between devices  71.8 us (34%)
  starting transfers between devices  51 us (24%)
  Pallas kernels  44.5 us (21%)
  between operations  16.8 us (8%)
  local copies, waits for them, and re-layouts  10.7 us (5%)
  matrix products  6.43 us (3%)
  other arithmetic  5.64 us (3%)
    ppermute x9, waiting for transfers between devices, turn(): lax.ppermute(x, 'seq', [(i, (i + 4 * hops) % seq_size) for i in range(seq...  27.7 us
    ppermute x13, waiting for transfers between devices, flip(): return lax.ppermute(x, 'seq', [(i, i ^ bit) for i in range(seq_size)])  22.5 us
    ppermute x9, waiting for transfers between devices, swap(): return lax.ppermute(x, ('dp', 'seq'), pairs)  20.6 us
    ppermute x9, starting transfers between devices, turn(): lax.ppermute(x, 'seq', [(i, (i + 4 * hops) % seq_size) for i in range(seq...  16.7 us
    ppermute x9, starting transfers between devices, swap(): return lax.ppermute(x, ('dp', 'seq'), pairs)  16 us
    pallas_call x1, Pallas kernels, critic(): pl.pallas_call(critic_kernel, in_specs=[smem()] + [anywhere()] * 5 + [vme...  14.9 us
    ppermute x13, starting transfers between devices, flip(): return lax.ppermute(x, 'seq', [(i, i ^ bit) for i in range(seq_size)])  14.6 us
    pallas_call x2, Pallas kernels, attend(): pl.pallas_call(attend_kernel, grid=(width // HEAD_DIM,), in_specs=[smem()...  12 us
  transfers between devices with their start and end apart: 34, of which 25 were waited for; matrix products, arithmetic and copies ran while one was open for 6% of the time, Pallas kernels for 10%

profile of v4, /device:TPU:32, one launch (start us, length us, event | category | flops | bytes accessed | tf_op | source)
XLA Modules:
  0.0 206.8 jit_solution(73007128130709079)
XLA Ops:
  8.1 3.2 %convolution_convert_fusion = bf16[48,1024]{1,0:T(8,128)(2,1)} fusion(bf16[48,1536]{1,0:T(8,128)(2,1)S(1)} %copy-done, bf16[1536,1024]{1,0:T(8,128)(2,1)} %disc_ref.1), kind=kOutput, calls=%fused_computation | convolution fusion | flops 151044096 | bytes 3391488 | tf_op jit(solution)/shard_map/dot_general | solution.py:476
  11.3 3.1 %collective-permute-start.4 = (bf16[64,4096]{1,0:T(8,128)(2,1)S(1)}, bf16[64,4096]{1,0:T(8,128)(2,1)S(1)}, u32[]{:S(2)}, u32[]{:S(2)}) collective-permute-start(bf16[64,4096]{1,0:T(8,128)(2,1)S(1)} %bitcast.26), channel_id=1, source_target_pairs={{0,2},{1,3},{2,0},{3,1},{4,6},{5,7},{6,4},{7,5},{8,10},{9,11},{10,... | collective-permute-start | bytes 1572872 | tf_op jit(solution)/shard_map/ppermute | solution.py:459
  14.6 3.3 %collective-permute-start.2 = (bf16[256,768]{1,0:T(8,128)(2,1)S(1)}, bf16[256,768]{1,0:T(8,128)(2,1)S(1)}, u32[]{:S(2)}, u32[]{:S(2)}) collective-permute-start(bf16[256,768]{1,0:T(8,128)(2,1)S(1)} %pad_maximum_fusion.9.refs_3_), channel_id=1, source_target_pairs={{0,8},{1,9},{2,10},{3,11},{4,12},{5,13},{6,14},{7,15},{8,0},{9,1},... | collective-permute-start | bytes 1179656 | tf_op jit(solution)/shard_map/ppermute | solution.py:462
  17.9 1.1 collective-permute-start.1
  19.9 1.1 collective-permute-start.3
  21.8 1.3 stack.80.meta_ref
  24.5 3.8 %collective-permute-done.2.refs_9_ = bf16[256,768]{1,0:T(8,128)(2,1)S(1)} collective-permute-done((bf16[256,768]{1,0:T(8,128)(2,1)S(1)}, bf16[256,768]{1,0:T(8,128)(2,1)S(1)}, u32[]{:S(2)}, u32[]{:S(2)}) %collective-permute-start.2) | collective-permute-done | bytes 393248 | tf_op jit(solution)/shard_map/ppermute | solution.py:462
  28.3 8.4 %collective-permute-done.1.refs_7_ = bf16[256,768]{1,0:T(8,128)(2,1)S(1)} collective-permute-done((bf16[256,768]{1,0:T(8,128)(2,1)S(1)}, bf16[256,768]{1,0:T(8,128)(2,1)S(1)}, u32[]{:S(2)}, u32[]{:S(2)}) %collective-permute-start.1) | collective-permute-done | bytes 393248 | tf_op jit(solution)/shard_map/ppermute | solution.py:462
  36.8 3.2 %collective-permute-start.7 = (bf16[256,768]{1,0:T(8,128)(2,1)}, bf16[256,768]{1,0:T(8,128)(2,1)S(1)}, u32[]{:S(2)}, u32[]{:S(2)}) collective-permute-start(bf16[256,768]{1,0:T(8,128)(2,1)} %collective-permute-done.3.refs_4_), channel_id=1, source_target_pairs={{0,8},{1,9},{2,10},{3,11},{4,12},{5,13},{6,14},{7,15},{8,0},{9,1},... | collective-permute-start | bytes 1179656 | tf_op jit(solution)/shard_map/ppermute | solution.py:462
  40.9 1.1 collective-permute-start.5
  44.1 2.4 %collective-permute-start.9 = (bf16[40,2304]{1,0:T(8,128)(2,1)S(1)}, bf16[40,2304]{1,0:T(8,128)(2,1)S(1)}, u32[]{:S(2)}, u32[]{:S(2)}) collective-permute-start(bf16[40,2304]{1,0:T(8,128)(2,1)S(1)} %pad_maximum_fusion.11), channel_id=1, source_target_pairs={{0,1},{1,2},{2,3},{3,4},{4,5},{5,6},{6,7},{7,8},{8,9},{9,10},{10,1... | collective-permute-start | bytes 552968 | tf_op jit(solution)/shard_map/ppermute | solution.py:506
  47.5 4.1 %collective-permute-done.7.refs_10_ = bf16[256,768]{1,0:T(8,128)(2,1)S(1)} collective-permute-done((bf16[256,768]{1,0:T(8,128)(2,1)}, bf16[256,768]{1,0:T(8,128)(2,1)S(1)}, u32[]{:S(2)}, u32[]{:S(2)}) %collective-permute-start.7) | collective-permute-done | bytes 393248 | tf_op jit(solution)/shard_map/ppermute | solution.py:462
  51.7 8.5 %collective-permute-done.6.refs_8_ = bf16[256,768]{1,0:T(8,128)(2,1)S(1)} collective-permute-done((bf16[256,768]{1,0:T(8,128)(2,1)}, bf16[256,768]{1,0:T(8,128)(2,1)S(1)}, u32[]{:S(2)}, u32[]{:S(2)}) %collective-permute-start.6) | collective-permute-done | bytes 393248 | tf_op jit(solution)/shard_map/ppermute | solution.py:462
  60.1 2.2 %collective-permute-done.5.refs_6_ = bf16[256,768]{1,0:T(8,128)(2,1)S(1)} collective-permute-done((bf16[256,768]{1,0:T(8,128)(2,1)}, bf16[256,768]{1,0:T(8,128)(2,1)S(1)}, u32[]{:S(2)}, u32[]{:S(2)}) %collective-permute-start.5) | collective-permute-done | bytes 393248 | tf_op jit(solution)/shard_map/ppermute | solution.py:462
  64.1 5.9 %shard_map.113 = (f32[4,64,384]{2,1,0:T(8,128)}, f32[4,64,384]{2,1,0:T(8,128)}) custom-call(s32[9]{0:T(128)} %stack.73.cols_ref, bf16[64,4096]{1,0:T(8,128)(2,1)} %bitcast.25, bf16[64,4096]{1,0:T(8,128)(2,1)} %copy-done.6, bf16[128,4096]{1,0:T(8,128)(2,1)} %copy-done.9, bf16[256,768]{1,0:T(8,128)(2,1)} %copy-done.7, ...), custom_call_target="tpu_custom_call" | custom-call | flops 800000000 | bytes 6000000 | tf_op jit(solution)/shard_map/pallas_call | solution.py:118
  70.1 1.9 collective-permute-done.10
  72.0 1.8 add.166
  73.9 1.3 collective-permute-start.14
  75.2 4.7 %collective-permute-start.13 = (f32[256,384]{1,0:T(8,128)}, f32[256,384]{1,0:T(8,128)S(1)}, u32[]{:S(2)}, u32[]{:S(2)}) collective-permute-start(f32[256,384]{1,0:T(8,128)} %bitcast.19.refs_0_), channel_id=1, source_target_pairs={{0,12},{1,13},{2,14},{3,15},{4,0},{5,1},{6,2},{7,3},{8,4},{9,5},{1... | collective-permute-start | bytes 1179656 | tf_op jit(solution)/shard_map/ppermute | solution.py:462
  81.3 8.6 %shard_map.114.conv_hbm = bf16[16,256,768]{2,1,0:T(8,128)(2,1)} custom-call(bf16[41,64,1024]{2,1,0:T(8,128)(2,1)} %w_ref), custom_call_target="tpu_custom_call" | custom-call | flops 20000000 | bytes 20000000 | tf_op jit(solution)/shard_map/pallas_call | solution.py:69
  89.9 1.1 pad_maximum_fusion.7
  91.1 3.5 %collective-permute-start.15 = (bf16[336,384]{1,0:T(8,128)(2,1)S(1)}, bf16[336,384]{1,0:T(8,128)(2,1)S(1)}, u32[]{:S(2)}, u32[]{:S(2)}) collective-permute-start(bf16[336,384]{1,0:T(8,128)(2,1)S(1)} %get-tuple-element.120), channel_id=1, source_target_pairs={{0,2},{1,3},{2,0},{3,1},{4,6},{5,7},{6,4},{7,5},{8,10},{9,11},{10,... | collective-permute-start | bytes 774152 | tf_op jit(solution)/shard_map/ppermute | solution.py:459
  94.6 3.2 %fusion.lifted_hbm = f32[336,1024]{1,0:T(8,128)} fusion(bf16[1536,1024]{1,0:T(8,128)(2,1)S(1)} %copy-done.1, bf16[40,2304]{1,0:T(8,128)(2,1)} %collective-permute-done.14, bf16[40,2304]{1,0:T(8,128)(2,1)S(1)} %copy-done.18, bf16[256,1536]{1,0:T(8,128)(2,1)S(1)} %bitcast.30, bf16[256,768]{1,0:T(8,128)(2,1)S(1)} %bitcast.33), kind=kOutput, calls=%fused_computation.3 | convolution fusion | flops 1061093376 | bytes 6070272 | tf_op jit(solution)/shard_map/dot_general | solution.py:538
  98.5 2.1 %collective-permute-done.15.q_ref = bf16[336,384]{1,0:T(8,128)(2,1)S(1)} collective-permute-done((bf16[336,384]{1,0:T(8,128)(2,1)S(1)}, bf16[336,384]{1,0:T(8,128)(2,1)S(1)}, u32[]{:S(2)}, u32[]{:S(2)}) %collective-permute-start.15) | collective-permute-done | bytes 258080 | tf_op jit(solution)/shard_map/ppermute | solution.py:459
  101.7 1.4 collective-permute-done.16.refs_4_
  104.0 6.0 %shard_map.116 = bf16[336,384]{1,0:T(8,128)(2,1)S(1)} custom-call(s32[4]{0:T(128)S(1)} %pad_add_fusion.meta_ref, bf16[336,384]{1,0:T(8,128)(2,1)S(1)} %collective-permute-done.15.q_ref, f32[256,384]{1,0:T(8,128)} %bitcast.19.refs_0_, f32[256,384]{1,0:T(8,128)S(1)} %collective-permute-done.11.refs_1_, f32[256,384]{1,0:T(8,128)S(1)} %collective-permute-done.12.refs_2_, ...), custom_call_target="tpu_custom_call" | custom-call | flops 1056964608 | bytes 4000000 | tf_op jit(solution)/shard_map/pallas_call | solution.py:175
  110.0 1.9 collective-permute-start.20
  111.9 6.0 %shard_map.115.mine_hbm = bf16[336,384]{1,0:T(8,128)(2,1)S(1)} custom-call(s32[4]{0:T(128)S(1)} %pad_add_fusion.meta_ref, bf16[336,384]{1,0:T(8,128)(2,1)S(1)} %get-tuple-element.93.q_ref, f32[256,384]{1,0:T(8,128)} %bitcast.19.refs_0_, f32[256,384]{1,0:T(8,128)S(1)} %collective-permute-done.11.refs_1_, f32[256,384]{1,0:T(8,128)S(1)} %collective-permute-done.12.refs_2_, ...), custom_call_target="tpu_custom_call" | custom-call | flops 1056964608 | bytes 4000000 | tf_op jit(solution)/shard_map/pallas_call | solution.py:175
  118.6 1.3 collective-permute-done.20.other_hbm
  120.6 14.9 %shard_map.117 = (f32[8,48,1024]{2,1,0:T(8,128)}, bf16[400,1024]{1,0:T(8,128)(2,1)}, f32[8,1024]{1,0:T(8,128)}) custom-call(s32[5]{0:T(128)} %stack.80.meta_ref, f32[336,1024]{1,0:T(8,128)} %fusion.lifted_hbm, bf16[336,384]{1,0:T(8,128)(2,1)} %copy-done.4, bf16[336,384]{1,0:T(8,128)(2,1)} %copy-done.21, ...), custom_call_target="tpu_custom_call" | custom-call | flops 3000000000 | bytes 14000000 | tf_op jit(solution)/shard_map/pallas_call | solution.py:415
  135.6 2.5 %collective-permute-done.21.arrived_ref = bf16[400,1024]{1,0:T(8,128)(2,1)S(1)} collective-permute-done((bf16[400,1024]{1,0:T(8,128)(2,1)}, bf16[400,1024]{1,0:T(8,128)(2,1)S(1)}, u32[]{:S(2)}, u32[]{:S(2)}) %collective-permute-start.21) | collective-permute-done | bytes 819232 | tf_op jit(solution)/shard_map/ppermute | solution.py:459
  138.1 1.4 copy-done.2
  141.7 3.1 %collective-permute-start.23 = (bf16[112,1024]{1,0:T(8,128)(2,1)S(1)}, bf16[112,1024]{1,0:T(8,128)(2,1)S(1)}, u32[]{:S(2)}, u32[]{:S(2)}) collective-permute-start(bf16[112,1024]{1,0:T(8,128)(2,1)S(1)} %get-tuple-element.106), channel_id=1, source_target_pairs={{0,8},{1,9},{2,10},{3,11},{4,12},{5,13},{6,14},{7,15},{8,0},{9,1},... | collective-permute-start | bytes 688136 | tf_op jit(solution)/shard_map/ppermute | solution.py:459
  145.8 3.7 %collective-permute-done.22.one_ref = bf16[112,1024]{1,0:T(8,128)(2,1)S(1)} collective-permute-done((bf16[112,1024]{1,0:T(8,128)(2,1)S(1)}, bf16[112,1024]{1,0:T(8,128)(2,1)S(1)}, u32[]{:S(2)}, u32[]{:S(2)}) %collective-permute-start.22) | collective-permute-done | bytes 229408 | tf_op jit(solution)/shard_map/ppermute | solution.py:459
  149.5 5.9 %collective-permute-done.23.two_ref = bf16[112,1024]{1,0:T(8,128)(2,1)S(1)} collective-permute-done((bf16[112,1024]{1,0:T(8,128)(2,1)S(1)}, bf16[112,1024]{1,0:T(8,128)(2,1)S(1)}, u32[]{:S(2)}, u32[]{:S(2)}) %collective-permute-start.23) | collective-permute-done | bytes 229408 | tf_op jit(solution)/shard_map/ppermute | solution.py:459
  155.5 2.6 %collective-permute-done.24.three_ref = bf16[112,1024]{1,0:T(8,128)(2,1)S(1)} collective-permute-done((bf16[112,1024]{1,0:T(8,128)(2,1)S(1)}, bf16[112,1024]{1,0:T(8,128)(2,1)S(1)}, u32[]{:S(2)}, u32[]{:S(2)}) %collective-permute-start.24) | collective-permute-done | bytes 229408 | tf_op jit(solution)/shard_map/ppermute | solution.py:459
  159.7 2.4 %collective-permute-start.26 = (f32[32,1024]{1,0:T(8,128)S(1)}, f32[32,1024]{1,0:T(8,128)S(1)}, u32[]{:S(2)}, u32[]{:S(2)}) collective-permute-start(f32[32,1024]{1,0:T(8,128)S(1)} %get-tuple-element.110), channel_id=1, source_target_pairs={{0,2},{1,3},{2,0},{3,1},{4,6},{5,7},{6,4},{7,5},{8,10},{9,11},{10,... | collective-permute-start | bytes 393224 | tf_op jit(solution)/shard_map/ppermute | solution.py:469
  162.1 1.5 collective-permute-start.27
  164.3 2.7 %collective-permute-done.26 = f32[32,1024]{1,0:T(8,128)S(1)} collective-permute-done((f32[32,1024]{1,0:T(8,128)S(1)}, f32[32,1024]{1,0:T(8,128)S(1)}, u32[]{:S(2)}, u32[]{:S(2)}) %collective-permute-start.26) | collective-permute-done | bytes 131104 | tf_op jit(solution)/shard_map/ppermute | solution.py:469
  167.1 1.5 collective-permute-done.27
  168.5 2.1 %collective-permute-start.30 = (f32[32,1024]{1,0:T(8,128)S(1)}, f32[32,1024]{1,0:T(8,128)S(1)}, u32[]{:S(2)}, u32[]{:S(2)}) collective-permute-start(f32[32,1024]{1,0:T(8,128)S(1)} %add_add_fusion.1), channel_id=1, source_target_pairs={{0,96},{1,97},{2,98},{3,99},{4,100},{5,101},{6,102},{7,103},{8,104... | collective-permute-start | bytes 393224 | tf_op jit(solution)/shard_map/ppermute | solution.py:469
  170.7 1.4 collective-permute-start.29
  172.1 1.4 collective-permute-start.28
  173.5 6.5 %collective-permute-done.30 = f32[32,1024]{1,0:T(8,128)S(1)} collective-permute-done((f32[32,1024]{1,0:T(8,128)S(1)}, f32[32,1024]{1,0:T(8,128)S(1)}, u32[]{:S(2)}, u32[]{:S(2)}) %collective-permute-start.30) | collective-permute-done | bytes 131104 | tf_op jit(solution)/shard_map/ppermute | solution.py:469
  181.2 5.1 %collective-permute-start.31 = (f32[32,1024]{1,0:T(8,128)S(1)}, f32[32,1024]{1,0:T(8,128)S(1)}, u32[]{:S(2)}, u32[]{:S(2)}) collective-permute-start(f32[32,1024]{1,0:T(8,128)S(1)} %add_add_fusion), channel_id=1, source_target_pairs={{0,128},{1,129},{2,130},{3,131},{4,132},{5,133},{6,134},{7,135},{8... | collective-permute-start | bytes 393224 | tf_op jit(solution)/shard_map/ppermute | solution.py:469
  186.2 5.1 %collective-permute-done.31 = f32[32,1024]{1,0:T(8,128)S(1)} collective-permute-done((f32[32,1024]{1,0:T(8,128)S(1)}, f32[32,1024]{1,0:T(8,128)S(1)}, u32[]{:S(2)}, u32[]{:S(2)}) %collective-permute-start.31) | collective-permute-done | bytes 131104 | tf_op jit(solution)/shard_map/ppermute | solution.py:469
  193.2 3.0 %collective-permute-done.32 = f32[24,1024]{1,0:T(8,128)} collective-permute-done((f32[24,1024]{1,0:T(8,128)S(1)}, f32[24,1024]{1,0:T(8,128)}, u32[]{:S(2)}, u32[]{:S(2)}) %collective-permute-start.32) | collective-permute-done | bytes 98336 | tf_op jit(solution)/shard_map/ppermute | solution.py:469
  197.1 1.8 shard_map.120
  (99 shorter events, 23.9 us)
Async XLA Ops:
  7.2 7.2 %copy-start.10 = (bf16[256,1536]{1,0:T(8,128)(2,1)S(1)}, bf16[256,1536]{1,0:T(8,128)(2,1)}, u32[]{:S(2)}) copy-start(bf16[256,1536]{1,0:T(8,128)(2,1)} %param.11) | copy-start | bytes 2359300
  7.2 4.1 %copy-start.5 = (bf16[1,64,4096]{2,1,0:T(8,128)(2,1)S(1)}, bf16[1,64,4096]{2,1,0:T(8,128)(2,1)}, u32[]{:S(2)}) copy-start(bf16[1,64,4096]{2,1,0:T(8,128)(2,1)} %param.10) | copy-start | bytes 1572868
  7.2 66.7 %all-gather.2.cloned.1.call-start = ((), (), s32[]{:S(2)}) async-start(), calls=%async_computation | async-start | bytes 1671168 | tf_op jit(solution)/shard_map/all_gather | solution.py:478
  11.3 9.8 %copy-start.19 = (s32[16]{0:T(128)S(1)}, s32[16]{0:T(128)}, u32[]{:S(2)}) copy-start(s32[16]{0:T(128)} %param.18) | copy-start | bytes 196
  11.3 9.8 %copy-start.20 = (s32[16]{0:T(128)S(1)}, s32[16]{0:T(128)}, u32[]{:S(2)}) copy-start(s32[16]{0:T(128)} %param.19) | copy-start | bytes 196
  11.3 25.4 %collective-permute-start.4 = (bf16[64,4096]{1,0:T(8,128)(2,1)S(1)}, bf16[64,4096]{1,0:T(8,128)(2,1)S(1)}, u32[]{:S(2)}, u32[]{:S(2)}) collective-permute-start(bf16[64,4096]{1,0:T(8,128)(2,1)S(1)} %bitcast.26), channel_id=1, source_target_pairs={{0,2},{1,3},{2,0},{3,1},{4,6},{5,7},{6,4},{7,5},{8,10},{9,11},{10,... | collective-permute-start | bytes 1572872 | tf_op jit(solution)/shard_map/ppermute | solution.py:459
  14.6 47.7 %copy-start.7 = (bf16[256,768]{1,0:T(8,128)(2,1)}, bf16[256,768]{1,0:T(8,128)(2,1)S(1)}, u32[]{:S(2)}) copy-start(bf16[256,768]{1,0:T(8,128)(2,1)S(1)} %pad_maximum_fusion.9.refs_3_) | copy-start | bytes 1179652
  14.6 13.7 %collective-permute-start.2 = (bf16[256,768]{1,0:T(8,128)(2,1)S(1)}, bf16[256,768]{1,0:T(8,128)(2,1)S(1)}, u32[]{:S(2)}, u32[]{:S(2)}) collective-permute-start(bf16[256,768]{1,0:T(8,128)(2,1)S(1)} %pad_maximum_fusion.9.refs_3_), channel_id=1, source_target_pairs={{0,8},{1,9},{2,10},{3,11},{4,12},{5,13},{6,14},{7,15},{8,0},{9,1},... | collective-permute-start | bytes 1179656 | tf_op jit(solution)/shard_map/ppermute | solution.py:462
  17.9 18.8 %collective-permute-start.1 = (bf16[256,768]{1,0:T(8,128)(2,1)S(1)}, bf16[256,768]{1,0:T(8,128)(2,1)S(1)}, u32[]{:S(2)}, u32[]{:S(2)}) collective-permute-start(bf16[256,768]{1,0:T(8,128)(2,1)S(1)} %pad_maximum_fusion.9.refs_3_), channel_id=1, source_target_pairs={{0,12},{1,13},{2,14},{3,15},{4,0},{5,1},{6,2},{7,3},{8,4},{9,5},{1... | collective-permute-start | bytes 1179656 | tf_op jit(solution)/shard_map/ppermute | solution.py:462
  19.0 17.8 %collective-permute-start = (bf16[256,768]{1,0:T(8,128)(2,1)S(1)}, bf16[256,768]{1,0:T(8,128)(2,1)}, u32[]{:S(2)}, u32[]{:S(2)}) collective-permute-start(bf16[256,768]{1,0:T(8,128)(2,1)S(1)} %pad_maximum_fusion.9.refs_3_), channel_id=1, source_target_pairs={{0,4},{1,5},{2,6},{3,7},{4,8},{5,9},{6,10},{7,11},{8,12},{9,13},{1... | collective-permute-start | bytes 1179656 | tf_op jit(solution)/shard_map/ppermute | solution.py:462
  19.9 16.8 %collective-permute-start.3 = (bf16[256,768]{1,0:T(8,128)(2,1)S(1)}, bf16[256,768]{1,0:T(8,128)(2,1)}, u32[]{:S(2)}, u32[]{:S(2)}) collective-permute-start(bf16[256,768]{1,0:T(8,128)(2,1)S(1)} %pad_maximum_fusion.8), channel_id=1, source_target_pairs={{0,18},{1,19},{2,16},{3,17},{4,22},{5,23},{6,20},{7,21},{8,26},{9,... | collective-permute-start | bytes 1179656 | tf_op jit(solution)/shard_map/ppermute | solution.py:469
  28.3 34.1 %copy-start.12 = (bf16[256,768]{1,0:T(8,128)(2,1)}, bf16[256,768]{1,0:T(8,128)(2,1)S(1)}, u32[]{:S(2)}) copy-start(bf16[256,768]{1,0:T(8,128)(2,1)S(1)} %collective-permute-done.2.refs_9_) | copy-start | bytes 1179652
  36.7 4.2 %copy-start.13 = (bf16[256,768]{1,0:T(8,128)(2,1)}, bf16[256,768]{1,0:T(8,128)(2,1)S(1)}, u32[]{:S(2)}) copy-start(bf16[256,768]{1,0:T(8,128)(2,1)S(1)} %collective-permute-done.1.refs_7_) | copy-start | bytes 1179652
  36.7 25.6 %copy-start.6 = (bf16[64,4096]{1,0:T(8,128)(2,1)}, bf16[64,4096]{1,0:T(8,128)(2,1)S(1)}, u32[]{:S(2)}) copy-start(bf16[64,4096]{1,0:T(8,128)(2,1)S(1)} %collective-permute-done.4.refs_1_) | copy-start | bytes 1572868
  36.8 14.9 %collective-permute-start.7 = (bf16[256,768]{1,0:T(8,128)(2,1)}, bf16[256,768]{1,0:T(8,128)(2,1)S(1)}, u32[]{:S(2)}, u32[]{:S(2)}) collective-permute-start(bf16[256,768]{1,0:T(8,128)(2,1)} %collective-permute-done.3.refs_4_), channel_id=1, source_target_pairs={{0,8},{1,9},{2,10},{3,11},{4,12},{5,13},{6,14},{7,15},{8,0},{9,1},... | collective-permute-start | bytes 1179656 | tf_op jit(solution)/shard_map/ppermute | solution.py:462
  40.0 20.1 %collective-permute-start.6 = (bf16[256,768]{1,0:T(8,128)(2,1)}, bf16[256,768]{1,0:T(8,128)(2,1)S(1)}, u32[]{:S(2)}, u32[]{:S(2)}) collective-permute-start(bf16[256,768]{1,0:T(8,128)(2,1)} %collective-permute-done.3.refs_4_), channel_id=1, source_target_pairs={{0,12},{1,13},{2,14},{3,15},{4,0},{5,1},{6,2},{7,3},{8,4},{9,5},{1... | collective-permute-start | bytes 1179656 | tf_op jit(solution)/shard_map/ppermute | solution.py:462
  40.9 21.5 %collective-permute-start.5 = (bf16[256,768]{1,0:T(8,128)(2,1)}, bf16[256,768]{1,0:T(8,128)(2,1)S(1)}, u32[]{:S(2)}, u32[]{:S(2)}) collective-permute-start(bf16[256,768]{1,0:T(8,128)(2,1)} %collective-permute-done.3.refs_4_), channel_id=1, source_target_pairs={{0,4},{1,5},{2,6},{3,7},{4,8},{5,9},{6,10},{7,11},{8,12},{9,13},{1... | collective-permute-start | bytes 1179656 | tf_op jit(solution)/shard_map/ppermute | solution.py:462
  42.1 20.2 %collective-permute-start.8 = (bf16[128,4096]{1,0:T(8,128)(2,1)S(1)}, bf16[128,4096]{1,0:T(8,128)(2,1)S(1)}, u32[]{:S(2)}, u32[]{:S(2)}) collective-permute-start(bf16[128,4096]{1,0:T(8,128)(2,1)S(1)} %pad_maximum_fusion), channel_id=1, source_target_pairs={{0,1},{1,0},{2,3},{3,2},{4,5},{5,4},{6,7},{7,6},{8,9},{9,8},{10,11... | collective-permute-start | bytes 3145736 | tf_op jit(solution)/shard_map/ppermute | solution.py:459
  44.1 3.4 %collective-permute-start.9 = (bf16[40,2304]{1,0:T(8,128)(2,1)S(1)}, bf16[40,2304]{1,0:T(8,128)(2,1)S(1)}, u32[]{:S(2)}, u32[]{:S(2)}) collective-permute-start(bf16[40,2304]{1,0:T(8,128)(2,1)S(1)} %pad_maximum_fusion.11), channel_id=1, source_target_pairs={{0,1},{1,2},{2,3},{3,4},{4,5},{5,6},{6,7},{7,8},{8,9},{9,10},{10,1... | collective-permute-start | bytes 552968 | tf_op jit(solution)/shard_map/ppermute | solution.py:506
  47.5 33.0 %copy-start.17 = (bf16[40,2304]{1,0:T(8,128)(2,1)}, bf16[40,2304]{1,0:T(8,128)(2,1)S(1)}, u32[]{:S(2)}) copy-start(bf16[40,2304]{1,0:T(8,128)(2,1)S(1)} %collective-permute-done.9) | copy-start | bytes 552964
  51.7 10.7 %copy-start.14 = (bf16[256,768]{1,0:T(8,128)(2,1)}, bf16[256,768]{1,0:T(8,128)(2,1)S(1)}, u32[]{:S(2)}) copy-start(bf16[256,768]{1,0:T(8,128)(2,1)S(1)} %collective-permute-done.7.refs_10_) | copy-start | bytes 1179652
  70.0 2.0 collective-permute-start.10
  73.9 16.0 %collective-permute-start.14 = (bf16[40,2304]{1,0:T(8,128)(2,1)S(1)}, bf16[40,2304]{1,0:T(8,128)(2,1)}, u32[]{:S(2)}, u32[]{:S(2)}) collective-permute-start(bf16[40,2304]{1,0:T(8,128)(2,1)S(1)} %pad_maximum_fusion.12), channel_id=1, source_target_pairs={{1,0},{2,1},{3,2},{4,3},{5,4},{6,5},{7,6},{8,7},{9,8},{10,9},{11,1... | collective-permute-start | bytes 552968 | tf_op jit(solution)/shard_map/ppermute | solution.py:534
  75.2 14.7 %copy-start.8 = (bf16[1,256,1536]{2,1,0:T(8,128)(2,1)S(1)}, bf16[1,256,1536]{2,1,0:T(8,128)(2,1)}, u32[]{:S(2)}) copy-start(bf16[1,256,1536]{2,1,0:T(8,128)(2,1)} %param.13) | copy-start | bytes 2359300
  75.2 22.6 %collective-permute-start.13 = (f32[256,384]{1,0:T(8,128)}, f32[256,384]{1,0:T(8,128)S(1)}, u32[]{:S(2)}, u32[]{:S(2)}) collective-permute-start(f32[256,384]{1,0:T(8,128)} %bitcast.19.refs_0_), channel_id=1, source_target_pairs={{0,12},{1,13},{2,14},{3,15},{4,0},{5,1},{6,2},{7,3},{8,4},{9,5},{1... | collective-permute-start | bytes 1179656 | tf_op jit(solution)/shard_map/ppermute | solution.py:462
  79.8 18.0 %collective-permute-start.12 = (f32[256,384]{1,0:T(8,128)}, f32[256,384]{1,0:T(8,128)S(1)}, u32[]{:S(2)}, u32[]{:S(2)}) collective-permute-start(f32[256,384]{1,0:T(8,128)} %bitcast.19.refs_0_), channel_id=1, source_target_pairs={{0,8},{1,9},{2,10},{3,11},{4,12},{5,13},{6,14},{7,15},{8,0},{9,1},... | collective-permute-start | bytes 1179656 | tf_op jit(solution)/shard_map/ppermute | solution.py:462
  80.5 18.0 %collective-permute-start.11 = (f32[256,384]{1,0:T(8,128)}, f32[256,384]{1,0:T(8,128)S(1)}, u32[]{:S(2)}, u32[]{:S(2)}) collective-permute-start(f32[256,384]{1,0:T(8,128)} %bitcast.19.refs_0_), channel_id=1, source_target_pairs={{0,4},{1,5},{2,6},{3,7},{4,8},{5,9},{6,10},{7,11},{8,12},{9,13},{1... | collective-permute-start | bytes 1179656 | tf_op jit(solution)/shard_map/ppermute | solution.py:462
  81.3 8.6 %copy-start.18 = (bf16[40,2304]{1,0:T(8,128)(2,1)S(1)}, bf16[40,2304]{1,0:T(8,128)(2,1)}, u32[]{:S(2)}) copy-start(bf16[40,2304]{1,0:T(8,128)(2,1)} %copy-done.17) | copy-start | bytes 552964
  81.3 13.3 %copy-start.1 = (bf16[1536,1024]{1,0:T(8,128)(2,1)S(1)}, bf16[1536,1024]{1,0:T(8,128)(2,1)}, u32[]{:S(2)}) copy-start(bf16[1536,1024]{1,0:T(8,128)(2,1)} %disc_ref.1) | copy-start | bytes 9437188
  89.8 4.7 %copy-start.11 = (bf16[1,256,768]{2,1,0:T(8,128)(2,1)S(1)}, bf16[1,256,768]{2,1,0:T(8,128)(2,1)}, u32[]{:S(2)}) copy-start(bf16[1,256,768]{2,1,0:T(8,128)(2,1)} %param.12) | copy-start | bytes 1179652
  91.1 9.6 %collective-permute-start.15 = (bf16[336,384]{1,0:T(8,128)(2,1)S(1)}, bf16[336,384]{1,0:T(8,128)(2,1)S(1)}, u32[]{:S(2)}, u32[]{:S(2)}) collective-permute-start(bf16[336,384]{1,0:T(8,128)(2,1)S(1)} %get-tuple-element.120), channel_id=1, source_target_pairs={{0,2},{1,3},{2,0},{3,1},{4,6},{5,7},{6,4},{7,5},{8,10},{9,11},{10,... | collective-permute-start | bytes 774152 | tf_op jit(solution)/shard_map/ppermute | solution.py:459
  100.6 2.5 %collective-permute-start.16 = (f32[256,384]{1,0:T(8,128)}, f32[256,384]{1,0:T(8,128)S(1)}, u32[]{:S(2)}, u32[]{:S(2)}) collective-permute-start(f32[256,384]{1,0:T(8,128)} %bitcast.19.refs_0_), channel_id=1, source_target_pairs={{0,1},{1,0},{2,3},{3,2},{4,5},{5,4},{6,7},{7,6},{8,9},{9,8},{10,11... | collective-permute-start | bytes 1179656 | tf_op jit(solution)/shard_map/ppermute | solution.py:459
  100.6 2.5 %collective-permute-start.17 = (f32[256,384]{1,0:T(8,128)S(1)}, f32[256,384]{1,0:T(8,128)S(1)}, u32[]{:S(2)}, u32[]{:S(2)}) collective-permute-start(f32[256,384]{1,0:T(8,128)S(1)} %collective-permute-done.11.refs_1_), channel_id=1, source_target_pairs={{0,1},{1,0},{2,3},{3,2},{4,5},{5,4},{6,7},{7,6},{8,9},{9,8},{10,11... | collective-permute-start | bytes 1179656 | tf_op jit(solution)/shard_map/ppermute | solution.py:459
  101.1 2.3 %collective-permute-start.18 = (f32[256,384]{1,0:T(8,128)S(1)}, f32[256,384]{1,0:T(8,128)S(1)}, u32[]{:S(2)}, u32[]{:S(2)}) collective-permute-start(f32[256,384]{1,0:T(8,128)S(1)} %collective-permute-done.12.refs_2_), channel_id=1, source_target_pairs={{0,1},{1,0},{2,3},{3,2},{4,5},{5,4},{6,7},{7,6},{8,9},{9,8},{10,11... | collective-permute-start | bytes 1179656 | tf_op jit(solution)/shard_map/ppermute | solution.py:459
  101.1 2.9 %collective-permute-start.19 = (f32[256,384]{1,0:T(8,128)S(1)}, f32[256,384]{1,0:T(8,128)S(1)}, u32[]{:S(2)}, u32[]{:S(2)}) collective-permute-start(f32[256,384]{1,0:T(8,128)S(1)} %collective-permute-done.13.refs_3_), channel_id=1, source_target_pairs={{0,1},{1,0},{2,3},{3,2},{4,5},{5,4},{6,7},{7,6},{8,9},{9,8},{10,11... | collective-permute-start | bytes 1179656 | tf_op jit(solution)/shard_map/ppermute | solution.py:459
  110.0 9.9 %collective-permute-start.20 = (bf16[336,384]{1,0:T(8,128)(2,1)S(1)}, bf16[336,384]{1,0:T(8,128)(2,1)S(1)}, u32[]{:S(2)}, u32[]{:S(2)}) collective-permute-start(bf16[336,384]{1,0:T(8,128)(2,1)S(1)} %shard_map.116), channel_id=1, source_target_pairs={{0,2},{1,3},{2,0},{3,1},{4,6},{5,7},{6,4},{7,5},{8,10},{9,11},{10,... | collective-permute-start | bytes 774152 | tf_op jit(solution)/shard_map/ppermute | solution.py:459
  135.5 2.6 %collective-permute-start.21 = (bf16[400,1024]{1,0:T(8,128)(2,1)}, bf16[400,1024]{1,0:T(8,128)(2,1)S(1)}, u32[]{:S(2)}, u32[]{:S(2)}) collective-permute-start(bf16[400,1024]{1,0:T(8,128)(2,1)} %get-tuple-element.102), channel_id=1, source_target_pairs={{0,1},{1,0},{2,3},{3,2},{4,5},{5,4},{6,7},{7,6},{8,9},{9,8},{10,11... | collective-permute-start | bytes 2457608 | tf_op jit(solution)/shard_map/ppermute | solution.py:459
  141.0 8.5 %collective-permute-start.22 = (bf16[112,1024]{1,0:T(8,128)(2,1)S(1)}, bf16[112,1024]{1,0:T(8,128)(2,1)S(1)}, u32[]{:S(2)}, u32[]{:S(2)}) collective-permute-start(bf16[112,1024]{1,0:T(8,128)(2,1)S(1)} %get-tuple-element.105), channel_id=1, source_target_pairs={{0,4},{1,5},{2,6},{3,7},{4,0},{5,1},{6,2},{7,3},{8,12},{9,13},{10,... | collective-permute-start | bytes 688136 | tf_op jit(solution)/shard_map/ppermute | solution.py:459
  141.7 13.8 %collective-permute-start.23 = (bf16[112,1024]{1,0:T(8,128)(2,1)S(1)}, bf16[112,1024]{1,0:T(8,128)(2,1)S(1)}, u32[]{:S(2)}, u32[]{:S(2)}) collective-permute-start(bf16[112,1024]{1,0:T(8,128)(2,1)S(1)} %get-tuple-element.106), channel_id=1, source_target_pairs={{0,8},{1,9},{2,10},{3,11},{4,12},{5,13},{6,14},{7,15},{8,0},{9,1},... | collective-permute-start | bytes 688136 | tf_op jit(solution)/shard_map/ppermute | solution.py:459
  144.8 13.2 %collective-permute-start.24 = (bf16[112,1024]{1,0:T(8,128)(2,1)S(1)}, bf16[112,1024]{1,0:T(8,128)(2,1)S(1)}, u32[]{:S(2)}, u32[]{:S(2)}) collective-permute-start(bf16[112,1024]{1,0:T(8,128)(2,1)S(1)} %get-tuple-element.107), channel_id=1, source_target_pairs={{0,12},{1,13},{2,14},{3,15},{4,8},{5,9},{6,10},{7,11},{8,4},{9,5},... | collective-permute-start | bytes 688136 | tf_op jit(solution)/shard_map/ppermute | solution.py:459
  158.8 5.6 %collective-permute-start.25 = (f32[32,1024]{1,0:T(8,128)S(1)}, f32[32,1024]{1,0:T(8,128)S(1)}, u32[]{:S(2)}, u32[]{:S(2)}) collective-permute-start(f32[32,1024]{1,0:T(8,128)S(1)} %get-tuple-element.109), channel_id=1, source_target_pairs={{0,16},{1,17},{2,18},{3,19},{4,20},{5,21},{6,22},{7,23},{8,24},{9,... | collective-permute-start | bytes 393224 | tf_op jit(solution)/shard_map/ppermute | solution.py:469
  159.7 7.3 %collective-permute-start.26 = (f32[32,1024]{1,0:T(8,128)S(1)}, f32[32,1024]{1,0:T(8,128)S(1)}, u32[]{:S(2)}, u32[]{:S(2)}) collective-permute-start(f32[32,1024]{1,0:T(8,128)S(1)} %get-tuple-element.110), channel_id=1, source_target_pairs={{0,2},{1,3},{2,0},{3,1},{4,6},{5,7},{6,4},{7,5},{8,10},{9,11},{10,... | collective-permute-start | bytes 393224 | tf_op jit(solution)/shard_map/ppermute | solution.py:469
  162.1 6.4 %collective-permute-start.27 = (f32[32,1024]{1,0:T(8,128)S(1)}, f32[32,1024]{1,0:T(8,128)S(1)}, u32[]{:S(2)}, u32[]{:S(2)}) collective-permute-start(f32[32,1024]{1,0:T(8,128)S(1)} %get-tuple-element.111), channel_id=1, source_target_pairs={{0,18},{1,19},{2,16},{3,17},{4,22},{5,23},{6,20},{7,21},{8,26},{9,... | collective-permute-start | bytes 393224 | tf_op jit(solution)/shard_map/ppermute | solution.py:469
  168.5 11.4 %collective-permute-start.30 = (f32[32,1024]{1,0:T(8,128)S(1)}, f32[32,1024]{1,0:T(8,128)S(1)}, u32[]{:S(2)}, u32[]{:S(2)}) collective-permute-start(f32[32,1024]{1,0:T(8,128)S(1)} %add_add_fusion.1), channel_id=1, source_target_pairs={{0,96},{1,97},{2,98},{3,99},{4,100},{5,101},{6,102},{7,103},{8,104... | collective-permute-start | bytes 393224 | tf_op jit(solution)/shard_map/ppermute | solution.py:469
  170.7 10.0 %collective-permute-start.29 = (f32[32,1024]{1,0:T(8,128)S(1)}, f32[32,1024]{1,0:T(8,128)S(1)}, u32[]{:S(2)}, u32[]{:S(2)}) collective-permute-start(f32[32,1024]{1,0:T(8,128)S(1)} %add_add_fusion.1), channel_id=1, source_target_pairs={{0,64},{1,65},{2,66},{3,67},{4,68},{5,69},{6,70},{7,71},{8,72},{9,... | collective-permute-start | bytes 393224 | tf_op jit(solution)/shard_map/ppermute | solution.py:469
  172.1 9.0 %collective-permute-start.28 = (f32[32,1024]{1,0:T(8,128)S(1)}, f32[32,1024]{1,0:T(8,128)S(1)}, u32[]{:S(2)}, u32[]{:S(2)}) collective-permute-start(f32[32,1024]{1,0:T(8,128)S(1)} %add_add_fusion.1), channel_id=1, source_target_pairs={{0,32},{1,33},{2,34},{3,35},{4,36},{5,37},{6,38},{7,39},{8,40},{9,... | collective-permute-start | bytes 393224 | tf_op jit(solution)/shard_map/ppermute | solution.py:469
  181.2 10.1 %collective-permute-start.31 = (f32[32,1024]{1,0:T(8,128)S(1)}, f32[32,1024]{1,0:T(8,128)S(1)}, u32[]{:S(2)}, u32[]{:S(2)}) collective-permute-start(f32[32,1024]{1,0:T(8,128)S(1)} %add_add_fusion), channel_id=1, source_target_pairs={{0,128},{1,129},{2,130},{3,131},{4,132},{5,133},{6,134},{7,135},{8... | collective-permute-start | bytes 393224 | tf_op jit(solution)/shard_map/ppermute | solution.py:469
  191.3 4.8 %collective-permute-start.32 = (f32[24,1024]{1,0:T(8,128)S(1)}, f32[24,1024]{1,0:T(8,128)}, u32[]{:S(2)}, u32[]{:S(2)}) collective-permute-start(f32[24,1024]{1,0:T(8,128)S(1)} %slice.32), channel_id=1, source_target_pairs={{0,16},{1,17},{2,18},{3,19},{4,20},{5,21},{6,22},{7,23},{8,24},{9,... | collective-permute-start | bytes 294920 | tf_op jit(solution)/shard_map/ppermute | solution.py:469
  (8 other events, 8.5 us)
Sparse Core Ops, SparseCore 0:
  11.4 54.4 all-gather.1

commit v5 on v4

--- a/solution.py
+++ b/solution.py
@@ -145,7 +145,7 @@
     for m, o in zip(mine, other):
         keys.append(jnp.where(first, m[...], o[...]))
         values.append(jnp.where(first, o[...], m[...]))
-    key_high, key_low = split(jnp.concatenate(keys, axis=0))
+    key_high, key_low = split(jnp.concatenate(keys, axis=0) * (1.0 / math.sqrt(HEAD_DIM)))
     value_high, value_low = split(jnp.concatenate(values, axis=0))
     spot = lax.broadcasted_iota(jnp.int32, (1, 1024), 1)
     hop, block, rest = (spot // 256, (spot // 64) % 4, spot % 64)
@@ -159,9 +159,9 @@
         q = q_ref[start : start + rows, :]
         scores = lax.dot_general(q, key_high, contract, preferred_element_type=F32)
         scores = scores + lax.dot_general(q, key_low, contract, preferred_element_type=F32)
-        scores = jnp.where(alive, scores * (1.0 / math.sqrt(HEAD_DIM)), -1e30)
+        scores = jnp.where(alive, scores, -1e30)
         top = jnp.max(scores, axis=1, keepdims=True)
-        expo = jnp.where(alive, jnp.exp(scores - top), 0.0)
+        expo = jnp.exp(scores - top)
         denom = jnp.sum(expo, axis=1, keepdims=True)
         weights = expo.astype(BF16)
         mixed = jnp.dot(weights, value_high, preferred_element_type=F32)
@@ -318,7 +318,7 @@
     for copy in conv_copies:
         copy.wait()
 
-    @pl.loop(0, tiles)
+    @pl.loop(0, tiles, unroll=2)
     def _(tile):
         lanes = pl.ds(pl.multiple_of(tile * 128, 128), 128)
         phase = [feed_s[tile, pl.ds(b, rows, stride=STRIDE), :] for b in range(STRIDE)]
@@ -362,7 +362,7 @@
     contract = (((1,), (1,)), ((), ()))
     low_back = low_lanes((own_out, 128))
 
-    @pl.loop(0, tiles)
+    @pl.loop(0, tiles, unroll=2)
     def _(tile):
         lanes = pl.ds(pl.multiple_of(tile * 128, 128), 128)
         turned_s[...] = roll_half(grad_s[:, lanes])
@@ -491,8 +491,8 @@
     hops = (1, 3, 2)
     near_turned = [turn(near, j) for j in hops]
     states_in = states[0]
-    near, near_turned, far, state_far, queries_in, hidden_in = lax.optimization_barrier(
-        (near, near_turned, far, flip(states_in, 2), queries[0], hidden[0])
+    near, near_turned, far, state_far, queries_in, hidden_in, conv_in = lax.optimization_barrier(
+        (near, near_turned, far, flip(states_in, 2), queries[0], hidden[0], conv_weight)
     )
 
     lower = clip % 2
@@ -518,16 +518,17 @@
     meta3 = jnp.stack([row, 2 * half + lower, clip // 2]).astype(jnp.int32)
     blocks = [b for pair in zip(near_blocks, far_blocks) for b in pair]
     tables = (cols, meta, meta2.astype(jnp.int32), meta3)
-    blocks, state_pair, tables, before, after = lax.optimization_barrier(
-        (blocks, state_pair, tables, before, after)
+    conv = arrange(conv_in)
+    blocks, state_pair, tables, before, after, conv = lax.optimization_barrier(
+        (blocks, state_pair, tables, before, after, conv)
     )
     cols, meta, meta2, meta3 = tables
     state_parts = [states_in, state_far, state_pair]
     kept, sent = project(cols, state_parts, blocks)
     mine_kv = (kept + flip(sent, 1)).reshape(256, HALF_ATT)
 
-    mine_kv, conv_in, proj, queries_in, hidden_in, before, after = lax.optimization_barrier(
-        (mine_kv, conv_weight, proj, queries[0], hidden[0], before, after)
+    mine_kv, proj, queries_in, hidden_in, before, after = lax.optimization_barrier(
+        (mine_kv, proj, queries[0], hidden[0], before, after)
     )
     got = [mine_kv] + [turn(mine_kv, j) for j in (1, 2, 3)]
     rows_in = jnp.concatenate([queries_in, hidden_in], axis=1)
@@ -536,10 +537,7 @@
     query_mine = lax.dynamic_slice_in_dim(query_ext, half * HALF_ATT, HALF_ATT, axis=1)
     query_far = flip(lax.dynamic_slice_in_dim(query_ext, (1 - half) * HALF_ATT, HALF_ATT, axis=1), 2)
     lifted = jnp.dot(hidden_ext, disc_in, preferred_element_type=F32)
-    conv = arrange(conv_in)
-    got, conv, query_mine, query_far, lifted = lax.optimization_barrier(
-        (got, conv, query_mine, query_far, lifted)
-    )
+    got, query_mine, query_far, lifted = lax.optimization_barrier((got, query_mine, query_far, lifted))
     other = [flip(g, 1) for g in got]
 
     attended_far = flip(attend(meta, query_far, got, other), 2)

time: 209 us -> 201 us (0.962)
  Pallas kernels: 44.5 us -> 41.8 us
    ppermute x9, starting transfers between devices: 16.7 us -> 14.3 us  [turn(): lax.ppermute(x, 'seq', [(i, (i + 4 * hops) % seq_size) for i in range(seq...]
    unnamed x44 -> x42, local copies, waits for them, and re-layouts: 6.19 us -> 5.43 us
  transfers between devices with their start and end apart: 34 -> 34, of which waited for: 25 -> 23; matrix products, arithmetic and copies ran while one was open for 6% -> 8% of each run, Pallas kernels for 10% -> 10%
where the time goes in v5:
time: 201 us; the launch traced here: 200 us
  waiting for transfers between devices  69.8 us (35%)
  starting transfers between devices  49.3 us (25%)
  Pallas kernels  41.8 us (21%)
  between operations  16.9 us (8%)
  local copies, waits for them, and re-layouts  9.83 us (5%)
  matrix products  6.53 us (3%)
  other arithmetic  5.72 us (3%)
    ppermute x9, waiting for transfers between devices, turn(): lax.ppermute(x, 'seq', [(i, (i + 4 * hops) % seq_size) for i in range(seq...  26.9 us
    ppermute x9, waiting for transfers between devices, swap(): return lax.ppermute(x, ('dp', 'seq'), pairs)  21.8 us
    ppermute x13, waiting for transfers between devices, flip(): return lax.ppermute(x, 'seq', [(i, i ^ bit) for i in range(seq_size)])  21.1 us
    ppermute x9, starting transfers between devices, swap(): return lax.ppermute(x, ('dp', 'seq'), pairs)  16.1 us
    ppermute x13, starting transfers between devices, flip(): return lax.ppermute(x, 'seq', [(i, i ^ bit) for i in range(seq_size)])  14.5 us
    ppermute x9, starting transfers between devices, turn(): lax.ppermute(x, 'seq', [(i, (i + 4 * hops) % seq_size) for i in range(seq...  14.3 us
    pallas_call x1, Pallas kernels, critic(): pl.pallas_call(critic_kernel, in_specs=[smem()] + [anywhere()] * 5 + [vme...  13 us
    pallas_call x2, Pallas kernels, attend(): pl.pallas_call(attend_kernel, grid=(width // HEAD_DIM,), in_specs=[smem()...  11.3 us
  transfers between devices with their start and end apart: 34, of which 23 were waited for; matrix products, arithmetic and copies ran while one was open for 8% of the time, Pallas kernels for 10%

profile of v5, /device:TPU:32, one launch (start us, length us, event | category | flops | bytes accessed | tf_op | source)
XLA Modules:
  0.0 199.9 jit_solution(15935971798618538102)
XLA Ops:
  7.2 3.1 %collective-permute-start.4 = (bf16[64,4096]{1,0:T(8,128)(2,1)}, bf16[64,4096]{1,0:T(8,128)(2,1)S(1)}, u32[]{:S(2)}, u32[]{:S(2)}) collective-permute-start(bf16[64,4096]{1,0:T(8,128)(2,1)} %bitcast.31), channel_id=1, source_target_pairs={{0,2},{1,3},{2,0},{3,1},{4,6},{5,7},{6,4},{7,5},{8,10},{9,11},{10,... | collective-permute-start | bytes 1572872 | tf_op jit(solution)/shard_map/ppermute | solution.py:459
  10.3 3.2 %convolution_convert_fusion = bf16[48,1024]{1,0:T(8,128)(2,1)} fusion(bf16[48,1536]{1,0:T(8,128)(2,1)S(1)} %copy-done, bf16[1536,1024]{1,0:T(8,128)(2,1)} %disc_ref.1), kind=kOutput, calls=%fused_computation | convolution fusion | flops 151044096 | bytes 3391488 | tf_op jit(solution)/shard_map/dot_general | solution.py:476
  13.8 1.7 collective-permute-start
  15.5 1.7 collective-permute-start.1
  17.2 2.0 collective-permute-start.2
  21.0 1.2 stack.80.meta_ref
  23.6 2.4 %collective-permute-done.refs_5_ = bf16[256,768]{1,0:T(8,128)(2,1)S(1)} collective-permute-done((bf16[256,768]{1,0:T(8,128)(2,1)S(1)}, bf16[256,768]{1,0:T(8,128)(2,1)S(1)}, u32[]{:S(2)}, u32[]{:S(2)}) %collective-permute-start) | collective-permute-done | bytes 393248 | tf_op jit(solution)/shard_map/ppermute | solution.py:462
  26.0 3.2 %collective-permute-done.1.refs_7_ = bf16[256,768]{1,0:T(8,128)(2,1)S(1)} collective-permute-done((bf16[256,768]{1,0:T(8,128)(2,1)S(1)}, bf16[256,768]{1,0:T(8,128)(2,1)S(1)}, u32[]{:S(2)}, u32[]{:S(2)}) %collective-permute-start.1) | collective-permute-done | bytes 393248 | tf_op jit(solution)/shard_map/ppermute | solution.py:462
  29.3 6.8 %collective-permute-done.2.refs_9_ = bf16[256,768]{1,0:T(8,128)(2,1)S(1)} collective-permute-done((bf16[256,768]{1,0:T(8,128)(2,1)S(1)}, bf16[256,768]{1,0:T(8,128)(2,1)S(1)}, u32[]{:S(2)}, u32[]{:S(2)}) %collective-permute-start.2) | collective-permute-done | bytes 393248 | tf_op jit(solution)/shard_map/ppermute | solution.py:462
  36.1 1.2 collective-permute-start.5
  37.3 2.1 %collective-permute-start.6 = (bf16[256,768]{1,0:T(8,128)(2,1)}, bf16[256,768]{1,0:T(8,128)(2,1)S(1)}, u32[]{:S(2)}, u32[]{:S(2)}) collective-permute-start(bf16[256,768]{1,0:T(8,128)(2,1)} %collective-permute-done.3.refs_4_), channel_id=1, source_target_pairs={{0,12},{1,13},{2,14},{3,15},{4,0},{5,1},{6,2},{7,3},{8,4},{9,5},{1... | collective-permute-start | bytes 1179656 | tf_op jit(solution)/shard_map/ppermute | solution.py:462
  41.6 3.1 %collective-permute-start.9 = (bf16[40,2304]{1,0:T(8,128)(2,1)S(1)}, bf16[40,2304]{1,0:T(8,128)(2,1)}, u32[]{:S(2)}, u32[]{:S(2)}) collective-permute-start(bf16[40,2304]{1,0:T(8,128)(2,1)S(1)} %pad_maximum_fusion.11), channel_id=1, source_target_pairs={{0,1},{1,2},{2,3},{3,4},{4,5},{5,6},{6,7},{7,8},{8,9},{9,10},{10,1... | collective-permute-start | bytes 552968 | tf_op jit(solution)/shard_map/ppermute | solution.py:506
  44.6 8.4 %shard_map.113.conv_hbm = bf16[16,256,768]{2,1,0:T(8,128)(2,1)} custom-call(bf16[41,64,1024]{2,1,0:T(8,128)(2,1)} %w_ref), custom_call_target="tpu_custom_call" | custom-call | flops 20000000 | bytes 20000000 | tf_op jit(solution)/shard_map/pallas_call | solution.py:69
  53.1 3.0 %collective-permute-done.6.refs_8_ = bf16[256,768]{1,0:T(8,128)(2,1)S(1)} collective-permute-done((bf16[256,768]{1,0:T(8,128)(2,1)}, bf16[256,768]{1,0:T(8,128)(2,1)S(1)}, u32[]{:S(2)}, u32[]{:S(2)}) %collective-permute-start.6) | collective-permute-done | bytes 393248 | tf_op jit(solution)/shard_map/ppermute | solution.py:462
  56.2 2.4 %collective-permute-done.7.refs_10_ = bf16[256,768]{1,0:T(8,128)(2,1)S(1)} collective-permute-done((bf16[256,768]{1,0:T(8,128)(2,1)}, bf16[256,768]{1,0:T(8,128)(2,1)S(1)}, u32[]{:S(2)}, u32[]{:S(2)}) %collective-permute-start.7) | collective-permute-done | bytes 393248 | tf_op jit(solution)/shard_map/ppermute | solution.py:462
  60.4 5.9 %shard_map.114 = (f32[4,64,384]{2,1,0:T(8,128)}, f32[4,64,384]{2,1,0:T(8,128)}) custom-call(s32[9]{0:T(128)} %stack.73.cols_ref, bf16[64,4096]{1,0:T(8,128)(2,1)} %bitcast.32, bf16[64,4096]{1,0:T(8,128)(2,1)} %copy-done.7, bf16[128,4096]{1,0:T(8,128)(2,1)} %copy-done.10, bf16[256,768]{1,0:T(8,128)(2,1)} %copy-done.8, ...), custom_call_target="tpu_custom_call" | custom-call | flops 800000000 | bytes 6000000 | tf_op jit(solution)/shard_map/pallas_call | solution.py:118
  66.4 1.9 collective-permute-done.10
  68.3 1.9 add.166
  70.2 1.3 collective-permute-start.14
  71.5 1.8 collective-permute-start.11
  73.3 2.0 collective-permute-start.12
  75.3 1.9 collective-permute-start.13
  78.4 3.4 %collective-permute-start.15 = (bf16[336,384]{1,0:T(8,128)(2,1)S(1)}, bf16[336,384]{1,0:T(8,128)(2,1)S(1)}, u32[]{:S(2)}, u32[]{:S(2)}) collective-permute-start(bf16[336,384]{1,0:T(8,128)(2,1)S(1)} %get-tuple-element.120), channel_id=1, source_target_pairs={{0,2},{1,3},{2,0},{3,1},{4,6},{5,7},{6,4},{7,5},{8,10},{9,11},{10,... | collective-permute-start | bytes 774152 | tf_op jit(solution)/shard_map/ppermute | solution.py:459
  81.8 3.3 %fusion.lifted_hbm = f32[336,1024]{1,0:T(8,128)} fusion(bf16[1536,1024]{1,0:T(8,128)(2,1)S(1)} %copy-done.1, bf16[40,2304]{1,0:T(8,128)(2,1)} %collective-permute-done.14, bf16[40,2304]{1,0:T(8,128)(2,1)} %collective-permute-done.9, bf16[256,1536]{1,0:T(8,128)(2,1)S(1)} %bitcast.36, bf16[256,768]{1,0:T(8,128)(2,1)} %bitcast.39), kind=kOutput, calls=%fused_computation.3 | convolution fusion | flops 1061093376 | bytes 6070272 | tf_op jit(solution)/shard_map/dot_general | solution.py:539
  85.2 8.3 %collective-permute-done.12.refs_2_ = f32[256,384]{1,0:T(8,128)S(1)} collective-permute-done((f32[256,384]{1,0:T(8,128)}, f32[256,384]{1,0:T(8,128)S(1)}, u32[]{:S(2)}, u32[]{:S(2)}) %collective-permute-start.12) | collective-permute-done | bytes 393248 | tf_op jit(solution)/shard_map/ppermute | solution.py:462
  97.6 5.6 %shard_map.116 = bf16[336,384]{1,0:T(8,128)(2,1)S(1)} custom-call(s32[4]{0:T(128)S(1)} %pad_add_fusion.meta_ref, bf16[336,384]{1,0:T(8,128)(2,1)S(1)} %collective-permute-done.15.q_ref, f32[256,384]{1,0:T(8,128)S(1)} %bitcast.29, f32[256,384]{1,0:T(8,128)S(1)} %collective-permute-done.11.refs_1_, f32[256,384]{1,0:T(8,128)S(1)} %collective-permute-done.12.refs_2_, ...), custom_call_target="tpu_custom_call" | custom-call | flops 1056964608 | bytes 4000000 | tf_op jit(solution)/shard_map/pallas_call | solution.py:175
  103.3 1.9 collective-permute-start.20
  105.2 5.6 %shard_map.115.mine_hbm = bf16[336,384]{1,0:T(8,128)(2,1)S(1)} custom-call(s32[4]{0:T(128)S(1)} %pad_add_fusion.meta_ref, bf16[336,384]{1,0:T(8,128)(2,1)S(1)} %get-tuple-element.93.q_ref, f32[256,384]{1,0:T(8,128)S(1)} %bitcast.30, f32[256,384]{1,0:T(8,128)S(1)} %collective-permute-done.11.refs_1_, f32[256,384]{1,0:T(8,128)S(1)} %collective-permute-done.12.refs_2_, ...), custom_call_target="tpu_custom_call" | custom-call | flops 1056964608 | bytes 4000000 | tf_op jit(solution)/shard_map/pallas_call | solution.py:175
  111.5 1.6 collective-permute-done.20.other_hbm
  113.9 13.0 %shard_map.117 = (f32[8,48,1024]{2,1,0:T(8,128)}, bf16[400,1024]{1,0:T(8,128)(2,1)}, f32[8,1024]{1,0:T(8,128)}) custom-call(s32[5]{0:T(128)} %stack.80.meta_ref, f32[336,1024]{1,0:T(8,128)} %fusion.lifted_hbm, bf16[336,384]{1,0:T(8,128)(2,1)} %copy-done.5, bf16[336,384]{1,0:T(8,128)(2,1)} %copy-done.20, ...), custom_call_target="tpu_custom_call" | custom-call | flops 3000000000 | bytes 14000000 | tf_op jit(solution)/shard_map/pallas_call | solution.py:415
  127.0 2.5 %collective-permute-done.21.arrived_ref = bf16[400,1024]{1,0:T(8,128)(2,1)S(1)} collective-permute-done((bf16[400,1024]{1,0:T(8,128)(2,1)}, bf16[400,1024]{1,0:T(8,128)(2,1)S(1)}, u32[]{:S(2)}, u32[]{:S(2)}) %collective-permute-start.21) | collective-permute-done | bytes 819232 | tf_op jit(solution)/shard_map/ppermute | solution.py:459
  129.5 1.4 copy-done.2
  132.4 1.7 collective-permute-start.22
  134.1 2.5 %collective-permute-start.23 = (bf16[112,1024]{1,0:T(8,128)(2,1)S(1)}, bf16[112,1024]{1,0:T(8,128)(2,1)S(1)}, u32[]{:S(2)}, u32[]{:S(2)}) collective-permute-start(bf16[112,1024]{1,0:T(8,128)(2,1)S(1)} %get-tuple-element.106), channel_id=1, source_target_pairs={{0,8},{1,9},{2,10},{3,11},{4,12},{5,13},{6,14},{7,15},{8,0},{9,1},... | collective-permute-start | bytes 688136 | tf_op jit(solution)/shard_map/ppermute | solution.py:459
  137.2 3.7 %collective-permute-done.22.one_ref = bf16[112,1024]{1,0:T(8,128)(2,1)S(1)} collective-permute-done((bf16[112,1024]{1,0:T(8,128)(2,1)S(1)}, bf16[112,1024]{1,0:T(8,128)(2,1)S(1)}, u32[]{:S(2)}, u32[]{:S(2)}) %collective-permute-start.22) | collective-permute-done | bytes 229408 | tf_op jit(solution)/shard_map/ppermute | solution.py:459
  140.9 6.3 %collective-permute-done.23.two_ref = bf16[112,1024]{1,0:T(8,128)(2,1)S(1)} collective-permute-done((bf16[112,1024]{1,0:T(8,128)(2,1)S(1)}, bf16[112,1024]{1,0:T(8,128)(2,1)S(1)}, u32[]{:S(2)}, u32[]{:S(2)}) %collective-permute-start.23) | collective-permute-done | bytes 229408 | tf_op jit(solution)/shard_map/ppermute | solution.py:459
  147.2 2.6 %collective-permute-done.24.three_ref = bf16[112,1024]{1,0:T(8,128)(2,1)S(1)} collective-permute-done((bf16[112,1024]{1,0:T(8,128)(2,1)S(1)}, bf16[112,1024]{1,0:T(8,128)(2,1)S(1)}, u32[]{:S(2)}, u32[]{:S(2)}) %collective-permute-start.24) | collective-permute-done | bytes 229408 | tf_op jit(solution)/shard_map/ppermute | solution.py:459
  150.9 2.4 %collective-permute-start.27 = (f32[32,1024]{1,0:T(8,128)S(1)}, f32[32,1024]{1,0:T(8,128)S(1)}, u32[]{:S(2)}, u32[]{:S(2)}) collective-permute-start(f32[32,1024]{1,0:T(8,128)S(1)} %get-tuple-element.111), channel_id=1, source_target_pairs={{0,18},{1,19},{2,16},{3,17},{4,22},{5,23},{6,20},{7,21},{8,26},{9,... | collective-permute-start | bytes 393224 | tf_op jit(solution)/shard_map/ppermute | solution.py:469
  154.1 3.5 %collective-permute-done.26 = f32[32,1024]{1,0:T(8,128)S(1)} collective-permute-done((f32[32,1024]{1,0:T(8,128)S(1)}, f32[32,1024]{1,0:T(8,128)S(1)}, u32[]{:S(2)}, u32[]{:S(2)}) %collective-permute-start.26) | collective-permute-done | bytes 131104 | tf_op jit(solution)/shard_map/ppermute | solution.py:469
  157.6 1.3 collective-permute-done.27
  159.0 3.4 %collective-permute-start.29 = (f32[32,1024]{1,0:T(8,128)S(1)}, f32[32,1024]{1,0:T(8,128)S(1)}, u32[]{:S(2)}, u32[]{:S(2)}) collective-permute-start(f32[32,1024]{1,0:T(8,128)S(1)} %add_add_fusion.1), channel_id=1, source_target_pairs={{0,64},{1,65},{2,66},{3,67},{4,68},{5,69},{6,70},{7,71},{8,72},{9,... | collective-permute-start | bytes 393224 | tf_op jit(solution)/shard_map/ppermute | solution.py:469
  162.4 1.6 collective-permute-start.28
  164.0 5.3 %collective-permute-done.29 = f32[32,1024]{1,0:T(8,128)S(1)} collective-permute-done((f32[32,1024]{1,0:T(8,128)S(1)}, f32[32,1024]{1,0:T(8,128)S(1)}, u32[]{:S(2)}, u32[]{:S(2)}) %collective-permute-start.29) | collective-permute-done | bytes 131104 | tf_op jit(solution)/shard_map/ppermute | solution.py:469
  169.3 2.7 %collective-permute-done.30 = f32[32,1024]{1,0:T(8,128)S(1)} collective-permute-done((f32[32,1024]{1,0:T(8,128)S(1)}, f32[32,1024]{1,0:T(8,128)S(1)}, u32[]{:S(2)}, u32[]{:S(2)}) %collective-permute-start.30) | collective-permute-done | bytes 131104 | tf_op jit(solution)/shard_map/ppermute | solution.py:469
  172.1 5.9 %collective-permute-start.31 = (f32[32,1024]{1,0:T(8,128)S(1)}, f32[32,1024]{1,0:T(8,128)S(1)}, u32[]{:S(2)}, u32[]{:S(2)}) collective-permute-start(f32[32,1024]{1,0:T(8,128)S(1)} %add_add_fusion), channel_id=1, source_target_pairs={{0,128},{1,129},{2,130},{3,131},{4,132},{5,133},{6,134},{7,135},{8... | collective-permute-start | bytes 393224 | tf_op jit(solution)/shard_map/ppermute | solution.py:469
  177.9 6.4 %collective-permute-done.31 = f32[32,1024]{1,0:T(8,128)S(1)} collective-permute-done((f32[32,1024]{1,0:T(8,128)S(1)}, f32[32,1024]{1,0:T(8,128)S(1)}, u32[]{:S(2)}, u32[]{:S(2)}) %collective-permute-start.31) | collective-permute-done | bytes 131104 | tf_op jit(solution)/shard_map/ppermute | solution.py:469
  186.7 2.5 %collective-permute-done.32 = f32[24,1024]{1,0:T(8,128)} collective-permute-done((f32[24,1024]{1,0:T(8,128)S(1)}, f32[24,1024]{1,0:T(8,128)}, u32[]{:S(2)}, u32[]{:S(2)}) %collective-permute-start.32) | collective-permute-done | bytes 98336 | tf_op jit(solution)/shard_map/ppermute | solution.py:469
  190.1 1.8 shard_map.120
  (97 shorter events, 20.4 us)
Async XLA Ops:
  7.2 3.2 %copy-start = (bf16[48,1536]{1,0:T(8,128)(2,1)S(1)}, bf16[48,1536]{1,0:T(8,128)(2,1)}, u32[]{:S(2)}) copy-start(bf16[48,1536]{1,0:T(8,128)(2,1)} %param.14) | copy-start | bytes 442372
  7.2 6.4 %copy-start.11 = (bf16[256,1536]{1,0:T(8,128)(2,1)S(1)}, bf16[256,1536]{1,0:T(8,128)(2,1)}, u32[]{:S(2)}) copy-start(bf16[256,1536]{1,0:T(8,128)(2,1)} %param.11) | copy-start | bytes 2359300
  7.2 63.0 %all-gather.2.cloned.1.call-start = ((), (), s32[]{:S(2)}) async-start(), calls=%async_computation | async-start | bytes 1671168 | tf_op jit(solution)/shard_map/all_gather | solution.py:478
  7.2 28.9 %collective-permute-start.4 = (bf16[64,4096]{1,0:T(8,128)(2,1)}, bf16[64,4096]{1,0:T(8,128)(2,1)S(1)}, u32[]{:S(2)}, u32[]{:S(2)}) collective-permute-start(bf16[64,4096]{1,0:T(8,128)(2,1)} %bitcast.31), channel_id=1, source_target_pairs={{0,2},{1,3},{2,0},{3,1},{4,6},{5,7},{6,4},{7,5},{8,10},{9,11},{10,... | collective-permute-start | bytes 1572872 | tf_op jit(solution)/shard_map/ppermute | solution.py:459
  13.5 6.7 %copy-start.18 = (s32[16]{0:T(128)S(1)}, s32[16]{0:T(128)}, u32[]{:S(2)}) copy-start(s32[16]{0:T(128)} %param.18) | copy-start | bytes 196
  13.5 6.7 %copy-start.19 = (s32[16]{0:T(128)S(1)}, s32[16]{0:T(128)}, u32[]{:S(2)}) copy-start(s32[16]{0:T(128)} %param.19) | copy-start | bytes 196
  13.5 25.9 %copy-start.6 = (bf16[1,64,4096]{2,1,0:T(8,128)(2,1)S(1)}, bf16[1,64,4096]{2,1,0:T(8,128)(2,1)}, u32[]{:S(2)}) copy-start(bf16[1,64,4096]{2,1,0:T(8,128)(2,1)} %param.10) | copy-start | bytes 1572868
  13.8 39.2 %copy-start.8 = (bf16[256,768]{1,0:T(8,128)(2,1)}, bf16[256,768]{1,0:T(8,128)(2,1)S(1)}, u32[]{:S(2)}) copy-start(bf16[256,768]{1,0:T(8,128)(2,1)S(1)} %pad_maximum_fusion.9.refs_3_) | copy-start | bytes 1179652
  13.8 12.2 %collective-permute-start = (bf16[256,768]{1,0:T(8,128)(2,1)S(1)}, bf16[256,768]{1,0:T(8,128)(2,1)S(1)}, u32[]{:S(2)}, u32[]{:S(2)}) collective-permute-start(bf16[256,768]{1,0:T(8,128)(2,1)S(1)} %pad_maximum_fusion.9.refs_3_), channel_id=1, source_target_pairs={{0,4},{1,5},{2,6},{3,7},{4,8},{5,9},{6,10},{7,11},{8,12},{9,13},{1... | collective-permute-start | bytes 1179656 | tf_op jit(solution)/shard_map/ppermute | solution.py:462
  15.5 13.8 %collective-permute-start.1 = (bf16[256,768]{1,0:T(8,128)(2,1)S(1)}, bf16[256,768]{1,0:T(8,128)(2,1)S(1)}, u32[]{:S(2)}, u32[]{:S(2)}) collective-permute-start(bf16[256,768]{1,0:T(8,128)(2,1)S(1)} %pad_maximum_fusion.9.refs_3_), channel_id=1, source_target_pairs={{0,12},{1,13},{2,14},{3,15},{4,0},{5,1},{6,2},{7,3},{8,4},{9,5},{1... | collective-permute-start | bytes 1179656 | tf_op jit(solution)/shard_map/ppermute | solution.py:462
  17.2 18.9 %collective-permute-start.2 = (bf16[256,768]{1,0:T(8,128)(2,1)S(1)}, bf16[256,768]{1,0:T(8,128)(2,1)S(1)}, u32[]{:S(2)}, u32[]{:S(2)}) collective-permute-start(bf16[256,768]{1,0:T(8,128)(2,1)S(1)} %pad_maximum_fusion.9.refs_3_), channel_id=1, source_target_pairs={{0,8},{1,9},{2,10},{3,11},{4,12},{5,13},{6,14},{7,15},{8,0},{9,1},... | collective-permute-start | bytes 1179656 | tf_op jit(solution)/shard_map/ppermute | solution.py:462
  19.1 17.0 %collective-permute-start.3 = (bf16[256,768]{1,0:T(8,128)(2,1)S(1)}, bf16[256,768]{1,0:T(8,128)(2,1)}, u32[]{:S(2)}, u32[]{:S(2)}) collective-permute-start(bf16[256,768]{1,0:T(8,128)(2,1)S(1)} %pad_maximum_fusion.8), channel_id=1, source_target_pairs={{0,18},{1,19},{2,16},{3,17},{4,22},{5,23},{6,20},{7,21},{8,26},{9,... | collective-permute-start | bytes 1179656 | tf_op jit(solution)/shard_map/ppermute | solution.py:469
  26.0 27.0 %copy-start.12 = (bf16[256,768]{1,0:T(8,128)(2,1)}, bf16[256,768]{1,0:T(8,128)(2,1)S(1)}, u32[]{:S(2)}) copy-start(bf16[256,768]{1,0:T(8,128)(2,1)S(1)} %collective-permute-done.refs_5_) | copy-start | bytes 1179652
  29.3 10.2 %copy-start.13 = (bf16[256,768]{1,0:T(8,128)(2,1)}, bf16[256,768]{1,0:T(8,128)(2,1)S(1)}, u32[]{:S(2)}) copy-start(bf16[256,768]{1,0:T(8,128)(2,1)S(1)} %collective-permute-done.1.refs_7_) | copy-start | bytes 1179652
  36.1 3.3 %copy-start.14 = (bf16[256,768]{1,0:T(8,128)(2,1)}, bf16[256,768]{1,0:T(8,128)(2,1)S(1)}, u32[]{:S(2)}) copy-start(bf16[256,768]{1,0:T(8,128)(2,1)S(1)} %collective-permute-done.2.refs_9_) | copy-start | bytes 1179652
  36.1 17.0 %copy-start.7 = (bf16[64,4096]{1,0:T(8,128)(2,1)}, bf16[64,4096]{1,0:T(8,128)(2,1)S(1)}, u32[]{:S(2)}) copy-start(bf16[64,4096]{1,0:T(8,128)(2,1)S(1)} %collective-permute-done.4.refs_1_) | copy-start | bytes 1572868
  36.1 17.0 %collective-permute-start.5 = (bf16[256,768]{1,0:T(8,128)(2,1)}, bf16[256,768]{1,0:T(8,128)(2,1)S(1)}, u32[]{:S(2)}, u32[]{:S(2)}) collective-permute-start(bf16[256,768]{1,0:T(8,128)(2,1)} %collective-permute-done.3.refs_4_), channel_id=1, source_target_pairs={{0,4},{1,5},{2,6},{3,7},{4,8},{5,9},{6,10},{7,11},{8,12},{9,13},{1... | collective-permute-start | bytes 1179656 | tf_op jit(solution)/shard_map/ppermute | solution.py:462
  37.3 18.8 %collective-permute-start.6 = (bf16[256,768]{1,0:T(8,128)(2,1)}, bf16[256,768]{1,0:T(8,128)(2,1)S(1)}, u32[]{:S(2)}, u32[]{:S(2)}) collective-permute-start(bf16[256,768]{1,0:T(8,128)(2,1)} %collective-permute-done.3.refs_4_), channel_id=1, source_target_pairs={{0,12},{1,13},{2,14},{3,15},{4,0},{5,1},{6,2},{7,3},{8,4},{9,5},{1... | collective-permute-start | bytes 1179656 | tf_op jit(solution)/shard_map/ppermute | solution.py:462
  39.4 19.1 %collective-permute-start.7 = (bf16[256,768]{1,0:T(8,128)(2,1)}, bf16[256,768]{1,0:T(8,128)(2,1)S(1)}, u32[]{:S(2)}, u32[]{:S(2)}) collective-permute-start(bf16[256,768]{1,0:T(8,128)(2,1)} %collective-permute-done.3.refs_4_), channel_id=1, source_target_pairs={{0,8},{1,9},{2,10},{3,11},{4,12},{5,13},{6,14},{7,15},{8,0},{9,1},... | collective-permute-start | bytes 1179656 | tf_op jit(solution)/shard_map/ppermute | solution.py:462
  39.6 19.0 %collective-permute-start.8 = (bf16[128,4096]{1,0:T(8,128)(2,1)S(1)}, bf16[128,4096]{1,0:T(8,128)(2,1)S(1)}, u32[]{:S(2)}, u32[]{:S(2)}) collective-permute-start(bf16[128,4096]{1,0:T(8,128)(2,1)S(1)} %pad_maximum_fusion), channel_id=1, source_target_pairs={{0,1},{1,0},{2,3},{3,2},{4,5},{5,4},{6,7},{7,6},{8,9},{9,8},{10,11... | collective-permute-start | bytes 3145736 | tf_op jit(solution)/shard_map/ppermute | solution.py:459
  41.6 11.5 %collective-permute-start.9 = (bf16[40,2304]{1,0:T(8,128)(2,1)S(1)}, bf16[40,2304]{1,0:T(8,128)(2,1)}, u32[]{:S(2)}, u32[]{:S(2)}) collective-permute-start(bf16[40,2304]{1,0:T(8,128)(2,1)S(1)} %pad_maximum_fusion.11), channel_id=1, source_target_pairs={{0,1},{1,2},{2,3},{3,4},{4,5},{5,6},{6,7},{7,8},{8,9},{9,10},{10,1... | collective-permute-start | bytes 552968 | tf_op jit(solution)/shard_map/ppermute | solution.py:506
  53.1 5.5 %copy-start.15 = (bf16[256,768]{1,0:T(8,128)(2,1)}, bf16[256,768]{1,0:T(8,128)(2,1)S(1)}, u32[]{:S(2)}) copy-start(bf16[256,768]{1,0:T(8,128)(2,1)S(1)} %collective-permute-done.5.refs_6_) | copy-start | bytes 1179652
  66.3 2.0 %collective-permute-start.10 = (f32[4,64,384]{2,1,0:T(8,128)}, f32[4,64,384]{2,1,0:T(8,128)S(1)}, u32[]{:S(2)}, u32[]{:S(2)}) collective-permute-start(f32[4,64,384]{2,1,0:T(8,128)} %get-tuple-element.82), channel_id=1, source_target_pairs={{0,1},{1,0},{2,3},{3,2},{4,5},{5,4},{6,7},{7,6},{8,9},{9,8},{10,11... | collective-permute-start | bytes 1179656 | tf_op jit(solution)/shard_map/ppermute | solution.py:459
  68.3 13.6 %copy-start.1 = (bf16[1536,1024]{1,0:T(8,128)(2,1)S(1)}, bf16[1536,1024]{1,0:T(8,128)(2,1)}, u32[]{:S(2)}) copy-start(bf16[1536,1024]{1,0:T(8,128)(2,1)} %disc_ref.1) | copy-start | bytes 9437188
  70.2 7.0 %collective-permute-start.14 = (bf16[40,2304]{1,0:T(8,128)(2,1)S(1)}, bf16[40,2304]{1,0:T(8,128)(2,1)}, u32[]{:S(2)}, u32[]{:S(2)}) collective-permute-start(bf16[40,2304]{1,0:T(8,128)(2,1)S(1)} %pad_maximum_fusion.12), channel_id=1, source_target_pairs={{1,0},{2,1},{3,2},{4,3},{5,4},{6,5},{7,6},{8,7},{9,8},{10,9},{11,1... | collective-permute-start | bytes 552968 | tf_op jit(solution)/shard_map/ppermute | solution.py:535
  71.5 10.3 %copy-start.9 = (bf16[1,256,1536]{2,1,0:T(8,128)(2,1)S(1)}, bf16[1,256,1536]{2,1,0:T(8,128)(2,1)}, u32[]{:S(2)}) copy-start(bf16[1,256,1536]{2,1,0:T(8,128)(2,1)} %param.13) | copy-start | bytes 2359300
  71.5 13.7 %collective-permute-start.11 = (f32[256,384]{1,0:T(8,128)}, f32[256,384]{1,0:T(8,128)S(1)}, u32[]{:S(2)}, u32[]{:S(2)}) collective-permute-start(f32[256,384]{1,0:T(8,128)} %bitcast.25), channel_id=1, source_target_pairs={{0,4},{1,5},{2,6},{3,7},{4,8},{5,9},{6,10},{7,11},{8,12},{9,13},{1... | collective-permute-start | bytes 1179656 | tf_op jit(solution)/shard_map/ppermute | solution.py:462
  73.3 20.1 %collective-permute-start.12 = (f32[256,384]{1,0:T(8,128)}, f32[256,384]{1,0:T(8,128)S(1)}, u32[]{:S(2)}, u32[]{:S(2)}) collective-permute-start(f32[256,384]{1,0:T(8,128)} %bitcast.26), channel_id=1, source_target_pairs={{0,8},{1,9},{2,10},{3,11},{4,12},{5,13},{6,14},{7,15},{8,0},{9,1},... | collective-permute-start | bytes 1179656 | tf_op jit(solution)/shard_map/ppermute | solution.py:462
  75.3 18.9 %collective-permute-start.13 = (f32[256,384]{1,0:T(8,128)}, f32[256,384]{1,0:T(8,128)S(1)}, u32[]{:S(2)}, u32[]{:S(2)}) collective-permute-start(f32[256,384]{1,0:T(8,128)} %bitcast.27), channel_id=1, source_target_pairs={{0,12},{1,13},{2,14},{3,15},{4,0},{5,1},{6,2},{7,3},{8,4},{9,5},{1... | collective-permute-start | bytes 1179656 | tf_op jit(solution)/shard_map/ppermute | solution.py:462
  78.4 15.8 %copy-start.3 = (f32[4,64,384]{2,1,0:T(8,128)S(1)}, f32[4,64,384]{2,1,0:T(8,128)}, u32[]{:S(2)}) copy-start(f32[4,64,384]{2,1,0:T(8,128)} %add.166) | copy-start | bytes 1179652
  78.4 15.8 %collective-permute-start.15 = (bf16[336,384]{1,0:T(8,128)(2,1)S(1)}, bf16[336,384]{1,0:T(8,128)(2,1)S(1)}, u32[]{:S(2)}, u32[]{:S(2)}) collective-permute-start(bf16[336,384]{1,0:T(8,128)(2,1)S(1)} %get-tuple-element.120), channel_id=1, source_target_pairs={{0,2},{1,3},{2,0},{3,1},{4,6},{5,7},{6,4},{7,5},{8,10},{9,11},{10,... | collective-permute-start | bytes 774152 | tf_op jit(solution)/shard_map/ppermute | solution.py:459
  94.2 1.7 collective-permute-start.16
  94.2 2.3 %collective-permute-start.17 = (f32[256,384]{1,0:T(8,128)S(1)}, f32[256,384]{1,0:T(8,128)S(1)}, u32[]{:S(2)}, u32[]{:S(2)}) collective-permute-start(f32[256,384]{1,0:T(8,128)S(1)} %collective-permute-done.11.refs_1_), channel_id=1, source_target_pairs={{0,1},{1,0},{2,3},{3,2},{4,5},{5,4},{6,7},{7,6},{8,9},{9,8},{10,11... | collective-permute-start | bytes 1179656 | tf_op jit(solution)/shard_map/ppermute | solution.py:459
  94.7 2.3 %collective-permute-start.18 = (f32[256,384]{1,0:T(8,128)S(1)}, f32[256,384]{1,0:T(8,128)S(1)}, u32[]{:S(2)}, u32[]{:S(2)}) collective-permute-start(f32[256,384]{1,0:T(8,128)S(1)} %collective-permute-done.12.refs_2_), channel_id=1, source_target_pairs={{0,1},{1,0},{2,3},{3,2},{4,5},{5,4},{6,7},{7,6},{8,9},{9,8},{10,11... | collective-permute-start | bytes 1179656 | tf_op jit(solution)/shard_map/ppermute | solution.py:459
  94.8 2.8 %collective-permute-start.19 = (f32[256,384]{1,0:T(8,128)S(1)}, f32[256,384]{1,0:T(8,128)S(1)}, u32[]{:S(2)}, u32[]{:S(2)}) collective-permute-start(f32[256,384]{1,0:T(8,128)S(1)} %collective-permute-done.13.refs_3_), channel_id=1, source_target_pairs={{0,1},{1,0},{2,3},{3,2},{4,5},{5,4},{6,7},{7,6},{8,9},{9,8},{10,11... | collective-permute-start | bytes 1179656 | tf_op jit(solution)/shard_map/ppermute | solution.py:459
  103.3 9.9 %collective-permute-start.20 = (bf16[336,384]{1,0:T(8,128)(2,1)S(1)}, bf16[336,384]{1,0:T(8,128)(2,1)S(1)}, u32[]{:S(2)}, u32[]{:S(2)}) collective-permute-start(bf16[336,384]{1,0:T(8,128)(2,1)S(1)} %shard_map.116), channel_id=1, source_target_pairs={{0,2},{1,3},{2,0},{3,1},{4,6},{5,7},{6,4},{7,5},{8,10},{9,11},{10,... | collective-permute-start | bytes 774152 | tf_op jit(solution)/shard_map/ppermute | solution.py:459
  126.9 2.6 %collective-permute-start.21 = (bf16[400,1024]{1,0:T(8,128)(2,1)}, bf16[400,1024]{1,0:T(8,128)(2,1)S(1)}, u32[]{:S(2)}, u32[]{:S(2)}) collective-permute-start(bf16[400,1024]{1,0:T(8,128)(2,1)} %get-tuple-element.102), channel_id=1, source_target_pairs={{0,1},{1,0},{2,3},{3,2},{4,5},{5,4},{6,7},{7,6},{8,9},{9,8},{10,11... | collective-permute-start | bytes 2457608 | tf_op jit(solution)/shard_map/ppermute | solution.py:459
  132.4 8.5 %collective-permute-start.22 = (bf16[112,1024]{1,0:T(8,128)(2,1)S(1)}, bf16[112,1024]{1,0:T(8,128)(2,1)S(1)}, u32[]{:S(2)}, u32[]{:S(2)}) collective-permute-start(bf16[112,1024]{1,0:T(8,128)(2,1)S(1)} %get-tuple-element.105), channel_id=1, source_target_pairs={{0,4},{1,5},{2,6},{3,7},{4,0},{5,1},{6,2},{7,3},{8,12},{9,13},{10,... | collective-permute-start | bytes 688136 | tf_op jit(solution)/shard_map/ppermute | solution.py:459
  134.1 13.1 %collective-permute-start.23 = (bf16[112,1024]{1,0:T(8,128)(2,1)S(1)}, bf16[112,1024]{1,0:T(8,128)(2,1)S(1)}, u32[]{:S(2)}, u32[]{:S(2)}) collective-permute-start(bf16[112,1024]{1,0:T(8,128)(2,1)S(1)} %get-tuple-element.106), channel_id=1, source_target_pairs={{0,8},{1,9},{2,10},{3,11},{4,12},{5,13},{6,14},{7,15},{8,0},{9,1},... | collective-permute-start | bytes 688136 | tf_op jit(solution)/shard_map/ppermute | solution.py:459
  136.6 13.2 %collective-permute-start.24 = (bf16[112,1024]{1,0:T(8,128)(2,1)S(1)}, bf16[112,1024]{1,0:T(8,128)(2,1)S(1)}, u32[]{:S(2)}, u32[]{:S(2)}) collective-permute-start(bf16[112,1024]{1,0:T(8,128)(2,1)S(1)} %get-tuple-element.107), channel_id=1, source_target_pairs={{0,12},{1,13},{2,14},{3,15},{4,8},{5,9},{6,10},{7,11},{8,4},{9,5},... | collective-permute-start | bytes 688136 | tf_op jit(solution)/shard_map/ppermute | solution.py:459
  150.5 7.1 %collective-permute-start.26 = (f32[32,1024]{1,0:T(8,128)S(1)}, f32[32,1024]{1,0:T(8,128)S(1)}, u32[]{:S(2)}, u32[]{:S(2)}) collective-permute-start(f32[32,1024]{1,0:T(8,128)S(1)} %get-tuple-element.110), channel_id=1, source_target_pairs={{0,2},{1,3},{2,0},{3,1},{4,6},{5,7},{6,4},{7,5},{8,10},{9,11},{10,... | collective-permute-start | bytes 393224 | tf_op jit(solution)/shard_map/ppermute | solution.py:469
  150.9 8.1 %collective-permute-start.27 = (f32[32,1024]{1,0:T(8,128)S(1)}, f32[32,1024]{1,0:T(8,128)S(1)}, u32[]{:S(2)}, u32[]{:S(2)}) collective-permute-start(f32[32,1024]{1,0:T(8,128)S(1)} %get-tuple-element.111), channel_id=1, source_target_pairs={{0,18},{1,19},{2,16},{3,17},{4,22},{5,23},{6,20},{7,21},{8,26},{9,... | collective-permute-start | bytes 393224 | tf_op jit(solution)/shard_map/ppermute | solution.py:469
  153.3 5.7 %collective-permute-start.25 = (f32[32,1024]{1,0:T(8,128)S(1)}, f32[32,1024]{1,0:T(8,128)S(1)}, u32[]{:S(2)}, u32[]{:S(2)}) collective-permute-start(f32[32,1024]{1,0:T(8,128)S(1)} %get-tuple-element.109), channel_id=1, source_target_pairs={{0,16},{1,17},{2,18},{3,19},{4,20},{5,21},{6,22},{7,23},{8,24},{9,... | collective-permute-start | bytes 393224 | tf_op jit(solution)/shard_map/ppermute | solution.py:469
  159.0 10.3 %collective-permute-start.29 = (f32[32,1024]{1,0:T(8,128)S(1)}, f32[32,1024]{1,0:T(8,128)S(1)}, u32[]{:S(2)}, u32[]{:S(2)}) collective-permute-start(f32[32,1024]{1,0:T(8,128)S(1)} %add_add_fusion.1), channel_id=1, source_target_pairs={{0,64},{1,65},{2,66},{3,67},{4,68},{5,69},{6,70},{7,71},{8,72},{9,... | collective-permute-start | bytes 393224 | tf_op jit(solution)/shard_map/ppermute | solution.py:469
  162.4 9.6 %collective-permute-start.30 = (f32[32,1024]{1,0:T(8,128)S(1)}, f32[32,1024]{1,0:T(8,128)S(1)}, u32[]{:S(2)}, u32[]{:S(2)}) collective-permute-start(f32[32,1024]{1,0:T(8,128)S(1)} %add_add_fusion.1), channel_id=1, source_target_pairs={{0,96},{1,97},{2,98},{3,99},{4,100},{5,101},{6,102},{7,103},{8,104... | collective-permute-start | bytes 393224 | tf_op jit(solution)/shard_map/ppermute | solution.py:469
  162.4 9.6 %collective-permute-start.28 = (f32[32,1024]{1,0:T(8,128)S(1)}, f32[32,1024]{1,0:T(8,128)S(1)}, u32[]{:S(2)}, u32[]{:S(2)}) collective-permute-start(f32[32,1024]{1,0:T(8,128)S(1)} %add_add_fusion.1), channel_id=1, source_target_pairs={{0,32},{1,33},{2,34},{3,35},{4,36},{5,37},{6,38},{7,39},{8,40},{9,... | collective-permute-start | bytes 393224 | tf_op jit(solution)/shard_map/ppermute | solution.py:469
  172.1 12.2 %collective-permute-start.31 = (f32[32,1024]{1,0:T(8,128)S(1)}, f32[32,1024]{1,0:T(8,128)S(1)}, u32[]{:S(2)}, u32[]{:S(2)}) collective-permute-start(f32[32,1024]{1,0:T(8,128)S(1)} %add_add_fusion), channel_id=1, source_target_pairs={{0,128},{1,129},{2,130},{3,131},{4,132},{5,133},{6,134},{7,135},{8... | collective-permute-start | bytes 393224 | tf_op jit(solution)/shard_map/ppermute | solution.py:469
  184.3 4.8 %collective-permute-start.32 = (f32[24,1024]{1,0:T(8,128)S(1)}, f32[24,1024]{1,0:T(8,128)}, u32[]{:S(2)}, u32[]{:S(2)}) collective-permute-start(f32[24,1024]{1,0:T(8,128)S(1)} %slice.32), channel_id=1, source_target_pairs={{0,16},{1,17},{2,18},{3,19},{4,20},{5,21},{6,22},{7,23},{8,24},{9,... | collective-permute-start | bytes 294920 | tf_op jit(solution)/shard_map/ppermute | solution.py:469
  (7 other events, 7.8 us)
Sparse Core Ops, SparseCore 0:
  13.7 55.7 all-gather.1

commit v6 on v5

--- a/solution.py
+++ b/solution.py
@@ -78,8 +78,8 @@
 
 
 def project_kernel(cols_ref, *refs):
-    states, weights, (keep_ref, send_ref) = (refs[:3], refs[3:11], refs[11:13])
-    state_s, weight_s, total_s, state_sem, weight_sem = refs[13:]
+    states, weights, (keep_ref, send_ref) = (refs[:3], refs[3:13], refs[13:15])
+    state_s, weight_s, total_s, state_sem, weight_sem = refs[15:]
     core = cols_ref[8]
     state_copies = [
         pltpu.make_async_copy(s, state_s.at[place], state_sem.at[i])
@@ -88,14 +88,23 @@
         )
     ]
     weight_copies = [
-        pltpu.make_async_copy(w, weight_s.at[i], weight_sem.at[i]) for i, w in enumerate(weights)
+        pltpu.make_async_copy(w, weight_s.at[i], weight_sem.at[i]) for i, w in enumerate(weights[:6])
     ]
+    half_rows = weights[6].shape[0]
+    for i in (6, 7):
+        for side in range(2):
+            source = 2 * i - 6 + side
+            rows = pl.ds(half_rows * side, half_rows)
+            weight_copies.append(
+                pltpu.make_async_copy(weights[source], weight_s.at[i, rows], weight_sem.at[source])
+            )
     for copy in state_copies + weight_copies:
         copy.start()
     for copy in state_copies:
         copy.wait()
-    for i, copy in enumerate(weight_copies):
-        copy.wait()
+    for i in range(8):
+        for copy in weight_copies[i : i + 1] if i < 6 else weight_copies[2 * i - 6 : 2 * i - 4]:
+            copy.wait()
         start = pl.multiple_of(cols_ref[i], 256)
         left = jnp.concatenate([state_s[j, :, pl.ds(start, 256)] for j in range(4)], axis=0)
         part = jnp.dot(left, weight_s[i], preferred_element_type=F32)
@@ -117,7 +126,7 @@
     out = jax.ShapeDtypeStruct((4, 64, HALF_ATT), F32)
     return pl.pallas_call(
         project_kernel,
-        in_specs=[smem()] + [anywhere()] * 11,
+        in_specs=[smem()] + [anywhere()] * 13,
         out_specs=[vmem(), vmem()],
         out_shape=[out, out],
         scratch_shapes=[
@@ -125,7 +134,7 @@
             pltpu.VMEM((8,) + weights[0].shape, BF16),
             pltpu.VMEM((256, width), F32),
             pltpu.SemaphoreType.DMA((4,)),
-            pltpu.SemaphoreType.DMA((8,)),
+            pltpu.SemaphoreType.DMA((10,)),
         ],
         compiler_params=params(58),
         cost_estimate=pl.CostEstimate(flops=800_000_000, bytes_accessed=6_000_000, transcendentals=0),
@@ -318,7 +327,7 @@
     for copy in conv_copies:
         copy.wait()
 
-    @pl.loop(0, tiles, unroll=2)
+    @pl.loop(0, tiles, unroll=4)
     def _(tile):
         lanes = pl.ds(pl.multiple_of(tile * 128, 128), 128)
         phase = [feed_s[tile, pl.ds(b, rows, stride=STRIDE), :] for b in range(STRIDE)]
@@ -362,7 +371,7 @@
     contract = (((1,), (1,)), ((), ()))
     low_back = low_lanes((own_out, 128))
 
-    @pl.loop(0, tiles, unroll=2)
+    @pl.loop(0, tiles, unroll=4)
     def _(tile):
         lanes = pl.ds(pl.multiple_of(tile * 128, 128), 128)
         turned_s[...] = roll_half(grad_s[:, lanes])
@@ -488,8 +497,12 @@
     far, kv_weight = lax.optimization_barrier((far, kv_weight))
     near = head_cols(half, kv_weight)
     far = swap(far, 1, 2)
-    hops = (1, 3, 2)
-    near_turned = [turn(near, j) for j in hops]
+    near_turned = [turn(near, j) for j in (1, 3)]
+
+    def pass_on(turned):
+        rows = near.shape[0] // 2
+        return [turn(turned[0][:rows], 1), turn(turned[1][rows:], 3)]
+
     states_in = states[0]
     near, near_turned, far, state_far, queries_in, hidden_in, conv_in = lax.optimization_barrier(
         (near, near_turned, far, flip(states_in, 2), queries[0], hidden[0], conv_weight)
@@ -497,11 +510,16 @@
 
     lower = clip % 2
     channels = disc_in.shape[1]
-    near_blocks = [near] + near_turned
-    far_blocks = [far] + [turn(far, j) for j in hops]
+    near_over = pass_on(near_turned)
+    far_turned = [turn(far, j) for j in (1, 3)]
     state_pair = flip(jnp.concatenate([states_in, state_far], axis=0), 1)
     up = [(i, i + 1) for i in range(seq_size - 1)]
     down = [(i + 1, i) for i in range(seq_size - 1)]
+    near_over, far_turned, state_pair, queries_in, hidden_in = lax.optimization_barrier(
+        (near_over, far_turned, state_pair, queries_in, hidden_in)
+    )
+
+    far_over = pass_on(far_turned)
     before = jnp.concatenate([queries_in[frames - HALO :], hidden_in[frames - HALO :]], axis=1)
     before = lax.ppermute(before, "seq", up)
     after = jnp.concatenate([queries_in[:HALO], hidden_in[:HALO]], axis=1)
@@ -516,7 +534,7 @@
     meta = jnp.stack([clip_states, core, half, row]).astype(jnp.int32)
     meta2 = jnp.stack([clip_frames, seq * frames, half, jnp.int32(total_frames), core])
     meta3 = jnp.stack([row, 2 * half + lower, clip // 2]).astype(jnp.int32)
-    blocks = [b for pair in zip(near_blocks, far_blocks) for b in pair]
+    blocks = [near, far, near_turned[0], far_turned[0], near_turned[1], far_turned[1]] + near_over + far_over
     tables = (cols, meta, meta2.astype(jnp.int32), meta3)
     conv = arrange(conv_in)
     blocks, state_pair, tables, before, after, conv = lax.optimization_barrier(

time: 201 us -> 207 us (1.030)
  starting transfers between devices: 49.3 us -> 65 us
  waiting for transfers between devices: 69.8 us -> 61.4 us
    ppermute x9 -> x11, waiting for transfers between devices: 26.9 us -> 17.3 us  [turn(): lax.ppermute(x, 'seq', [(i, (i + 4 * hops) % seq_size) for i in range(seq...]
    ppermute x9 -> x11, starting transfers between devices: 14.3 us -> 22.4 us  [turn(): lax.ppermute(x, 'seq', [(i, (i + 4 * hops) % seq_size) for i in range(seq...]
    ppermute x13, starting transfers between devices: 14.5 us -> 21.1 us  [flip(): return lax.ppermute(x, 'seq', [(i, i ^ bit) for i in range(seq_size)])]
    ppermute x9, waiting for transfers between devices: 21.8 us -> 25.8 us  [swap(): return lax.ppermute(x, ('dp', 'seq'), pairs)]
    ppermute x13, waiting for transfers between devices: 21.1 us -> 17.3 us  [flip(): return lax.ppermute(x, 'seq', [(i, i ^ bit) for i in range(seq_size)])]
    ppermute x9, starting transfers between devices: 16.1 us -> 18.9 us  [swap(): return lax.ppermute(x, ('dp', 'seq'), pairs)]
    unnamed x42 -> x46, local copies, waits for them, and re-layouts: 5.43 us -> 4.39 us
  transfers between devices with their start and end apart: 34 -> 36, of which waited for: 23 -> 22; matrix products, arithmetic and copies ran while one was open for 8% -> 8% of each run, Pallas kernels for 10% -> 10%
where the time goes in v6:
time: 207 us; the launch traced here: 206 us
  starting transfers between devices  65 us (31%)
  waiting for transfers between devices  61.4 us (30%)
  Pallas kernels  41.1 us (20%)
  between operations  16.9 us (8%)
  local copies, waits for them, and re-layouts  9.83 us (5%)
  matrix products  6.45 us (3%)
  other arithmetic  5.84 us (3%)
    ppermute x9, waiting for transfers between devices, swap(): return lax.ppermute(x, ('dp', 'seq'), pairs)  25.8 us
    ppermute x11, starting transfers between devices, turn(): lax.ppermute(x, 'seq', [(i, (i + 4 * hops) % seq_size) for i in range(seq...  22.4 us
    ppermute x13, starting transfers between devices, flip(): return lax.ppermute(x, 'seq', [(i, i ^ bit) for i in range(seq_size)])  21.1 us
    ppermute x9, starting transfers between devices, swap(): return lax.ppermute(x, ('dp', 'seq'), pairs)  18.9 us
    ppermute x11, waiting for transfers between devices, turn(): lax.ppermute(x, 'seq', [(i, (i + 4 * hops) % seq_size) for i in range(seq...  17.3 us
    ppermute x13, waiting for transfers between devices, flip(): return lax.ppermute(x, 'seq', [(i, i ^ bit) for i in range(seq_size)])  17.3 us
    pallas_call x1, Pallas kernels, critic(): pl.pallas_call(critic_kernel, in_specs=[smem()] + [anywhere()] * 5 + [vme...  12.2 us
    pallas_call x2, Pallas kernels, attend(): pl.pallas_call(attend_kernel, grid=(width // HEAD_DIM,), in_specs=[smem()...  11.3 us
  transfers between devices with their start and end apart: 36, of which 22 were waited for; matrix products, arithmetic and copies ran while one was open for 8% of the time, Pallas kernels for 10%

profile of v6, /device:TPU:32, one launch (start us, length us, event | category | flops | bytes accessed | tf_op | source)
XLA Modules:
  0.0 206.4 jit_solution(6491794894097745798)
XLA Ops:
  7.2 3.1 %collective-permute-start.3 = (bf16[64,4096]{1,0:T(8,128)(2,1)}, bf16[64,4096]{1,0:T(8,128)(2,1)S(1)}, u32[]{:S(2)}, u32[]{:S(2)}) collective-permute-start(bf16[64,4096]{1,0:T(8,128)(2,1)} %bitcast.31), channel_id=1, source_target_pairs={{0,2},{1,3},{2,0},{3,1},{4,6},{5,7},{6,4},{7,5},{8,10},{9,11},{10,... | collective-permute-start | bytes 1572872 | tf_op jit(solution)/shard_map/ppermute | solution.py:468
  10.3 3.2 %convolution_convert_fusion = bf16[48,1024]{1,0:T(8,128)(2,1)} fusion(bf16[48,1536]{1,0:T(8,128)(2,1)S(1)} %copy-done, bf16[1536,1024]{1,0:T(8,128)(2,1)} %disc_ref.1), kind=kOutput, calls=%fused_computation | convolution fusion | flops 151044096 | bytes 3391488 | tf_op jit(solution)/shard_map/dot_general | solution.py:485
  13.8 1.7 collective-permute-start
  15.4 1.7 collective-permute-start.1
  18.2 7.4 %collective-permute-done.refs_5_ = bf16[256,768]{1,0:T(8,128)(2,1)S(1)} collective-permute-done((bf16[256,768]{1,0:T(8,128)(2,1)S(1)}, bf16[256,768]{1,0:T(8,128)(2,1)S(1)}, u32[]{:S(2)}, u32[]{:S(2)}) %collective-permute-start) | collective-permute-done | bytes 393248 | tf_op jit(solution)/shard_map/ppermute | solution.py:471
  25.7 5.5 %collective-permute-done.2.refs_4_ = bf16[256,768]{1,0:T(8,128)(2,1)} collective-permute-done((bf16[256,768]{1,0:T(8,128)(2,1)S(1)}, bf16[256,768]{1,0:T(8,128)(2,1)}, u32[]{:S(2)}, u32[]{:S(2)}) %collective-permute-start.2) | collective-permute-done | bytes 393248 | tf_op jit(solution)/shard_map/ppermute | solution.py:478
  31.4 1.7 collective-permute-start.6
  33.1 1.7 collective-permute-start.7
  35.5 1.3 stack.80.meta_ref
  37.9 2.9 %collective-permute-start.5 = (bf16[128,768]{1,0:T(8,128)(2,1)S(1)}, bf16[128,768]{1,0:T(8,128)(2,1)S(1)}, u32[]{:S(2)}, u32[]{:S(2)}) collective-permute-start(bf16[128,768]{1,0:T(8,128)(2,1)S(1)} %slice.37), channel_id=1, source_target_pairs={{0,12},{1,13},{2,14},{3,15},{4,0},{5,1},{6,2},{7,3},{8,4},{9,5},{1... | collective-permute-start | bytes 589832 | tf_op jit(solution)/shard_map/ppermute | solution.py:471
  41.7 8.4 %shard_map.113.conv_hbm = bf16[16,256,768]{2,1,0:T(8,128)(2,1)} custom-call(bf16[41,64,1024]{2,1,0:T(8,128)(2,1)} %w_ref), custom_call_target="tpu_custom_call" | custom-call | flops 20000000 | bytes 20000000 | tf_op jit(solution)/shard_map/pallas_call | solution.py:69
  50.2 1.2 collective-permute-start.9
  52.4 2.2 %collective-permute-start.10 = (bf16[128,768]{1,0:T(8,128)(2,1)S(1)}, bf16[128,768]{1,0:T(8,128)(2,1)S(1)}, u32[]{:S(2)}, u32[]{:S(2)}) collective-permute-start(bf16[128,768]{1,0:T(8,128)(2,1)S(1)} %slice.39), channel_id=1, source_target_pairs={{0,12},{1,13},{2,14},{3,15},{4,0},{5,1},{6,2},{7,3},{8,4},{9,5},{1... | collective-permute-start | bytes 589832 | tf_op jit(solution)/shard_map/ppermute | solution.py:471
  56.4 1.3 collective-permute-start.11
  60.1 6.0 %shard_map.114 = (f32[4,64,384]{2,1,0:T(8,128)}, f32[4,64,384]{2,1,0:T(8,128)}) custom-call(s32[9]{0:T(128)} %stack.73.cols_ref, bf16[64,4096]{1,0:T(8,128)(2,1)} %bitcast.32, bf16[64,4096]{1,0:T(8,128)(2,1)} %copy-done.7, bf16[128,4096]{1,0:T(8,128)(2,1)} %collective-permute-done.8.refs_2_, bf16[256,768]{1,0:T(8,128)(2,1)} %copy-done.8, ...), custom_call_target="tpu_custom_call" | custom-call | flops 800000000 | bytes 6000000 | tf_op jit(solution)/shard_map/pallas_call | solution.py:127
  66.2 5.3 %collective-permute-start.12 = (f32[4,64,384]{2,1,0:T(8,128)}, f32[4,64,384]{2,1,0:T(8,128)S(1)}, u32[]{:S(2)}, u32[]{:S(2)}) collective-permute-start(f32[4,64,384]{2,1,0:T(8,128)} %get-tuple-element.98), channel_id=1, source_target_pairs={{0,1},{1,0},{2,3},{3,2},{4,5},{5,4},{6,7},{7,6},{8,9},{9,8},{10,11... | collective-permute-start | bytes 1179656 | tf_op jit(solution)/shard_map/ppermute | solution.py:468
  71.5 1.6 collective-permute-done.12
  73.0 2.0 add.166
  75.0 1.3 collective-permute-start.16
  76.3 6.3 %collective-permute-start.13 = (f32[256,384]{1,0:T(8,128)}, f32[256,384]{1,0:T(8,128)S(1)}, u32[]{:S(2)}, u32[]{:S(2)}) collective-permute-start(f32[256,384]{1,0:T(8,128)} %bitcast.25), channel_id=1, source_target_pairs={{0,4},{1,5},{2,6},{3,7},{4,8},{5,9},{6,10},{7,11},{8,12},{9,13},{1... | collective-permute-start | bytes 1179656 | tf_op jit(solution)/shard_map/ppermute | solution.py:471
  82.6 1.2 collective-permute-start.14
  83.8 1.6 collective-permute-start.15
  86.6 1.3 collective-permute-start.17
  87.9 3.3 %fusion.lifted_hbm = f32[336,1024]{1,0:T(8,128)} fusion(bf16[1536,1024]{1,0:T(8,128)(2,1)S(1)} %copy-done.1, bf16[40,2304]{1,0:T(8,128)(2,1)} %collective-permute-done.16, bf16[40,2304]{1,0:T(8,128)(2,1)S(1)} %copy-done.19, bf16[256,1536]{1,0:T(8,128)(2,1)S(1)} %bitcast.36, bf16[256,768]{1,0:T(8,128)(2,1)} %bitcast.39), kind=kOutput, calls=%fused_computation.3 | convolution fusion | flops 1061093376 | bytes 6070272 | tf_op jit(solution)/shard_map/dot_general | solution.py:557
  91.2 1.3 collective-permute-done.13.refs_1_
  92.5 7.9 %collective-permute-done.14.refs_2_ = f32[256,384]{1,0:T(8,128)S(1)} collective-permute-done((f32[256,384]{1,0:T(8,128)}, f32[256,384]{1,0:T(8,128)S(1)}, u32[]{:S(2)}, u32[]{:S(2)}) %collective-permute-start.14) | collective-permute-done | bytes 393248 | tf_op jit(solution)/shard_map/ppermute | solution.py:471
  103.9 5.6 %shard_map.116 = bf16[336,384]{1,0:T(8,128)(2,1)S(1)} custom-call(s32[4]{0:T(128)S(1)} %pad_add_fusion.meta_ref, bf16[336,384]{1,0:T(8,128)(2,1)S(1)} %collective-permute-done.17.q_ref, f32[256,384]{1,0:T(8,128)S(1)} %bitcast.29, f32[256,384]{1,0:T(8,128)S(1)} %collective-permute-done.13.refs_1_, f32[256,384]{1,0:T(8,128)S(1)} %collective-permute-done.14.refs_2_, ...), custom_call_target="tpu_custom_call" | custom-call | flops 1056964608 | bytes 4000000 | tf_op jit(solution)/shard_map/pallas_call | solution.py:184
  109.5 5.0 %collective-permute-start.22 = (bf16[336,384]{1,0:T(8,128)(2,1)S(1)}, bf16[336,384]{1,0:T(8,128)(2,1)S(1)}, u32[]{:S(2)}, u32[]{:S(2)}) collective-permute-start(bf16[336,384]{1,0:T(8,128)(2,1)S(1)} %shard_map.116), channel_id=1, source_target_pairs={{0,2},{1,3},{2,0},{3,1},{4,6},{5,7},{6,4},{7,5},{8,10},{9,11},{10,... | collective-permute-start | bytes 774152 | tf_op jit(solution)/shard_map/ppermute | solution.py:468
  114.5 5.6 %shard_map.115.mine_hbm = bf16[336,384]{1,0:T(8,128)(2,1)S(1)} custom-call(s32[4]{0:T(128)S(1)} %pad_add_fusion.meta_ref, bf16[336,384]{1,0:T(8,128)(2,1)S(1)} %get-tuple-element.109.q_ref, f32[256,384]{1,0:T(8,128)S(1)} %bitcast.30, f32[256,384]{1,0:T(8,128)S(1)} %collective-permute-done.13.refs_1_, f32[256,384]{1,0:T(8,128)S(1)} %collective-permute-done.14.refs_2_, ...), custom_call_target="tpu_custom_call" | custom-call | flops 1056964608 | bytes 4000000 | tf_op jit(solution)/shard_map/pallas_call | solution.py:184
  121.7 12.2 %shard_map.117 = (f32[8,48,1024]{2,1,0:T(8,128)}, bf16[400,1024]{1,0:T(8,128)(2,1)}, f32[8,1024]{1,0:T(8,128)}) custom-call(s32[5]{0:T(128)} %stack.80.meta_ref, f32[336,1024]{1,0:T(8,128)} %fusion.lifted_hbm, bf16[336,384]{1,0:T(8,128)(2,1)} %copy-done.5, bf16[336,384]{1,0:T(8,128)(2,1)} %copy-done.22, ...), custom_call_target="tpu_custom_call" | custom-call | flops 3000000000 | bytes 14000000 | tf_op jit(solution)/shard_map/pallas_call | solution.py:424
  134.2 2.5 %collective-permute-done.23.arrived_ref = bf16[400,1024]{1,0:T(8,128)(2,1)S(1)} collective-permute-done((bf16[400,1024]{1,0:T(8,128)(2,1)}, bf16[400,1024]{1,0:T(8,128)(2,1)S(1)}, u32[]{:S(2)}, u32[]{:S(2)}) %collective-permute-start.23) | collective-permute-done | bytes 819232 | tf_op jit(solution)/shard_map/ppermute | solution.py:468
  136.8 1.4 copy-done.2
  140.1 1.8 collective-permute-start.25
  141.8 2.6 %collective-permute-start.26 = (bf16[112,1024]{1,0:T(8,128)(2,1)S(1)}, bf16[112,1024]{1,0:T(8,128)(2,1)S(1)}, u32[]{:S(2)}, u32[]{:S(2)}) collective-permute-start(bf16[112,1024]{1,0:T(8,128)(2,1)S(1)} %get-tuple-element.123), channel_id=1, source_target_pairs={{0,12},{1,13},{2,14},{3,15},{4,8},{5,9},{6,10},{7,11},{8,4},{9,5},... | collective-permute-start | bytes 688136 | tf_op jit(solution)/shard_map/ppermute | solution.py:468
  144.4 3.7 %collective-permute-done.24.one_ref = bf16[112,1024]{1,0:T(8,128)(2,1)S(1)} collective-permute-done((bf16[112,1024]{1,0:T(8,128)(2,1)S(1)}, bf16[112,1024]{1,0:T(8,128)(2,1)S(1)}, u32[]{:S(2)}, u32[]{:S(2)}) %collective-permute-start.24) | collective-permute-done | bytes 229408 | tf_op jit(solution)/shard_map/ppermute | solution.py:468
  148.2 4.3 %collective-permute-done.25.two_ref = bf16[112,1024]{1,0:T(8,128)(2,1)S(1)} collective-permute-done((bf16[112,1024]{1,0:T(8,128)(2,1)S(1)}, bf16[112,1024]{1,0:T(8,128)(2,1)S(1)}, u32[]{:S(2)}, u32[]{:S(2)}) %collective-permute-start.25) | collective-permute-done | bytes 229408 | tf_op jit(solution)/shard_map/ppermute | solution.py:468
  152.5 2.6 %collective-permute-done.26.three_ref = bf16[112,1024]{1,0:T(8,128)(2,1)S(1)} collective-permute-done((bf16[112,1024]{1,0:T(8,128)(2,1)S(1)}, bf16[112,1024]{1,0:T(8,128)(2,1)S(1)}, u32[]{:S(2)}, u32[]{:S(2)}) %collective-permute-start.26) | collective-permute-done | bytes 229408 | tf_op jit(solution)/shard_map/ppermute | solution.py:468
  155.8 3.3 %collective-permute-start.28 = (f32[32,1024]{1,0:T(8,128)S(1)}, f32[32,1024]{1,0:T(8,128)S(1)}, u32[]{:S(2)}, u32[]{:S(2)}) collective-permute-start(f32[32,1024]{1,0:T(8,128)S(1)} %get-tuple-element.126), channel_id=1, source_target_pairs={{0,2},{1,3},{2,0},{3,1},{4,6},{5,7},{6,4},{7,5},{8,10},{9,11},{10,... | collective-permute-start | bytes 393224 | tf_op jit(solution)/shard_map/ppermute | solution.py:478
  159.8 2.7 %collective-permute-done.28 = f32[32,1024]{1,0:T(8,128)S(1)} collective-permute-done((f32[32,1024]{1,0:T(8,128)S(1)}, f32[32,1024]{1,0:T(8,128)S(1)}, u32[]{:S(2)}, u32[]{:S(2)}) %collective-permute-start.28) | collective-permute-done | bytes 131104 | tf_op jit(solution)/shard_map/ppermute | solution.py:478
  162.4 2.8 %collective-permute-done.29 = f32[32,1024]{1,0:T(8,128)S(1)} collective-permute-done((f32[32,1024]{1,0:T(8,128)S(1)}, f32[32,1024]{1,0:T(8,128)S(1)}, u32[]{:S(2)}, u32[]{:S(2)}) %collective-permute-start.29) | collective-permute-done | bytes 131104 | tf_op jit(solution)/shard_map/ppermute | solution.py:478
  165.3 3.2 %collective-permute-start.31 = (f32[32,1024]{1,0:T(8,128)S(1)}, f32[32,1024]{1,0:T(8,128)S(1)}, u32[]{:S(2)}, u32[]{:S(2)}) collective-permute-start(f32[32,1024]{1,0:T(8,128)S(1)} %add_add_fusion.1), channel_id=1, source_target_pairs={{0,64},{1,65},{2,66},{3,67},{4,68},{5,69},{6,70},{7,71},{8,72},{9,... | collective-permute-start | bytes 393224 | tf_op jit(solution)/shard_map/ppermute | solution.py:478
  168.5 1.6 collective-permute-start.30
  170.0 5.1 %collective-permute-done.31 = f32[32,1024]{1,0:T(8,128)S(1)} collective-permute-done((f32[32,1024]{1,0:T(8,128)S(1)}, f32[32,1024]{1,0:T(8,128)S(1)}, u32[]{:S(2)}, u32[]{:S(2)}) %collective-permute-start.31) | collective-permute-done | bytes 131104 | tf_op jit(solution)/shard_map/ppermute | solution.py:478
  175.2 2.7 %collective-permute-done.32 = f32[32,1024]{1,0:T(8,128)S(1)} collective-permute-done((f32[32,1024]{1,0:T(8,128)S(1)}, f32[32,1024]{1,0:T(8,128)S(1)}, u32[]{:S(2)}, u32[]{:S(2)}) %collective-permute-start.32) | collective-permute-done | bytes 131104 | tf_op jit(solution)/shard_map/ppermute | solution.py:478
  177.9 8.7 %collective-permute-start.33 = (f32[32,1024]{1,0:T(8,128)S(1)}, f32[32,1024]{1,0:T(8,128)S(1)}, u32[]{:S(2)}, u32[]{:S(2)}) collective-permute-start(f32[32,1024]{1,0:T(8,128)S(1)} %add_add_fusion), channel_id=1, source_target_pairs={{0,128},{1,129},{2,130},{3,131},{4,132},{5,133},{6,134},{7,135},{8... | collective-permute-start | bytes 393224 | tf_op jit(solution)/shard_map/ppermute | solution.py:478
  186.6 4.2 %collective-permute-done.33 = f32[32,1024]{1,0:T(8,128)S(1)} collective-permute-done((f32[32,1024]{1,0:T(8,128)S(1)}, f32[32,1024]{1,0:T(8,128)S(1)}, u32[]{:S(2)}, u32[]{:S(2)}) %collective-permute-start.33) | collective-permute-done | bytes 131104 | tf_op jit(solution)/shard_map/ppermute | solution.py:478
  193.0 2.7 %collective-permute-done.34 = f32[24,1024]{1,0:T(8,128)} collective-permute-done((f32[24,1024]{1,0:T(8,128)S(1)}, f32[24,1024]{1,0:T(8,128)}, u32[]{:S(2)}, u32[]{:S(2)}) %collective-permute-start.34) | collective-permute-done | bytes 98336 | tf_op jit(solution)/shard_map/ppermute | solution.py:478
  196.6 1.8 shard_map.120
  (109 shorter events, 21.2 us)
Async XLA Ops:
  7.2 67.8 %all-gather.2.cloned.1.call-start = ((), (), s32[]{:S(2)}) async-start(), calls=%async_computation | async-start | bytes 1671168 | tf_op jit(solution)/shard_map/all_gather | solution.py:487
  7.2 24.0 %collective-permute-start.3 = (bf16[64,4096]{1,0:T(8,128)(2,1)}, bf16[64,4096]{1,0:T(8,128)(2,1)S(1)}, u32[]{:S(2)}, u32[]{:S(2)}) collective-permute-start(bf16[64,4096]{1,0:T(8,128)(2,1)} %bitcast.31), channel_id=1, source_target_pairs={{0,2},{1,3},{2,0},{3,1},{4,6},{5,7},{6,4},{7,5},{8,10},{9,11},{10,... | collective-permute-start | bytes 1572872 | tf_op jit(solution)/shard_map/ppermute | solution.py:468
  13.5 17.7 %copy-start.6 = (bf16[1,64,4096]{2,1,0:T(8,128)(2,1)S(1)}, bf16[1,64,4096]{2,1,0:T(8,128)(2,1)}, u32[]{:S(2)}) copy-start(bf16[1,64,4096]{2,1,0:T(8,128)(2,1)} %param.10) | copy-start | bytes 1572868
  13.6 21.1 %copy-start.20 = (s32[16]{0:T(128)S(1)}, s32[16]{0:T(128)}, u32[]{:S(2)}) copy-start(s32[16]{0:T(128)} %param.18) | copy-start | bytes 196
  13.6 21.1 %copy-start.21 = (s32[16]{0:T(128)S(1)}, s32[16]{0:T(128)}, u32[]{:S(2)}) copy-start(s32[16]{0:T(128)} %param.19) | copy-start | bytes 196
  13.7 36.4 %copy-start.8 = (bf16[256,768]{1,0:T(8,128)(2,1)}, bf16[256,768]{1,0:T(8,128)(2,1)S(1)}, u32[]{:S(2)}) copy-start(bf16[256,768]{1,0:T(8,128)(2,1)S(1)} %pad_maximum_fusion.9.refs_3_) | copy-start | bytes 1179652
  13.8 11.9 %collective-permute-start = (bf16[256,768]{1,0:T(8,128)(2,1)S(1)}, bf16[256,768]{1,0:T(8,128)(2,1)S(1)}, u32[]{:S(2)}, u32[]{:S(2)}) collective-permute-start(bf16[256,768]{1,0:T(8,128)(2,1)S(1)} %pad_maximum_fusion.9.refs_3_), channel_id=1, source_target_pairs={{0,4},{1,5},{2,6},{3,7},{4,8},{5,9},{6,10},{7,11},{8,12},{9,13},{1... | collective-permute-start | bytes 1179656 | tf_op jit(solution)/shard_map/ppermute | solution.py:471
  15.4 10.3 %collective-permute-start.1 = (bf16[256,768]{1,0:T(8,128)(2,1)S(1)}, bf16[256,768]{1,0:T(8,128)(2,1)S(1)}, u32[]{:S(2)}, u32[]{:S(2)}) collective-permute-start(bf16[256,768]{1,0:T(8,128)(2,1)S(1)} %pad_maximum_fusion.9.refs_3_), channel_id=1, source_target_pairs={{0,12},{1,13},{2,14},{3,15},{4,0},{5,1},{6,2},{7,3},{8,4},{9,5},{1... | collective-permute-start | bytes 1179656 | tf_op jit(solution)/shard_map/ppermute | solution.py:471
  17.1 14.2 %collective-permute-start.2 = (bf16[256,768]{1,0:T(8,128)(2,1)S(1)}, bf16[256,768]{1,0:T(8,128)(2,1)}, u32[]{:S(2)}, u32[]{:S(2)}) collective-permute-start(bf16[256,768]{1,0:T(8,128)(2,1)S(1)} %pad_maximum_fusion.8), channel_id=1, source_target_pairs={{0,18},{1,19},{2,16},{3,17},{4,22},{5,23},{6,20},{7,21},{8,26},{9,... | collective-permute-start | bytes 1179656 | tf_op jit(solution)/shard_map/ppermute | solution.py:478
  25.7 24.4 %copy-start.10 = (bf16[256,768]{1,0:T(8,128)(2,1)}, bf16[256,768]{1,0:T(8,128)(2,1)S(1)}, u32[]{:S(2)}) copy-start(bf16[256,768]{1,0:T(8,128)(2,1)S(1)} %collective-permute-done.refs_5_) | copy-start | bytes 1179652
  25.7 15.2 %copy-start.11 = (bf16[256,768]{1,0:T(8,128)(2,1)}, bf16[256,768]{1,0:T(8,128)(2,1)S(1)}, u32[]{:S(2)}) copy-start(bf16[256,768]{1,0:T(8,128)(2,1)S(1)} %collective-permute-done.1.refs_7_) | copy-start | bytes 1179652
  31.2 18.9 %copy-start.7 = (bf16[64,4096]{1,0:T(8,128)(2,1)}, bf16[64,4096]{1,0:T(8,128)(2,1)S(1)}, u32[]{:S(2)}) copy-start(bf16[64,4096]{1,0:T(8,128)(2,1)S(1)} %collective-permute-done.3.refs_1_) | copy-start | bytes 1572868
  31.3 18.8 %collective-permute-start.8 = (bf16[128,4096]{1,0:T(8,128)(2,1)S(1)}, bf16[128,4096]{1,0:T(8,128)(2,1)}, u32[]{:S(2)}, u32[]{:S(2)}) collective-permute-start(bf16[128,4096]{1,0:T(8,128)(2,1)S(1)} %pad_maximum_fusion), channel_id=1, source_target_pairs={{0,1},{1,0},{2,3},{3,2},{4,5},{5,4},{6,7},{7,6},{8,9},{9,8},{10,11... | collective-permute-start | bytes 3145736 | tf_op jit(solution)/shard_map/ppermute | solution.py:468
  31.4 18.7 %collective-permute-start.6 = (bf16[256,768]{1,0:T(8,128)(2,1)}, bf16[256,768]{1,0:T(8,128)(2,1)S(1)}, u32[]{:S(2)}, u32[]{:S(2)}) collective-permute-start(bf16[256,768]{1,0:T(8,128)(2,1)} %collective-permute-done.2.refs_4_), channel_id=1, source_target_pairs={{0,4},{1,5},{2,6},{3,7},{4,8},{5,9},{6,10},{7,11},{8,12},{9,13},{1... | collective-permute-start | bytes 1179656 | tf_op jit(solution)/shard_map/ppermute | solution.py:471
  33.1 17.1 %collective-permute-start.7 = (bf16[256,768]{1,0:T(8,128)(2,1)}, bf16[256,768]{1,0:T(8,128)(2,1)}, u32[]{:S(2)}, u32[]{:S(2)}) collective-permute-start(bf16[256,768]{1,0:T(8,128)(2,1)} %collective-permute-done.2.refs_4_), channel_id=1, source_target_pairs={{0,12},{1,13},{2,14},{3,15},{4,0},{5,1},{6,2},{7,3},{8,4},{9,5},{1... | collective-permute-start | bytes 1179656 | tf_op jit(solution)/shard_map/ppermute | solution.py:471
  37.4 12.7 %collective-permute-start.4 = (bf16[128,768]{1,0:T(8,128)(2,1)S(1)}, bf16[128,768]{1,0:T(8,128)(2,1)S(1)}, u32[]{:S(2)}, u32[]{:S(2)}) collective-permute-start(bf16[128,768]{1,0:T(8,128)(2,1)S(1)} %slice.36), channel_id=1, source_target_pairs={{0,4},{1,5},{2,6},{3,7},{4,8},{5,9},{6,10},{7,11},{8,12},{9,13},{1... | collective-permute-start | bytes 589832 | tf_op jit(solution)/shard_map/ppermute | solution.py:471
  37.9 12.2 %collective-permute-start.5 = (bf16[128,768]{1,0:T(8,128)(2,1)S(1)}, bf16[128,768]{1,0:T(8,128)(2,1)S(1)}, u32[]{:S(2)}, u32[]{:S(2)}) collective-permute-start(bf16[128,768]{1,0:T(8,128)(2,1)S(1)} %slice.37), channel_id=1, source_target_pairs={{0,12},{1,13},{2,14},{3,15},{4,0},{5,1},{6,2},{7,3},{8,4},{9,5},{1... | collective-permute-start | bytes 589832 | tf_op jit(solution)/shard_map/ppermute | solution.py:471
  50.2 8.6 %collective-permute-start.9 = (bf16[128,768]{1,0:T(8,128)(2,1)S(1)}, bf16[128,768]{1,0:T(8,128)(2,1)S(1)}, u32[]{:S(2)}, u32[]{:S(2)}) collective-permute-start(bf16[128,768]{1,0:T(8,128)(2,1)S(1)} %slice.38), channel_id=1, source_target_pairs={{0,4},{1,5},{2,6},{3,7},{4,8},{5,9},{6,10},{7,11},{8,12},{9,13},{1... | collective-permute-start | bytes 589832 | tf_op jit(solution)/shard_map/ppermute | solution.py:471
  52.4 7.0 %collective-permute-start.10 = (bf16[128,768]{1,0:T(8,128)(2,1)S(1)}, bf16[128,768]{1,0:T(8,128)(2,1)S(1)}, u32[]{:S(2)}, u32[]{:S(2)}) collective-permute-start(bf16[128,768]{1,0:T(8,128)(2,1)S(1)} %slice.39), channel_id=1, source_target_pairs={{0,12},{1,13},{2,14},{3,15},{4,0},{5,1},{6,2},{7,3},{8,4},{9,5},{1... | collective-permute-start | bytes 589832 | tf_op jit(solution)/shard_map/ppermute | solution.py:471
  56.4 2.3 %collective-permute-start.11 = (bf16[40,2304]{1,0:T(8,128)(2,1)S(1)}, bf16[40,2304]{1,0:T(8,128)(2,1)S(1)}, u32[]{:S(2)}, u32[]{:S(2)}) collective-permute-start(bf16[40,2304]{1,0:T(8,128)(2,1)S(1)} %pad_maximum_fusion.11), channel_id=1, source_target_pairs={{0,1},{1,2},{2,3},{3,4},{4,5},{5,6},{6,7},{7,8},{8,9},{9,10},{10,1... | collective-permute-start | bytes 552968 | tf_op jit(solution)/shard_map/ppermute | solution.py:524
  58.8 14.3 %copy-start.18 = (bf16[40,2304]{1,0:T(8,128)(2,1)}, bf16[40,2304]{1,0:T(8,128)(2,1)S(1)}, u32[]{:S(2)}) copy-start(bf16[40,2304]{1,0:T(8,128)(2,1)S(1)} %collective-permute-done.11) | copy-start | bytes 552964
  66.2 6.9 %collective-permute-start.12 = (f32[4,64,384]{2,1,0:T(8,128)}, f32[4,64,384]{2,1,0:T(8,128)S(1)}, u32[]{:S(2)}, u32[]{:S(2)}) collective-permute-start(f32[4,64,384]{2,1,0:T(8,128)} %get-tuple-element.98), channel_id=1, source_target_pairs={{0,1},{1,0},{2,3},{3,2},{4,5},{5,4},{6,7},{7,6},{8,9},{9,8},{10,11... | collective-permute-start | bytes 1179656 | tf_op jit(solution)/shard_map/ppermute | solution.py:468
  73.0 14.9 %copy-start.1 = (bf16[1536,1024]{1,0:T(8,128)(2,1)S(1)}, bf16[1536,1024]{1,0:T(8,128)(2,1)}, u32[]{:S(2)}) copy-start(bf16[1536,1024]{1,0:T(8,128)(2,1)} %disc_ref.1) | copy-start | bytes 9437188
  75.0 10.4 %collective-permute-start.16 = (bf16[40,2304]{1,0:T(8,128)(2,1)S(1)}, bf16[40,2304]{1,0:T(8,128)(2,1)}, u32[]{:S(2)}, u32[]{:S(2)}) collective-permute-start(bf16[40,2304]{1,0:T(8,128)(2,1)S(1)} %pad_maximum_fusion.12), channel_id=1, source_target_pairs={{1,0},{2,1},{3,2},{4,3},{5,4},{6,5},{7,6},{8,7},{9,8},{10,9},{11,1... | collective-permute-start | bytes 552968 | tf_op jit(solution)/shard_map/ppermute | solution.py:553
  76.3 11.6 %copy-start.9 = (bf16[1,256,1536]{2,1,0:T(8,128)(2,1)S(1)}, bf16[1,256,1536]{2,1,0:T(8,128)(2,1)}, u32[]{:S(2)}) copy-start(bf16[1,256,1536]{2,1,0:T(8,128)(2,1)} %param.13) | copy-start | bytes 2359300
  76.3 11.6 %copy-start.19 = (bf16[40,2304]{1,0:T(8,128)(2,1)S(1)}, bf16[40,2304]{1,0:T(8,128)(2,1)}, u32[]{:S(2)}) copy-start(bf16[40,2304]{1,0:T(8,128)(2,1)} %copy-done.18) | copy-start | bytes 552964
  76.3 16.1 %collective-permute-start.13 = (f32[256,384]{1,0:T(8,128)}, f32[256,384]{1,0:T(8,128)S(1)}, u32[]{:S(2)}, u32[]{:S(2)}) collective-permute-start(f32[256,384]{1,0:T(8,128)} %bitcast.25), channel_id=1, source_target_pairs={{0,4},{1,5},{2,6},{3,7},{4,8},{5,9},{6,10},{7,11},{8,12},{9,13},{1... | collective-permute-start | bytes 1179656 | tf_op jit(solution)/shard_map/ppermute | solution.py:471
  82.6 17.8 %collective-permute-start.14 = (f32[256,384]{1,0:T(8,128)}, f32[256,384]{1,0:T(8,128)S(1)}, u32[]{:S(2)}, u32[]{:S(2)}) collective-permute-start(f32[256,384]{1,0:T(8,128)} %bitcast.26), channel_id=1, source_target_pairs={{0,8},{1,9},{2,10},{3,11},{4,12},{5,13},{6,14},{7,15},{8,0},{9,1},... | collective-permute-start | bytes 1179656 | tf_op jit(solution)/shard_map/ppermute | solution.py:471
  83.8 16.6 %collective-permute-start.15 = (f32[256,384]{1,0:T(8,128)}, f32[256,384]{1,0:T(8,128)S(1)}, u32[]{:S(2)}, u32[]{:S(2)}) collective-permute-start(f32[256,384]{1,0:T(8,128)} %bitcast.27), channel_id=1, source_target_pairs={{0,12},{1,13},{2,14},{3,15},{4,0},{5,1},{6,2},{7,3},{8,4},{9,5},{1... | collective-permute-start | bytes 1179656 | tf_op jit(solution)/shard_map/ppermute | solution.py:471
  86.6 13.8 %copy-start.3 = (f32[4,64,384]{2,1,0:T(8,128)S(1)}, f32[4,64,384]{2,1,0:T(8,128)}, u32[]{:S(2)}) copy-start(f32[4,64,384]{2,1,0:T(8,128)} %add.166) | copy-start | bytes 1179652
  86.6 13.8 %collective-permute-start.17 = (bf16[336,384]{1,0:T(8,128)(2,1)S(1)}, bf16[336,384]{1,0:T(8,128)(2,1)S(1)}, u32[]{:S(2)}, u32[]{:S(2)}) collective-permute-start(bf16[336,384]{1,0:T(8,128)(2,1)S(1)} %get-tuple-element.136), channel_id=1, source_target_pairs={{0,2},{1,3},{2,0},{3,1},{4,6},{5,7},{6,4},{7,5},{8,10},{9,11},{10,... | collective-permute-start | bytes 774152 | tf_op jit(solution)/shard_map/ppermute | solution.py:468
  100.4 1.8 collective-permute-start.18
  100.5 2.3 %collective-permute-start.19 = (f32[256,384]{1,0:T(8,128)S(1)}, f32[256,384]{1,0:T(8,128)S(1)}, u32[]{:S(2)}, u32[]{:S(2)}) collective-permute-start(f32[256,384]{1,0:T(8,128)S(1)} %collective-permute-done.13.refs_1_), channel_id=1, source_target_pairs={{0,1},{1,0},{2,3},{3,2},{4,5},{5,4},{6,7},{7,6},{8,9},{9,8},{10,11... | collective-permute-start | bytes 1179656 | tf_op jit(solution)/shard_map/ppermute | solution.py:468
  101.0 2.3 %collective-permute-start.20 = (f32[256,384]{1,0:T(8,128)S(1)}, f32[256,384]{1,0:T(8,128)S(1)}, u32[]{:S(2)}, u32[]{:S(2)}) collective-permute-start(f32[256,384]{1,0:T(8,128)S(1)} %collective-permute-done.14.refs_2_), channel_id=1, source_target_pairs={{0,1},{1,0},{2,3},{3,2},{4,5},{5,4},{6,7},{7,6},{8,9},{9,8},{10,11... | collective-permute-start | bytes 1179656 | tf_op jit(solution)/shard_map/ppermute | solution.py:468
  101.1 2.8 %collective-permute-start.21 = (f32[256,384]{1,0:T(8,128)S(1)}, f32[256,384]{1,0:T(8,128)S(1)}, u32[]{:S(2)}, u32[]{:S(2)}) collective-permute-start(f32[256,384]{1,0:T(8,128)S(1)} %collective-permute-done.15.refs_3_), channel_id=1, source_target_pairs={{0,1},{1,0},{2,3},{3,2},{4,5},{5,4},{6,7},{7,6},{8,9},{9,8},{10,11... | collective-permute-start | bytes 1179656 | tf_op jit(solution)/shard_map/ppermute | solution.py:468
  109.5 11.5 %collective-permute-start.22 = (bf16[336,384]{1,0:T(8,128)(2,1)S(1)}, bf16[336,384]{1,0:T(8,128)(2,1)S(1)}, u32[]{:S(2)}, u32[]{:S(2)}) collective-permute-start(bf16[336,384]{1,0:T(8,128)(2,1)S(1)} %shard_map.116), channel_id=1, source_target_pairs={{0,2},{1,3},{2,0},{3,1},{4,6},{5,7},{6,4},{7,5},{8,10},{9,11},{10,... | collective-permute-start | bytes 774152 | tf_op jit(solution)/shard_map/ppermute | solution.py:468
  133.9 2.9 %collective-permute-start.23 = (bf16[400,1024]{1,0:T(8,128)(2,1)}, bf16[400,1024]{1,0:T(8,128)(2,1)S(1)}, u32[]{:S(2)}, u32[]{:S(2)}) collective-permute-start(bf16[400,1024]{1,0:T(8,128)(2,1)} %get-tuple-element.118), channel_id=1, source_target_pairs={{0,1},{1,0},{2,3},{3,2},{4,5},{5,4},{6,7},{7,6},{8,9},{9,8},{10,11... | collective-permute-start | bytes 2457608 | tf_op jit(solution)/shard_map/ppermute | solution.py:468
  139.6 8.5 %collective-permute-start.24 = (bf16[112,1024]{1,0:T(8,128)(2,1)S(1)}, bf16[112,1024]{1,0:T(8,128)(2,1)S(1)}, u32[]{:S(2)}, u32[]{:S(2)}) collective-permute-start(bf16[112,1024]{1,0:T(8,128)(2,1)S(1)} %get-tuple-element.121), channel_id=1, source_target_pairs={{0,4},{1,5},{2,6},{3,7},{4,0},{5,1},{6,2},{7,3},{8,12},{9,13},{10,... | collective-permute-start | bytes 688136 | tf_op jit(solution)/shard_map/ppermute | solution.py:468
  140.1 12.4 %collective-permute-start.25 = (bf16[112,1024]{1,0:T(8,128)(2,1)S(1)}, bf16[112,1024]{1,0:T(8,128)(2,1)S(1)}, u32[]{:S(2)}, u32[]{:S(2)}) collective-permute-start(bf16[112,1024]{1,0:T(8,128)(2,1)S(1)} %get-tuple-element.122), channel_id=1, source_target_pairs={{0,8},{1,9},{2,10},{3,11},{4,12},{5,13},{6,14},{7,15},{8,0},{9,1},... | collective-permute-start | bytes 688136 | tf_op jit(solution)/shard_map/ppermute | solution.py:468
  141.8 13.2 %collective-permute-start.26 = (bf16[112,1024]{1,0:T(8,128)(2,1)S(1)}, bf16[112,1024]{1,0:T(8,128)(2,1)S(1)}, u32[]{:S(2)}, u32[]{:S(2)}) collective-permute-start(bf16[112,1024]{1,0:T(8,128)(2,1)S(1)} %get-tuple-element.123), channel_id=1, source_target_pairs={{0,12},{1,13},{2,14},{3,15},{4,8},{5,9},{6,10},{7,11},{8,4},{9,5},... | collective-permute-start | bytes 688136 | tf_op jit(solution)/shard_map/ppermute | solution.py:468
  155.8 6.7 %collective-permute-start.28 = (f32[32,1024]{1,0:T(8,128)S(1)}, f32[32,1024]{1,0:T(8,128)S(1)}, u32[]{:S(2)}, u32[]{:S(2)}) collective-permute-start(f32[32,1024]{1,0:T(8,128)S(1)} %get-tuple-element.126), channel_id=1, source_target_pairs={{0,2},{1,3},{2,0},{3,1},{4,6},{5,7},{6,4},{7,5},{8,10},{9,11},{10,... | collective-permute-start | bytes 393224 | tf_op jit(solution)/shard_map/ppermute | solution.py:478
  159.1 6.2 %collective-permute-start.29 = (f32[32,1024]{1,0:T(8,128)S(1)}, f32[32,1024]{1,0:T(8,128)S(1)}, u32[]{:S(2)}, u32[]{:S(2)}) collective-permute-start(f32[32,1024]{1,0:T(8,128)S(1)} %get-tuple-element.127), channel_id=1, source_target_pairs={{0,18},{1,19},{2,16},{3,17},{4,22},{5,23},{6,20},{7,21},{8,26},{9,... | collective-permute-start | bytes 393224 | tf_op jit(solution)/shard_map/ppermute | solution.py:478
  159.8 5.5 %collective-permute-start.27 = (f32[32,1024]{1,0:T(8,128)S(1)}, f32[32,1024]{1,0:T(8,128)S(1)}, u32[]{:S(2)}, u32[]{:S(2)}) collective-permute-start(f32[32,1024]{1,0:T(8,128)S(1)} %get-tuple-element.125), channel_id=1, source_target_pairs={{0,16},{1,17},{2,18},{3,19},{4,20},{5,21},{6,22},{7,23},{8,24},{9,... | collective-permute-start | bytes 393224 | tf_op jit(solution)/shard_map/ppermute | solution.py:478
  165.3 9.8 %collective-permute-start.31 = (f32[32,1024]{1,0:T(8,128)S(1)}, f32[32,1024]{1,0:T(8,128)S(1)}, u32[]{:S(2)}, u32[]{:S(2)}) collective-permute-start(f32[32,1024]{1,0:T(8,128)S(1)} %add_add_fusion.1), channel_id=1, source_target_pairs={{0,64},{1,65},{2,66},{3,67},{4,68},{5,69},{6,70},{7,71},{8,72},{9,... | collective-permute-start | bytes 393224 | tf_op jit(solution)/shard_map/ppermute | solution.py:478
  168.5 9.4 %collective-permute-start.32 = (f32[32,1024]{1,0:T(8,128)S(1)}, f32[32,1024]{1,0:T(8,128)S(1)}, u32[]{:S(2)}, u32[]{:S(2)}) collective-permute-start(f32[32,1024]{1,0:T(8,128)S(1)} %add_add_fusion.1), channel_id=1, source_target_pairs={{0,96},{1,97},{2,98},{3,99},{4,100},{5,101},{6,102},{7,103},{8,104... | collective-permute-start | bytes 393224 | tf_op jit(solution)/shard_map/ppermute | solution.py:478
  168.5 9.4 %collective-permute-start.30 = (f32[32,1024]{1,0:T(8,128)S(1)}, f32[32,1024]{1,0:T(8,128)S(1)}, u32[]{:S(2)}, u32[]{:S(2)}) collective-permute-start(f32[32,1024]{1,0:T(8,128)S(1)} %add_add_fusion.1), channel_id=1, source_target_pairs={{0,32},{1,33},{2,34},{3,35},{4,36},{5,37},{6,38},{7,39},{8,40},{9,... | collective-permute-start | bytes 393224 | tf_op jit(solution)/shard_map/ppermute | solution.py:478
  177.9 12.9 %collective-permute-start.33 = (f32[32,1024]{1,0:T(8,128)S(1)}, f32[32,1024]{1,0:T(8,128)S(1)}, u32[]{:S(2)}, u32[]{:S(2)}) collective-permute-start(f32[32,1024]{1,0:T(8,128)S(1)} %add_add_fusion), channel_id=1, source_target_pairs={{0,128},{1,129},{2,130},{3,131},{4,132},{5,133},{6,134},{7,135},{8... | collective-permute-start | bytes 393224 | tf_op jit(solution)/shard_map/ppermute | solution.py:478
  190.8 4.8 %collective-permute-start.34 = (f32[24,1024]{1,0:T(8,128)S(1)}, f32[24,1024]{1,0:T(8,128)}, u32[]{:S(2)}, u32[]{:S(2)}) collective-permute-start(f32[24,1024]{1,0:T(8,128)S(1)} %slice.48), channel_id=1, source_target_pairs={{0,16},{1,17},{2,18},{3,19},{4,20},{5,21},{6,22},{7,23},{8,24},{9,... | collective-permute-start | bytes 294920 | tf_op jit(solution)/shard_map/ppermute | solution.py:478
  (11 other events, 42.2 us)
Sparse Core Ops, SparseCore 0:
  18.3 52.8 all-gather.1

commit v7 on v6

--- a/solution.py
+++ b/solution.py
@@ -504,8 +504,8 @@
         return [turn(turned[0][:rows], 1), turn(turned[1][rows:], 3)]
 
     states_in = states[0]
-    near, near_turned, far, state_far, queries_in, hidden_in, conv_in = lax.optimization_barrier(
-        (near, near_turned, far, flip(states_in, 2), queries[0], hidden[0], conv_weight)
+    near, near_turned, far, state_far, queries_in, hidden_in, conv = lax.optimization_barrier(
+        (near, near_turned, far, flip(states_in, 2), queries[0], hidden[0], arrange(conv_weight))
     )
 
     lower = clip % 2
@@ -536,9 +536,8 @@
     meta3 = jnp.stack([row, 2 * half + lower, clip // 2]).astype(jnp.int32)
     blocks = [near, far, near_turned[0], far_turned[0], near_turned[1], far_turned[1]] + near_over + far_over
     tables = (cols, meta, meta2.astype(jnp.int32), meta3)
-    conv = arrange(conv_in)
-    blocks, state_pair, tables, before, after, conv = lax.optimization_barrier(
-        (blocks, state_pair, tables, before, after, conv)
+    blocks, state_pair, tables, before, after = lax.optimization_barrier(
+        (blocks, state_pair, tables, before, after)
     )
     cols, meta, meta2, meta3 = tables
     state_parts = [states_in, state_far, state_pair]

time: 207 us -> 207 us (level)
    unnamed x46 -> x44, local copies, waits for them, and re-layouts: 4.39 us -> 4.31 us
  transfers between devices with their start and end apart: 36 -> 36, of which waited for: 22 -> 22; matrix products, arithmetic and copies ran while one was open for 8% -> 9% of each run, Pallas kernels for 10% -> 10%
where the time goes in v7:
time: 207 us; the launch traced here: 206 us
  starting transfers between devices  63.2 us (31%)
  waiting for transfers between devices  60.8 us (29%)
  Pallas kernels  41.1 us (20%)
  between operations  16.9 us (8%)
  local copies, waits for them, and re-layouts  11.7 us (6%)
  matrix products  6.47 us (3%)
  other arithmetic  5.65 us (3%)
    ppermute x9, waiting for transfers between devices, swap(): return lax.ppermute(x, ('dp', 'seq'), pairs)  26.1 us
    ppermute x11, starting transfers between devices, turn(): lax.ppermute(x, 'seq', [(i, (i + 4 * hops) % seq_size) for i in range(seq...  22.8 us
    ppermute x13, starting transfers between devices, flip(): return lax.ppermute(x, 'seq', [(i, i ^ bit) for i in range(seq_size)])  20.5 us
    ppermute x13, waiting for transfers between devices, flip(): return lax.ppermute(x, 'seq', [(i, i ^ bit) for i in range(seq_size)])  17.3 us
    ppermute x9, starting transfers between devices, swap(): return lax.ppermute(x, ('dp', 'seq'), pairs)  17.2 us
    ppermute x11, waiting for transfers between devices, turn(): lax.ppermute(x, 'seq', [(i, (i + 4 * hops) % seq_size) for i in range(seq...  16.4 us
    pallas_call x1, Pallas kernels, critic(): pl.pallas_call(critic_kernel, in_specs=[smem()] + [anywhere()] * 5 + [vme...  12.2 us
    pallas_call x2, Pallas kernels, attend(): pl.pallas_call(attend_kernel, grid=(width // HEAD_DIM,), in_specs=[smem()...  11.3 us
  transfers between devices with their start and end apart: 36, of which 22 were waited for; matrix products, arithmetic and copies ran while one was open for 9% of the time, Pallas kernels for 10%

profile of v7, /device:TPU:32, one launch (start us, length us, event | category | flops | bytes accessed | tf_op | source)
XLA Modules:
  0.0 205.9 jit_solution(16286769200204272561)
XLA Ops:
  7.2 3.1 %collective-permute-start.3 = (bf16[64,4096]{1,0:T(8,128)(2,1)}, bf16[64,4096]{1,0:T(8,128)(2,1)S(1)}, u32[]{:S(2)}, u32[]{:S(2)}) collective-permute-start(bf16[64,4096]{1,0:T(8,128)(2,1)} %bitcast.31), channel_id=1, source_target_pairs={{0,2},{1,3},{2,0},{3,1},{4,6},{5,7},{6,4},{7,5},{8,10},{9,11},{10,... | collective-permute-start | bytes 1572872 | tf_op jit(solution)/shard_map/ppermute | solution.py:468
  10.3 3.2 %convolution_convert_fusion = bf16[48,1024]{1,0:T(8,128)(2,1)} fusion(bf16[48,1536]{1,0:T(8,128)(2,1)S(1)} %copy-done, bf16[1536,1024]{1,0:T(8,128)(2,1)} %disc_ref.1), kind=kOutput, calls=%fused_computation | convolution fusion | flops 151044096 | bytes 3391488 | tf_op jit(solution)/shard_map/dot_general | solution.py:485
  13.7 1.7 collective-permute-start
  15.4 1.7 collective-permute-start.1
  17.1 1.1 collective-permute-start.2
  18.2 8.4 %shard_map.113.conv_hbm = bf16[16,256,768]{2,1,0:T(8,128)(2,1)} custom-call(bf16[41,64,1024]{2,1,0:T(8,128)(2,1)} %w_ref.1), custom_call_target="tpu_custom_call" | custom-call | flops 20000000 | bytes 20000000 | tf_op jit(solution)/shard_map/pallas_call | solution.py:69
  26.7 4.5 %collective-permute-done.2.refs_4_ = bf16[256,768]{1,0:T(8,128)(2,1)} collective-permute-done((bf16[256,768]{1,0:T(8,128)(2,1)S(1)}, bf16[256,768]{1,0:T(8,128)(2,1)}, u32[]{:S(2)}, u32[]{:S(2)}) %collective-permute-start.2) | collective-permute-done | bytes 393248 | tf_op jit(solution)/shard_map/ppermute | solution.py:478
  31.4 1.6 collective-permute-start.6
  33.1 1.7 collective-permute-start.7
  35.5 1.3 stack.80.meta_ref
  39.8 2.9 %collective-permute-start.5 = (bf16[128,768]{1,0:T(8,128)(2,1)S(1)}, bf16[128,768]{1,0:T(8,128)(2,1)S(1)}, u32[]{:S(2)}, u32[]{:S(2)}) collective-permute-start(bf16[128,768]{1,0:T(8,128)(2,1)S(1)} %slice.37), channel_id=1, source_target_pairs={{0,12},{1,13},{2,14},{3,15},{4,0},{5,1},{6,2},{7,3},{8,4},{9,5},{1... | collective-permute-start | bytes 589832 | tf_op jit(solution)/shard_map/ppermute | solution.py:471
  43.5 6.2 %collective-permute-done.4.refs_9_ = bf16[128,768]{1,0:T(8,128)(2,1)S(1)} collective-permute-done((bf16[128,768]{1,0:T(8,128)(2,1)S(1)}, bf16[128,768]{1,0:T(8,128)(2,1)S(1)}, u32[]{:S(2)}, u32[]{:S(2)}) %collective-permute-start.4) | collective-permute-done | bytes 196640 | tf_op jit(solution)/shard_map/ppermute | solution.py:471
  49.8 1.7 collective-permute-start.9
  52.4 1.9 collective-permute-start.10
  56.1 1.3 collective-permute-start.11
  60.1 6.0 %shard_map.114 = (f32[4,64,384]{2,1,0:T(8,128)}, f32[4,64,384]{2,1,0:T(8,128)}) custom-call(s32[9]{0:T(128)} %stack.73.cols_ref, bf16[64,4096]{1,0:T(8,128)(2,1)} %bitcast.32, bf16[64,4096]{1,0:T(8,128)(2,1)} %copy-done.7, bf16[128,4096]{1,0:T(8,128)(2,1)} %copy-done.10, bf16[256,768]{1,0:T(8,128)(2,1)} %copy-done.8, ...), custom_call_target="tpu_custom_call" | custom-call | flops 800000000 | bytes 6000000 | tf_op jit(solution)/shard_map/pallas_call | solution.py:127
  66.1 5.1 %collective-permute-start.12 = (f32[4,64,384]{2,1,0:T(8,128)}, f32[4,64,384]{2,1,0:T(8,128)S(1)}, u32[]{:S(2)}, u32[]{:S(2)}) collective-permute-start(f32[4,64,384]{2,1,0:T(8,128)} %get-tuple-element.96), channel_id=1, source_target_pairs={{0,1},{1,0},{2,3},{3,2},{4,5},{5,4},{6,7},{7,6},{8,9},{9,8},{10,11... | collective-permute-start | bytes 1179656 | tf_op jit(solution)/shard_map/ppermute | solution.py:468
  71.2 1.6 collective-permute-done.12
  72.8 1.9 add.166
  74.7 1.3 collective-permute-start.16
  76.1 6.3 %collective-permute-start.13 = (f32[256,384]{1,0:T(8,128)}, f32[256,384]{1,0:T(8,128)S(1)}, u32[]{:S(2)}, u32[]{:S(2)}) collective-permute-start(f32[256,384]{1,0:T(8,128)} %bitcast.25), channel_id=1, source_target_pairs={{0,4},{1,5},{2,6},{3,7},{4,8},{5,9},{6,10},{7,11},{8,12},{9,13},{1... | collective-permute-start | bytes 1179656 | tf_op jit(solution)/shard_map/ppermute | solution.py:471
  82.3 1.5 collective-permute-start.14
  83.8 1.6 collective-permute-start.15
  86.6 1.3 collective-permute-start.17
  87.9 3.3 %fusion.lifted_hbm = f32[336,1024]{1,0:T(8,128)} fusion(bf16[1536,1024]{1,0:T(8,128)(2,1)S(1)} %copy-done.1, bf16[40,2304]{1,0:T(8,128)(2,1)} %collective-permute-done.16, bf16[40,2304]{1,0:T(8,128)(2,1)S(1)} %copy-done.18, bf16[256,1536]{1,0:T(8,128)(2,1)S(1)} %bitcast.36, bf16[256,768]{1,0:T(8,128)(2,1)} %bitcast.39), kind=kOutput, calls=%fused_computation.3 | convolution fusion | flops 1061093376 | bytes 6070272 | tf_op jit(solution)/shard_map/dot_general | solution.py:556
  92.2 8.2 %collective-permute-done.14.refs_2_ = f32[256,384]{1,0:T(8,128)S(1)} collective-permute-done((f32[256,384]{1,0:T(8,128)}, f32[256,384]{1,0:T(8,128)S(1)}, u32[]{:S(2)}, u32[]{:S(2)}) %collective-permute-start.14) | collective-permute-done | bytes 393248 | tf_op jit(solution)/shard_map/ppermute | solution.py:471
  103.9 5.6 %shard_map.116 = bf16[336,384]{1,0:T(8,128)(2,1)S(1)} custom-call(s32[4]{0:T(128)S(1)} %pad_add_fusion.meta_ref, bf16[336,384]{1,0:T(8,128)(2,1)S(1)} %collective-permute-done.17.q_ref, f32[256,384]{1,0:T(8,128)S(1)} %bitcast.29, f32[256,384]{1,0:T(8,128)S(1)} %collective-permute-done.13.refs_1_, f32[256,384]{1,0:T(8,128)S(1)} %collective-permute-done.14.refs_2_, ...), custom_call_target="tpu_custom_call" | custom-call | flops 1056964608 | bytes 4000000 | tf_op jit(solution)/shard_map/pallas_call | solution.py:184
  109.5 4.7 %collective-permute-start.22 = (bf16[336,384]{1,0:T(8,128)(2,1)S(1)}, bf16[336,384]{1,0:T(8,128)(2,1)S(1)}, u32[]{:S(2)}, u32[]{:S(2)}) collective-permute-start(bf16[336,384]{1,0:T(8,128)(2,1)S(1)} %shard_map.116), channel_id=1, source_target_pairs={{0,2},{1,3},{2,0},{3,1},{4,6},{5,7},{6,4},{7,5},{8,10},{9,11},{10,... | collective-permute-start | bytes 774152 | tf_op jit(solution)/shard_map/ppermute | solution.py:468
  114.2 5.6 %shard_map.115.mine_hbm = bf16[336,384]{1,0:T(8,128)(2,1)S(1)} custom-call(s32[4]{0:T(128)S(1)} %pad_add_fusion.meta_ref, bf16[336,384]{1,0:T(8,128)(2,1)S(1)} %get-tuple-element.107.q_ref, f32[256,384]{1,0:T(8,128)S(1)} %bitcast.30, f32[256,384]{1,0:T(8,128)S(1)} %collective-permute-done.13.refs_1_, f32[256,384]{1,0:T(8,128)S(1)} %collective-permute-done.14.refs_2_, ...), custom_call_target="tpu_custom_call" | custom-call | flops 1056964608 | bytes 4000000 | tf_op jit(solution)/shard_map/pallas_call | solution.py:184
  121.5 12.2 %shard_map.117 = (f32[8,48,1024]{2,1,0:T(8,128)}, bf16[400,1024]{1,0:T(8,128)(2,1)}, f32[8,1024]{1,0:T(8,128)}) custom-call(s32[5]{0:T(128)} %stack.80.meta_ref, f32[336,1024]{1,0:T(8,128)} %fusion.lifted_hbm, bf16[336,384]{1,0:T(8,128)(2,1)} %copy-done.5, bf16[336,384]{1,0:T(8,128)(2,1)} %copy-done.21, ...), custom_call_target="tpu_custom_call" | custom-call | flops 3000000000 | bytes 14000000 | tf_op jit(solution)/shard_map/pallas_call | solution.py:424
  134.0 2.5 %collective-permute-done.23.arrived_ref = bf16[400,1024]{1,0:T(8,128)(2,1)S(1)} collective-permute-done((bf16[400,1024]{1,0:T(8,128)(2,1)}, bf16[400,1024]{1,0:T(8,128)(2,1)S(1)}, u32[]{:S(2)}, u32[]{:S(2)}) %collective-permute-start.23) | collective-permute-done | bytes 819232 | tf_op jit(solution)/shard_map/ppermute | solution.py:468
  136.5 1.4 copy-done.2
  140.1 1.5 collective-permute-start.25
  141.6 2.6 %collective-permute-start.26 = (bf16[112,1024]{1,0:T(8,128)(2,1)S(1)}, bf16[112,1024]{1,0:T(8,128)(2,1)S(1)}, u32[]{:S(2)}, u32[]{:S(2)}) collective-permute-start(bf16[112,1024]{1,0:T(8,128)(2,1)S(1)} %get-tuple-element.121), channel_id=1, source_target_pairs={{0,12},{1,13},{2,14},{3,15},{4,8},{5,9},{6,10},{7,11},{8,4},{9,5},... | collective-permute-start | bytes 688136 | tf_op jit(solution)/shard_map/ppermute | solution.py:468
  144.1 3.7 %collective-permute-done.24.one_ref = bf16[112,1024]{1,0:T(8,128)(2,1)S(1)} collective-permute-done((bf16[112,1024]{1,0:T(8,128)(2,1)S(1)}, bf16[112,1024]{1,0:T(8,128)(2,1)S(1)}, u32[]{:S(2)}, u32[]{:S(2)}) %collective-permute-start.24) | collective-permute-done | bytes 229408 | tf_op jit(solution)/shard_map/ppermute | solution.py:468
  147.9 4.3 %collective-permute-done.25.two_ref = bf16[112,1024]{1,0:T(8,128)(2,1)S(1)} collective-permute-done((bf16[112,1024]{1,0:T(8,128)(2,1)S(1)}, bf16[112,1024]{1,0:T(8,128)(2,1)S(1)}, u32[]{:S(2)}, u32[]{:S(2)}) %collective-permute-start.25) | collective-permute-done | bytes 229408 | tf_op jit(solution)/shard_map/ppermute | solution.py:468
  152.2 2.6 %collective-permute-done.26.three_ref = bf16[112,1024]{1,0:T(8,128)(2,1)S(1)} collective-permute-done((bf16[112,1024]{1,0:T(8,128)(2,1)S(1)}, bf16[112,1024]{1,0:T(8,128)(2,1)S(1)}, u32[]{:S(2)}, u32[]{:S(2)}) %collective-permute-start.26) | collective-permute-done | bytes 229408 | tf_op jit(solution)/shard_map/ppermute | solution.py:468
  155.5 3.3 %collective-permute-start.28 = (f32[32,1024]{1,0:T(8,128)S(1)}, f32[32,1024]{1,0:T(8,128)S(1)}, u32[]{:S(2)}, u32[]{:S(2)}) collective-permute-start(f32[32,1024]{1,0:T(8,128)S(1)} %get-tuple-element.124), channel_id=1, source_target_pairs={{0,2},{1,3},{2,0},{3,1},{4,6},{5,7},{6,4},{7,5},{8,10},{9,11},{10,... | collective-permute-start | bytes 393224 | tf_op jit(solution)/shard_map/ppermute | solution.py:478
  159.8 2.4 %collective-permute-done.28 = f32[32,1024]{1,0:T(8,128)S(1)} collective-permute-done((f32[32,1024]{1,0:T(8,128)S(1)}, f32[32,1024]{1,0:T(8,128)S(1)}, u32[]{:S(2)}, u32[]{:S(2)}) %collective-permute-start.28) | collective-permute-done | bytes 131104 | tf_op jit(solution)/shard_map/ppermute | solution.py:478
  162.2 2.8 %collective-permute-done.29 = f32[32,1024]{1,0:T(8,128)S(1)} collective-permute-done((f32[32,1024]{1,0:T(8,128)S(1)}, f32[32,1024]{1,0:T(8,128)S(1)}, u32[]{:S(2)}, u32[]{:S(2)}) %collective-permute-start.29) | collective-permute-done | bytes 131104 | tf_op jit(solution)/shard_map/ppermute | solution.py:478
  165.1 3.2 %collective-permute-start.31 = (f32[32,1024]{1,0:T(8,128)S(1)}, f32[32,1024]{1,0:T(8,128)S(1)}, u32[]{:S(2)}, u32[]{:S(2)}) collective-permute-start(f32[32,1024]{1,0:T(8,128)S(1)} %add_add_fusion.1), channel_id=1, source_target_pairs={{0,64},{1,65},{2,66},{3,67},{4,68},{5,69},{6,70},{7,71},{8,72},{9,... | collective-permute-start | bytes 393224 | tf_op jit(solution)/shard_map/ppermute | solution.py:478
  168.3 1.6 collective-permute-start.30
  169.8 5.1 %collective-permute-done.31 = f32[32,1024]{1,0:T(8,128)S(1)} collective-permute-done((f32[32,1024]{1,0:T(8,128)S(1)}, f32[32,1024]{1,0:T(8,128)S(1)}, u32[]{:S(2)}, u32[]{:S(2)}) %collective-permute-start.31) | collective-permute-done | bytes 131104 | tf_op jit(solution)/shard_map/ppermute | solution.py:478
  174.9 2.7 %collective-permute-done.32 = f32[32,1024]{1,0:T(8,128)S(1)} collective-permute-done((f32[32,1024]{1,0:T(8,128)S(1)}, f32[32,1024]{1,0:T(8,128)S(1)}, u32[]{:S(2)}, u32[]{:S(2)}) %collective-permute-start.32) | collective-permute-done | bytes 131104 | tf_op jit(solution)/shard_map/ppermute | solution.py:478
  177.7 7.0 %collective-permute-start.33 = (f32[32,1024]{1,0:T(8,128)S(1)}, f32[32,1024]{1,0:T(8,128)S(1)}, u32[]{:S(2)}, u32[]{:S(2)}) collective-permute-start(f32[32,1024]{1,0:T(8,128)S(1)} %add_add_fusion), channel_id=1, source_target_pairs={{0,128},{1,129},{2,130},{3,131},{4,132},{5,133},{6,134},{7,135},{8... | collective-permute-start | bytes 393224 | tf_op jit(solution)/shard_map/ppermute | solution.py:478
  184.6 5.7 %collective-permute-done.33 = f32[32,1024]{1,0:T(8,128)S(1)} collective-permute-done((f32[32,1024]{1,0:T(8,128)S(1)}, f32[32,1024]{1,0:T(8,128)S(1)}, u32[]{:S(2)}, u32[]{:S(2)}) %collective-permute-start.33) | collective-permute-done | bytes 131104 | tf_op jit(solution)/shard_map/ppermute | solution.py:478
  192.3 2.8 %collective-permute-done.34 = f32[24,1024]{1,0:T(8,128)} collective-permute-done((f32[24,1024]{1,0:T(8,128)S(1)}, f32[24,1024]{1,0:T(8,128)}, u32[]{:S(2)}, u32[]{:S(2)}) %collective-permute-start.34) | collective-permute-done | bytes 98336 | tf_op jit(solution)/shard_map/ppermute | solution.py:478
  196.1 1.8 shard_map.120
  (107 shorter events, 23.4 us)
Async XLA Ops:
  7.2 67.5 %all-gather.2.cloned.1.call-start = ((), (), s32[]{:S(2)}) async-start(), calls=%async_computation | async-start | bytes 1671168 | tf_op jit(solution)/shard_map/all_gather | solution.py:487
  7.2 24.0 %collective-permute-start.3 = (bf16[64,4096]{1,0:T(8,128)(2,1)}, bf16[64,4096]{1,0:T(8,128)(2,1)S(1)}, u32[]{:S(2)}, u32[]{:S(2)}) collective-permute-start(bf16[64,4096]{1,0:T(8,128)(2,1)} %bitcast.31), channel_id=1, source_target_pairs={{0,2},{1,3},{2,0},{3,1},{4,6},{5,7},{6,4},{7,5},{8,10},{9,11},{10,... | collective-permute-start | bytes 1572872 | tf_op jit(solution)/shard_map/ppermute | solution.py:468
  13.7 12.9 %copy-start.8 = (bf16[256,768]{1,0:T(8,128)(2,1)}, bf16[256,768]{1,0:T(8,128)(2,1)S(1)}, u32[]{:S(2)}) copy-start(bf16[256,768]{1,0:T(8,128)(2,1)S(1)} %pad_maximum_fusion.9.refs_3_) | copy-start | bytes 1179652
  13.7 12.9 %collective-permute-start = (bf16[256,768]{1,0:T(8,128)(2,1)S(1)}, bf16[256,768]{1,0:T(8,128)(2,1)}, u32[]{:S(2)}, u32[]{:S(2)}) collective-permute-start(bf16[256,768]{1,0:T(8,128)(2,1)S(1)} %pad_maximum_fusion.9.refs_3_), channel_id=1, source_target_pairs={{0,4},{1,5},{2,6},{3,7},{4,8},{5,9},{6,10},{7,11},{8,12},{9,13},{1... | collective-permute-start | bytes 1179656 | tf_op jit(solution)/shard_map/ppermute | solution.py:471
  15.4 11.3 %collective-permute-start.1 = (bf16[256,768]{1,0:T(8,128)(2,1)S(1)}, bf16[256,768]{1,0:T(8,128)(2,1)}, u32[]{:S(2)}, u32[]{:S(2)}) collective-permute-start(bf16[256,768]{1,0:T(8,128)(2,1)S(1)} %pad_maximum_fusion.9.refs_3_), channel_id=1, source_target_pairs={{0,12},{1,13},{2,14},{3,15},{4,0},{5,1},{6,2},{7,3},{8,4},{9,5},{1... | collective-permute-start | bytes 1179656 | tf_op jit(solution)/shard_map/ppermute | solution.py:471
  17.1 14.2 %collective-permute-start.2 = (bf16[256,768]{1,0:T(8,128)(2,1)S(1)}, bf16[256,768]{1,0:T(8,128)(2,1)}, u32[]{:S(2)}, u32[]{:S(2)}) collective-permute-start(bf16[256,768]{1,0:T(8,128)(2,1)S(1)} %pad_maximum_fusion.8), channel_id=1, source_target_pairs={{0,18},{1,19},{2,16},{3,17},{4,22},{5,23},{6,20},{7,21},{8,26},{9,... | collective-permute-start | bytes 1179656 | tf_op jit(solution)/shard_map/ppermute | solution.py:478
  18.2 13.0 %copy-start.6 = (bf16[1,64,4096]{2,1,0:T(8,128)(2,1)S(1)}, bf16[1,64,4096]{2,1,0:T(8,128)(2,1)}, u32[]{:S(2)}) copy-start(bf16[1,64,4096]{2,1,0:T(8,128)(2,1)} %param.10) | copy-start | bytes 1572868
  31.2 23.9 %copy-start.7 = (bf16[64,4096]{1,0:T(8,128)(2,1)}, bf16[64,4096]{1,0:T(8,128)(2,1)S(1)}, u32[]{:S(2)}) copy-start(bf16[64,4096]{1,0:T(8,128)(2,1)S(1)} %collective-permute-done.3.refs_1_) | copy-start | bytes 1572868
  31.3 18.4 %collective-permute-start.8 = (bf16[128,4096]{1,0:T(8,128)(2,1)S(1)}, bf16[128,4096]{1,0:T(8,128)(2,1)S(1)}, u32[]{:S(2)}, u32[]{:S(2)}) collective-permute-start(bf16[128,4096]{1,0:T(8,128)(2,1)S(1)} %pad_maximum_fusion), channel_id=1, source_target_pairs={{0,1},{1,0},{2,3},{3,2},{4,5},{5,4},{6,7},{7,6},{8,9},{9,8},{10,11... | collective-permute-start | bytes 3145736 | tf_op jit(solution)/shard_map/ppermute | solution.py:468
  31.4 18.3 %collective-permute-start.6 = (bf16[256,768]{1,0:T(8,128)(2,1)}, bf16[256,768]{1,0:T(8,128)(2,1)S(1)}, u32[]{:S(2)}, u32[]{:S(2)}) collective-permute-start(bf16[256,768]{1,0:T(8,128)(2,1)} %collective-permute-done.2.refs_4_), channel_id=1, source_target_pairs={{0,4},{1,5},{2,6},{3,7},{4,8},{5,9},{6,10},{7,11},{8,12},{9,13},{1... | collective-permute-start | bytes 1179656 | tf_op jit(solution)/shard_map/ppermute | solution.py:471
  33.1 16.7 %collective-permute-start.7 = (bf16[256,768]{1,0:T(8,128)(2,1)}, bf16[256,768]{1,0:T(8,128)(2,1)}, u32[]{:S(2)}, u32[]{:S(2)}) collective-permute-start(bf16[256,768]{1,0:T(8,128)(2,1)} %collective-permute-done.2.refs_4_), channel_id=1, source_target_pairs={{0,12},{1,13},{2,14},{3,15},{4,0},{5,1},{6,2},{7,3},{8,4},{9,5},{1... | collective-permute-start | bytes 1179656 | tf_op jit(solution)/shard_map/ppermute | solution.py:471
  38.4 11.3 %collective-permute-start.4 = (bf16[128,768]{1,0:T(8,128)(2,1)S(1)}, bf16[128,768]{1,0:T(8,128)(2,1)S(1)}, u32[]{:S(2)}, u32[]{:S(2)}) collective-permute-start(bf16[128,768]{1,0:T(8,128)(2,1)S(1)} %slice.36), channel_id=1, source_target_pairs={{0,4},{1,5},{2,6},{3,7},{4,8},{5,9},{6,10},{7,11},{8,12},{9,13},{1... | collective-permute-start | bytes 589832 | tf_op jit(solution)/shard_map/ppermute | solution.py:471
  39.8 9.9 %collective-permute-start.5 = (bf16[128,768]{1,0:T(8,128)(2,1)S(1)}, bf16[128,768]{1,0:T(8,128)(2,1)S(1)}, u32[]{:S(2)}, u32[]{:S(2)}) collective-permute-start(bf16[128,768]{1,0:T(8,128)(2,1)S(1)} %slice.37), channel_id=1, source_target_pairs={{0,12},{1,13},{2,14},{3,15},{4,0},{5,1},{6,2},{7,3},{8,4},{9,5},{1... | collective-permute-start | bytes 589832 | tf_op jit(solution)/shard_map/ppermute | solution.py:471
  49.7 9.7 %copy-start.13 = (bf16[128,768]{1,0:T(8,128)(2,1)}, bf16[128,768]{1,0:T(8,128)(2,1)S(1)}, u32[]{:S(2)}) copy-start(bf16[128,768]{1,0:T(8,128)(2,1)S(1)} %collective-permute-done.4.refs_9_) | copy-start | bytes 589828
  49.7 9.6 %copy-start.14 = (bf16[128,768]{1,0:T(8,128)(2,1)}, bf16[128,768]{1,0:T(8,128)(2,1)S(1)}, u32[]{:S(2)}) copy-start(bf16[128,768]{1,0:T(8,128)(2,1)S(1)} %collective-permute-done.5.refs_10_) | copy-start | bytes 589828
  49.8 9.6 %copy-start.11 = (bf16[256,768]{1,0:T(8,128)(2,1)}, bf16[256,768]{1,0:T(8,128)(2,1)S(1)}, u32[]{:S(2)}) copy-start(bf16[256,768]{1,0:T(8,128)(2,1)S(1)} %collective-permute-done.6.refs_6_) | copy-start | bytes 1179652
  49.8 9.6 %copy-start.10 = (bf16[128,4096]{1,0:T(8,128)(2,1)}, bf16[128,4096]{1,0:T(8,128)(2,1)S(1)}, u32[]{:S(2)}) copy-start(bf16[128,4096]{1,0:T(8,128)(2,1)S(1)} %collective-permute-done.8.refs_2_) | copy-start | bytes 3145732
  49.8 8.7 %collective-permute-start.9 = (bf16[128,768]{1,0:T(8,128)(2,1)S(1)}, bf16[128,768]{1,0:T(8,128)(2,1)S(1)}, u32[]{:S(2)}, u32[]{:S(2)}) collective-permute-start(bf16[128,768]{1,0:T(8,128)(2,1)S(1)} %slice.38), channel_id=1, source_target_pairs={{0,4},{1,5},{2,6},{3,7},{4,8},{5,9},{6,10},{7,11},{8,12},{9,13},{1... | collective-permute-start | bytes 589832 | tf_op jit(solution)/shard_map/ppermute | solution.py:471
  52.4 7.0 %collective-permute-start.10 = (bf16[128,768]{1,0:T(8,128)(2,1)S(1)}, bf16[128,768]{1,0:T(8,128)(2,1)S(1)}, u32[]{:S(2)}, u32[]{:S(2)}) collective-permute-start(bf16[128,768]{1,0:T(8,128)(2,1)S(1)} %slice.39), channel_id=1, source_target_pairs={{0,12},{1,13},{2,14},{3,15},{4,0},{5,1},{6,2},{7,3},{8,4},{9,5},{1... | collective-permute-start | bytes 589832 | tf_op jit(solution)/shard_map/ppermute | solution.py:471
  56.1 2.3 %collective-permute-start.11 = (bf16[40,2304]{1,0:T(8,128)(2,1)S(1)}, bf16[40,2304]{1,0:T(8,128)(2,1)S(1)}, u32[]{:S(2)}, u32[]{:S(2)}) collective-permute-start(bf16[40,2304]{1,0:T(8,128)(2,1)S(1)} %pad_maximum_fusion.11), channel_id=1, source_target_pairs={{0,1},{1,2},{2,3},{3,4},{4,5},{5,6},{6,7},{7,8},{8,9},{9,10},{10,1... | collective-permute-start | bytes 552968 | tf_op jit(solution)/shard_map/ppermute | solution.py:524
  58.5 14.3 %copy-start.17 = (bf16[40,2304]{1,0:T(8,128)(2,1)}, bf16[40,2304]{1,0:T(8,128)(2,1)S(1)}, u32[]{:S(2)}) copy-start(bf16[40,2304]{1,0:T(8,128)(2,1)S(1)} %collective-permute-done.11) | copy-start | bytes 552964
  66.1 6.7 %collective-permute-start.12 = (f32[4,64,384]{2,1,0:T(8,128)}, f32[4,64,384]{2,1,0:T(8,128)S(1)}, u32[]{:S(2)}, u32[]{:S(2)}) collective-permute-start(f32[4,64,384]{2,1,0:T(8,128)} %get-tuple-element.96), channel_id=1, source_target_pairs={{0,1},{1,0},{2,3},{3,2},{4,5},{5,4},{6,7},{7,6},{8,9},{9,8},{10,11... | collective-permute-start | bytes 1179656 | tf_op jit(solution)/shard_map/ppermute | solution.py:468
  72.8 15.1 %copy-start.1 = (bf16[1536,1024]{1,0:T(8,128)(2,1)S(1)}, bf16[1536,1024]{1,0:T(8,128)(2,1)}, u32[]{:S(2)}) copy-start(bf16[1536,1024]{1,0:T(8,128)(2,1)} %disc_ref.1) | copy-start | bytes 9437188
  74.7 10.6 %collective-permute-start.16 = (bf16[40,2304]{1,0:T(8,128)(2,1)S(1)}, bf16[40,2304]{1,0:T(8,128)(2,1)}, u32[]{:S(2)}, u32[]{:S(2)}) collective-permute-start(bf16[40,2304]{1,0:T(8,128)(2,1)S(1)} %pad_maximum_fusion.12), channel_id=1, source_target_pairs={{1,0},{2,1},{3,2},{4,3},{5,4},{6,5},{7,6},{8,7},{9,8},{10,9},{11,1... | collective-permute-start | bytes 552968 | tf_op jit(solution)/shard_map/ppermute | solution.py:552
  76.0 11.9 %copy-start.9 = (bf16[1,256,1536]{2,1,0:T(8,128)(2,1)S(1)}, bf16[1,256,1536]{2,1,0:T(8,128)(2,1)}, u32[]{:S(2)}) copy-start(bf16[1,256,1536]{2,1,0:T(8,128)(2,1)} %param.13) | copy-start | bytes 2359300
  76.0 11.9 %copy-start.18 = (bf16[40,2304]{1,0:T(8,128)(2,1)S(1)}, bf16[40,2304]{1,0:T(8,128)(2,1)}, u32[]{:S(2)}) copy-start(bf16[40,2304]{1,0:T(8,128)(2,1)} %copy-done.17) | copy-start | bytes 552964
  76.1 16.2 %collective-permute-start.13 = (f32[256,384]{1,0:T(8,128)}, f32[256,384]{1,0:T(8,128)S(1)}, u32[]{:S(2)}, u32[]{:S(2)}) collective-permute-start(f32[256,384]{1,0:T(8,128)} %bitcast.25), channel_id=1, source_target_pairs={{0,4},{1,5},{2,6},{3,7},{4,8},{5,9},{6,10},{7,11},{8,12},{9,13},{1... | collective-permute-start | bytes 1179656 | tf_op jit(solution)/shard_map/ppermute | solution.py:471
  82.3 18.0 %collective-permute-start.14 = (f32[256,384]{1,0:T(8,128)}, f32[256,384]{1,0:T(8,128)S(1)}, u32[]{:S(2)}, u32[]{:S(2)}) collective-permute-start(f32[256,384]{1,0:T(8,128)} %bitcast.26), channel_id=1, source_target_pairs={{0,8},{1,9},{2,10},{3,11},{4,12},{5,13},{6,14},{7,15},{8,0},{9,1},... | collective-permute-start | bytes 1179656 | tf_op jit(solution)/shard_map/ppermute | solution.py:471
  83.8 16.5 %collective-permute-start.15 = (f32[256,384]{1,0:T(8,128)}, f32[256,384]{1,0:T(8,128)S(1)}, u32[]{:S(2)}, u32[]{:S(2)}) collective-permute-start(f32[256,384]{1,0:T(8,128)} %bitcast.27), channel_id=1, source_target_pairs={{0,12},{1,13},{2,14},{3,15},{4,0},{5,1},{6,2},{7,3},{8,4},{9,5},{1... | collective-permute-start | bytes 1179656 | tf_op jit(solution)/shard_map/ppermute | solution.py:471
  86.6 13.8 %copy-start.3 = (f32[4,64,384]{2,1,0:T(8,128)S(1)}, f32[4,64,384]{2,1,0:T(8,128)}, u32[]{:S(2)}) copy-start(f32[4,64,384]{2,1,0:T(8,128)} %add.166) | copy-start | bytes 1179652
  86.6 13.8 %collective-permute-start.17 = (bf16[336,384]{1,0:T(8,128)(2,1)S(1)}, bf16[336,384]{1,0:T(8,128)(2,1)S(1)}, u32[]{:S(2)}, u32[]{:S(2)}) collective-permute-start(bf16[336,384]{1,0:T(8,128)(2,1)S(1)} %get-tuple-element.134), channel_id=1, source_target_pairs={{0,2},{1,3},{2,0},{3,1},{4,6},{5,7},{6,4},{7,5},{8,10},{9,11},{10,... | collective-permute-start | bytes 774152 | tf_op jit(solution)/shard_map/ppermute | solution.py:468
  100.4 1.8 collective-permute-start.18
  100.5 2.3 %collective-permute-start.19 = (f32[256,384]{1,0:T(8,128)S(1)}, f32[256,384]{1,0:T(8,128)S(1)}, u32[]{:S(2)}, u32[]{:S(2)}) collective-permute-start(f32[256,384]{1,0:T(8,128)S(1)} %collective-permute-done.13.refs_1_), channel_id=1, source_target_pairs={{0,1},{1,0},{2,3},{3,2},{4,5},{5,4},{6,7},{7,6},{8,9},{9,8},{10,11... | collective-permute-start | bytes 1179656 | tf_op jit(solution)/shard_map/ppermute | solution.py:468
  101.0 2.3 %collective-permute-start.20 = (f32[256,384]{1,0:T(8,128)S(1)}, f32[256,384]{1,0:T(8,128)S(1)}, u32[]{:S(2)}, u32[]{:S(2)}) collective-permute-start(f32[256,384]{1,0:T(8,128)S(1)} %collective-permute-done.14.refs_2_), channel_id=1, source_target_pairs={{0,1},{1,0},{2,3},{3,2},{4,5},{5,4},{6,7},{7,6},{8,9},{9,8},{10,11... | collective-permute-start | bytes 1179656 | tf_op jit(solution)/shard_map/ppermute | solution.py:468
  101.1 2.8 %collective-permute-start.21 = (f32[256,384]{1,0:T(8,128)S(1)}, f32[256,384]{1,0:T(8,128)S(1)}, u32[]{:S(2)}, u32[]{:S(2)}) collective-permute-start(f32[256,384]{1,0:T(8,128)S(1)} %collective-permute-done.15.refs_3_), channel_id=1, source_target_pairs={{0,1},{1,0},{2,3},{3,2},{4,5},{5,4},{6,7},{7,6},{8,9},{9,8},{10,11... | collective-permute-start | bytes 1179656 | tf_op jit(solution)/shard_map/ppermute | solution.py:468
  109.5 11.2 %collective-permute-start.22 = (bf16[336,384]{1,0:T(8,128)(2,1)S(1)}, bf16[336,384]{1,0:T(8,128)(2,1)S(1)}, u32[]{:S(2)}, u32[]{:S(2)}) collective-permute-start(bf16[336,384]{1,0:T(8,128)(2,1)S(1)} %shard_map.116), channel_id=1, source_target_pairs={{0,2},{1,3},{2,0},{3,1},{4,6},{5,7},{6,4},{7,5},{8,10},{9,11},{10,... | collective-permute-start | bytes 774152 | tf_op jit(solution)/shard_map/ppermute | solution.py:468
  133.6 2.9 %collective-permute-start.23 = (bf16[400,1024]{1,0:T(8,128)(2,1)}, bf16[400,1024]{1,0:T(8,128)(2,1)S(1)}, u32[]{:S(2)}, u32[]{:S(2)}) collective-permute-start(bf16[400,1024]{1,0:T(8,128)(2,1)} %get-tuple-element.116), channel_id=1, source_target_pairs={{0,1},{1,0},{2,3},{3,2},{4,5},{5,4},{6,7},{7,6},{8,9},{9,8},{10,11... | collective-permute-start | bytes 2457608 | tf_op jit(solution)/shard_map/ppermute | solution.py:468
  139.4 8.5 %collective-permute-start.24 = (bf16[112,1024]{1,0:T(8,128)(2,1)S(1)}, bf16[112,1024]{1,0:T(8,128)(2,1)S(1)}, u32[]{:S(2)}, u32[]{:S(2)}) collective-permute-start(bf16[112,1024]{1,0:T(8,128)(2,1)S(1)} %get-tuple-element.119), channel_id=1, source_target_pairs={{0,4},{1,5},{2,6},{3,7},{4,0},{5,1},{6,2},{7,3},{8,12},{9,13},{10,... | collective-permute-start | bytes 688136 | tf_op jit(solution)/shard_map/ppermute | solution.py:468
  140.1 12.1 %collective-permute-start.25 = (bf16[112,1024]{1,0:T(8,128)(2,1)S(1)}, bf16[112,1024]{1,0:T(8,128)(2,1)S(1)}, u32[]{:S(2)}, u32[]{:S(2)}) collective-permute-start(bf16[112,1024]{1,0:T(8,128)(2,1)S(1)} %get-tuple-element.120), channel_id=1, source_target_pairs={{0,8},{1,9},{2,10},{3,11},{4,12},{5,13},{6,14},{7,15},{8,0},{9,1},... | collective-permute-start | bytes 688136 | tf_op jit(solution)/shard_map/ppermute | solution.py:468
  141.6 13.2 %collective-permute-start.26 = (bf16[112,1024]{1,0:T(8,128)(2,1)S(1)}, bf16[112,1024]{1,0:T(8,128)(2,1)S(1)}, u32[]{:S(2)}, u32[]{:S(2)}) collective-permute-start(bf16[112,1024]{1,0:T(8,128)(2,1)S(1)} %get-tuple-element.121), channel_id=1, source_target_pairs={{0,12},{1,13},{2,14},{3,15},{4,8},{5,9},{6,10},{7,11},{8,4},{9,5},... | collective-permute-start | bytes 688136 | tf_op jit(solution)/shard_map/ppermute | solution.py:468
  155.5 6.7 %collective-permute-start.28 = (f32[32,1024]{1,0:T(8,128)S(1)}, f32[32,1024]{1,0:T(8,128)S(1)}, u32[]{:S(2)}, u32[]{:S(2)}) collective-permute-start(f32[32,1024]{1,0:T(8,128)S(1)} %get-tuple-element.124), channel_id=1, source_target_pairs={{0,2},{1,3},{2,0},{3,1},{4,6},{5,7},{6,4},{7,5},{8,10},{9,11},{10,... | collective-permute-start | bytes 393224 | tf_op jit(solution)/shard_map/ppermute | solution.py:478
  158.8 6.2 %collective-permute-start.29 = (f32[32,1024]{1,0:T(8,128)S(1)}, f32[32,1024]{1,0:T(8,128)S(1)}, u32[]{:S(2)}, u32[]{:S(2)}) collective-permute-start(f32[32,1024]{1,0:T(8,128)S(1)} %get-tuple-element.125), channel_id=1, source_target_pairs={{0,18},{1,19},{2,16},{3,17},{4,22},{5,23},{6,20},{7,21},{8,26},{9,... | collective-permute-start | bytes 393224 | tf_op jit(solution)/shard_map/ppermute | solution.py:478
  159.8 5.3 %collective-permute-start.27 = (f32[32,1024]{1,0:T(8,128)S(1)}, f32[32,1024]{1,0:T(8,128)S(1)}, u32[]{:S(2)}, u32[]{:S(2)}) collective-permute-start(f32[32,1024]{1,0:T(8,128)S(1)} %get-tuple-element.123), channel_id=1, source_target_pairs={{0,16},{1,17},{2,18},{3,19},{4,20},{5,21},{6,22},{7,23},{8,24},{9,... | collective-permute-start | bytes 393224 | tf_op jit(solution)/shard_map/ppermute | solution.py:478
  165.1 9.8 %collective-permute-start.31 = (f32[32,1024]{1,0:T(8,128)S(1)}, f32[32,1024]{1,0:T(8,128)S(1)}, u32[]{:S(2)}, u32[]{:S(2)}) collective-permute-start(f32[32,1024]{1,0:T(8,128)S(1)} %add_add_fusion.1), channel_id=1, source_target_pairs={{0,64},{1,65},{2,66},{3,67},{4,68},{5,69},{6,70},{7,71},{8,72},{9,... | collective-permute-start | bytes 393224 | tf_op jit(solution)/shard_map/ppermute | solution.py:478
  168.3 9.3 %collective-permute-start.32 = (f32[32,1024]{1,0:T(8,128)S(1)}, f32[32,1024]{1,0:T(8,128)S(1)}, u32[]{:S(2)}, u32[]{:S(2)}) collective-permute-start(f32[32,1024]{1,0:T(8,128)S(1)} %add_add_fusion.1), channel_id=1, source_target_pairs={{0,96},{1,97},{2,98},{3,99},{4,100},{5,101},{6,102},{7,103},{8,104... | collective-permute-start | bytes 393224 | tf_op jit(solution)/shard_map/ppermute | solution.py:478
  168.3 9.3 %collective-permute-start.30 = (f32[32,1024]{1,0:T(8,128)S(1)}, f32[32,1024]{1,0:T(8,128)S(1)}, u32[]{:S(2)}, u32[]{:S(2)}) collective-permute-start(f32[32,1024]{1,0:T(8,128)S(1)} %add_add_fusion.1), channel_id=1, source_target_pairs={{0,32},{1,33},{2,34},{3,35},{4,36},{5,37},{6,38},{7,39},{8,40},{9,... | collective-permute-start | bytes 393224 | tf_op jit(solution)/shard_map/ppermute | solution.py:478
  177.7 12.6 %collective-permute-start.33 = (f32[32,1024]{1,0:T(8,128)S(1)}, f32[32,1024]{1,0:T(8,128)S(1)}, u32[]{:S(2)}, u32[]{:S(2)}) collective-permute-start(f32[32,1024]{1,0:T(8,128)S(1)} %add_add_fusion), channel_id=1, source_target_pairs={{0,128},{1,129},{2,130},{3,131},{4,132},{5,133},{6,134},{7,135},{8... | collective-permute-start | bytes 393224 | tf_op jit(solution)/shard_map/ppermute | solution.py:478
  190.3 4.8 %collective-permute-start.34 = (f32[24,1024]{1,0:T(8,128)S(1)}, f32[24,1024]{1,0:T(8,128)}, u32[]{:S(2)}, u32[]{:S(2)}) collective-permute-start(f32[24,1024]{1,0:T(8,128)S(1)} %slice.48), channel_id=1, source_target_pairs={{0,16},{1,17},{2,18},{3,19},{4,20},{5,21},{6,22},{7,23},{8,24},{9,... | collective-permute-start | bytes 294920 | tf_op jit(solution)/shard_map/ppermute | solution.py:478
  (10 other events, 30.9 us)
Sparse Core Ops, SparseCore 0:
  18.3 52.8 all-gather.1

commit v8 on v5

--- a/solution.py
+++ b/solution.py
@@ -318,7 +318,7 @@
     for copy in conv_copies:
         copy.wait()
 
-    @pl.loop(0, tiles, unroll=2)
+    @pl.loop(0, tiles, unroll=4)
     def _(tile):
         lanes = pl.ds(pl.multiple_of(tile * 128, 128), 128)
         phase = [feed_s[tile, pl.ds(b, rows, stride=STRIDE), :] for b in range(STRIDE)]
@@ -362,7 +362,7 @@
     contract = (((1,), (1,)), ((), ()))
     low_back = low_lanes((own_out, 128))
 
-    @pl.loop(0, tiles, unroll=2)
+    @pl.loop(0, tiles, unroll=4)
     def _(tile):
         lanes = pl.ds(pl.multiple_of(tile * 128, 128), 128)
         turned_s[...] = roll_half(grad_s[:, lanes])

time: 201 us -> 200 us (level)
  no operation moved by 1% of the time
where the time goes in v8:
time: 200 us; the launch traced here: 199 us
  waiting for transfers between devices  69.7 us (35%)
  starting transfers between devices  49.7 us (25%)
  Pallas kernels  40.9 us (20%)
  between operations  16.9 us (8%)
  local copies, waits for them, and re-layouts  9.83 us (5%)
  matrix products  6.53 us (3%)
  other arithmetic  5.72 us (3%)
    ppermute x9, waiting for transfers between devices, turn(): lax.ppermute(x, 'seq', [(i, (i + 4 * hops) % seq_size) for i in range(seq...  26.9 us
    ppermute x9, waiting for transfers between devices, swap(): return lax.ppermute(x, ('dp', 'seq'), pairs)  21.6 us
    ppermute x13, waiting for transfers between devices, flip(): return lax.ppermute(x, 'seq', [(i, i ^ bit) for i in range(seq_size)])  21.1 us
    ppermute x9, starting transfers between devices, swap(): return lax.ppermute(x, ('dp', 'seq'), pairs)  16.5 us
    ppermute x13, starting transfers between devices, flip(): return lax.ppermute(x, 'seq', [(i, i ^ bit) for i in range(seq_size)])  14.5 us
    ppermute x9, starting transfers between devices, turn(): lax.ppermute(x, 'seq', [(i, (i + 4 * hops) % seq_size) for i in range(seq...  14.3 us
    pallas_call x1, Pallas kernels, critic(): pl.pallas_call(critic_kernel, in_specs=[smem()] + [anywhere()] * 5 + [vme...  12.2 us
    pallas_call x2, Pallas kernels, attend(): pl.pallas_call(attend_kernel, grid=(width // HEAD_DIM,), in_specs=[smem()...  11.3 us
  transfers between devices with their start and end apart: 34, of which 23 were waited for; matrix products, arithmetic and copies ran while one was open for 8% of the time, Pallas kernels for 10%

profile of v8, /device:TPU:32, one launch (start us, length us, event | category | flops | bytes accessed | tf_op | source)
XLA Modules:
  0.0 199.2 jit_solution(8336945283264357831)
XLA Ops:
  7.2 3.1 %collective-permute-start.4 = (bf16[64,4096]{1,0:T(8,128)(2,1)}, bf16[64,4096]{1,0:T(8,128)(2,1)S(1)}, u32[]{:S(2)}, u32[]{:S(2)}) collective-permute-start(bf16[64,4096]{1,0:T(8,128)(2,1)} %bitcast.31), channel_id=1, source_target_pairs={{0,2},{1,3},{2,0},{3,1},{4,6},{5,7},{6,4},{7,5},{8,10},{9,11},{10,... | collective-permute-start | bytes 1572872 | tf_op jit(solution)/shard_map/ppermute | solution.py:459
  10.3 3.2 %convolution_convert_fusion = bf16[48,1024]{1,0:T(8,128)(2,1)} fusion(bf16[48,1536]{1,0:T(8,128)(2,1)S(1)} %copy-done, bf16[1536,1024]{1,0:T(8,128)(2,1)} %disc_ref.1), kind=kOutput, calls=%fused_computation | convolution fusion | flops 151044096 | bytes 3391488 | tf_op jit(solution)/shard_map/dot_general | solution.py:476
  13.8 1.7 collective-permute-start
  15.5 1.7 collective-permute-start.1
  17.2 2.0 collective-permute-start.2
  19.1 1.1 collective-permute-start.3
  21.0 1.2 stack.80.meta_ref
  23.6 2.4 %collective-permute-done.refs_5_ = bf16[256,768]{1,0:T(8,128)(2,1)S(1)} collective-permute-done((bf16[256,768]{1,0:T(8,128)(2,1)S(1)}, bf16[256,768]{1,0:T(8,128)(2,1)S(1)}, u32[]{:S(2)}, u32[]{:S(2)}) %collective-permute-start) | collective-permute-done | bytes 393248 | tf_op jit(solution)/shard_map/ppermute | solution.py:462
  26.0 3.2 %collective-permute-done.1.refs_7_ = bf16[256,768]{1,0:T(8,128)(2,1)S(1)} collective-permute-done((bf16[256,768]{1,0:T(8,128)(2,1)S(1)}, bf16[256,768]{1,0:T(8,128)(2,1)S(1)}, u32[]{:S(2)}, u32[]{:S(2)}) %collective-permute-start.1) | collective-permute-done | bytes 393248 | tf_op jit(solution)/shard_map/ppermute | solution.py:462
  29.3 6.8 %collective-permute-done.2.refs_9_ = bf16[256,768]{1,0:T(8,128)(2,1)S(1)} collective-permute-done((bf16[256,768]{1,0:T(8,128)(2,1)S(1)}, bf16[256,768]{1,0:T(8,128)(2,1)S(1)}, u32[]{:S(2)}, u32[]{:S(2)}) %collective-permute-start.2) | collective-permute-done | bytes 393248 | tf_op jit(solution)/shard_map/ppermute | solution.py:462
  36.1 1.2 collective-permute-start.5
  37.3 2.1 %collective-permute-start.6 = (bf16[256,768]{1,0:T(8,128)(2,1)}, bf16[256,768]{1,0:T(8,128)(2,1)S(1)}, u32[]{:S(2)}, u32[]{:S(2)}) collective-permute-start(bf16[256,768]{1,0:T(8,128)(2,1)} %collective-permute-done.3.refs_4_), channel_id=1, source_target_pairs={{0,12},{1,13},{2,14},{3,15},{4,0},{5,1},{6,2},{7,3},{8,4},{9,5},{1... | collective-permute-start | bytes 1179656 | tf_op jit(solution)/shard_map/ppermute | solution.py:462
  41.6 3.1 %collective-permute-start.9 = (bf16[40,2304]{1,0:T(8,128)(2,1)S(1)}, bf16[40,2304]{1,0:T(8,128)(2,1)}, u32[]{:S(2)}, u32[]{:S(2)}) collective-permute-start(bf16[40,2304]{1,0:T(8,128)(2,1)S(1)} %pad_maximum_fusion.11), channel_id=1, source_target_pairs={{0,1},{1,2},{2,3},{3,4},{4,5},{5,6},{6,7},{7,8},{8,9},{9,10},{10,1... | collective-permute-start | bytes 552968 | tf_op jit(solution)/shard_map/ppermute | solution.py:506
  44.6 8.4 %shard_map.113.conv_hbm = bf16[16,256,768]{2,1,0:T(8,128)(2,1)} custom-call(bf16[41,64,1024]{2,1,0:T(8,128)(2,1)} %w_ref), custom_call_target="tpu_custom_call" | custom-call | flops 20000000 | bytes 20000000 | tf_op jit(solution)/shard_map/pallas_call | solution.py:69
  53.1 3.0 %collective-permute-done.6.refs_8_ = bf16[256,768]{1,0:T(8,128)(2,1)S(1)} collective-permute-done((bf16[256,768]{1,0:T(8,128)(2,1)}, bf16[256,768]{1,0:T(8,128)(2,1)S(1)}, u32[]{:S(2)}, u32[]{:S(2)}) %collective-permute-start.6) | collective-permute-done | bytes 393248 | tf_op jit(solution)/shard_map/ppermute | solution.py:462
  56.2 2.4 %collective-permute-done.7.refs_10_ = bf16[256,768]{1,0:T(8,128)(2,1)S(1)} collective-permute-done((bf16[256,768]{1,0:T(8,128)(2,1)}, bf16[256,768]{1,0:T(8,128)(2,1)S(1)}, u32[]{:S(2)}, u32[]{:S(2)}) %collective-permute-start.7) | collective-permute-done | bytes 393248 | tf_op jit(solution)/shard_map/ppermute | solution.py:462
  60.4 5.9 %shard_map.114 = (f32[4,64,384]{2,1,0:T(8,128)}, f32[4,64,384]{2,1,0:T(8,128)}) custom-call(s32[9]{0:T(128)} %stack.73.cols_ref, bf16[64,4096]{1,0:T(8,128)(2,1)} %bitcast.32, bf16[64,4096]{1,0:T(8,128)(2,1)} %copy-done.7, bf16[128,4096]{1,0:T(8,128)(2,1)} %copy-done.10, bf16[256,768]{1,0:T(8,128)(2,1)} %copy-done.8, ...), custom_call_target="tpu_custom_call" | custom-call | flops 800000000 | bytes 6000000 | tf_op jit(solution)/shard_map/pallas_call | solution.py:118
  66.4 1.9 collective-permute-done.10
  68.3 1.9 add.166
  70.2 1.3 collective-permute-start.14
  71.5 1.8 collective-permute-start.11
  73.3 2.0 collective-permute-start.12
  75.3 1.9 collective-permute-start.13
  78.4 3.4 %collective-permute-start.15 = (bf16[336,384]{1,0:T(8,128)(2,1)S(1)}, bf16[336,384]{1,0:T(8,128)(2,1)S(1)}, u32[]{:S(2)}, u32[]{:S(2)}) collective-permute-start(bf16[336,384]{1,0:T(8,128)(2,1)S(1)} %get-tuple-element.120), channel_id=1, source_target_pairs={{0,2},{1,3},{2,0},{3,1},{4,6},{5,7},{6,4},{7,5},{8,10},{9,11},{10,... | collective-permute-start | bytes 774152 | tf_op jit(solution)/shard_map/ppermute | solution.py:459
  81.8 3.3 %fusion.lifted_hbm = f32[336,1024]{1,0:T(8,128)} fusion(bf16[1536,1024]{1,0:T(8,128)(2,1)S(1)} %copy-done.1, bf16[40,2304]{1,0:T(8,128)(2,1)} %collective-permute-done.14, bf16[40,2304]{1,0:T(8,128)(2,1)} %collective-permute-done.9, bf16[256,1536]{1,0:T(8,128)(2,1)S(1)} %bitcast.36, bf16[256,768]{1,0:T(8,128)(2,1)} %bitcast.39), kind=kOutput, calls=%fused_computation.3 | convolution fusion | flops 1061093376 | bytes 6070272 | tf_op jit(solution)/shard_map/dot_general | solution.py:539
  85.2 8.3 %collective-permute-done.12.refs_2_ = f32[256,384]{1,0:T(8,128)S(1)} collective-permute-done((f32[256,384]{1,0:T(8,128)}, f32[256,384]{1,0:T(8,128)S(1)}, u32[]{:S(2)}, u32[]{:S(2)}) %collective-permute-start.12) | collective-permute-done | bytes 393248 | tf_op jit(solution)/shard_map/ppermute | solution.py:462
  97.6 5.6 %shard_map.116 = bf16[336,384]{1,0:T(8,128)(2,1)S(1)} custom-call(s32[4]{0:T(128)S(1)} %pad_add_fusion.meta_ref, bf16[336,384]{1,0:T(8,128)(2,1)S(1)} %collective-permute-done.15.q_ref, f32[256,384]{1,0:T(8,128)S(1)} %bitcast.29, f32[256,384]{1,0:T(8,128)S(1)} %collective-permute-done.11.refs_1_, f32[256,384]{1,0:T(8,128)S(1)} %collective-permute-done.12.refs_2_, ...), custom_call_target="tpu_custom_call" | custom-call | flops 1056964608 | bytes 4000000 | tf_op jit(solution)/shard_map/pallas_call | solution.py:175
  103.3 1.9 collective-permute-start.20
  105.2 5.6 %shard_map.115.mine_hbm = bf16[336,384]{1,0:T(8,128)(2,1)S(1)} custom-call(s32[4]{0:T(128)S(1)} %pad_add_fusion.meta_ref, bf16[336,384]{1,0:T(8,128)(2,1)S(1)} %get-tuple-element.93.q_ref, f32[256,384]{1,0:T(8,128)S(1)} %bitcast.30, f32[256,384]{1,0:T(8,128)S(1)} %collective-permute-done.11.refs_1_, f32[256,384]{1,0:T(8,128)S(1)} %collective-permute-done.12.refs_2_, ...), custom_call_target="tpu_custom_call" | custom-call | flops 1056964608 | bytes 4000000 | tf_op jit(solution)/shard_map/pallas_call | solution.py:175
  111.5 1.6 collective-permute-done.20.other_hbm
  113.9 12.2 %shard_map.117 = (f32[8,48,1024]{2,1,0:T(8,128)}, bf16[400,1024]{1,0:T(8,128)(2,1)}, f32[8,1024]{1,0:T(8,128)}) custom-call(s32[5]{0:T(128)} %stack.80.meta_ref, f32[336,1024]{1,0:T(8,128)} %fusion.lifted_hbm, bf16[336,384]{1,0:T(8,128)(2,1)} %copy-done.5, bf16[336,384]{1,0:T(8,128)(2,1)} %copy-done.20, ...), custom_call_target="tpu_custom_call" | custom-call | flops 3000000000 | bytes 14000000 | tf_op jit(solution)/shard_map/pallas_call | solution.py:415
  126.1 2.5 %collective-permute-done.21.arrived_ref = bf16[400,1024]{1,0:T(8,128)(2,1)S(1)} collective-permute-done((bf16[400,1024]{1,0:T(8,128)(2,1)}, bf16[400,1024]{1,0:T(8,128)(2,1)S(1)}, u32[]{:S(2)}, u32[]{:S(2)}) %collective-permute-start.21) | collective-permute-done | bytes 819232 | tf_op jit(solution)/shard_map/ppermute | solution.py:459
  128.7 1.4 copy-done.2
  131.5 1.7 collective-permute-start.22
  133.2 2.5 %collective-permute-start.23 = (bf16[112,1024]{1,0:T(8,128)(2,1)S(1)}, bf16[112,1024]{1,0:T(8,128)(2,1)S(1)}, u32[]{:S(2)}, u32[]{:S(2)}) collective-permute-start(bf16[112,1024]{1,0:T(8,128)(2,1)S(1)} %get-tuple-element.106), channel_id=1, source_target_pairs={{0,8},{1,9},{2,10},{3,11},{4,12},{5,13},{6,14},{7,15},{8,0},{9,1},... | collective-permute-start | bytes 688136 | tf_op jit(solution)/shard_map/ppermute | solution.py:459
  136.3 3.7 %collective-permute-done.22.one_ref = bf16[112,1024]{1,0:T(8,128)(2,1)S(1)} collective-permute-done((bf16[112,1024]{1,0:T(8,128)(2,1)S(1)}, bf16[112,1024]{1,0:T(8,128)(2,1)S(1)}, u32[]{:S(2)}, u32[]{:S(2)}) %collective-permute-start.22) | collective-permute-done | bytes 229408 | tf_op jit(solution)/shard_map/ppermute | solution.py:459
  140.1 6.3 %collective-permute-done.23.two_ref = bf16[112,1024]{1,0:T(8,128)(2,1)S(1)} collective-permute-done((bf16[112,1024]{1,0:T(8,128)(2,1)S(1)}, bf16[112,1024]{1,0:T(8,128)(2,1)S(1)}, u32[]{:S(2)}, u32[]{:S(2)}) %collective-permute-start.23) | collective-permute-done | bytes 229408 | tf_op jit(solution)/shard_map/ppermute | solution.py:459
  146.3 2.6 %collective-permute-done.24.three_ref = bf16[112,1024]{1,0:T(8,128)(2,1)S(1)} collective-permute-done((bf16[112,1024]{1,0:T(8,128)(2,1)S(1)}, bf16[112,1024]{1,0:T(8,128)(2,1)S(1)}, u32[]{:S(2)}, u32[]{:S(2)}) %collective-permute-start.24) | collective-permute-done | bytes 229408 | tf_op jit(solution)/shard_map/ppermute | solution.py:459
  150.2 2.4 %collective-permute-start.27 = (f32[32,1024]{1,0:T(8,128)S(1)}, f32[32,1024]{1,0:T(8,128)S(1)}, u32[]{:S(2)}, u32[]{:S(2)}) collective-permute-start(f32[32,1024]{1,0:T(8,128)S(1)} %get-tuple-element.111), channel_id=1, source_target_pairs={{0,18},{1,19},{2,16},{3,17},{4,22},{5,23},{6,20},{7,21},{8,26},{9,... | collective-permute-start | bytes 393224 | tf_op jit(solution)/shard_map/ppermute | solution.py:469
  153.4 3.6 %collective-permute-done.26 = f32[32,1024]{1,0:T(8,128)S(1)} collective-permute-done((f32[32,1024]{1,0:T(8,128)S(1)}, f32[32,1024]{1,0:T(8,128)S(1)}, u32[]{:S(2)}, u32[]{:S(2)}) %collective-permute-start.26) | collective-permute-done | bytes 131104 | tf_op jit(solution)/shard_map/ppermute | solution.py:469
  158.2 3.6 %collective-permute-start.29 = (f32[32,1024]{1,0:T(8,128)S(1)}, f32[32,1024]{1,0:T(8,128)S(1)}, u32[]{:S(2)}, u32[]{:S(2)}) collective-permute-start(f32[32,1024]{1,0:T(8,128)S(1)} %add_add_fusion.1), channel_id=1, source_target_pairs={{0,64},{1,65},{2,66},{3,67},{4,68},{5,69},{6,70},{7,71},{8,72},{9,... | collective-permute-start | bytes 393224 | tf_op jit(solution)/shard_map/ppermute | solution.py:469
  161.8 1.6 collective-permute-start.28
  163.4 5.3 %collective-permute-done.29 = f32[32,1024]{1,0:T(8,128)S(1)} collective-permute-done((f32[32,1024]{1,0:T(8,128)S(1)}, f32[32,1024]{1,0:T(8,128)S(1)}, u32[]{:S(2)}, u32[]{:S(2)}) %collective-permute-start.29) | collective-permute-done | bytes 131104 | tf_op jit(solution)/shard_map/ppermute | solution.py:469
  168.7 2.7 %collective-permute-done.30 = f32[32,1024]{1,0:T(8,128)S(1)} collective-permute-done((f32[32,1024]{1,0:T(8,128)S(1)}, f32[32,1024]{1,0:T(8,128)S(1)}, u32[]{:S(2)}, u32[]{:S(2)}) %collective-permute-start.30) | collective-permute-done | bytes 131104 | tf_op jit(solution)/shard_map/ppermute | solution.py:469
  171.4 5.8 %collective-permute-start.31 = (f32[32,1024]{1,0:T(8,128)S(1)}, f32[32,1024]{1,0:T(8,128)S(1)}, u32[]{:S(2)}, u32[]{:S(2)}) collective-permute-start(f32[32,1024]{1,0:T(8,128)S(1)} %add_add_fusion), channel_id=1, source_target_pairs={{0,128},{1,129},{2,130},{3,131},{4,132},{5,133},{6,134},{7,135},{8... | collective-permute-start | bytes 393224 | tf_op jit(solution)/shard_map/ppermute | solution.py:469
  177.3 6.4 %collective-permute-done.31 = f32[32,1024]{1,0:T(8,128)S(1)} collective-permute-done((f32[32,1024]{1,0:T(8,128)S(1)}, f32[32,1024]{1,0:T(8,128)S(1)}, u32[]{:S(2)}, u32[]{:S(2)}) %collective-permute-start.31) | collective-permute-done | bytes 131104 | tf_op jit(solution)/shard_map/ppermute | solution.py:469
  186.0 2.5 %collective-permute-done.32 = f32[24,1024]{1,0:T(8,128)} collective-permute-done((f32[24,1024]{1,0:T(8,128)S(1)}, f32[24,1024]{1,0:T(8,128)}, u32[]{:S(2)}, u32[]{:S(2)}) %collective-permute-start.32) | collective-permute-done | bytes 98336 | tf_op jit(solution)/shard_map/ppermute | solution.py:469
  189.4 1.8 shard_map.120
  (97 shorter events, 20.6 us)
Async XLA Ops:
  7.2 3.2 %copy-start = (bf16[48,1536]{1,0:T(8,128)(2,1)S(1)}, bf16[48,1536]{1,0:T(8,128)(2,1)}, u32[]{:S(2)}) copy-start(bf16[48,1536]{1,0:T(8,128)(2,1)} %param.14) | copy-start | bytes 442372
  7.2 6.4 %copy-start.11 = (bf16[256,1536]{1,0:T(8,128)(2,1)S(1)}, bf16[256,1536]{1,0:T(8,128)(2,1)}, u32[]{:S(2)}) copy-start(bf16[256,1536]{1,0:T(8,128)(2,1)} %param.11) | copy-start | bytes 2359300
  7.2 63.0 %all-gather.2.cloned.1.call-start = ((), (), s32[]{:S(2)}) async-start(), calls=%async_computation | async-start | bytes 1671168 | tf_op jit(solution)/shard_map/all_gather | solution.py:478
  7.2 28.9 %collective-permute-start.4 = (bf16[64,4096]{1,0:T(8,128)(2,1)}, bf16[64,4096]{1,0:T(8,128)(2,1)S(1)}, u32[]{:S(2)}, u32[]{:S(2)}) collective-permute-start(bf16[64,4096]{1,0:T(8,128)(2,1)} %bitcast.31), channel_id=1, source_target_pairs={{0,2},{1,3},{2,0},{3,1},{4,6},{5,7},{6,4},{7,5},{8,10},{9,11},{10,... | collective-permute-start | bytes 1572872 | tf_op jit(solution)/shard_map/ppermute | solution.py:459
  13.5 6.7 %copy-start.18 = (s32[16]{0:T(128)S(1)}, s32[16]{0:T(128)}, u32[]{:S(2)}) copy-start(s32[16]{0:T(128)} %param.18) | copy-start | bytes 196
  13.5 6.7 %copy-start.19 = (s32[16]{0:T(128)S(1)}, s32[16]{0:T(128)}, u32[]{:S(2)}) copy-start(s32[16]{0:T(128)} %param.19) | copy-start | bytes 196
  13.5 25.9 %copy-start.6 = (bf16[1,64,4096]{2,1,0:T(8,128)(2,1)S(1)}, bf16[1,64,4096]{2,1,0:T(8,128)(2,1)}, u32[]{:S(2)}) copy-start(bf16[1,64,4096]{2,1,0:T(8,128)(2,1)} %param.10) | copy-start | bytes 1572868
  13.8 39.2 %copy-start.8 = (bf16[256,768]{1,0:T(8,128)(2,1)}, bf16[256,768]{1,0:T(8,128)(2,1)S(1)}, u32[]{:S(2)}) copy-start(bf16[256,768]{1,0:T(8,128)(2,1)S(1)} %pad_maximum_fusion.9.refs_3_) | copy-start | bytes 1179652
  13.8 12.2 %collective-permute-start = (bf16[256,768]{1,0:T(8,128)(2,1)S(1)}, bf16[256,768]{1,0:T(8,128)(2,1)S(1)}, u32[]{:S(2)}, u32[]{:S(2)}) collective-permute-start(bf16[256,768]{1,0:T(8,128)(2,1)S(1)} %pad_maximum_fusion.9.refs_3_), channel_id=1, source_target_pairs={{0,4},{1,5},{2,6},{3,7},{4,8},{5,9},{6,10},{7,11},{8,12},{9,13},{1... | collective-permute-start | bytes 1179656 | tf_op jit(solution)/shard_map/ppermute | solution.py:462
  15.5 13.8 %collective-permute-start.1 = (bf16[256,768]{1,0:T(8,128)(2,1)S(1)}, bf16[256,768]{1,0:T(8,128)(2,1)S(1)}, u32[]{:S(2)}, u32[]{:S(2)}) collective-permute-start(bf16[256,768]{1,0:T(8,128)(2,1)S(1)} %pad_maximum_fusion.9.refs_3_), channel_id=1, source_target_pairs={{0,12},{1,13},{2,14},{3,15},{4,0},{5,1},{6,2},{7,3},{8,4},{9,5},{1... | collective-permute-start | bytes 1179656 | tf_op jit(solution)/shard_map/ppermute | solution.py:462
  17.2 18.9 %collective-permute-start.2 = (bf16[256,768]{1,0:T(8,128)(2,1)S(1)}, bf16[256,768]{1,0:T(8,128)(2,1)S(1)}, u32[]{:S(2)}, u32[]{:S(2)}) collective-permute-start(bf16[256,768]{1,0:T(8,128)(2,1)S(1)} %pad_maximum_fusion.9.refs_3_), channel_id=1, source_target_pairs={{0,8},{1,9},{2,10},{3,11},{4,12},{5,13},{6,14},{7,15},{8,0},{9,1},... | collective-permute-start | bytes 1179656 | tf_op jit(solution)/shard_map/ppermute | solution.py:462
  19.1 17.0 %collective-permute-start.3 = (bf16[256,768]{1,0:T(8,128)(2,1)S(1)}, bf16[256,768]{1,0:T(8,128)(2,1)}, u32[]{:S(2)}, u32[]{:S(2)}) collective-permute-start(bf16[256,768]{1,0:T(8,128)(2,1)S(1)} %pad_maximum_fusion.8), channel_id=1, source_target_pairs={{0,18},{1,19},{2,16},{3,17},{4,22},{5,23},{6,20},{7,21},{8,26},{9,... | collective-permute-start | bytes 1179656 | tf_op jit(solution)/shard_map/ppermute | solution.py:469
  26.0 27.0 %copy-start.12 = (bf16[256,768]{1,0:T(8,128)(2,1)}, bf16[256,768]{1,0:T(8,128)(2,1)S(1)}, u32[]{:S(2)}) copy-start(bf16[256,768]{1,0:T(8,128)(2,1)S(1)} %collective-permute-done.refs_5_) | copy-start | bytes 1179652
  29.3 10.2 %copy-start.13 = (bf16[256,768]{1,0:T(8,128)(2,1)}, bf16[256,768]{1,0:T(8,128)(2,1)S(1)}, u32[]{:S(2)}) copy-start(bf16[256,768]{1,0:T(8,128)(2,1)S(1)} %collective-permute-done.1.refs_7_) | copy-start | bytes 1179652
  36.1 3.3 %copy-start.14 = (bf16[256,768]{1,0:T(8,128)(2,1)}, bf16[256,768]{1,0:T(8,128)(2,1)S(1)}, u32[]{:S(2)}) copy-start(bf16[256,768]{1,0:T(8,128)(2,1)S(1)} %collective-permute-done.2.refs_9_) | copy-start | bytes 1179652
  36.1 17.0 %copy-start.7 = (bf16[64,4096]{1,0:T(8,128)(2,1)}, bf16[64,4096]{1,0:T(8,128)(2,1)S(1)}, u32[]{:S(2)}) copy-start(bf16[64,4096]{1,0:T(8,128)(2,1)S(1)} %collective-permute-done.4.refs_1_) | copy-start | bytes 1572868
  36.1 17.0 %collective-permute-start.5 = (bf16[256,768]{1,0:T(8,128)(2,1)}, bf16[256,768]{1,0:T(8,128)(2,1)S(1)}, u32[]{:S(2)}, u32[]{:S(2)}) collective-permute-start(bf16[256,768]{1,0:T(8,128)(2,1)} %collective-permute-done.3.refs_4_), channel_id=1, source_target_pairs={{0,4},{1,5},{2,6},{3,7},{4,8},{5,9},{6,10},{7,11},{8,12},{9,13},{1... | collective-permute-start | bytes 1179656 | tf_op jit(solution)/shard_map/ppermute | solution.py:462
  37.3 18.8 %collective-permute-start.6 = (bf16[256,768]{1,0:T(8,128)(2,1)}, bf16[256,768]{1,0:T(8,128)(2,1)S(1)}, u32[]{:S(2)}, u32[]{:S(2)}) collective-permute-start(bf16[256,768]{1,0:T(8,128)(2,1)} %collective-permute-done.3.refs_4_), channel_id=1, source_target_pairs={{0,12},{1,13},{2,14},{3,15},{4,0},{5,1},{6,2},{7,3},{8,4},{9,5},{1... | collective-permute-start | bytes 1179656 | tf_op jit(solution)/shard_map/ppermute | solution.py:462
  39.4 19.1 %collective-permute-start.7 = (bf16[256,768]{1,0:T(8,128)(2,1)}, bf16[256,768]{1,0:T(8,128)(2,1)S(1)}, u32[]{:S(2)}, u32[]{:S(2)}) collective-permute-start(bf16[256,768]{1,0:T(8,128)(2,1)} %collective-permute-done.3.refs_4_), channel_id=1, source_target_pairs={{0,8},{1,9},{2,10},{3,11},{4,12},{5,13},{6,14},{7,15},{8,0},{9,1},... | collective-permute-start | bytes 1179656 | tf_op jit(solution)/shard_map/ppermute | solution.py:462
  39.6 19.0 %collective-permute-start.8 = (bf16[128,4096]{1,0:T(8,128)(2,1)S(1)}, bf16[128,4096]{1,0:T(8,128)(2,1)S(1)}, u32[]{:S(2)}, u32[]{:S(2)}) collective-permute-start(bf16[128,4096]{1,0:T(8,128)(2,1)S(1)} %pad_maximum_fusion), channel_id=1, source_target_pairs={{0,1},{1,0},{2,3},{3,2},{4,5},{5,4},{6,7},{7,6},{8,9},{9,8},{10,11... | collective-permute-start | bytes 3145736 | tf_op jit(solution)/shard_map/ppermute | solution.py:459
  41.6 11.5 %collective-permute-start.9 = (bf16[40,2304]{1,0:T(8,128)(2,1)S(1)}, bf16[40,2304]{1,0:T(8,128)(2,1)}, u32[]{:S(2)}, u32[]{:S(2)}) collective-permute-start(bf16[40,2304]{1,0:T(8,128)(2,1)S(1)} %pad_maximum_fusion.11), channel_id=1, source_target_pairs={{0,1},{1,2},{2,3},{3,4},{4,5},{5,6},{6,7},{7,8},{8,9},{9,10},{10,1... | collective-permute-start | bytes 552968 | tf_op jit(solution)/shard_map/ppermute | solution.py:506
  53.1 5.5 %copy-start.15 = (bf16[256,768]{1,0:T(8,128)(2,1)}, bf16[256,768]{1,0:T(8,128)(2,1)S(1)}, u32[]{:S(2)}) copy-start(bf16[256,768]{1,0:T(8,128)(2,1)S(1)} %collective-permute-done.5.refs_6_) | copy-start | bytes 1179652
  66.3 2.0 %collective-permute-start.10 = (f32[4,64,384]{2,1,0:T(8,128)}, f32[4,64,384]{2,1,0:T(8,128)S(1)}, u32[]{:S(2)}, u32[]{:S(2)}) collective-permute-start(f32[4,64,384]{2,1,0:T(8,128)} %get-tuple-element.82), channel_id=1, source_target_pairs={{0,1},{1,0},{2,3},{3,2},{4,5},{5,4},{6,7},{7,6},{8,9},{9,8},{10,11... | collective-permute-start | bytes 1179656 | tf_op jit(solution)/shard_map/ppermute | solution.py:459
  68.3 13.6 %copy-start.1 = (bf16[1536,1024]{1,0:T(8,128)(2,1)S(1)}, bf16[1536,1024]{1,0:T(8,128)(2,1)}, u32[]{:S(2)}) copy-start(bf16[1536,1024]{1,0:T(8,128)(2,1)} %disc_ref.1) | copy-start | bytes 9437188
  70.2 7.0 %collective-permute-start.14 = (bf16[40,2304]{1,0:T(8,128)(2,1)S(1)}, bf16[40,2304]{1,0:T(8,128)(2,1)}, u32[]{:S(2)}, u32[]{:S(2)}) collective-permute-start(bf16[40,2304]{1,0:T(8,128)(2,1)S(1)} %pad_maximum_fusion.12), channel_id=1, source_target_pairs={{1,0},{2,1},{3,2},{4,3},{5,4},{6,5},{7,6},{8,7},{9,8},{10,9},{11,1... | collective-permute-start | bytes 552968 | tf_op jit(solution)/shard_map/ppermute | solution.py:535
  71.5 10.3 %copy-start.9 = (bf16[1,256,1536]{2,1,0:T(8,128)(2,1)S(1)}, bf16[1,256,1536]{2,1,0:T(8,128)(2,1)}, u32[]{:S(2)}) copy-start(bf16[1,256,1536]{2,1,0:T(8,128)(2,1)} %param.13) | copy-start | bytes 2359300
  71.5 13.7 %collective-permute-start.11 = (f32[256,384]{1,0:T(8,128)}, f32[256,384]{1,0:T(8,128)S(1)}, u32[]{:S(2)}, u32[]{:S(2)}) collective-permute-start(f32[256,384]{1,0:T(8,128)} %bitcast.25), channel_id=1, source_target_pairs={{0,4},{1,5},{2,6},{3,7},{4,8},{5,9},{6,10},{7,11},{8,12},{9,13},{1... | collective-permute-start | bytes 1179656 | tf_op jit(solution)/shard_map/ppermute | solution.py:462
  73.3 20.1 %collective-permute-start.12 = (f32[256,384]{1,0:T(8,128)}, f32[256,384]{1,0:T(8,128)S(1)}, u32[]{:S(2)}, u32[]{:S(2)}) collective-permute-start(f32[256,384]{1,0:T(8,128)} %bitcast.26), channel_id=1, source_target_pairs={{0,8},{1,9},{2,10},{3,11},{4,12},{5,13},{6,14},{7,15},{8,0},{9,1},... | collective-permute-start | bytes 1179656 | tf_op jit(solution)/shard_map/ppermute | solution.py:462
  75.3 18.9 %collective-permute-start.13 = (f32[256,384]{1,0:T(8,128)}, f32[256,384]{1,0:T(8,128)S(1)}, u32[]{:S(2)}, u32[]{:S(2)}) collective-permute-start(f32[256,384]{1,0:T(8,128)} %bitcast.27), channel_id=1, source_target_pairs={{0,12},{1,13},{2,14},{3,15},{4,0},{5,1},{6,2},{7,3},{8,4},{9,5},{1... | collective-permute-start | bytes 1179656 | tf_op jit(solution)/shard_map/ppermute | solution.py:462
  78.4 15.8 %copy-start.3 = (f32[4,64,384]{2,1,0:T(8,128)S(1)}, f32[4,64,384]{2,1,0:T(8,128)}, u32[]{:S(2)}) copy-start(f32[4,64,384]{2,1,0:T(8,128)} %add.166) | copy-start | bytes 1179652
  78.4 15.8 %collective-permute-start.15 = (bf16[336,384]{1,0:T(8,128)(2,1)S(1)}, bf16[336,384]{1,0:T(8,128)(2,1)S(1)}, u32[]{:S(2)}, u32[]{:S(2)}) collective-permute-start(bf16[336,384]{1,0:T(8,128)(2,1)S(1)} %get-tuple-element.120), channel_id=1, source_target_pairs={{0,2},{1,3},{2,0},{3,1},{4,6},{5,7},{6,4},{7,5},{8,10},{9,11},{10,... | collective-permute-start | bytes 774152 | tf_op jit(solution)/shard_map/ppermute | solution.py:459
  94.2 1.7 collective-permute-start.16
  94.2 2.3 %collective-permute-start.17 = (f32[256,384]{1,0:T(8,128)S(1)}, f32[256,384]{1,0:T(8,128)S(1)}, u32[]{:S(2)}, u32[]{:S(2)}) collective-permute-start(f32[256,384]{1,0:T(8,128)S(1)} %collective-permute-done.11.refs_1_), channel_id=1, source_target_pairs={{0,1},{1,0},{2,3},{3,2},{4,5},{5,4},{6,7},{7,6},{8,9},{9,8},{10,11... | collective-permute-start | bytes 1179656 | tf_op jit(solution)/shard_map/ppermute | solution.py:459
  94.7 2.3 %collective-permute-start.18 = (f32[256,384]{1,0:T(8,128)S(1)}, f32[256,384]{1,0:T(8,128)S(1)}, u32[]{:S(2)}, u32[]{:S(2)}) collective-permute-start(f32[256,384]{1,0:T(8,128)S(1)} %collective-permute-done.12.refs_2_), channel_id=1, source_target_pairs={{0,1},{1,0},{2,3},{3,2},{4,5},{5,4},{6,7},{7,6},{8,9},{9,8},{10,11... | collective-permute-start | bytes 1179656 | tf_op jit(solution)/shard_map/ppermute | solution.py:459
  94.8 2.8 %collective-permute-start.19 = (f32[256,384]{1,0:T(8,128)S(1)}, f32[256,384]{1,0:T(8,128)S(1)}, u32[]{:S(2)}, u32[]{:S(2)}) collective-permute-start(f32[256,384]{1,0:T(8,128)S(1)} %collective-permute-done.13.refs_3_), channel_id=1, source_target_pairs={{0,1},{1,0},{2,3},{3,2},{4,5},{5,4},{6,7},{7,6},{8,9},{9,8},{10,11... | collective-permute-start | bytes 1179656 | tf_op jit(solution)/shard_map/ppermute | solution.py:459
  103.3 9.9 %collective-permute-start.20 = (bf16[336,384]{1,0:T(8,128)(2,1)S(1)}, bf16[336,384]{1,0:T(8,128)(2,1)S(1)}, u32[]{:S(2)}, u32[]{:S(2)}) collective-permute-start(bf16[336,384]{1,0:T(8,128)(2,1)S(1)} %shard_map.116), channel_id=1, source_target_pairs={{0,2},{1,3},{2,0},{3,1},{4,6},{5,7},{6,4},{7,5},{8,10},{9,11},{10,... | collective-permute-start | bytes 774152 | tf_op jit(solution)/shard_map/ppermute | solution.py:459
  126.0 2.6 %collective-permute-start.21 = (bf16[400,1024]{1,0:T(8,128)(2,1)}, bf16[400,1024]{1,0:T(8,128)(2,1)S(1)}, u32[]{:S(2)}, u32[]{:S(2)}) collective-permute-start(bf16[400,1024]{1,0:T(8,128)(2,1)} %get-tuple-element.102), channel_id=1, source_target_pairs={{0,1},{1,0},{2,3},{3,2},{4,5},{5,4},{6,7},{7,6},{8,9},{9,8},{10,11... | collective-permute-start | bytes 2457608 | tf_op jit(solution)/shard_map/ppermute | solution.py:459
  131.5 8.5 %collective-permute-start.22 = (bf16[112,1024]{1,0:T(8,128)(2,1)S(1)}, bf16[112,1024]{1,0:T(8,128)(2,1)S(1)}, u32[]{:S(2)}, u32[]{:S(2)}) collective-permute-start(bf16[112,1024]{1,0:T(8,128)(2,1)S(1)} %get-tuple-element.105), channel_id=1, source_target_pairs={{0,4},{1,5},{2,6},{3,7},{4,0},{5,1},{6,2},{7,3},{8,12},{9,13},{10,... | collective-permute-start | bytes 688136 | tf_op jit(solution)/shard_map/ppermute | solution.py:459
  133.2 13.1 %collective-permute-start.23 = (bf16[112,1024]{1,0:T(8,128)(2,1)S(1)}, bf16[112,1024]{1,0:T(8,128)(2,1)S(1)}, u32[]{:S(2)}, u32[]{:S(2)}) collective-permute-start(bf16[112,1024]{1,0:T(8,128)(2,1)S(1)} %get-tuple-element.106), channel_id=1, source_target_pairs={{0,8},{1,9},{2,10},{3,11},{4,12},{5,13},{6,14},{7,15},{8,0},{9,1},... | collective-permute-start | bytes 688136 | tf_op jit(solution)/shard_map/ppermute | solution.py:459
  135.7 13.2 %collective-permute-start.24 = (bf16[112,1024]{1,0:T(8,128)(2,1)S(1)}, bf16[112,1024]{1,0:T(8,128)(2,1)S(1)}, u32[]{:S(2)}, u32[]{:S(2)}) collective-permute-start(bf16[112,1024]{1,0:T(8,128)(2,1)S(1)} %get-tuple-element.107), channel_id=1, source_target_pairs={{0,12},{1,13},{2,14},{3,15},{4,8},{5,9},{6,10},{7,11},{8,4},{9,5},... | collective-permute-start | bytes 688136 | tf_op jit(solution)/shard_map/ppermute | solution.py:459
  149.6 7.4 %collective-permute-start.26 = (f32[32,1024]{1,0:T(8,128)S(1)}, f32[32,1024]{1,0:T(8,128)S(1)}, u32[]{:S(2)}, u32[]{:S(2)}) collective-permute-start(f32[32,1024]{1,0:T(8,128)S(1)} %get-tuple-element.110), channel_id=1, source_target_pairs={{0,2},{1,3},{2,0},{3,1},{4,6},{5,7},{6,4},{7,5},{8,10},{9,11},{10,... | collective-permute-start | bytes 393224 | tf_op jit(solution)/shard_map/ppermute | solution.py:469
  150.2 7.9 %collective-permute-start.27 = (f32[32,1024]{1,0:T(8,128)S(1)}, f32[32,1024]{1,0:T(8,128)S(1)}, u32[]{:S(2)}, u32[]{:S(2)}) collective-permute-start(f32[32,1024]{1,0:T(8,128)S(1)} %get-tuple-element.111), channel_id=1, source_target_pairs={{0,18},{1,19},{2,16},{3,17},{4,22},{5,23},{6,20},{7,21},{8,26},{9,... | collective-permute-start | bytes 393224 | tf_op jit(solution)/shard_map/ppermute | solution.py:469
  152.6 5.5 %collective-permute-start.25 = (f32[32,1024]{1,0:T(8,128)S(1)}, f32[32,1024]{1,0:T(8,128)S(1)}, u32[]{:S(2)}, u32[]{:S(2)}) collective-permute-start(f32[32,1024]{1,0:T(8,128)S(1)} %get-tuple-element.109), channel_id=1, source_target_pairs={{0,16},{1,17},{2,18},{3,19},{4,20},{5,21},{6,22},{7,23},{8,24},{9,... | collective-permute-start | bytes 393224 | tf_op jit(solution)/shard_map/ppermute | solution.py:469
  158.2 10.5 %collective-permute-start.29 = (f32[32,1024]{1,0:T(8,128)S(1)}, f32[32,1024]{1,0:T(8,128)S(1)}, u32[]{:S(2)}, u32[]{:S(2)}) collective-permute-start(f32[32,1024]{1,0:T(8,128)S(1)} %add_add_fusion.1), channel_id=1, source_target_pairs={{0,64},{1,65},{2,66},{3,67},{4,68},{5,69},{6,70},{7,71},{8,72},{9,... | collective-permute-start | bytes 393224 | tf_op jit(solution)/shard_map/ppermute | solution.py:469
  161.8 9.6 %collective-permute-start.30 = (f32[32,1024]{1,0:T(8,128)S(1)}, f32[32,1024]{1,0:T(8,128)S(1)}, u32[]{:S(2)}, u32[]{:S(2)}) collective-permute-start(f32[32,1024]{1,0:T(8,128)S(1)} %add_add_fusion.1), channel_id=1, source_target_pairs={{0,96},{1,97},{2,98},{3,99},{4,100},{5,101},{6,102},{7,103},{8,104... | collective-permute-start | bytes 393224 | tf_op jit(solution)/shard_map/ppermute | solution.py:469
  161.8 9.6 %collective-permute-start.28 = (f32[32,1024]{1,0:T(8,128)S(1)}, f32[32,1024]{1,0:T(8,128)S(1)}, u32[]{:S(2)}, u32[]{:S(2)}) collective-permute-start(f32[32,1024]{1,0:T(8,128)S(1)} %add_add_fusion.1), channel_id=1, source_target_pairs={{0,32},{1,33},{2,34},{3,35},{4,36},{5,37},{6,38},{7,39},{8,40},{9,... | collective-permute-start | bytes 393224 | tf_op jit(solution)/shard_map/ppermute | solution.py:469
  171.4 12.2 %collective-permute-start.31 = (f32[32,1024]{1,0:T(8,128)S(1)}, f32[32,1024]{1,0:T(8,128)S(1)}, u32[]{:S(2)}, u32[]{:S(2)}) collective-permute-start(f32[32,1024]{1,0:T(8,128)S(1)} %add_add_fusion), channel_id=1, source_target_pairs={{0,128},{1,129},{2,130},{3,131},{4,132},{5,133},{6,134},{7,135},{8... | collective-permute-start | bytes 393224 | tf_op jit(solution)/shard_map/ppermute | solution.py:469
  183.7 4.8 %collective-permute-start.32 = (f32[24,1024]{1,0:T(8,128)S(1)}, f32[24,1024]{1,0:T(8,128)}, u32[]{:S(2)}, u32[]{:S(2)}) collective-permute-start(f32[24,1024]{1,0:T(8,128)S(1)} %slice.32), channel_id=1, source_target_pairs={{0,16},{1,17},{2,18},{3,19},{4,20},{5,21},{6,22},{7,23},{8,24},{9,... | collective-permute-start | bytes 294920 | tf_op jit(solution)/shard_map/ppermute | solution.py:469
  (7 other events, 7.8 us)
Sparse Core Ops, SparseCore 0:
  13.7 55.7 all-gather.1
